TPU v7x, 256 devices: a whole 4x4x8 slice. The times are simulated.
256 devices in a mesh: lon: 32 (over x_lo, z, core), lat: 8 (over x_hi, y).
Axes of the slice: x: 4 (x_hi: 2, x_lo: 2; x = x_hi * 2 + x_lo), y: 4, z: 8, core: 2. Of those that a mesh axis runs over, the one named last changes fastest.
Arguments:
- cotangent: bfloat16 [1440, 160, 1024], P('lon', None, 'lat'), may hold values from -6 to 6
- winds: bfloat16 [1440, 64, 1024], P('lon', None, 'lat'), may hold values from -0.44921875 to 0.44921875
- filter_ops: bfloat16 [16, 1440, 1440], P('lat', 'lon'), may hold values from -0.3125 to 0.3125
- block_band: int32 [16], replicated, may hold values from 0 to 7, as said below
- block_row: int32 [16], replicated, may hold values from 0 to 127
Outputs:
- adjoint_state: float32 [1440, 160, 1024], P('lon', None, 'lat')
Inputs may be any that keep to these rules, and one draw needn't show every extreme that they name: `block_band`: band 0 and band 8 - 1 each read exactly 5 blocks; the remaining blocks are spread over the other bands as evenly as possible, in an order drawn from the seed.
All inputs are finite; a program needn't handle non-finite values.
Results may differ from a plain program's by a relative error of at most 0.006.
Values may be sent and summed in bfloat16 or wider, within the bound.
No kernel may reach another device: no remote copies, remote signals or barrier semaphores. Data moves between devices by JAX's collectives and lax.ppermute only.
A program may use at most 128 MiB of HBM per device.

v0:
```python
import jax
import jax.numpy as jnp
from jax import lax
from jax.sharding import PartitionSpec as P

VAR = 5
LEV = 32
NSUB = 2


def padded(cells, sides, width, closed):
    for axis, dim in sides:
        count = lax.axis_size(axis)
        ends = count if closed else count - 1
        head = lax.slice_in_dim(cells, 0, width, axis=dim)
        tail = lax.slice_in_dim(cells, cells.shape[dim] - width, cells.shape[dim], axis=dim)
        cells = jnp.concatenate(
            [
                lax.ppermute(tail, axis, [(i, (i + 1) % count) for i in range(ends)]),
                cells,
                lax.ppermute(head, axis, [((i + 1) % count, i) for i in range(ends)]),
            ],
            axis=dim,
        )
    return cells


def rims(values):
    cycle_cells = padded(values, (("lon", 0),), 1, True)
    band_cells = padded(values, (("lat", 2),), 1, False)
    return (cycle_cells, band_cells)


def spread(coef):
    return jnp.tile(coef, (1, VAR, 1))


def filter_rows(slot_ops, picked):
    return lax.psum_scatter(
        jnp.einsum("kji,kjc->ikc", slot_ops, picked, preferred_element_type=jnp.float32),
        "lon",
        scatter_dimension=0,
        tiled=True,
    )


def shards(cotangent, winds, filter_ops, block_band, block_row):
    rows_here = cotangent.shape[2]
    band_total = lax.axis_size("lat")
    band_index = lax.axis_index("lat")
    wind_cycle, wind_band = rims(winds)
    courant_x = winds[:, :LEV, :].astype(jnp.float32)
    west_x = wind_cycle[:-2, :LEV, :].astype(jnp.float32)
    global_rows = band_index * rows_here - 1 + jnp.arange(rows_here + 2, dtype=jnp.int32)
    inside = (global_rows < band_total * rows_here - 1).astype(jnp.float32)[None, None, :]
    courant_y = wind_band[:, LEV:, :].astype(jnp.float32) * inside
    east_coef = spread(jnp.maximum(courant_x, 0.0))
    west_coef = spread(jnp.minimum(west_x, 0.0))
    north_coef = spread(jnp.maximum(courant_y[:, :, 1:-1], 0.0))
    south_coef = spread(jnp.minimum(courant_y[:, :, :-2], 0.0))
    owned_here = block_band == band_index
    row_match = block_row[:, None] == jnp.arange(rows_here, dtype=jnp.int32)[None, :]
    slot_count = filter_ops.shape[0] * (band_total + 2) // 4
    order_rank = jnp.cumsum(owned_here.astype(jnp.int32)) - 1
    chosen = owned_here[None, :] & (
        order_rank[None, :] == jnp.arange(slot_count, dtype=jnp.int32)[:, None]
    )
    chosen_weights = chosen.astype(jnp.bfloat16)
    slot_ops = jnp.einsum(
        "pb,bji->pji",
        chosen_weights,
        lax.all_gather(filter_ops, "lat", axis=0, tiled=True),
        preferred_element_type=jnp.float32,
    ).astype(jnp.bfloat16)
    slot_rows = jnp.einsum("pb,bl->pl", chosen.astype(jnp.float32), row_match.astype(jnp.float32))
    send_weights = slot_rows.astype(jnp.bfloat16)
    adjoint = cotangent.astype(jnp.float32)
    for substep in range(NSUB):
        rounded = adjoint.astype(jnp.bfloat16)
        widened = lax.optimization_barrier(rounded).astype(jnp.float32)
        picked = jnp.einsum(
            "pl,xcl->pxc", send_weights, rounded, preferred_element_type=jnp.float32
        )
        picked = picked.astype(jnp.bfloat16)
        filtered = filter_rows(slot_ops, picked)
        correction = jnp.einsum("kl,xkc->xcl", slot_rows, filtered)
        smoothed = (widened + correction).astype(jnp.bfloat16)
        cycle_cells, band_cells = rims(smoothed)
        centre = lax.optimization_barrier(smoothed).astype(jnp.float32)
        east_side = cycle_cells[2:].astype(jnp.float32)
        west_side = cycle_cells[:-2].astype(jnp.float32)
        north_side = band_cells[:, :, 2:].astype(jnp.float32)
        south_side = band_cells[:, :, :-2].astype(jnp.float32)
        adjoint = (
            centre
            + east_coef * (east_side - centre)
            + west_coef * (centre - west_side)
            + north_coef * (north_side - centre)
            + south_coef * (centre - south_side)
        )
    return adjoint


def solution(mesh):
    return jax.shard_map(
        shards,
        mesh=mesh,
        in_specs=(P("lon", None, "lat"), P("lon", None, "lat"), P("lat", "lon", None), P(), P()),
        out_specs=P("lon", None, "lat"),
        check_vma=False,
    )
```

profile of v0, /device:TPU:2, one launch (start us, length us, event | category | flops | bytes accessed | tf_op | source)
XLA Modules:
  0.0 438.4 jit_solution(5854807081802948387)
XLA Ops:
  6.5 1.7 copy.51
  8.3 0.7 convert_bitcast_fusion
  9.2 0.8 fusion.11
  10.1 2.6 convolution_convert_fusion.1
  12.6 60.5 %all-gather.2.cloned.1.call-done = bf16[16,45,1440]{2,1,0:T(8,128)(2,1)} async-done(((bf16[2,45,1440]{2,1,0:T(8,128)(2,1)}), bf16[16,45,1440]{2,1,0:T(8,128)(2,1)}) %all-gather.2.cloned.1.call-update) | async-done | bytes 2073616 | tf_op jit(solution)/shard_map/all_gather | solution.py:72
  73.1 3.0 fusion.7
  76.1 1.0 copy-done.5
  77.1 3.0 convolution_bitcast_fusion.1
  80.2 9.3 %copy.55 = f32[1440,5,160]{2,1,0:T(8,128)} copy(f32[1440,5,160]{0,2,1:T(8,128)} %convolution_bitcast_fusion.1) | data formatting | bytes 9216000 | tf_op jit(solution)/shard_map/kji,kjc->ikc/transpose | solution.py:40
  89.6 1.0 copy-done.2
  90.6 0.6 slice.84
  91.6 0.4 copy.71
  91.9 1.3 collective-permute-start.4
  93.6 4.5 %collective-permute-start.3 = (bf16[45,64,1]{1,0,2:T(8,128)(2,1)S(1)}, bf16[45,64,1]{1,0,2:T(8,128)(2,1)S(1)}, u32[]{:S(2)}, u32[]{:S(2)}) collective-permute-start(bf16[45,64,1]{1,0,2:T(8,128)(2,1)S(1)} %copy.70), channel_id=1, source_target_pairs={{0,1},{1,2},{2,3},{3,4},{4,5},{5,6},{6,7},{8,9},{9,10},{10,11},{11... | collective-permute-start | bytes 17288 | tf_op jit(solution)/shard_map/ppermute | solution.py:19
  98.2 1.4 collective-permute-done.3
  99.5 0.4 copy.58
  100.0 1.2 copy.59
  101.2 1.5 convert_multiply_fusion
  102.7 1.2 slice_maximum_fusion
  103.8 119.0 %reduce-scatter.3.cloned.1.call-done = f32[45,5,160]{2,1,0:T(8,128)} async-done(((f32[1440,5,160]{2,1,0:T(8,128)}), f32[45,5,160]{2,1,0:T(8,128)}) %reduce-scatter.3.cloned.1.call-update) | async-done | bytes 144016 | tf_op jit(solution)/shard_map/reduce_scatter | solution.py:39
  222.9 2.5 add_convert_fusion.1
  225.4 2.5 fusion.31
  227.9 0.7 collective-permute-start
  228.6 2.9 copy.60
  231.5 2.3 copy.62
  233.8 3.4 collective-permute-start.6
  237.2 1.5 collective-permute-start.5
  238.7 1.3 convert_maximum_fusion
  240.0 3.2 collective-permute-done.5
  243.2 2.6 copy.61
  245.8 1.8 copy.63
  247.6 6.4 %fusion.3 = bf16[45,160,128]{2,1,0:T(8,128)(2,1)S(1)} fusion(bf16[45,160,128]{2,1,0:T(8,128)(2,1)S(1)} %add_convert_fusion.1, bf16[45,160,1]{2,1,0:T(8,128)(2,1)} %copy.63, bf16[45,160,1]{2,1,0:T(8,128)(2,1)} %copy.61, bf16[1,160,128]{2,1,0:T(8,128)(2,1)S(1)} %collective-permute-done.2, bf16[1,160,128]{2,1,0:T(8,128)(2,1)S(1)} %collective-permute-done, ...), kind=kLoop, calls=%fused_computation.23 | loop fusion | flops 27648000 | bytes 6746240 | tf_op jit(solution)/shard_map/convert_element_type | solution.py:79
  254.0 1.2 copy-done
  255.2 1.1 convolution_convert_fusion
  256.3 3.1 convolution_bitcast_fusion
  259.3 9.3 %copy.65 = f32[1440,5,160]{2,1,0:T(8,128)} copy(f32[1440,5,160]{0,2,1:T(8,128)} %convolution_bitcast_fusion) | data formatting | bytes 9216000 | tf_op jit(solution)/shard_map/kji,kjc->ikc/transpose | solution.py:40
  268.7 134.6 %reduce-scatter.5.cloned.1.call-done = f32[45,5,160]{2,1,0:T(8,128)} async-done(((f32[1440,5,160]{2,1,0:T(8,128)}), f32[45,5,160]{2,1,0:T(8,128)}) %reduce-scatter.5.cloned.1.call-update) | async-done | bytes 144016 | tf_op jit(solution)/shard_map/reduce_scatter | solution.py:39
  403.3 2.0 fusion.12
  405.3 0.5 add_convert_fusion
  405.8 0.7 collective-permute-start.7
  406.5 2.5 fusion.29
  409.0 2.3 copy.66
  411.3 1.3 collective-permute-start.9
  412.6 2.3 copy.68
  414.9 5.1 %collective-permute-start.10 = (bf16[45,160,1]{1,0,2:T(8,128)(2,1)S(1)}, bf16[45,160,1]{1,0,2:T(8,128)(2,1)}, u32[]{:S(2)}, u32[]{:S(2)}) collective-permute-start(bf16[45,160,1]{1,0,2:T(8,128)(2,1)S(1)} %copy.68), channel_id=1, source_target_pairs={{0,1},{1,2},{2,3},{3,4},{4,5},{5,6},{6,7},{8,9},{9,10},{10,11},{11... | collective-permute-start | bytes 43208 | tf_op jit(solution)/shard_map/ppermute | solution.py:19
  420.1 1.8 copy.67
  421.9 2.6 copy.69
  424.5 7.4 %fusion.6 = f32[45,160,128]{2,1,0:T(8,128)} fusion(bf16[45,160,128]{2,1,0:T(8,128)(2,1)S(1)} %add_convert_fusion, bf16[45,160,1]{2,1,0:T(8,128)(2,1)} %copy.69, bf16[45,160,1]{2,1,0:T(8,128)(2,1)} %copy.67, bf16[1,160,128]{2,1,0:T(8,128)(2,1)S(1)} %collective-permute-done.8, bf16[1,160,128]{2,1,0:T(8,128)(2,1)S(1)} %collective-permute-done.7, ...), kind=kLoop, calls=%fused_computation.26 | loop fusion | flops 26726400 | bytes 8589440 | tf_op jit(solution)/shard_map/add | solution.py:95
  (37 shorter events, 1.2 us)
Async XLA Ops:
  6.5 66.6 %all-gather.2.cloned.1.call-start = ((), (), s32[]{:S(2)}) async-start(), calls=%async_computation.2 | async-start | bytes 2654208 | tf_op jit(solution)/shard_map/all_gather | solution.py:72
  8.3 214.6 %reduce-scatter.3.cloned.1.call-start = ((), (), s32[]{:S(2)}) async-start(), calls=%async_computation.3 | async-start | bytes 12165120 | tf_op jit(solution)/shard_map/reduce_scatter | solution.py:39
  76.1 1.0 copy-start.5
  89.5 1.1 copy-start.2
  89.5 313.8 %reduce-scatter.5.cloned.1.call-start = ((), (), s32[]{:S(2)}) async-start(), calls=%async_computation.4 | async-start | bytes 12165120 | tf_op jit(solution)/shard_map/reduce_scatter | solution.py:39
  91.2 147.4 %collective-permute-start.1 = (bf16[1,64,128]{2,1,0:T(8,128)(2,1)}, bf16[1,64,128]{2,1,0:T(8,128)(2,1)S(1)}, u32[]{:S(2)}, u32[]{:S(2)}) collective-permute-start(bf16[1,64,128]{2,1,0:T(8,128)(2,1)} %slice.84), channel_id=1, source_target_pairs={{0,8},{8,16},{16,24},{24,32},{32,40},{40,48},{48,56},{56,64},{64,7... | collective-permute-start | bytes 49160 | tf_op jit(solution)/shard_map/ppermute | solution.py:19
  91.9 8.1 %collective-permute-start.4 = (bf16[45,64,1]{1,0,2:T(8,128)(2,1)S(1)}, bf16[45,64,1]{1,0,2:T(8,128)(2,1)S(1)}, u32[]{:S(2)}, u32[]{:S(2)}) collective-permute-start(bf16[45,64,1]{1,0,2:T(8,128)(2,1)S(1)} %copy.71), channel_id=1, source_target_pairs={{1,0},{2,1},{3,2},{4,3},{5,4},{6,5},{7,6},{9,8},{10,9},{11,10},{12... | collective-permute-start | bytes 17288 | tf_op jit(solution)/shard_map/ppermute | solution.py:21
  93.6 5.9 %collective-permute-start.3 = (bf16[45,64,1]{1,0,2:T(8,128)(2,1)S(1)}, bf16[45,64,1]{1,0,2:T(8,128)(2,1)S(1)}, u32[]{:S(2)}, u32[]{:S(2)}) collective-permute-start(bf16[45,64,1]{1,0,2:T(8,128)(2,1)S(1)} %copy.70), channel_id=1, source_target_pairs={{0,1},{1,2},{2,3},{3,4},{4,5},{5,6},{6,7},{8,9},{9,10},{10,11},{11... | collective-permute-start | bytes 17288 | tf_op jit(solution)/shard_map/ppermute | solution.py:19
  227.9 19.6 %collective-permute-start = (bf16[1,160,128]{2,1,0:T(8,128)(2,1)S(1)}, bf16[1,160,128]{2,1,0:T(8,128)(2,1)S(1)}, u32[]{:S(2)}, u32[]{:S(2)}) collective-permute-start(bf16[1,160,128]{2,1,0:T(8,128)(2,1)S(1)} %get-tuple-element.11), channel_id=1, source_target_pairs={{8,0},{16,8},{24,16},{32,24},{40,32},{48,40},{56,48},{64,56},{72,6... | collective-permute-start | bytes 122888 | tf_op jit(solution)/shard_map/ppermute | solution.py:21
  228.6 19.0 %collective-permute-start.2 = (bf16[1,160,128]{2,1,0:T(8,128)(2,1)S(1)}, bf16[1,160,128]{2,1,0:T(8,128)(2,1)S(1)}, u32[]{:S(2)}, u32[]{:S(2)}) collective-permute-start(bf16[1,160,128]{2,1,0:T(8,128)(2,1)S(1)} %get-tuple-element.12), channel_id=1, source_target_pairs={{0,8},{8,16},{16,24},{24,32},{32,40},{40,48},{48,56},{56,64},{64,7... | collective-permute-start | bytes 122888 | tf_op jit(solution)/shard_map/ppermute | solution.py:19
  233.8 12.0 %collective-permute-start.6 = (bf16[45,160,1]{1,0,2:T(8,128)(2,1)S(1)}, bf16[45,160,1]{1,0,2:T(8,128)(2,1)S(1)}, u32[]{:S(2)}, u32[]{:S(2)}) collective-permute-start(bf16[45,160,1]{1,0,2:T(8,128)(2,1)S(1)} %copy.62), channel_id=1, source_target_pairs={{0,1},{1,2},{2,3},{3,4},{4,5},{5,6},{6,7},{8,9},{9,10},{10,11},{11... | collective-permute-start | bytes 43208 | tf_op jit(solution)/shard_map/ppermute | solution.py:19
  237.2 6.0 %collective-permute-start.5 = (bf16[45,160,1]{1,0,2:T(8,128)(2,1)}, bf16[45,160,1]{1,0,2:T(8,128)(2,1)}, u32[]{:S(2)}, u32[]{:S(2)}) collective-permute-start(bf16[45,160,1]{1,0,2:T(8,128)(2,1)} %copy.60), channel_id=1, source_target_pairs={{1,0},{2,1},{3,2},{4,3},{5,4},{6,5},{7,6},{9,8},{10,9},{11,10},{12... | collective-permute-start | bytes 43208 | tf_op jit(solution)/shard_map/ppermute | solution.py:21
  240.0 7.6 %copy-start.3 = (f32[45,32,128]{2,1,0:T(8,128)S(1)}, f32[45,32,128]{2,1,0:T(8,128)}, u32[]{:S(2)}) copy-start(f32[45,32,128]{2,1,0:T(8,128)} %get-tuple-element.16) | copy-start | bytes 2211844
  247.6 8.7 %copy-start.6 = (bf16[5,45,1440]{2,0,1:T(8,128)(2,1)S(1)}, bf16[5,45,1440]{2,0,1:T(8,128)(2,1)}, u32[]{:S(2)}) copy-start(bf16[5,45,1440]{2,0,1:T(8,128)(2,1)} %copy-done.5) | copy-start | bytes 1944004
  254.0 1.2 copy-start
  403.3 2.0 copy-start.1
  405.8 18.6 %collective-permute-start.7 = (bf16[1,160,128]{2,1,0:T(8,128)(2,1)S(1)}, bf16[1,160,128]{2,1,0:T(8,128)(2,1)S(1)}, u32[]{:S(2)}, u32[]{:S(2)}) collective-permute-start(bf16[1,160,128]{2,1,0:T(8,128)(2,1)S(1)} %get-tuple-element.7), channel_id=1, source_target_pairs={{8,0},{16,8},{24,16},{32,24},{40,32},{48,40},{56,48},{64,56},{72,6... | collective-permute-start | bytes 122888 | tf_op jit(solution)/shard_map/ppermute | solution.py:21
  406.5 17.9 %collective-permute-start.8 = (bf16[1,160,128]{2,1,0:T(8,128)(2,1)S(1)}, bf16[1,160,128]{2,1,0:T(8,128)(2,1)S(1)}, u32[]{:S(2)}, u32[]{:S(2)}) collective-permute-start(bf16[1,160,128]{2,1,0:T(8,128)(2,1)S(1)} %get-tuple-element.8), channel_id=1, source_target_pairs={{0,8},{8,16},{16,24},{24,32},{32,40},{40,48},{48,56},{56,64},{64,7... | collective-permute-start | bytes 122888 | tf_op jit(solution)/shard_map/ppermute | solution.py:19
  409.0 15.4 %copy-start.4 = (f32[45,32,128]{2,1,0:T(8,128)S(1)}, f32[45,32,128]{2,1,0:T(8,128)}, u32[]{:S(2)}) copy-start(f32[45,32,128]{2,1,0:T(8,128)} %get-tuple-element.16) | copy-start | bytes 2211844
  411.3 8.7 %collective-permute-start.9 = (bf16[45,160,1]{1,0,2:T(8,128)(2,1)S(1)}, bf16[45,160,1]{1,0,2:T(8,128)(2,1)S(1)}, u32[]{:S(2)}, u32[]{:S(2)}) collective-permute-start(bf16[45,160,1]{1,0,2:T(8,128)(2,1)S(1)} %copy.66), channel_id=1, source_target_pairs={{1,0},{2,1},{3,2},{4,3},{5,4},{6,5},{7,6},{9,8},{10,9},{11,10},{12... | collective-permute-start | bytes 43208 | tf_op jit(solution)/shard_map/ppermute | solution.py:21
  414.9 7.0 %collective-permute-start.10 = (bf16[45,160,1]{1,0,2:T(8,128)(2,1)S(1)}, bf16[45,160,1]{1,0,2:T(8,128)(2,1)}, u32[]{:S(2)}, u32[]{:S(2)}) collective-permute-start(bf16[45,160,1]{1,0,2:T(8,128)(2,1)S(1)} %copy.68), channel_id=1, source_target_pairs={{0,1},{1,2},{2,3},{3,4},{4,5},{5,6},{6,7},{8,9},{9,10},{10,11},{11... | collective-permute-start | bytes 43208 | tf_op jit(solution)/shard_map/ppermute | solution.py:19
Sparse Core Ops, SparseCore 0:
  9.9 63.1 all-gather.1
  89.6 133.1 reduce-scatter.2
  268.8 134.4 reduce-scatter.4
where the time goes:
time: 446 us; the launch traced here: 438 us
  waiting for transfers between devices  319 us (72%)
  local copies, waits for them, and re-layouts  50.6 us (11%)
  other arithmetic  19 us (4%)
  starting transfers between devices  18.6 us (4%)
  matrix products  18.1 us (4%)
  between operations  13.3 us (3%)
    reduce_scatter x2, waiting for transfers between devices, filter_rows(): lax.psum_scatter(jnp.einsum('kji,kjc->ikc', slot_ops, picked, preferred_e...  254 us
    all_gather x1, waiting for transfers between devices, shards(): lax.all_gather(filter_ops, 'lat', axis=0, tiled=True)  60.5 us
    transpose x2, local copies, waits for them, and re-layouts, filter_rows(): jnp.einsum('kji,kjc->ikc', slot_ops, picked, preferred_element_type=jnp.f...  18.7 us
    ppermute x6, starting transfers between devices, padded(): lax.ppermute(tail, axis, [(i, (i + 1) % count) for i in range(ends)])  13.1 us
    slice x6, local copies, waits for them, and re-layouts, padded(): head = lax.slice_in_dim(cells, 0, width, axis=dim)  10.2 us
  transfers between devices with their start and end apart: 14, of which 5 were waited for; matrix products, arithmetic and copies ran while one was open for 9% of the time, Pallas kernels for 0%

commit v1 on v0

v1 whole, which is shorter than its diff:
```python
import functools

import jax
import jax.numpy as jnp
from jax import lax
from jax.experimental import pallas as pl
from jax.experimental.pallas import tpu as pltpu
from jax.sharding import PartitionSpec as P

VAR = 5
LEV = 32
COLS = VAR * LEV
XS = 45
ROWS = 48
LANES = 128
BANDS = 8
NLON = 1440
LON_DEV = 32
TARGETS = 16
BLOCKS = 16
WIRE = 192
PACK = 120

F32 = jnp.float32
BF16 = jnp.bfloat16
VM = pl.BlockSpec(memory_space=pltpu.VMEM)
SM = pl.BlockSpec(memory_space=pltpu.SMEM)


def shape(dims, kind):
    return jax.ShapeDtypeStruct(dims, kind)


def params(mib):
    return pltpu.CompilerParams(vmem_limit_bytes=mib * 2**20)


def iotas(dims):
    return (
        lax.broadcasted_iota(jnp.int32, dims, 0),
        lax.broadcasted_iota(jnp.int32, dims, 1),
    )


def lanes_below(value, limit):
    lane = lax.broadcasted_iota(jnp.int32, value.shape, 1)
    return jnp.where(lane < limit, value, jnp.zeros_like(value))


def dot_nt(a, b):
    return lax.dot_general(a, b, (((1,), (1,)), ((), ())), preferred_element_type=F32)


def dot_tn(a, b):
    return lax.dot_general(a, b, (((0,), (0,)), ((), ())), preferred_element_type=F32)


def slot(block):
    return (block % 2) * BANDS + block // 2


def operator_kernel(core_ref, ops_ref, own_ref, send_ref):
    core = core_ref[0]
    for t in range(TARGETS):
        tiles = []
        for parity in range(2):
            start = XS * (2 * t + parity) - 1
            total = None
            first = max(start, 0) // LANES * LANES
            spans = [(first, min(first + 2 * LANES, NLON))]
            if start < 0:
                spans.append(((NLON - 1) // LANES * LANES, NLON))
            if start + XS + 2 > NLON:
                spans.append((0, LANES))
            for low, high in spans:
                row, lane = iotas((ROWS, high - low))
                wanted = start + row
                wanted = jnp.where(wanted < 0, wanted + NLON, wanted)
                wanted = jnp.where(wanted >= NLON, wanted - NLON, wanted)
                hit = (lane + low == wanted) & (row < XS + 2)
                pick = jnp.where(hit, 1.0, 0.0).astype(BF16)
                window = ops_ref[:, :, low:high].reshape(2 * ROWS, high - low)
                part = dot_nt(pick, window)
                total = part if total is None else total + part
            tiles.append(total)
        rows = slice(ROWS * t, ROWS * (t + 1))
        mine = core == 0
        own_ref[rows, :] = jnp.where(mine, tiles[0], tiles[1]).astype(BF16)
        send_ref[rows, :] = jnp.where(mine, tiles[1], tiles[0]).astype(BF16)


def prepare_operators(core, ops):
    out = shape((TARGETS * ROWS, 2 * ROWS), BF16)
    return pl.pallas_call(
        operator_kernel,
        out_shape=(out, out),
        in_specs=[SM, VM],
        out_specs=(VM, VM),
        compiler_params=params(16),
        name="operators",
    )(core, ops)


def pick_weights(me, band_ref, row_ref):
    sub, lane = iotas((24, LANES))
    target = jnp.full((24, LANES), -1, jnp.int32)
    for block in range(BLOCKS):
        wanted = jnp.where(band_ref[block] == me, row_ref[block], -1)
        target = jnp.where(sub == slot(block), wanted, target)
    target = jnp.where((sub >= 16) & (sub == 15 + me), 0, target)
    target = jnp.where((sub >= 16) & (sub == 17 + me), LANES - 1, target)
    return jnp.where(lane == target, 1.0, 0.0).astype(BF16)


def pack_messages(main_ref, rest_ref, send_ref):
    for d in range(BANDS):
        rest = None
        for e in range(3):
            rows = slice((e * 8 + d) * ROWS, (e * 8 + d + 1) * ROWS)
            send_ref[d, e * ROWS : (e + 1) * ROWS, :] = main_ref[rows, :].astype(BF16)
            piece = rest_ref[rows, :]
            if e < 2:
                piece = lanes_below(piece, LEV)
            if e:
                piece = pltpu.roll(piece, LEV * e, axis=1)
            rest = piece if rest is None else rest + piece
        send_ref[d, 3 * ROWS :, :] = rest.astype(BF16)


def clear(*refs):
    for ref in refs:
        ref[...] = jnp.zeros(ref.shape, ref.dtype)


def pick_kernel(me_ref, band_ref, row_ref, cells_ref, winds_ref, send_ref, east_ref, west_ref, main_ref, rest_ref):
    clear(main_ref, rest_ref)
    weights = pick_weights(me_ref[0], band_ref, row_ref)
    blank = jnp.zeros((2 * LEV, LANES), BF16)

    def body(x, carry):
        main = dot_nt(weights, cells_ref[x, :LANES, :])
        tail = jnp.concatenate([cells_ref[x, LANES:, :], winds_ref[x, LEV:, :], blank], axis=0)
        rest = dot_nt(weights, tail)
        main_ref[pl.ds(x + 1, 24, stride=ROWS), :] = main
        rest_ref[pl.ds(x + 1, 24, stride=ROWS), :] = rest
        return carry

    lax.fori_loop(0, XS, body, 0, unroll=5)
    pack_messages(main_ref, rest_ref, send_ref)
    east_ref[:COLS, :] = cells_ref[XS - 1]
    east_ref[COLS:, :] = winds_ref[XS - 1, :LEV, :]
    west_ref[...] = cells_ref[0]


STAGE = pltpu.VMEM((24 * ROWS, LANES), F32)


def pick_rows(me, band, row, cells, winds):
    return pl.pallas_call(
        pick_kernel,
        out_shape=(
            shape((BANDS, WIRE, LANES), BF16),
            shape((COLS + LEV, LANES), BF16),
            shape((COLS, LANES), BF16),
        ),
        in_specs=[SM, SM, SM, VM, VM],
        out_specs=(VM, VM, VM),
        scratch_shapes=[STAGE, STAGE],
        compiler_params=params(16),
        name="pick",
    )(me, band, row, cells, winds)


def unpack_kernel(me_ref, recv_ref, rows_ref, halo_ref):
    me = me_ref[0]
    total = recv_ref[0].astype(F32)
    for s in range(1, BANDS):
        total = total + recv_ref[s].astype(F32)
    rows_ref[: 2 * ROWS, :] = total[: 2 * ROWS].astype(BF16)
    rows_ref[2 * ROWS :, :] = lanes_below(total[3 * ROWS :], 2 * LEV).astype(BF16)
    for at, (near, there) in enumerate(((me - 1, me > 0), (me + 1, me < BANDS - 1))):
        source = jnp.clip(near, 0, BANDS - 1)
        message = recv_ref[source].astype(F32)
        main = message[2 * ROWS : 3 * ROWS]
        rest = lanes_below(pltpu.roll(message[3 * ROWS :], 2 * LEV, axis=1), 2 * LEV)
        halo_ref[2 * at] = jnp.where(there, main, 0.0)
        halo_ref[2 * at + 1] = jnp.where(there, rest, 0.0)


def unpack_rows(me, recv):
    return pl.pallas_call(
        unpack_kernel,
        out_shape=(shape((3 * ROWS, LANES), BF16), shape((4, ROWS, LANES), F32)),
        in_specs=[SM, VM],
        out_specs=(VM, VM),
        compiler_params=params(16),
        name="unpack",
    )(me, recv)


def spread_blocks(rows_ref):
    first = rows_ref[:ROWS, :]
    second = rows_ref[ROWS : 2 * ROWS, :]
    rest = rows_ref[2 * ROWS :, :].astype(F32)
    lower = lanes_below(rest, LEV)
    upper = rest - lower
    blank = jnp.zeros_like(first)
    return jnp.concatenate(
        [
            jnp.concatenate([first, blank, lower.astype(BF16)], axis=1),
            jnp.concatenate([blank, second, upper.astype(BF16)], axis=1),
        ],
        axis=0,
    )


def product_kernel(rows_ref, other_ref, own_ops_ref, other_ops_ref, out_ref):
    mine = spread_blocks(rows_ref)
    theirs = spread_blocks(other_ref)
    for q in range(4):
        span = slice(4 * ROWS * q, 4 * ROWS * (q + 1))
        made = jnp.dot(own_ops_ref[span, :], mine, preferred_element_type=F32)
        made = made + jnp.dot(other_ops_ref[span, :], theirs, preferred_element_type=F32)
        for s in range(4):
            part = made[ROWS * s : ROWS * (s + 1)]
            rest = part[:, 2 * LANES :]
            t = 4 * q + s
            out_ref[t, :ROWS, :] = part[:, :LANES].astype(BF16)
            out_ref[t, ROWS : 2 * ROWS, :] = part[:, LANES : 2 * LANES].astype(BF16)
            packed = rest[: ROWS // 2] + pltpu.roll(rest[ROWS // 2 :], 2 * LEV, axis=1)
            out_ref[t, 2 * ROWS :, :] = packed.astype(BF16)


def products(rows, other, own_ops, other_ops):
    return pl.pallas_call(
        product_kernel,
        out_shape=shape((TARGETS, PACK, LANES), BF16),
        in_specs=[VM] * 4,
        out_specs=VM,
        compiler_params=params(24),
        name="product",
    )(rows, other, own_ops, other_ops)


def total_kernel(recv_ref, out_ref):
    total = recv_ref[0].astype(F32)
    for s in range(1, TARGETS):
        total = total + recv_ref[s].astype(F32)
    total = total.astype(BF16)
    for d in range(BANDS):
        out_ref[d] = total


def totals(recv):
    return pl.pallas_call(
        total_kernel,
        out_shape=shape((BANDS, PACK, LANES), BF16),
        in_specs=[VM],
        out_specs=VM,
        compiler_params=params(16),
        name="total",
    )(recv)


def stage_corrections(me, band_ref, row_ref, recv_ref, halo_ref, wind_halo_ref, main_ref, rest_ref):
    clear(main_ref, rest_ref)
    half = ROWS // 2
    for source in range(BANDS):
        packed = recv_ref[source, 2 * ROWS :, :].astype(F32)
        for b in range(2):
            at = (b * BANDS + source) * ROWS
            main_ref[at : at + ROWS, :] = recv_ref[source, b * ROWS : (b + 1) * ROWS, :].astype(F32)
            low = pltpu.roll(packed, LANES - LEV, axis=1) if b else packed
            high = pltpu.roll(packed, LEV if b else 2 * LEV, axis=1)
            rest_ref[at : at + half, :] = lanes_below(low, LEV)
            rest_ref[at + half : at + ROWS, :] = lanes_below(high, LEV)
    for at, (near, edge) in enumerate(((me - 1, LANES - 1), (me + 1, 0))):
        main = jnp.zeros((ROWS, LANES), F32)
        rest = jnp.zeros((ROWS, LANES), F32)
        for block in range(BLOCKS):
            hit = (band_ref[block] == near) & (row_ref[block] == edge)
            share = jnp.where(hit, 1.0, 0.0)
            k = slot(block) * ROWS
            main = main + share * main_ref[k : k + ROWS, :]
            rest = rest + share * rest_ref[k : k + ROWS, :]
        k = (16 + at) * ROWS
        main = halo_ref[2 * at] + main
        rest = lanes_below(halo_ref[2 * at + 1], LEV) + rest
        main_ref[k : k + ROWS, :] = main.astype(BF16).astype(F32)
        rest_ref[k : k + ROWS, :] = rest.astype(BF16).astype(F32)
    wind = wind_halo_ref[1]
    rest_ref[18 * ROWS : 19 * ROWS, :] = wind - lanes_below(wind, LEV)


def place_weights(me, band_ref, row_ref):
    sub, lane = iotas((24, 2 * LANES))
    target = jnp.full((24, 2 * LANES), -1, jnp.int32)
    for block in range(BLOCKS):
        wanted = jnp.where(band_ref[block] == me, row_ref[block], -1)
        target = jnp.where(sub == slot(block), wanted, target)
    target = jnp.where((sub == 16) | (sub == 18), LANES, target)
    target = jnp.where(sub == 17, 2 * LANES - 1, target)
    return jnp.where(lane == target, 1.0, 0.0).astype(BF16)


def smooth_all(weights, cells_ref, west_ref, east_ref, main_ref, rest_ref, smooth_ref, edge_ref, wind_ref):
    def placed(r):
        main = main_ref[pl.ds(r, 24, stride=ROWS), :].astype(BF16)
        rest = rest_ref[pl.ds(r, 24, stride=ROWS), :].astype(BF16)
        return dot_tn(main, weights), dot_tn(rest, weights)

    def store(r, base):
        main, rest = placed(r)
        base = base.astype(F32)
        smooth_ref[r, :LANES, :] = (base[:LANES] + main[:, :LANES]).astype(BF16).astype(F32)
        smooth_ref[r, LANES:, :] = (base[LANES:] + rest[:LEV, :LANES]).astype(BF16).astype(F32)
        return main, rest

    store(0, west_ref[:COLS, :])
    store(XS + 1, east_ref[...])

    def body(x, carry):
        main, rest = store(x + 1, cells_ref[x])
        edge_ref[x, :LANES, :] = main[:, LANES:]
        edge_ref[x, LANES:, :] = rest[:LEV, LANES:]
        wind_ref[x] = rest[LEV : 2 * LEV, LANES:]
        return carry

    lax.fori_loop(0, XS, body, 0, unroll=3)


def stencil(x, top, winds_ref, west_ref, smooth_ref, edge_ref, wind_ref):
    lane = lax.broadcasted_iota(jnp.int32, (LEV, LANES), 1)
    courant = winds_ref[x].astype(F32)
    before = winds_ref[jnp.maximum(x - 1, 0), :LEV, :].astype(F32)
    before = jnp.where(x == 0, west_ref[COLS:, :].astype(F32), before)
    across = courant[:LEV]
    along = jnp.where(top & (lane == LANES - 1), 0.0, courant[LEV:])
    south_along = jnp.where(lane == 0, wind_ref[x], pltpu.roll(along, 1, axis=1))
    east = jnp.maximum(across, 0.0)
    west = jnp.minimum(before, 0.0)
    north = jnp.maximum(along, 0.0)
    south = jnp.minimum(south_along, 0.0)
    centre = 1.0 - east + west - north + south
    made = []
    for v in range(VAR):
        span = slice(v * LEV, (v + 1) * LEV)
        here = smooth_ref[x + 1, span, :]
        edge = edge_ref[x, span, :]
        above = jnp.where(lane == LANES - 1, edge, pltpu.roll(here, LANES - 1, axis=1))
        below = jnp.where(lane == 0, edge, pltpu.roll(here, 1, axis=1))
        made.append(
            centre * here
            + (east * smooth_ref[x + 2, span, :] - west * smooth_ref[x, span, :])
            + (north * above - south * below)
        )
    return made


SCRATCH = [
    STAGE,
    STAGE,
    pltpu.VMEM((XS + 2, COLS, LANES), F32),
    pltpu.VMEM((XS, COLS, LANES), F32),
    pltpu.VMEM((XS, LEV, LANES), F32),
]


def first_kernel(
    me_ref, band_ref, row_ref, cells_ref, winds_ref, west_ref, east_ref, recv_ref, halo_ref, wind_halo_ref,
    out_ref, send_ref, to_east_ref, to_west_ref, main_ref, rest_ref, smooth_ref, edge_ref, wind_ref,
):
    me = me_ref[0]
    stage_corrections(me, band_ref, row_ref, recv_ref, halo_ref, wind_halo_ref, main_ref, rest_ref)
    smooth_all(
        place_weights(me, band_ref, row_ref), cells_ref, west_ref, east_ref, main_ref, rest_ref, smooth_ref, edge_ref,
        wind_ref,
    )
    clear(main_ref, rest_ref)
    weights = pick_weights(me, band_ref, row_ref)
    top = me == BANDS - 1
    blank = jnp.zeros((3 * LEV, LANES), BF16)

    def body(x, carry):
        made = [m.astype(BF16) for m in stencil(x, top, winds_ref, west_ref, smooth_ref, edge_ref, wind_ref)]
        for v in range(VAR):
            out_ref[x, v * LEV : (v + 1) * LEV, :] = made[v]
        main = dot_nt(weights, jnp.concatenate(made[:4], axis=0))
        rest = dot_nt(weights, jnp.concatenate([made[4], blank], axis=0))
        main_ref[pl.ds(x + 1, 24, stride=ROWS), :] = main
        rest_ref[pl.ds(x + 1, 24, stride=ROWS), :] = rest
        return carry

    lax.fori_loop(0, XS, body, 0, unroll=3)
    pack_messages(main_ref, rest_ref, send_ref)
    to_east_ref[...] = out_ref[XS - 1]
    to_west_ref[...] = out_ref[0]


def first_substep(*args):
    return pl.pallas_call(
        first_kernel,
        out_shape=(
            shape((XS, COLS, LANES), BF16),
            shape((BANDS, WIRE, LANES), BF16),
            shape((COLS, LANES), BF16),
            shape((COLS, LANES), BF16),
        ),
        in_specs=[SM] * 3 + [VM] * 7,
        out_specs=(VM,) * 4,
        scratch_shapes=SCRATCH,
        compiler_params=params(32),
        name="first",
    )(*args)


CHUNK = 9


def last_kernel(
    me_ref, band_ref, row_ref, cells_ref, winds_ref, west_ref, east_ref, recv_ref, halo_ref, wind_halo_ref, wind_west_ref,
    out_ref, main_ref, rest_ref, smooth_ref, edge_ref, wind_ref,
):
    me = me_ref[0]
    step = pl.program_id(0)

    @pl.when(step == 0)
    def _():
        stage_corrections(me, band_ref, row_ref, recv_ref, halo_ref, wind_halo_ref, main_ref, rest_ref)
        smooth_all(
            place_weights(me, band_ref, row_ref), cells_ref, west_ref, east_ref, main_ref, rest_ref, smooth_ref,
            edge_ref, wind_ref,
        )

    top = me == BANDS - 1

    def body(y, carry):
        x = step * CHUNK + y
        made = stencil(x, top, winds_ref, wind_west_ref, smooth_ref, edge_ref, wind_ref)
        for v in range(VAR):
            out_ref[y, v * LEV : (v + 1) * LEV, :] = made[v]
        return carry

    lax.fori_loop(0, CHUNK, body, 0, unroll=3)


def last_substep(*args):
    return pl.pallas_call(
        last_kernel,
        grid=(XS // CHUNK,),
        out_shape=shape((XS, COLS, LANES), F32),
        in_specs=[SM] * 3 + [VM] * 8,
        out_specs=pl.BlockSpec((CHUNK, COLS, LANES), lambda i: (i, 0, 0)),
        scratch_shapes=SCRATCH,
        compiler_params=params(32),
        name="last",
    )(*args)


SWAP = [(i, i ^ 1) for i in range(LON_DEV)]
EASTWARD = [(i, (i + 1) % LON_DEV) for i in range(LON_DEV)]
WESTWARD = [(i, (i - 1) % LON_DEV) for i in range(LON_DEV)]
SAME_CORE = [[2 * t + core for t in range(TARGETS)] for core in range(2)]


def corrections(me, recv, own_ops, other_ops):
    rows, halo = unpack_rows(me, recv)
    other = lax.ppermute(rows, "lon", SWAP)
    partial = products(rows, other, own_ops, other_ops)
    swapped = lax.all_to_all(partial, "lon", 0, 0, tiled=True, axis_index_groups=SAME_CORE)
    return lax.all_to_all(totals(swapped), "lat", 0, 0, tiled=True), halo


def shards(cotangent, winds, filter_ops, block_band, block_row):
    me = lax.axis_index("lat").astype(jnp.int32).reshape(1)
    core = (lax.axis_index("lon") % 2).astype(jnp.int32).reshape(1)
    own_ops, send_ops = prepare_operators(core, jnp.pad(filter_ops, ((0, 0), (1, 2), (0, 0))))
    other_ops = lax.ppermute(send_ops, "lon", SWAP)
    send, to_east, to_west = pick_rows(me, block_band, block_row, cotangent, winds)
    west = lax.ppermute(to_east, "lon", EASTWARD)
    east = lax.ppermute(to_west, "lon", WESTWARD)
    recv = lax.all_to_all(send, "lat", 0, 0, tiled=True)
    given, halo = corrections(me, recv, own_ops, other_ops)
    state, send, to_east, to_west = first_substep(
        me, block_band, block_row, cotangent, winds, west, east, given, halo, halo
    )
    west2 = lax.ppermute(to_east, "lon", EASTWARD)
    east2 = lax.ppermute(to_west, "lon", WESTWARD)
    recv = lax.all_to_all(send, "lat", 0, 0, tiled=True)
    given, halo2 = corrections(me, recv, own_ops, other_ops)
    return last_substep(me, block_band, block_row, state, winds, west2, east2, given, halo2, halo, west)


def solution(mesh):
    return jax.shard_map(
        shards,
        mesh=mesh,
        in_specs=(P("lon", None, "lat"), P("lon", None, "lat"), P("lat", "lon", None), P(), P()),
        out_specs=P("lon", None, "lat"),
        check_vma=False,
    )
```

time: 446 us -> 135 us (0.30); the launches traced: 438 us -> 134 us
  waiting for transfers between devices: 319 us -> 20 us
  blocking collectives: 0 us -> 57.5 us
  local copies, waits for them, and re-layouts: 50.6 us -> 6.18 us
  Pallas kernels: 0 us -> 28.8 us
  other arithmetic: 19 us -> 0 us
  matrix products: 18.1 us -> 0 us
  between operations: 13.3 us -> 0.15 us
    reduce_scatter x2 -> x0, waiting for transfers between devices: 254 us -> none  [filter_rows(): lax.psum_scatter(jnp.einsum('kji,kjc->ikc', slot_ops, picked, preferred_e...]
    all_gather x1 -> x0, waiting for transfers between devices: 60.5 us -> none  [shards(): lax.all_gather(filter_ops, 'lat', axis=0, tiled=True)]
    all_to_all x0 -> x3, blocking collectives: none -> 57.5 us  [the longest x2 42.9 us: corrections(): lax.all_to_all(partial, 'lon', 0, 0, tiled=True, axis_index_groups=SAME_C...]
    pallas_call x0 -> x10, Pallas kernels: none -> 28.8 us  [the longest x1 10.8 us: first_substep(): pl.pallas_call(first_kernel, out_shape=(shape((XS, COLS, LANES), BF16), s...]
    transpose x2 -> x0, local copies, waits for them, and re-layouts: 18.7 us -> none  [filter_rows(): jnp.einsum('kji,kjc->ikc', slot_ops, picked, preferred_element_type=jnp.f...]
    dot_general x8 -> x0, matrix products: 18.1 us -> none  [the longest x2 6.1 us: filter_rows(): jnp.einsum('kji,kjc->ikc', slot_ops, picked, preferred_element_type=jnp.f...]
    slice x10 -> x0, local copies, waits for them, and re-layouts: 15.7 us -> none  [the longest x6 10.2 us: padded(): head = lax.slice_in_dim(cells, 0, width, axis=dim)]
    all_to_all x0 -> x3, waiting for transfers between devices: none -> 14 us  [the longest x1 8.33 us: shards(): recv = lax.all_to_all(send, 'lat', 0, 0, tiled=True)]
  transfers between devices with their start and end apart: 14 -> 10, of which waited for: 5 -> 7; matrix products, arithmetic and copies ran while one was open for 9% -> 0% of each run, Pallas kernels for 0% -> 1%
where the time goes in v1:
time: 135 us; the launch traced here: 134 us
  blocking collectives  57.5 us (43%)
  Pallas kernels  28.8 us (21%)
  starting transfers between devices  20.9 us (15%)
  waiting for transfers between devices  20 us (15%)
  local copies, waits for them, and re-layouts  6.18 us (5%)
    all_to_all x2, blocking collectives, corrections(): lax.all_to_all(partial, 'lon', 0, 0, tiled=True, axis_index_groups=SAME_C...  42.9 us
    all_to_all x1, blocking collectives, shards(): recv = lax.all_to_all(send, 'lat', 0, 0, tiled=True)  14.6 us
    pallas_call x1, Pallas kernels, first_substep(): pl.pallas_call(first_kernel, out_shape=(shape((XS, COLS, LANES), BF16), s...  10.8 us
    pallas_call x1, Pallas kernels, last_substep(): pl.pallas_call(last_kernel, grid=(XS // CHUNK,), out_shape=shape((XS, COL...  10.1 us
    all_to_all x1, waiting for transfers between devices, shards(): recv = lax.all_to_all(send, 'lat', 0, 0, tiled=True)  8.33 us
    all_to_all x2, starting transfers between devices, corrections(): return (lax.all_to_all(totals(swapped), 'lat', 0, 0, tiled=True), halo)  6.81 us
    unnamed x25, local copies, waits for them, and re-layouts  6.1 us
    all_to_all x1, starting transfers between devices, shards(): recv = lax.all_to_all(send, 'lat', 0, 0, tiled=True)  6.03 us
  transfers between devices with their start and end apart: 10, of which 7 were waited for; matrix products, arithmetic and copies ran while one was open for 0% of the time, Pallas kernels for 1%

profile of v1, /device:TPU:2, one launch (start us, length us, event | category | flops | bytes accessed | tf_op | source)
XLA Modules:
  0.0 133.6 jit_solution(7072943828134960805)
XLA Ops:
  0.0 0.0 copy-start
  0.0 1.5 %copy-done = bf16[45,160,128]{2,1,0:T(8,128)(2,1)S(1)} copy-done((bf16[45,160,128]{2,1,0:T(8,128)(2,1)S(1)}, bf16[45,160,128]{2,1,0:T(8,128)(2,1)}, u32[]{:S(2)}) %copy-start) | copy-done | bytes 1843224
  1.5 1.1 copy-done.2
  2.6 0.7 copy-done.6
  3.3 0.7 copy-done.8
  3.9 3.8 %pick.1 = (bf16[8,192,128]{2,1,0:T(8,128)(2,1)}, bf16[192,128]{1,0:T(8,128)(2,1)S(1)}, bf16[160,128]{1,0:T(8,128)(2,1)S(1)}) custom-call(s32[1]{0:T(128)} %bitcast.me_ref, s32[16]{0:T(128)S(1)} %copy-done.6, s32[16]{0:T(128)S(1)} %copy-done.8, bf16[45,160,128]{2,1,0:T(8,128)(2,1)S(1)} %copy-done, bf16[45,64,128]{2,1,0:T(8,128)(2,1)S(1)} %copy-done.2), custom_call_target="tpu_custom_call" | custom-call | tf_op jit(solution)/shard_map/pick/pallas_call | solution.py:159
  7.8 0.6 copy-done.10
  8.4 6.0 %all-to-all-start = ((bf16[8,192,128]{2,1,0:T(8,128)(2,1)}), bf16[8,192,128]{2,1,0:T(8,128)(2,1)S(1)}, u32[]{:S(2)}, u32[]{:S(2)}) async-start(bf16[8,192,128]{2,1,0:T(8,128)(2,1)} %get-tuple-element.20), calls=%async_computation | async-start | bytes 786432 | tf_op jit(solution)/shard_map/all_to_all | solution.py:482
  14.4 0.0 copy-done.11
  14.5 0.1 pad.4.ops_ref
  14.5 1.4 %operators.1 = (bf16[768,96]{1,0:T(8,128)(2,1)S(1)}, bf16[768,96]{1,0:T(8,128)(2,1)}) custom-call(s32[1]{0:T(128)} %bitcast.1.core_ref, bf16[2,48,1440]{2,1,0:T(8,128)(2,1)S(1)} %pad.4.ops_ref), custom_call_target="tpu_custom_call" | custom-call | tf_op jit(solution)/shard_map/operators/pallas_call | solution.py:94
  15.9 0.1 collective-permute-start.3
  16.0 8.3 %all-to-all-done.recv_ref = bf16[8,192,128]{2,1,0:T(8,128)(2,1)S(1)} async-done(((bf16[8,192,128]{2,1,0:T(8,128)(2,1)}), bf16[8,192,128]{2,1,0:T(8,128)(2,1)S(1)}, u32[]{:S(2)}, u32[]{:S(2)}) %all-to-all-start) | async-done | bytes 393248 | tf_op jit(solution)/shard_map/all_to_all | solution.py:482
  24.3 0.1 unpack.2
  24.4 0.1 collective-permute-start.2
  24.5 0.0 collective-permute-done.3.other_ops_ref
  24.5 1.2 collective-permute-done.2.other_ref
  25.7 0.5 product.2
  26.2 24.0 %all_to_all.30.recv_ref = bf16[16,120,128]{2,1,0:T(8,128)(2,1)S(1)} all-to-all(bf16[16,120,128]{2,1,0:T(8,128)(2,1)S(1)} %product.2), channel_id=1, replica_groups={{0,16,32,48,64,80,96,112,128,144,160,176,192,208,224,240},{8,24,40,56,7..., dimensions={0} | all-to-all | bytes 983040 | tf_op jit(solution)/shard_map/all_to_all | solution.py:470
  50.3 0.8 total.2
  51.0 3.4 %all-to-all-start.2 = ((bf16[8,120,128]{2,1,0:T(8,128)(2,1)}), bf16[8,120,128]{2,1,0:T(8,128)(2,1)S(1)}, u32[]{:S(2)}, u32[]{:S(2)}) async-start(bf16[8,120,128]{2,1,0:T(8,128)(2,1)} %total.2), calls=%async_computation.2 | async-start | bytes 491520 | tf_op jit(solution)/shard_map/all_to_all | solution.py:471
  54.5 0.1 collective-permute-start
  54.6 3.8 %collective-permute-start.1 = (bf16[160,128]{1,0:T(8,128)(2,1)}, bf16[160,128]{1,0:T(8,128)(2,1)S(1)}, u32[]{:S(2)}, u32[]{:S(2)}) collective-permute-start(bf16[160,128]{1,0:T(8,128)(2,1)} %copy-done.10), channel_id=1, source_target_pairs={{0,248},{8,0},{16,8},{24,16},{32,24},{40,32},{48,40},{56,48},{64,5... | collective-permute-start | bytes 122888 | tf_op jit(solution)/shard_map/ppermute | solution.py:481
  58.4 2.0 %collective-permute-done.1.east_ref = bf16[160,128]{1,0:T(8,128)(2,1)S(1)} collective-permute-done((bf16[160,128]{1,0:T(8,128)(2,1)}, bf16[160,128]{1,0:T(8,128)(2,1)S(1)}, u32[]{:S(2)}, u32[]{:S(2)}) %collective-permute-start.1) | collective-permute-done | bytes 40992 | tf_op jit(solution)/shard_map/ppermute | solution.py:481
  60.4 0.0 collective-permute-done.west_ref.wind_west_ref
  60.4 2.7 %all-to-all-done.2.recv_ref = bf16[8,120,128]{2,1,0:T(8,128)(2,1)S(1)} async-done(((bf16[8,120,128]{2,1,0:T(8,128)(2,1)}), bf16[8,120,128]{2,1,0:T(8,128)(2,1)S(1)}, u32[]{:S(2)}, u32[]{:S(2)}) %all-to-all-start.2) | async-done | bytes 245792 | tf_op jit(solution)/shard_map/all_to_all | solution.py:471
  63.1 0.0 copy-done.1
  63.1 0.0 copy-done.3
  63.1 0.0 copy-done.7
  63.1 0.0 copy-done.9
  63.1 10.8 %first.1 = (bf16[45,160,128]{2,1,0:T(8,128)(2,1)S(1)}, bf16[8,192,128]{2,1,0:T(8,128)(2,1)S(1)}, bf16[160,128]{1,0:T(8,128)(2,1)S(1)}, bf16[160,128]{1,0:T(8,128)(2,1)S(1)}) custom-call(s32[1]{0:T(128)} %bitcast.me_ref, s32[16]{0:T(128)S(1)} %copy-done.7, s32[16]{0:T(128)S(1)} %copy-done.9, bf16[45,160,128]{2,1,0:T(8,128)(2,1)S(1)} %copy-done.1, ...), custom_call_target="tpu_custom_call" | custom-call | tf_op jit(solution)/shard_map/first/pallas_call | solution.py:401
  73.8 0.0 copy-start.4
  73.9 14.6 %all_to_all.31.recv_ref = bf16[8,192,128]{2,1,0:T(8,128)(2,1)S(1)} all-to-all(bf16[8,192,128]{2,1,0:T(8,128)(2,1)S(1)} %get-tuple-element.28), channel_id=1, replica_groups=mesh['lon'=32,'lat'=8] {'lat'}, dimensions={0} | all-to-all | bytes 786432 | tf_op jit(solution)/shard_map/all_to_all | solution.py:489
  88.5 0.1 unpack.3
  88.6 0.1 collective-permute-start.6
  88.6 1.2 collective-permute-done.6.other_ref
  89.8 0.5 product.3
  90.4 18.9 %all_to_all.32.recv_ref = bf16[16,120,128]{2,1,0:T(8,128)(2,1)S(1)} all-to-all(bf16[16,120,128]{2,1,0:T(8,128)(2,1)S(1)} %product.3), channel_id=1, replica_groups={{0,16,32,48,64,80,96,112,128,144,160,176,192,208,224,240},{8,24,40,56,7..., dimensions={0} | all-to-all | bytes 983040 | tf_op jit(solution)/shard_map/all_to_all | solution.py:470
  109.2 0.0 copy-done.4
  109.2 0.8 total.3
  110.0 3.4 %all-to-all-start.5 = ((bf16[8,120,128]{2,1,0:T(8,128)(2,1)}), bf16[8,120,128]{2,1,0:T(8,128)(2,1)S(1)}, u32[]{:S(2)}, u32[]{:S(2)}) async-start(bf16[8,120,128]{2,1,0:T(8,128)(2,1)} %total.3), calls=%async_computation.5 | async-start | bytes 491520 | tf_op jit(solution)/shard_map/all_to_all | solution.py:471
  113.4 0.1 collective-permute-start.4
  113.5 3.8 %collective-permute-start.5 = (bf16[160,128]{1,0:T(8,128)(2,1)S(1)}, bf16[160,128]{1,0:T(8,128)(2,1)S(1)}, u32[]{:S(2)}, u32[]{:S(2)}) collective-permute-start(bf16[160,128]{1,0:T(8,128)(2,1)S(1)} %get-tuple-element.27), channel_id=1, source_target_pairs={{0,248},{8,0},{16,8},{24,16},{32,24},{40,32},{48,40},{56,48},{64,5... | collective-permute-start | bytes 122888 | tf_op jit(solution)/shard_map/ppermute | solution.py:488
  117.4 1.7 %collective-permute-done.4.west_ref = bf16[160,128]{1,0:T(8,128)(2,1)S(1)} collective-permute-done((bf16[160,128]{1,0:T(8,128)(2,1)S(1)}, bf16[160,128]{1,0:T(8,128)(2,1)S(1)}, u32[]{:S(2)}, u32[]{:S(2)}) %collective-permute-start.4) | collective-permute-done | bytes 40992 | tf_op jit(solution)/shard_map/ppermute | solution.py:487
  119.0 0.0 collective-permute-done.5.east_ref
  119.1 3.0 %all-to-all-done.5.recv_ref = bf16[8,120,128]{2,1,0:T(8,128)(2,1)S(1)} async-done(((bf16[8,120,128]{2,1,0:T(8,128)(2,1)}), bf16[8,120,128]{2,1,0:T(8,128)(2,1)S(1)}, u32[]{:S(2)}, u32[]{:S(2)}) %all-to-all-start.5) | async-done | bytes 245792 | tf_op jit(solution)/shard_map/all_to_all | solution.py:471
  122.0 1.5 %copy-done.5 = bf16[45,160,128]{2,1,0:T(8,128)(2,1)S(1)} copy-done((bf16[45,160,128]{2,1,0:T(8,128)(2,1)S(1)}, bf16[45,160,128]{2,1,0:T(8,128)(2,1)}, u32[]{:S(2)}) %copy-start.5) | copy-done | bytes 1843224
  123.5 10.1 %last.1 = f32[45,160,128]{2,1,0:T(8,128)} custom-call(s32[1]{0:T(128)} %bitcast.me_ref, s32[16]{0:T(128)S(1)} %copy-done.7, s32[16]{0:T(128)S(1)} %copy-done.9, bf16[45,160,128]{2,1,0:T(8,128)(2,1)S(1)} %copy-done.5, bf16[45,64,128]{2,1,0:T(8,128)(2,1)S(1)} %copy-done.3, bf16[160,128]{1,0:T(8,128)(2,1)S(1)} %collective-permute-done.4.west_ref, ...), custom_call_target="tpu_custom_call" | custom-call | tf_op jit(solution)/shard_map/last/pallas_call | solution.py:448
  (11 shorter events, 0.0 us)
Async XLA Ops:
  0.0 1.5 %copy-start = (bf16[45,160,128]{2,1,0:T(8,128)(2,1)S(1)}, bf16[45,160,128]{2,1,0:T(8,128)(2,1)}, u32[]{:S(2)}) copy-start(bf16[45,160,128]{2,1,0:T(8,128)(2,1)} %cells_ref.3) | copy-start | bytes 5529604
  1.5 1.1 copy-start.2
  2.6 0.7 copy-start.6
  3.3 0.7 copy-start.8
  3.9 10.5 %copy-start.11 = (bf16[2,45,1440]{2,0,1:T(2,128)(2,1)S(1)}, bf16[2,45,1440]{2,0,1:T(2,128)(2,1)}, u32[]{:S(2)}) copy-start(bf16[2,45,1440]{2,0,1:T(2,128)(2,1)} %param.7) | copy-start | bytes 777604
  7.8 0.6 copy-start.10
  8.4 16.0 %all-to-all-start = ((bf16[8,192,128]{2,1,0:T(8,128)(2,1)}), bf16[8,192,128]{2,1,0:T(8,128)(2,1)S(1)}, u32[]{:S(2)}, u32[]{:S(2)}) async-start(bf16[8,192,128]{2,1,0:T(8,128)(2,1)} %get-tuple-element.20), calls=%async_computation | async-start | bytes 786432 | tf_op jit(solution)/shard_map/all_to_all | solution.py:482
  15.9 47.2 %copy-start.1 = (bf16[45,160,128]{2,1,0:T(8,128)(2,1)S(1)}, bf16[45,160,128]{2,1,0:T(8,128)(2,1)}, u32[]{:S(2)}) copy-start(bf16[45,160,128]{2,1,0:T(8,128)(2,1)} %cells_ref.3) | copy-start | bytes 5529604
  15.9 47.2 %copy-start.3 = (bf16[45,64,128]{2,1,0:T(8,128)(2,1)S(1)}, bf16[45,64,128]{2,1,0:T(8,128)(2,1)}, u32[]{:S(2)}) copy-start(bf16[45,64,128]{2,1,0:T(8,128)(2,1)} %winds_ref.5) | copy-start | bytes 2211844
  15.9 47.2 %copy-start.7 = (s32[16]{0:T(128)S(1)}, s32[16]{0:T(128)}, u32[]{:S(2)}) copy-start(s32[16]{0:T(128)} %band_ref.5) | copy-start | bytes 196
  15.9 47.2 %copy-start.9 = (s32[16]{0:T(128)S(1)}, s32[16]{0:T(128)}, u32[]{:S(2)}) copy-start(s32[16]{0:T(128)} %row_ref.5) | copy-start | bytes 196
  15.9 8.6 %collective-permute-start.3 = (bf16[768,96]{1,0:T(8,128)(2,1)}, bf16[768,96]{1,0:T(8,128)(2,1)S(1)}, u32[]{:S(2)}, u32[]{:S(2)}) collective-permute-start(bf16[768,96]{1,0:T(8,128)(2,1)} %get-tuple-element.23), channel_id=1, source_target_pairs={{0,8},{8,0},{16,24},{24,16},{32,40},{40,32},{48,56},{56,48},{64,72... | collective-permute-start | bytes 442376 | tf_op jit(solution)/shard_map/ppermute | solution.py:478
  24.4 1.3 collective-permute-start.2
  51.0 12.0 %all-to-all-start.2 = ((bf16[8,120,128]{2,1,0:T(8,128)(2,1)}), bf16[8,120,128]{2,1,0:T(8,128)(2,1)S(1)}, u32[]{:S(2)}, u32[]{:S(2)}) async-start(bf16[8,120,128]{2,1,0:T(8,128)(2,1)} %total.2), calls=%async_computation.2 | async-start | bytes 491520 | tf_op jit(solution)/shard_map/all_to_all | solution.py:471
  54.5 5.9 %collective-permute-start = (bf16[192,128]{1,0:T(8,128)(2,1)S(1)}, bf16[192,128]{1,0:T(8,128)(2,1)S(1)}, u32[]{:S(2)}, u32[]{:S(2)}) collective-permute-start(bf16[192,128]{1,0:T(8,128)(2,1)S(1)} %get-tuple-element.18), channel_id=1, source_target_pairs={{0,8},{8,16},{16,24},{24,32},{32,40},{40,48},{48,56},{56,64},{64,7... | collective-permute-start | bytes 147464 | tf_op jit(solution)/shard_map/ppermute | solution.py:480
  54.6 5.8 %collective-permute-start.1 = (bf16[160,128]{1,0:T(8,128)(2,1)}, bf16[160,128]{1,0:T(8,128)(2,1)S(1)}, u32[]{:S(2)}, u32[]{:S(2)}) collective-permute-start(bf16[160,128]{1,0:T(8,128)(2,1)} %copy-done.10), channel_id=1, source_target_pairs={{0,248},{8,0},{16,8},{24,16},{32,24},{40,32},{48,40},{56,48},{64,5... | collective-permute-start | bytes 122888 | tf_op jit(solution)/shard_map/ppermute | solution.py:481
  73.8 35.4 %copy-start.4 = (bf16[45,160,128]{2,1,0:T(8,128)(2,1)}, bf16[45,160,128]{2,1,0:T(8,128)(2,1)S(1)}, u32[]{:S(2)}) copy-start(bf16[45,160,128]{2,1,0:T(8,128)(2,1)S(1)} %get-tuple-element.25.cells_ref) | copy-start | bytes 5529604
  88.6 1.3 collective-permute-start.6
  110.0 12.0 %all-to-all-start.5 = ((bf16[8,120,128]{2,1,0:T(8,128)(2,1)}), bf16[8,120,128]{2,1,0:T(8,128)(2,1)S(1)}, u32[]{:S(2)}, u32[]{:S(2)}) async-start(bf16[8,120,128]{2,1,0:T(8,128)(2,1)} %total.3), calls=%async_computation.5 | async-start | bytes 491520 | tf_op jit(solution)/shard_map/all_to_all | solution.py:471
  113.4 5.6 %collective-permute-start.4 = (bf16[160,128]{1,0:T(8,128)(2,1)S(1)}, bf16[160,128]{1,0:T(8,128)(2,1)S(1)}, u32[]{:S(2)}, u32[]{:S(2)}) collective-permute-start(bf16[160,128]{1,0:T(8,128)(2,1)S(1)} %get-tuple-element.26), channel_id=1, source_target_pairs={{0,8},{8,16},{16,24},{24,32},{32,40},{40,48},{48,56},{56,64},{64,7... | collective-permute-start | bytes 122888 | tf_op jit(solution)/shard_map/ppermute | solution.py:487
  113.5 5.5 %collective-permute-start.5 = (bf16[160,128]{1,0:T(8,128)(2,1)S(1)}, bf16[160,128]{1,0:T(8,128)(2,1)S(1)}, u32[]{:S(2)}, u32[]{:S(2)}) collective-permute-start(bf16[160,128]{1,0:T(8,128)(2,1)S(1)} %get-tuple-element.27), channel_id=1, source_target_pairs={{0,248},{8,0},{16,8},{24,16},{32,24},{40,32},{48,40},{56,48},{64,5... | collective-permute-start | bytes 122888 | tf_op jit(solution)/shard_map/ppermute | solution.py:488
  122.0 1.5 %copy-start.5 = (bf16[45,160,128]{2,1,0:T(8,128)(2,1)S(1)}, bf16[45,160,128]{2,1,0:T(8,128)(2,1)}, u32[]{:S(2)}) copy-start(bf16[45,160,128]{2,1,0:T(8,128)(2,1)} %copy-done.4) | copy-start | bytes 5529604

commit v2 on v1

v2 whole, which is shorter than its diff:
```python
import jax
import jax.numpy as jnp
from jax import lax
from jax.experimental import pallas as pl
from jax.experimental.pallas import tpu as pltpu
from jax.sharding import PartitionSpec as P

VAR = 5
LEV = 32
COLS = VAR * LEV
XS = 45
ROWS = 48
LANES = 128
BANDS = 8
NLON = 1440
LON_DEV = 32
TARGETS = 16
BLOCKS = 16
PIECES = 7
WIRE = (PIECES + 4) * ROWS
PACK = 120
HALO = 72
CHUNK = 9

F32 = jnp.float32
BF16 = jnp.bfloat16
VM = pl.BlockSpec(memory_space=pltpu.VMEM)
SM = pl.BlockSpec(memory_space=pltpu.SMEM)


def shape(dims, kind):
    return jax.ShapeDtypeStruct(dims, kind)


def params(mib):
    return pltpu.CompilerParams(vmem_limit_bytes=mib * 2**20)


def iotas(dims):
    return (
        lax.broadcasted_iota(jnp.int32, dims, 0),
        lax.broadcasted_iota(jnp.int32, dims, 1),
    )


def lanes_below(value, limit):
    lane = lax.broadcasted_iota(jnp.int32, value.shape, 1)
    return jnp.where(lane < limit, value, jnp.zeros_like(value))


def dot_nt(a, b):
    return lax.dot_general(a, b, (((1,), (1,)), ((), ())), preferred_element_type=F32)


def dot_tn(a, b):
    return lax.dot_general(a, b, (((0,), (0,)), ((), ())), preferred_element_type=F32)


def operator_kernel(meta_ref, ops_ref, own_ref, send_ref):
    core = meta_ref[1]
    for t in range(TARGETS):
        tiles = []
        for parity in range(2):
            start = XS * (2 * t + parity) - 1
            total = None
            first = max(start, 0) // LANES * LANES
            spans = [(first, min(first + 2 * LANES, NLON))]
            if start < 0:
                spans.append(((NLON - 1) // LANES * LANES, NLON))
            if start + XS + 2 > NLON:
                spans.append((0, LANES))
            for low, high in spans:
                row, lane = iotas((ROWS, high - low))
                wanted = start + row
                wanted = jnp.where(wanted < 0, wanted + NLON, wanted)
                wanted = jnp.where(wanted >= NLON, wanted - NLON, wanted)
                hit = (lane + low == wanted) & (row < XS + 2)
                pick = jnp.where(hit, 1.0, 0.0).astype(BF16)
                window = ops_ref[:, :, low:high].reshape(2 * ROWS, high - low)
                part = dot_nt(pick, window)
                total = part if total is None else total + part
            tiles.append(total)
        rows = slice(ROWS * t, ROWS * (t + 1))
        mine = core == 0
        own_ref[rows, :] = jnp.where(mine, tiles[0], tiles[1]).astype(BF16)
        send_ref[rows, :] = jnp.where(mine, tiles[1], tiles[0]).astype(BF16)


def prepare_operators(meta, ops):
    out = shape((TARGETS * ROWS, 2 * ROWS), BF16)
    return pl.pallas_call(
        operator_kernel,
        out_shape=(out, out),
        in_specs=[SM, VM],
        out_specs=(VM, VM),
        compiler_params=params(16),
        name="operators",
    )(meta, ops)


def slot(block):
    return (block % 2) * BANDS + block // 2


def global_row(meta_ref, block):
    return meta_ref[2 + block] * LANES + meta_ref[2 + BLOCKS + block]


def clear_rims(ref, count):
    blank = jnp.zeros((count, LANES), ref.dtype)
    for r in (0, XS + 1, XS + 2):
        ref[pl.ds(r, count, stride=ROWS), :] = blank


def pick_weights(meta_ref):
    me = meta_ref[0]
    sub, lane = iotas((PIECES * BANDS, LANES))
    target = jnp.full(sub.shape, -1, jnp.int32)
    for block in range(BLOCKS):
        at = global_row(meta_ref, block) - me * LANES
        for near in range(3):
            k = near * 2 * BANDS + slot(block)
            target = jnp.where(sub == k, at + (near - 1), target)
    base = 6 * BANDS
    target = jnp.where((sub >= base) & (sub == base - 1 + me), 0, target)
    target = jnp.where((sub >= base) & (sub == base + 1 + me), LANES - 1, target)
    return jnp.where(lane == target, 1.0, 0.0).astype(BF16)


def keep(value, *starts):
    lane = lax.broadcasted_iota(jnp.int32, value.shape, 1)
    hit = (lane >= starts[0]) & (lane < starts[0] + LEV)
    for start in starts[1:]:
        hit = hit | ((lane >= start) & (lane < start + LEV))
    return jnp.where(hit, value, jnp.zeros_like(value))


def pull(value, start):
    moved = pltpu.roll(value, LANES - start, axis=1) if start else value
    return lanes_below(moved, LEV)


def pack_messages(main_ref, rest_ref, send_ref):
    for d in range(BANDS):
        pieces = []
        for p in range(PIECES):
            rows = slice((p * BANDS + d) * ROWS, (p * BANDS + d + 1) * ROWS)
            send_ref[d, p * ROWS : (p + 1) * ROWS, :] = main_ref[rows, :].astype(BF16)
            pieces.append(rest_ref[rows, :])
        tails = [
            pieces[2 + e] + pltpu.roll(keep(pieces[4 + e], 0), 3 * LEV, axis=1) for e in range(2)
        ]
        tails.append(keep(pieces[0], 0, 2 * LEV) + pltpu.roll(keep(pieces[1], 0, 2 * LEV), LEV, axis=1))
        tails.append(pieces[6])
        for p, tail in enumerate(tails):
            at = (PIECES + p) * ROWS
            send_ref[d, at : at + ROWS, :] = tail.astype(BF16)


def clear(*refs):
    for ref in refs:
        ref[...] = jnp.zeros(ref.shape, ref.dtype)


def pick_kernel(meta_ref, cells_ref, winds_ref, send_ref, east_ref, west_ref, main_ref, rest_ref):
    step = pl.program_id(0)

    @pl.when(step == 0)
    def _():
        clear_rims(main_ref, PIECES * BANDS)
        clear_rims(rest_ref, PIECES * BANDS)
        west_ref[...] = cells_ref[0]

    weights = pick_weights(meta_ref)
    blank = jnp.zeros((LEV, LANES), BF16)
    for y in range(CHUNK):
        main = dot_nt(weights, cells_ref[y, :LANES, :])
        tail = jnp.concatenate([cells_ref[y, LANES:, :], winds_ref[y], blank], axis=0)
        rest = dot_nt(weights, tail)
        at = pl.ds(step * CHUNK + y + 1, PIECES * BANDS, stride=ROWS)
        main_ref[at, :] = main
        rest_ref[at, :] = rest

    @pl.when(step == XS // CHUNK - 1)
    def _():
        pack_messages(main_ref, rest_ref, send_ref)
        east_ref[:COLS, :] = cells_ref[CHUNK - 1]
        east_ref[COLS:, :] = winds_ref[CHUNK - 1, :LEV, :]


STAGE = pltpu.VMEM((24 * ROWS, LANES), F32)
PICKED = pltpu.VMEM((PIECES * BANDS * ROWS, LANES), F32)


def pick_rows(meta, cells, winds):
    return pl.pallas_call(
        pick_kernel,
        grid=(XS // CHUNK,),
        out_shape=(
            shape((BANDS, WIRE, LANES), BF16),
            shape((COLS + LEV, LANES), BF16),
            shape((COLS, LANES), BF16),
        ),
        in_specs=[
            SM,
            pl.BlockSpec((CHUNK, COLS, LANES), lambda i: (i, 0, 0)),
            pl.BlockSpec((CHUNK, 2 * LEV, LANES), lambda i: (i, 0, 0)),
        ],
        out_specs=(VM, VM, VM),
        scratch_shapes=[PICKED, PICKED],
        compiler_params=params(24),
        name="pick",
    )(meta, cells, winds)


def unpack_kernel(meta_ref, recv_ref, rows_ref, context_ref, to_east_ref, to_west_ref, halo_ref):
    me = meta_ref[0]

    def added(tile):
        span = slice(tile * ROWS, (tile + 1) * ROWS)
        total = recv_ref[0, span, :].astype(F32)
        for s in range(1, BANDS):
            total = total + recv_ref[s, span, :].astype(F32)
        return total

    tiles = [added(p) for p in (0, 1, 2, 3, 4, 5, 7, 8, 9)]
    for p, tile in enumerate(tiles):
        context_ref[p * ROWS : (p + 1) * ROWS, :] = tile.astype(BF16)
    rows_ref[:ROWS, :] = tiles[2].astype(BF16)
    rows_ref[ROWS : 2 * ROWS, :] = tiles[3].astype(BF16)
    rest = lanes_below(tiles[6], LEV) + pltpu.roll(lanes_below(tiles[7], LEV), LEV, axis=1)
    rows_ref[2 * ROWS :, :] = rest.astype(BF16)
    clear(to_east_ref, to_west_ref)
    for at, p in enumerate((2, 3, 6, 7)):
        to_east_ref[at : at + 1, :] = tiles[p][XS : XS + 1]
        to_west_ref[at : at + 1, :] = tiles[p][1:2]
    for at, (near, there) in enumerate(((me - 1, me > 0), (me + 1, me < BANDS - 1))):
        source = jnp.clip(near, 0, BANDS - 1)
        main = recv_ref[source, 6 * ROWS : 7 * ROWS, :].astype(F32)
        rest = recv_ref[source, 10 * ROWS :, :].astype(F32)
        rest = pull(rest, 0) + pltpu.roll(pull(rest, 2 * LEV), LEV, axis=1)
        halo_ref[2 * at] = jnp.where(there, main, 0.0)
        halo_ref[2 * at + 1] = jnp.where(there, rest, 0.0)


def unpack_rows(meta, recv):
    edge = shape((8, LANES), F32)
    return pl.pallas_call(
        unpack_kernel,
        out_shape=(
            shape((3 * ROWS, LANES), BF16), shape((9 * ROWS, LANES), BF16), edge, edge, shape((4, ROWS, LANES), F32)
        ),
        in_specs=[SM, VM],
        out_specs=(VM,) * 5,
        compiler_params=params(16),
        name="unpack",
    )(meta, recv)


def spread_blocks(rows_ref):
    first = rows_ref[:ROWS, :]
    second = rows_ref[ROWS : 2 * ROWS, :]
    rest = rows_ref[2 * ROWS :, :].astype(F32)
    lower = lanes_below(rest, LEV)
    upper = rest - lower
    blank = jnp.zeros_like(first)
    return jnp.concatenate(
        [
            jnp.concatenate([first, blank, lower.astype(BF16)], axis=1),
            jnp.concatenate([blank, second, upper.astype(BF16)], axis=1),
        ],
        axis=0,
    )


def product_kernel(rows_ref, other_ref, own_ops_ref, other_ops_ref, out_ref):
    mine = spread_blocks(rows_ref)
    theirs = spread_blocks(other_ref)
    for q in range(4):
        span = slice(4 * ROWS * q, 4 * ROWS * (q + 1))
        made = jnp.dot(own_ops_ref[span, :], mine, preferred_element_type=F32)
        made = made + jnp.dot(other_ops_ref[span, :], theirs, preferred_element_type=F32)
        for s in range(4):
            part = made[ROWS * s : ROWS * (s + 1)]
            rest = part[:, 2 * LANES :]
            t = 4 * q + s
            out_ref[t, :ROWS, :] = part[:, :LANES].astype(BF16)
            out_ref[t, ROWS : 2 * ROWS, :] = part[:, LANES : 2 * LANES].astype(BF16)
            packed = rest[: ROWS // 2] + pltpu.roll(rest[ROWS // 2 :], 2 * LEV, axis=1)
            out_ref[t, 2 * ROWS :, :] = packed.astype(BF16)


def products(rows, other, own_ops, other_ops):
    return pl.pallas_call(
        product_kernel,
        out_shape=shape((TARGETS, PACK, LANES), BF16),
        in_specs=[VM] * 4,
        out_specs=VM,
        compiler_params=params(24),
        name="product",
    )(rows, other, own_ops, other_ops)


def total_kernel(meta_ref, recv_ref, *refs):
    out_ref = refs[-1]
    total = recv_ref[0].astype(F32)
    for s in range(1, TARGETS):
        total = total + recv_ref[s].astype(F32)
    total = total.astype(BF16)
    for d in range(BANDS):
        out_ref[d, :PACK, :] = total
    if len(refs) > 1:
        me = meta_ref[0]
        for d in range(BANDS):
            edge = jnp.where(d == me + 1, refs[0][1], jnp.zeros((HALO, LANES), BF16))
            out_ref[d, PACK:, :] = jnp.where(d == me - 1, refs[0][0], edge)


def totals(meta, recv, *halo):
    return pl.pallas_call(
        total_kernel,
        out_shape=shape((BANDS, PACK + (HALO if halo else 0), LANES), BF16),
        in_specs=[SM] + [VM] * (1 + len(halo)),
        out_specs=VM,
        compiler_params=params(16),
        name="total",
    )(meta, recv, *halo)


def stage_blocks(recv_ref, main_ref, rest_ref):
    half = ROWS // 2
    for source in range(BANDS):
        packed = recv_ref[source, 2 * ROWS : PACK, :].astype(F32)
        for b in range(2):
            at = (b * BANDS + source) * ROWS
            main_ref[at : at + ROWS, :] = recv_ref[source, b * ROWS : (b + 1) * ROWS, :].astype(F32)
            rest_ref[at : at + half, :] = pull(packed, b * LEV)
            rest_ref[at + half : at + ROWS, :] = pull(packed, (2 + b) * LEV)


def block_sum(meta_ref, row, main_ref, rest_ref):
    main = jnp.zeros((ROWS, LANES), F32)
    rest = jnp.zeros((ROWS, LANES), F32)
    for block in range(BLOCKS):
        share = jnp.where(global_row(meta_ref, block) == row, 1.0, 0.0)
        k = slot(block) * ROWS
        main = main + share * main_ref[k : k + ROWS, :]
        rest = rest + share * rest_ref[k : k + ROWS, :]
    return main, rest


def stage_corrections(meta_ref, recv_ref, halos, wind, main_ref, rest_ref):
    stage_blocks(recv_ref, main_ref, rest_ref)
    main_ref[18 * ROWS :, :] = jnp.zeros((6 * ROWS, LANES), F32)
    rest_ref[18 * ROWS :, :] = jnp.zeros((6 * ROWS, LANES), F32)
    me = meta_ref[0]
    for at, row in enumerate((me * LANES - 1, (me + 1) * LANES)):
        main, rest = block_sum(meta_ref, row, main_ref, rest_ref)
        k = (16 + at) * ROWS
        main_ref[k : k + ROWS, :] = (halos[at][0] + main).astype(BF16).astype(F32)
        rest_ref[k : k + ROWS, :] = (halos[at][1] + rest).astype(BF16).astype(F32)
    rest_ref[18 * ROWS : 19 * ROWS, :] = keep(wind, LEV)


def rows_kernel(meta_ref, context_ref, west_ref, east_ref, recv_ref, out_ref, main_ref, rest_ref):
    stage_blocks(recv_ref, main_ref, rest_ref)
    me = meta_ref[0]
    sub = lax.broadcasted_iota(jnp.int32, (ROWS, LANES), 0)
    inner = (sub >= 1) & (sub <= XS)

    def tile(p):
        return context_ref[p * ROWS : (p + 1) * ROWS, :].astype(F32)

    def rimmed(value, at):
        value = jnp.where(sub == 0, west_ref[at : at + 1, :], value)
        return jnp.where(sub == XS + 1, east_ref[at : at + 1, :], value)

    def rounded(value):
        return value.astype(BF16).astype(F32)

    def wide(value):
        value = value + pltpu.roll(value, LEV, axis=1)
        return value + pltpu.roll(value, 2 * LEV, axis=1)

    last = None
    behind = tile(8)
    for e in range(2):
        row = global_row(meta_ref, 2 * me + e)
        tail = rimmed(tile(6 + e), 2 + e)
        mains = [tile(e), rimmed(tile(2 + e), e), tile(4 + e)]
        rests = [pull(behind, e * LEV), pull(tail, 0), pull(tail, 3 * LEV)]
        for near in range(3):
            main, rest = block_sum(meta_ref, row + (near - 1), main_ref, rest_ref)
            mains[near] = rounded(mains[near] + main)
            rests[near] = rounded(rests[near] + rest)
        across = pull(tail, LEV)
        along = pull(tail, 2 * LEV)
        before = pull(behind, (2 + e) * LEV)
        east = jnp.maximum(across, 0.0)
        west = jnp.minimum(pltpu.roll(across, 1, axis=0), 0.0)
        north = jnp.where(row == BANDS * LANES - 1, 0.0, jnp.maximum(along, 0.0))
        south = jnp.minimum(before, 0.0)
        coefs = (east, west, north, south)

        def moved(coefs, values):
            east, west, north, south = coefs
            centre = 1.0 - east + west - north + south
            below, here, above = values
            made = (
                centre * here
                + (east * pltpu.roll(here, ROWS - 1, axis=0) - west * pltpu.roll(here, 1, axis=0))
                + (north * above - south * below)
            )
            return jnp.where(inner, made, 0.0)

        out_ref[e * ROWS : (e + 1) * ROWS, :] = moved([wide(c) for c in coefs], mains).astype(BF16)
        rest = lanes_below(moved(coefs, rests), LEV)
        last = rest if e == 0 else last + pltpu.roll(rest, LEV, axis=1)
    out_ref[2 * ROWS :, :] = last.astype(BF16)


def next_rows(*args):
    return pl.pallas_call(
        rows_kernel,
        out_shape=shape((3 * ROWS, LANES), BF16),
        in_specs=[SM] + [VM] * 4,
        out_specs=VM,
        scratch_shapes=[STAGE, STAGE],
        compiler_params=params(16),
        name="rows",
    )(*args)


def place_weights(meta_ref):
    sub, lane = iotas((24, 2 * LANES))
    target = jnp.full(sub.shape, -1, jnp.int32)
    for block in range(BLOCKS):
        at = global_row(meta_ref, block) - meta_ref[0] * LANES
        target = jnp.where(sub == slot(block), jnp.where((at >= 0) & (at < LANES), at, -1), target)
    target = jnp.where((sub == 16) | (sub == 18), LANES, target)
    target = jnp.where(sub == 17, 2 * LANES - 1, target)
    return jnp.where(lane == target, 1.0, 0.0).astype(BF16)


def smooth_all(weights, cells_ref, west_ref, east_ref, main_ref, rest_ref, smooth_ref, edge_ref, wind_ref):
    def placed(r):
        main = main_ref[pl.ds(r, 24, stride=ROWS), :].astype(BF16)
        rest = rest_ref[pl.ds(r, 24, stride=ROWS), :].astype(BF16)
        return dot_tn(main, weights), dot_tn(rest, weights)

    def store(r, base):
        main, rest = placed(r)
        base = base.astype(F32)
        smooth_ref[r, :LANES, :] = (base[:LANES] + main[:, :LANES]).astype(BF16).astype(F32)
        smooth_ref[r, LANES:, :] = (base[LANES:] + rest[:LEV, :LANES]).astype(BF16).astype(F32)
        return main, rest

    store(0, west_ref[:COLS, :])
    store(XS + 1, east_ref[...])

    def body(x, carry):
        main, rest = store(x + 1, cells_ref[x])
        edge_ref[x, :LANES, :] = main[:, LANES:]
        edge_ref[x, LANES:, :] = rest[:LEV, LANES:]
        wind_ref[x] = rest[LEV : 2 * LEV, LANES:]
        return carry

    lax.fori_loop(0, XS, body, 0, unroll=3)


def stencil(x, top, winds_ref, west_ref, smooth_ref, edge_ref, wind_ref):
    lane = lax.broadcasted_iota(jnp.int32, (LEV, LANES), 1)
    courant = winds_ref[x].astype(F32)
    before = winds_ref[jnp.maximum(x - 1, 0), :LEV, :].astype(F32)
    before = jnp.where(x == 0, west_ref[COLS:, :].astype(F32), before)
    across = courant[:LEV]
    along = jnp.where(top & (lane == LANES - 1), 0.0, courant[LEV:])
    south_along = jnp.where(lane == 0, wind_ref[x], pltpu.roll(along, 1, axis=1))
    east = jnp.maximum(across, 0.0)
    west = jnp.minimum(before, 0.0)
    north = jnp.maximum(along, 0.0)
    south = jnp.minimum(south_along, 0.0)
    centre = 1.0 - east + west - north + south
    made = []
    for v in range(VAR):
        span = slice(v * LEV, (v + 1) * LEV)
        here = smooth_ref[x + 1, span, :]
        edge = edge_ref[x, span, :]
        above = jnp.where(lane == LANES - 1, edge, pltpu.roll(here, LANES - 1, axis=1))
        below = jnp.where(lane == 0, edge, pltpu.roll(here, 1, axis=1))
        made.append(
            centre * here
            + (east * smooth_ref[x + 2, span, :] - west * smooth_ref[x, span, :])
            + (north * above - south * below)
        )
    return made


SCRATCH = [
    STAGE,
    STAGE,
    pltpu.VMEM((XS + 2, COLS, LANES), F32),
    pltpu.VMEM((XS, COLS, LANES), F32),
    pltpu.VMEM((XS, LEV, LANES), F32),
]


def first_kernel(
    meta_ref, cells_ref, winds_ref, west_ref, east_ref, recv_ref, halo_ref,
    out_ref, edges_ref, to_east_ref, to_west_ref, main_ref, rest_ref, smooth_ref, edge_ref, wind_ref,
):
    halos = [(halo_ref[2 * at], lanes_below(halo_ref[2 * at + 1], LEV)) for at in range(2)]
    stage_corrections(meta_ref, recv_ref, halos, halo_ref[1], main_ref, rest_ref)
    smooth_all(
        place_weights(meta_ref), cells_ref, west_ref, east_ref, main_ref, rest_ref, smooth_ref, edge_ref, wind_ref
    )
    clear_rims(main_ref, 2)
    clear_rims(rest_ref, 2)
    sub, lane = iotas((8, LANES))
    ends = jnp.where((lane == 0) & (sub == 0) | (lane == LANES - 1) & (sub == 1), 1.0, 0.0).astype(BF16)
    top = meta_ref[0] == BANDS - 1
    blank = jnp.zeros((3 * LEV, LANES), BF16)

    def body(x, carry):
        made = [m.astype(BF16) for m in stencil(x, top, winds_ref, west_ref, smooth_ref, edge_ref, wind_ref)]
        for v in range(VAR):
            out_ref[x, v * LEV : (v + 1) * LEV, :] = made[v]
        at = pl.ds(x + 1, 2, stride=ROWS)
        main_ref[at, :] = dot_nt(ends, jnp.concatenate(made[:4], axis=0))[:2]
        rest_ref[at, :] = dot_nt(ends, jnp.concatenate([made[4], blank], axis=0))[:2]
        return carry

    lax.fori_loop(0, XS, body, 0, unroll=3)
    for at in range(2):
        k = at * ROWS
        edges_ref[at, :ROWS, :] = main_ref[k : k + ROWS, :].astype(BF16)
        rest = rest_ref[k : k + ROWS, :]
        packed = rest[: ROWS // 2] + pltpu.roll(rest[ROWS // 2 :], LEV, axis=1)
        edges_ref[at, ROWS:, :] = packed.astype(BF16)
    to_east_ref[...] = out_ref[XS - 1]
    to_west_ref[...] = out_ref[0]


def first_substep(*args):
    return pl.pallas_call(
        first_kernel,
        out_shape=(
            shape((XS, COLS, LANES), BF16),
            shape((2, HALO, LANES), BF16),
            shape((COLS, LANES), BF16),
            shape((COLS, LANES), BF16),
        ),
        in_specs=[SM] + [VM] * 6,
        out_specs=(VM,) * 4,
        scratch_shapes=SCRATCH,
        compiler_params=params(32),
        name="first",
    )(*args)


def last_kernel(
    meta_ref, cells_ref, winds_ref, west_ref, east_ref, recv_ref, wind_halo_ref, wind_west_ref,
    out_ref, main_ref, rest_ref, smooth_ref, edge_ref, wind_ref,
):
    me = meta_ref[0]
    step = pl.program_id(0)

    @pl.when(step == 0)
    def _():
        halos = []
        for near, there in ((me - 1, me > 0), (me + 1, me < BANDS - 1)):
            source = jnp.clip(near, 0, BANDS - 1)
            main = recv_ref[source, PACK : PACK + ROWS, :].astype(F32)
            rest = recv_ref[source, PACK + ROWS :, :].astype(F32)
            rest = jnp.concatenate([pull(rest, 0), pull(rest, LEV)], axis=0)
            halos.append((jnp.where(there, main, 0.0), jnp.where(there, rest, 0.0)))
        stage_corrections(meta_ref, recv_ref, halos, wind_halo_ref[1], main_ref, rest_ref)
        smooth_all(
            place_weights(meta_ref), cells_ref, west_ref, east_ref, main_ref, rest_ref, smooth_ref, edge_ref, wind_ref
        )

    top = me == BANDS - 1

    def body(y, carry):
        x = step * CHUNK + y
        made = stencil(x, top, winds_ref, wind_west_ref, smooth_ref, edge_ref, wind_ref)
        for v in range(VAR):
            out_ref[y, v * LEV : (v + 1) * LEV, :] = made[v]
        return carry

    lax.fori_loop(0, CHUNK, body, 0, unroll=3)


def last_substep(*args):
    return pl.pallas_call(
        last_kernel,
        grid=(XS // CHUNK,),
        out_shape=shape((XS, COLS, LANES), F32),
        in_specs=[SM] + [VM] * 7,
        out_specs=pl.BlockSpec((CHUNK, COLS, LANES), lambda i: (i, 0, 0)),
        scratch_shapes=SCRATCH,
        compiler_params=params(32),
        name="last",
    )(*args)


SWAP = [(i, i ^ 1) for i in range(LON_DEV)]
EASTWARD = [(i, (i + 1) % LON_DEV) for i in range(LON_DEV)]
WESTWARD = [(i, (i - 1) % LON_DEV) for i in range(LON_DEV)]
SAME_CORE = [[2 * t + core for t in range(TARGETS)] for core in range(2)]


def by_lat(messages):
    return lax.all_to_all(messages, "lat", 0, 0, tiled=True)


def filtered(rows, own_ops, other_ops):
    other = lax.ppermute(rows, "lon", SWAP)
    partial = products(rows, other, own_ops, other_ops)
    return lax.all_to_all(partial, "lon", 0, 0, tiled=True, axis_index_groups=SAME_CORE)


def shards(cotangent, winds, filter_ops, block_band, block_row):
    me = lax.axis_index("lat").astype(jnp.int32).reshape(1)
    core = (lax.axis_index("lon") & 1).astype(jnp.int32).reshape(1)
    meta = jnp.concatenate([me, core, block_band, block_row])
    own_ops, send_ops = prepare_operators(meta, jnp.pad(filter_ops, ((0, 0), (1, 2), (0, 0))))
    other_ops = lax.ppermute(send_ops, "lon", SWAP)
    send, to_east, to_west = pick_rows(meta, cotangent, winds)
    west = lax.ppermute(to_east, "lon", EASTWARD)
    east = lax.ppermute(to_west, "lon", WESTWARD)
    rows, context, row_east, row_west, halo = unpack_rows(meta, by_lat(send))
    swapped = filtered(rows, own_ops, other_ops)
    row_from_west = lax.ppermute(row_east, "lon", EASTWARD)
    row_from_east = lax.ppermute(row_west, "lon", WESTWARD)
    given = by_lat(totals(meta, swapped))
    rows = next_rows(meta, context, row_from_west, row_from_east, given)
    swapped = filtered(rows, own_ops, other_ops)
    state, edges, to_east, to_west = first_substep(meta, cotangent, winds, west, east, given, halo)
    west2 = lax.ppermute(to_east, "lon", EASTWARD)
    east2 = lax.ppermute(to_west, "lon", WESTWARD)
    given = by_lat(totals(meta, swapped, edges))
    return last_substep(meta, state, winds, west2, east2, given, halo, west)


def solution(mesh):
    return jax.shard_map(
        shards,
        mesh=mesh,
        in_specs=(P("lon", None, "lat"), P("lon", None, "lat"), P("lat", "lon", None), P(), P()),
        out_specs=P("lon", None, "lat"),
        check_vma=False,
    )
```

time: 135 us -> 137 us (1.015)
  blocking collectives: 57.5 us -> 24.1 us
  waiting for transfers between devices: 20 us -> 37.3 us
  starting transfers between devices: 20.9 us -> 32.1 us
  local copies, waits for them, and re-layouts: 6.18 us -> 10.1 us
  Pallas kernels: 28.8 us -> 31.7 us
    all_to_all x3 -> x1, blocking collectives: 57.5 us -> 24.1 us  [filtered(): lax.all_to_all(partial, 'lon', 0, 0, tiled=True, axis_index_groups=SAME_C...]
    all_to_all x3 -> x4, waiting for transfers between devices: 14 us -> 22.5 us  [the longest x3 22.5 us: by_lat(): return lax.all_to_all(messages, 'lat', 0, 0, tiled=True)]
    all_to_all x3 -> x4, starting transfers between devices: 12.8 us -> 20.3 us  [the longest x3 14.4 us: by_lat(): return lax.all_to_all(messages, 'lat', 0, 0, tiled=True)]
    ppermute x1, waiting for transfers between devices: 1.99 us -> 6.74 us  [shards(): east = lax.ppermute(to_west, 'lon', WESTWARD)]
    unnamed x25 -> x29, local copies, waits for them, and re-layouts: 6.1 us -> 10 us
    ppermute x2 -> x4, starting transfers between devices: 0.15 us -> 4.03 us  [the longest x1 3.85 us: shards(): row_from_east = lax.ppermute(row_west, 'lon', WESTWARD)]
    pallas_call x3 -> x4, Pallas kernels: 5.36 us -> 8.14 us  [the longest x1 4.39 us: pick_rows(): pl.pallas_call(pick_kernel, grid=(XS // CHUNK,), out_shape=(shape((BANDS,...]
    ppermute x1, waiting for transfers between devices: 0.01 us -> 2.33 us  [shards(): west = lax.ppermute(to_east, 'lon', EASTWARD)]
  transfers between devices with their start and end apart: 10 -> 13, of which waited for: 7 -> 9; matrix products, arithmetic and copies ran while one was open for 0% -> 0% of each run, Pallas kernels for 1% -> 9%
where the time goes in v2:
time: 137 us; the launch traced here: 136 us
  waiting for transfers between devices  37.3 us (27%)
  starting transfers between devices  32.1 us (23%)
  Pallas kernels  31.7 us (23%)
  blocking collectives  24.1 us (18%)
  local copies, waits for them, and re-layouts  10.1 us (7%)
    all_to_all x1, blocking collectives, filtered(): lax.all_to_all(partial, 'lon', 0, 0, tiled=True, axis_index_groups=SAME_C...  24.1 us
    all_to_all x3, waiting for transfers between devices, by_lat(): return lax.all_to_all(messages, 'lat', 0, 0, tiled=True)  22.5 us
    all_to_all x3, starting transfers between devices, by_lat(): return lax.all_to_all(messages, 'lat', 0, 0, tiled=True)  14.4 us
    pallas_call x1, Pallas kernels, first_substep(): pl.pallas_call(first_kernel, out_shape=(shape((XS, COLS, LANES), BF16), s...  10.6 us
    pallas_call x1, Pallas kernels, last_substep(): pl.pallas_call(last_kernel, grid=(XS // CHUNK,), out_shape=shape((XS, COL...  10.1 us
    unnamed x29, local copies, waits for them, and re-layouts  10 us
    ppermute x1, waiting for transfers between devices, shards(): east = lax.ppermute(to_west, 'lon', WESTWARD)  6.74 us
    all_to_all x1, starting transfers between devices, filtered(): lax.all_to_all(partial, 'lon', 0, 0, tiled=True, axis_index_groups=SAME_C...  5.84 us
  transfers between devices with their start and end apart: 13, of which 9 were waited for; matrix products, arithmetic and copies ran while one was open for 0% of the time, Pallas kernels for 9%

profile of v2, /device:TPU:2, one launch (start us, length us, event | category | flops | bytes accessed | tf_op | source)
XLA Modules:
  0.0 136.1 jit_solution(13426445776685180886)
XLA Ops:
  0.0 0.7 pad_add_fusion.meta_ref
  0.8 1.5 %copy-done = bf16[45,160,128]{2,1,0:T(8,128)(2,1)S(1)} copy-done((bf16[45,160,128]{2,1,0:T(8,128)(2,1)S(1)}, bf16[45,160,128]{2,1,0:T(8,128)(2,1)}, u32[]{:S(2)}) %copy-start) | copy-done | bytes 1843224
  2.3 1.1 copy-done.2
  3.4 4.4 %pick.1 = (bf16[8,528,128]{2,1,0:T(8,128)(2,1)}, bf16[192,128]{1,0:T(8,128)(2,1)S(1)}, bf16[160,128]{1,0:T(8,128)(2,1)S(1)}) custom-call(s32[34]{0:T(128)S(1)} %pad_add_fusion.meta_ref, bf16[45,160,128]{2,1,0:T(8,128)(2,1)S(1)} %copy-done, bf16[45,64,128]{2,1,0:T(8,128)(2,1)S(1)} %copy-done.2), custom_call_target="tpu_custom_call" | custom-call | tf_op jit(solution)/shard_map/pick/pallas_call | solution.py:196
  7.8 0.6 copy-done.9
  8.4 0.6 copy-done.10
  9.0 6.0 %all-to-all-start = ((bf16[8,528,128]{2,1,0:T(8,128)(2,1)}), bf16[8,528,128]{2,1,0:T(8,128)(2,1)S(1)}, u32[]{:S(2)}, u32[]{:S(2)}) async-start(bf16[8,528,128]{2,1,0:T(8,128)(2,1)} %get-tuple-element.21), calls=%async_computation | async-start | bytes 2162688 | tf_op jit(solution)/shard_map/all_to_all | solution.py:614
  15.1 0.1 pad.4.ops_ref
  15.1 1.2 operators.1
  16.4 0.1 collective-permute-start.3
  16.5 14.7 %all-to-all-done.recv_ref = bf16[8,528,128]{2,1,0:T(8,128)(2,1)S(1)} async-done(((bf16[8,528,128]{2,1,0:T(8,128)(2,1)}), bf16[8,528,128]{2,1,0:T(8,128)(2,1)S(1)}, u32[]{:S(2)}, u32[]{:S(2)}) %all-to-all-start) | async-done | bytes 1081376 | tf_op jit(solution)/shard_map/all_to_all | solution.py:614
  31.2 0.7 unpack.1
  31.9 0.1 collective-permute-start.2
  32.0 0.0 collective-permute-done.3.other_ops_ref
  32.0 1.2 collective-permute-done.2.other_ref
  33.2 0.5 product.2
  33.7 24.1 %all_to_all.25.recv_ref = bf16[16,120,128]{2,1,0:T(8,128)(2,1)S(1)} all-to-all(bf16[16,120,128]{2,1,0:T(8,128)(2,1)S(1)} %product.2), channel_id=1, replica_groups={{0,16,32,48,64,80,96,112,128,144,160,176,192,208,224,240},{8,24,40,56,7..., dimensions={0} | all-to-all | bytes 983040 | tf_op jit(solution)/shard_map/all_to_all | solution.py:620
  57.8 1.3 total.2
  59.1 4.1 %all-to-all-start.2 = ((bf16[8,120,128]{2,1,0:T(8,128)(2,1)}), bf16[8,120,128]{2,1,0:T(8,128)(2,1)S(1)}, u32[]{:S(2)}, u32[]{:S(2)}) async-start(bf16[8,120,128]{2,1,0:T(8,128)(2,1)} %total.2), calls=%async_computation.2 | async-start | bytes 491520 | tf_op jit(solution)/shard_map/all_to_all | solution.py:614
  63.2 0.0 collective-permute-start.6
  63.2 3.8 %collective-permute-start.7 = (f32[8,128]{1,0:T(8,128)S(1)}, f32[8,128]{1,0:T(8,128)S(1)}, u32[]{:S(2)}, u32[]{:S(2)}) collective-permute-start(f32[8,128]{1,0:T(8,128)S(1)} %get-tuple-element.31), channel_id=1, source_target_pairs={{0,248},{8,0},{16,8},{24,16},{32,24},{40,32},{48,40},{56,48},{64,5... | collective-permute-start | bytes 12296 | tf_op jit(solution)/shard_map/ppermute | solution.py:635
  67.0 1.3 collective-permute-done.6.west_ref
  68.3 0.0 collective-permute-done.7.east_ref
  68.4 3.5 %all-to-all-done.2.recv_ref = bf16[8,120,128]{2,1,0:T(8,128)(2,1)S(1)} async-done(((bf16[8,120,128]{2,1,0:T(8,128)(2,1)}), bf16[8,120,128]{2,1,0:T(8,128)(2,1)S(1)}, u32[]{:S(2)}, u32[]{:S(2)}) %all-to-all-start.2) | async-done | bytes 245792 | tf_op jit(solution)/shard_map/all_to_all | solution.py:614
  71.8 1.1 rows.1.rows_ref
  72.9 0.1 collective-permute-start.8
  73.0 1.2 collective-permute-done.8.other_ref
  74.2 0.5 product.3
  74.8 0.8 copy-done.4
  75.5 5.8 %all-to-all-start.3 = ((bf16[16,120,128]{2,1,0:T(8,128)(2,1)}), bf16[16,120,128]{2,1,0:T(8,128)(2,1)S(1)}, u32[]{:S(2)}, u32[]{:S(2)}) async-start(bf16[16,120,128]{2,1,0:T(8,128)(2,1)} %copy-done.4), calls=%async_computation.3 | async-start | bytes 983040 | tf_op jit(solution)/shard_map/all_to_all | solution.py:620
  81.4 3.8 %collective-permute-start.1 = (bf16[160,128]{1,0:T(8,128)(2,1)}, bf16[160,128]{1,0:T(8,128)(2,1)S(1)}, u32[]{:S(2)}, u32[]{:S(2)}) collective-permute-start(bf16[160,128]{1,0:T(8,128)(2,1)} %copy-done.10), channel_id=1, source_target_pairs={{0,248},{8,0},{16,8},{24,16},{32,24},{40,32},{48,40},{56,48},{64,5... | collective-permute-start | bytes 122888 | tf_op jit(solution)/shard_map/ppermute | solution.py:631
  85.2 6.7 %collective-permute-done.1.east_ref = bf16[160,128]{1,0:T(8,128)(2,1)S(1)} collective-permute-done((bf16[160,128]{1,0:T(8,128)(2,1)}, bf16[160,128]{1,0:T(8,128)(2,1)S(1)}, u32[]{:S(2)}, u32[]{:S(2)}) %collective-permute-start.1) | collective-permute-done | bytes 40992 | tf_op jit(solution)/shard_map/ppermute | solution.py:631
  92.0 2.3 %collective-permute-done.west_ref.wind_west_ref = bf16[192,128]{1,0:T(8,128)(2,1)S(1)} collective-permute-done((bf16[192,128]{1,0:T(8,128)(2,1)}, bf16[192,128]{1,0:T(8,128)(2,1)S(1)}, u32[]{:S(2)}, u32[]{:S(2)}) %collective-permute-start) | collective-permute-done | bytes 49184 | tf_op jit(solution)/shard_map/ppermute | solution.py:630
  94.3 10.6 %first.1 = (bf16[45,160,128]{2,1,0:T(8,128)(2,1)S(1)}, bf16[2,72,128]{2,1,0:T(8,128)(2,1)S(1)}, bf16[160,128]{1,0:T(8,128)(2,1)S(1)}, bf16[160,128]{1,0:T(8,128)(2,1)S(1)}) custom-call(s32[34]{0:T(128)S(1)} %pad_add_fusion.meta_ref, bf16[45,160,128]{2,1,0:T(8,128)(2,1)S(1)} %copy-done.1, bf16[45,64,128]{2,1,0:T(8,128)(2,1)S(1)} %copy-done.3, ...), custom_call_target="tpu_custom_call" | custom-call | tf_op jit(solution)/shard_map/first/pallas_call | solution.py:545
  104.9 1.2 copy-done.5
  106.1 0.6 copy-done.7
  106.7 0.6 copy-done.11
  107.3 0.6 copy-done.12
  107.9 0.8 copy-done.8
  108.7 1.4 %total.3 = bf16[8,192,128]{2,1,0:T(8,128)(2,1)} custom-call(s32[34]{0:T(128)S(1)} %pad_add_fusion.meta_ref, bf16[16,120,128]{2,1,0:T(8,128)(2,1)S(1)} %all-to-all-done.3.recv_ref, bf16[2,72,128]{2,1,0:T(8,128)(2,1)S(1)} %copy-done.8), custom_call_target="tpu_custom_call" | custom-call | tf_op jit(solution)/shard_map/total/pallas_call | solution.py:320
  110.1 4.3 %all-to-all-start.4 = ((bf16[8,192,128]{2,1,0:T(8,128)(2,1)}), bf16[8,192,128]{2,1,0:T(8,128)(2,1)S(1)}, u32[]{:S(2)}, u32[]{:S(2)}) async-start(bf16[8,192,128]{2,1,0:T(8,128)(2,1)} %total.3), calls=%async_computation.4 | async-start | bytes 786432 | tf_op jit(solution)/shard_map/all_to_all | solution.py:614
  114.4 0.0 collective-permute-start.4
  114.4 3.8 %collective-permute-start.5 = (bf16[160,128]{1,0:T(8,128)(2,1)}, bf16[160,128]{1,0:T(8,128)(2,1)S(1)}, u32[]{:S(2)}, u32[]{:S(2)}) collective-permute-start(bf16[160,128]{1,0:T(8,128)(2,1)} %copy-done.11), channel_id=1, source_target_pairs={{0,248},{8,0},{16,8},{24,16},{32,24},{40,32},{48,40},{56,48},{64,5... | collective-permute-start | bytes 122888 | tf_op jit(solution)/shard_map/ppermute | solution.py:641
  118.2 2.0 %collective-permute-done.4.west_ref = bf16[160,128]{1,0:T(8,128)(2,1)S(1)} collective-permute-done((bf16[160,128]{1,0:T(8,128)(2,1)}, bf16[160,128]{1,0:T(8,128)(2,1)S(1)}, u32[]{:S(2)}, u32[]{:S(2)}) %collective-permute-start.4) | collective-permute-done | bytes 40992 | tf_op jit(solution)/shard_map/ppermute | solution.py:640
  120.2 0.0 collective-permute-done.5.east_ref
  120.2 4.3 %all-to-all-done.4.recv_ref = bf16[8,192,128]{2,1,0:T(8,128)(2,1)S(1)} async-done(((bf16[8,192,128]{2,1,0:T(8,128)(2,1)}), bf16[8,192,128]{2,1,0:T(8,128)(2,1)S(1)}, u32[]{:S(2)}, u32[]{:S(2)}) %all-to-all-start.4) | async-done | bytes 393248 | tf_op jit(solution)/shard_map/all_to_all | solution.py:614
  124.5 1.5 %copy-done.6 = bf16[45,160,128]{2,1,0:T(8,128)(2,1)S(1)} copy-done((bf16[45,160,128]{2,1,0:T(8,128)(2,1)S(1)}, bf16[45,160,128]{2,1,0:T(8,128)(2,1)}, u32[]{:S(2)}) %copy-start.6) | copy-done | bytes 1843224
  126.0 10.1 %last.1 = f32[45,160,128]{2,1,0:T(8,128)} custom-call(s32[34]{0:T(128)S(1)} %pad_add_fusion.meta_ref, bf16[45,160,128]{2,1,0:T(8,128)(2,1)S(1)} %copy-done.6, bf16[45,64,128]{2,1,0:T(8,128)(2,1)S(1)} %copy-done.3, bf16[160,128]{1,0:T(8,128)(2,1)S(1)} %collective-permute-done.4.west_ref, bf16[160,128]{1,0:T(8,128)(2,1)S(1)} %collective-permute-done.5.east_ref, ...), custom_call_target="tpu_custom_call" | custom-call | tf_op jit(solution)/shard_map/last/pallas_call | solution.py:595
  (20 shorter events, 0.1 us)
Async XLA Ops:
  0.7 1.5 %copy-start = (bf16[45,160,128]{2,1,0:T(8,128)(2,1)S(1)}, bf16[45,160,128]{2,1,0:T(8,128)(2,1)}, u32[]{:S(2)}) copy-start(bf16[45,160,128]{2,1,0:T(8,128)(2,1)} %cells_ref.3) | copy-start | bytes 5529604
  2.3 1.1 copy-start.2
  3.4 11.7 %copy-start.13 = (bf16[2,45,1440]{2,0,1:T(2,128)(2,1)S(1)}, bf16[2,45,1440]{2,0,1:T(2,128)(2,1)}, u32[]{:S(2)}) copy-start(bf16[2,45,1440]{2,0,1:T(2,128)(2,1)} %param.7) | copy-start | bytes 777604
  7.8 0.6 copy-start.9
  8.4 0.6 copy-start.10
  9.0 22.2 %all-to-all-start = ((bf16[8,528,128]{2,1,0:T(8,128)(2,1)}), bf16[8,528,128]{2,1,0:T(8,128)(2,1)S(1)}, u32[]{:S(2)}, u32[]{:S(2)}) async-start(bf16[8,528,128]{2,1,0:T(8,128)(2,1)} %get-tuple-element.21), calls=%async_computation | async-start | bytes 2162688 | tf_op jit(solution)/shard_map/all_to_all | solution.py:614
  16.4 15.6 %collective-permute-start.3 = (bf16[768,96]{1,0:T(8,128)(2,1)S(1)}, bf16[768,96]{1,0:T(8,128)(2,1)S(1)}, u32[]{:S(2)}, u32[]{:S(2)}) collective-permute-start(bf16[768,96]{1,0:T(8,128)(2,1)S(1)} %get-tuple-element.24), channel_id=1, source_target_pairs={{0,8},{8,0},{16,24},{24,16},{32,40},{40,32},{48,56},{56,48},{64,72... | collective-permute-start | bytes 442376 | tf_op jit(solution)/shard_map/ppermute | solution.py:628
  31.9 1.3 collective-permute-start.2
  57.7 36.6 %copy-start.1 = (bf16[45,160,128]{2,1,0:T(8,128)(2,1)S(1)}, bf16[45,160,128]{2,1,0:T(8,128)(2,1)}, u32[]{:S(2)}) copy-start(bf16[45,160,128]{2,1,0:T(8,128)(2,1)} %cells_ref.3) | copy-start | bytes 5529604
  57.7 36.6 %copy-start.3 = (bf16[45,64,128]{2,1,0:T(8,128)(2,1)S(1)}, bf16[45,64,128]{2,1,0:T(8,128)(2,1)}, u32[]{:S(2)}) copy-start(bf16[45,64,128]{2,1,0:T(8,128)(2,1)} %winds_ref.5) | copy-start | bytes 2211844
  59.1 12.8 %all-to-all-start.2 = ((bf16[8,120,128]{2,1,0:T(8,128)(2,1)}), bf16[8,120,128]{2,1,0:T(8,128)(2,1)S(1)}, u32[]{:S(2)}, u32[]{:S(2)}) async-start(bf16[8,120,128]{2,1,0:T(8,128)(2,1)} %total.2), calls=%async_computation.2 | async-start | bytes 491520 | tf_op jit(solution)/shard_map/all_to_all | solution.py:614
  63.2 5.1 %collective-permute-start.6 = (f32[8,128]{1,0:T(8,128)S(1)}, f32[8,128]{1,0:T(8,128)S(1)}, u32[]{:S(2)}, u32[]{:S(2)}) collective-permute-start(f32[8,128]{1,0:T(8,128)S(1)} %get-tuple-element.30), channel_id=1, source_target_pairs={{0,8},{8,16},{16,24},{24,32},{32,40},{40,48},{48,56},{56,64},{64,7... | collective-permute-start | bytes 12296 | tf_op jit(solution)/shard_map/ppermute | solution.py:634
  63.2 5.2 %collective-permute-start.7 = (f32[8,128]{1,0:T(8,128)S(1)}, f32[8,128]{1,0:T(8,128)S(1)}, u32[]{:S(2)}, u32[]{:S(2)}) collective-permute-start(f32[8,128]{1,0:T(8,128)S(1)} %get-tuple-element.31), channel_id=1, source_target_pairs={{0,248},{8,0},{16,8},{24,16},{32,24},{40,32},{48,40},{56,48},{64,5... | collective-permute-start | bytes 12296 | tf_op jit(solution)/shard_map/ppermute | solution.py:635
  72.9 1.3 collective-permute-start.8
  74.8 0.8 copy-start.4
  75.5 32.4 %all-to-all-start.3 = ((bf16[16,120,128]{2,1,0:T(8,128)(2,1)}), bf16[16,120,128]{2,1,0:T(8,128)(2,1)S(1)}, u32[]{:S(2)}, u32[]{:S(2)}) async-start(bf16[16,120,128]{2,1,0:T(8,128)(2,1)} %copy-done.4), calls=%async_computation.3 | async-start | bytes 983040 | tf_op jit(solution)/shard_map/all_to_all | solution.py:620
  81.4 12.9 %collective-permute-start = (bf16[192,128]{1,0:T(8,128)(2,1)}, bf16[192,128]{1,0:T(8,128)(2,1)S(1)}, u32[]{:S(2)}, u32[]{:S(2)}) collective-permute-start(bf16[192,128]{1,0:T(8,128)(2,1)} %copy-done.9), channel_id=1, source_target_pairs={{0,8},{8,16},{16,24},{24,32},{32,40},{40,48},{48,56},{56,64},{64,7... | collective-permute-start | bytes 147464 | tf_op jit(solution)/shard_map/ppermute | solution.py:630
  81.4 10.6 %collective-permute-start.1 = (bf16[160,128]{1,0:T(8,128)(2,1)}, bf16[160,128]{1,0:T(8,128)(2,1)S(1)}, u32[]{:S(2)}, u32[]{:S(2)}) collective-permute-start(bf16[160,128]{1,0:T(8,128)(2,1)} %copy-done.10), channel_id=1, source_target_pairs={{0,248},{8,0},{16,8},{24,16},{32,24},{40,32},{48,40},{56,48},{64,5... | collective-permute-start | bytes 122888 | tf_op jit(solution)/shard_map/ppermute | solution.py:631
  104.9 1.2 copy-start.5
  106.1 0.6 copy-start.7
  106.7 0.6 copy-start.11
  107.3 0.6 copy-start.12
  107.9 0.8 copy-start.8
  110.1 14.4 %all-to-all-start.4 = ((bf16[8,192,128]{2,1,0:T(8,128)(2,1)}), bf16[8,192,128]{2,1,0:T(8,128)(2,1)S(1)}, u32[]{:S(2)}, u32[]{:S(2)}) async-start(bf16[8,192,128]{2,1,0:T(8,128)(2,1)} %total.3), calls=%async_computation.4 | async-start | bytes 786432 | tf_op jit(solution)/shard_map/all_to_all | solution.py:614
  114.4 5.8 %collective-permute-start.4 = (bf16[160,128]{1,0:T(8,128)(2,1)}, bf16[160,128]{1,0:T(8,128)(2,1)S(1)}, u32[]{:S(2)}, u32[]{:S(2)}) collective-permute-start(bf16[160,128]{1,0:T(8,128)(2,1)} %copy-done.12), channel_id=1, source_target_pairs={{0,8},{8,16},{16,24},{24,32},{32,40},{40,48},{48,56},{56,64},{64,7... | collective-permute-start | bytes 122888 | tf_op jit(solution)/shard_map/ppermute | solution.py:640
  114.4 5.8 %collective-permute-start.5 = (bf16[160,128]{1,0:T(8,128)(2,1)}, bf16[160,128]{1,0:T(8,128)(2,1)S(1)}, u32[]{:S(2)}, u32[]{:S(2)}) collective-permute-start(bf16[160,128]{1,0:T(8,128)(2,1)} %copy-done.11), channel_id=1, source_target_pairs={{0,248},{8,0},{16,8},{24,16},{32,24},{40,32},{48,40},{56,48},{64,5... | collective-permute-start | bytes 122888 | tf_op jit(solution)/shard_map/ppermute | solution.py:641
  124.5 1.5 %copy-start.6 = (bf16[45,160,128]{2,1,0:T(8,128)(2,1)S(1)}, bf16[45,160,128]{2,1,0:T(8,128)(2,1)}, u32[]{:S(2)}) copy-start(bf16[45,160,128]{2,1,0:T(8,128)(2,1)} %copy-done.5) | copy-start | bytes 5529604

commit v3 on v2

--- a/solution.py
+++ b/solution.py
@@ -16,8 +16,8 @@
 LON_DEV = 32
 TARGETS = 16
 BLOCKS = 16
-PIECES = 7
-WIRE = (PIECES + 4) * ROWS
+PICKS = 56
+WIRE = 6 * ROWS + 24
 PACK = 120
 HALO = 72
 CHUNK = 9
@@ -114,16 +114,15 @@
 
 def pick_weights(meta_ref):
     me = meta_ref[0]
-    sub, lane = iotas((PIECES * BANDS, LANES))
+    sub, lane = iotas((PICKS, LANES))
     target = jnp.full(sub.shape, -1, jnp.int32)
     for block in range(BLOCKS):
         at = global_row(meta_ref, block) - me * LANES
         for near in range(3):
-            k = near * 2 * BANDS + slot(block)
+            k = near * BLOCKS + slot(block)
             target = jnp.where(sub == k, at + (near - 1), target)
-    base = 6 * BANDS
-    target = jnp.where((sub >= base) & (sub == base - 1 + me), 0, target)
-    target = jnp.where((sub >= base) & (sub == base + 1 + me), LANES - 1, target)
+    target = jnp.where(sub == 3 * BLOCKS, 0, target)
+    target = jnp.where(sub == 3 * BLOCKS + 1, LANES - 1, target)
     return jnp.where(lane == target, 1.0, 0.0).astype(BF16)
 
 
@@ -140,21 +139,60 @@
     return lanes_below(moved, LEV)
 
 
-def pack_messages(main_ref, rest_ref, send_ref):
+def wide(value):
+    value = value + pltpu.roll(value, LEV, axis=1)
+    return value + pltpu.roll(value, 2 * LEV, axis=1)
+
+
+def folded(value, width):
+    half = ROWS // 2
+    return value[:half] + pltpu.roll(value[half:], width, axis=1)
+
+
+def unfolded(value, start, width, limit):
+    low = pltpu.roll(value, LANES - start, axis=1) if start else value
+    high = pltpu.roll(value, LANES - start - width, axis=1)
+    return jnp.concatenate([lanes_below(low, limit), lanes_below(high, limit)], axis=0)
+
+
+def pack_messages(meta_ref, main_ref, rest_ref, send_ref, edges_ref):
+    me = meta_ref[0]
+
+    def picked(ref, k):
+        return ref[k * ROWS : (k + 1) * ROWS, :]
+
     for d in range(BANDS):
-        pieces = []
-        for p in range(PIECES):
-            rows = slice((p * BANDS + d) * ROWS, (p * BANDS + d + 1) * ROWS)
-            send_ref[d, p * ROWS : (p + 1) * ROWS, :] = main_ref[rows, :].astype(BF16)
-            pieces.append(rest_ref[rows, :])
-        tails = [
-            pieces[2 + e] + pltpu.roll(keep(pieces[4 + e], 0), 3 * LEV, axis=1) for e in range(2)
-        ]
-        tails.append(keep(pieces[0], 0, 2 * LEV) + pltpu.roll(keep(pieces[1], 0, 2 * LEV), LEV, axis=1))
-        tails.append(pieces[6])
-        for p, tail in enumerate(tails):
-            at = (PIECES + p) * ROWS
-            send_ref[d, at : at + ROWS, :] = tail.astype(BF16)
+        tails, winds, souths = [], [], []
+        for e in range(2):
+            k = e * BANDS + d
+            here = picked(rest_ref, BLOCKS + k)
+            behind = picked(rest_ref, k)
+            ahead = picked(rest_ref, 2 * BLOCKS + k)
+            mine = meta_ref[2 + 2 * d + e] == me
+            along = pull(here, 2 * LEV)
+            before = pull(behind, 2 * LEV)
+            north = jnp.where(mine, jnp.maximum(along, 0.0), lanes_below(jnp.ones_like(along), LEV))
+            south = jnp.where(mine, jnp.minimum(before, 0.0), -lanes_below(jnp.ones_like(along), LEV))
+            main = wide(north) * picked(main_ref, 2 * BLOCKS + k) - wide(south) * picked(main_ref, k)
+            rest = north * ahead - south * behind
+            send_ref[d, e * ROWS : (e + 1) * ROWS, :] = picked(main_ref, BLOCKS + k).astype(BF16)
+            send_ref[d, (2 + e) * ROWS : (3 + e) * ROWS, :] = main.astype(BF16)
+            tails.append((keep(here, 0), rest))
+            winds.append(keep(here, LEV, 2 * LEV))
+            souths.append(before)
+        tail = tails[0][0] + pltpu.roll(tails[1][0], LEV, axis=1)
+        tail = tail + pltpu.roll(tails[0][1], 2 * LEV, axis=1) + pltpu.roll(tails[1][1], 3 * LEV, axis=1)
+        send_ref[d, 4 * ROWS : 5 * ROWS, :] = tail.astype(BF16)
+        wind = pltpu.roll(winds[0], 3 * LEV, axis=1) + pltpu.roll(winds[1], LEV, axis=1)
+        send_ref[d, 5 * ROWS : 6 * ROWS, :] = wind.astype(BF16)
+        south = souths[0] + pltpu.roll(souths[1], LEV, axis=1)
+        send_ref[d, 6 * ROWS :, :] = folded(south, 2 * LEV).astype(BF16)
+    for at in range(2):
+        k = 3 * BLOCKS + at
+        edges_ref[at, :ROWS, :] = picked(main_ref, k).astype(BF16)
+        rest = picked(rest_ref, k)
+        rest = folded(keep(rest, 0), LEV) + folded(keep(rest, 2 * LEV), LEV)
+        edges_ref[at, ROWS:, :] = rest.astype(BF16)
 
 
 def clear(*refs):
@@ -162,13 +200,13 @@
         ref[...] = jnp.zeros(ref.shape, ref.dtype)
 
 
-def pick_kernel(meta_ref, cells_ref, winds_ref, send_ref, east_ref, west_ref, main_ref, rest_ref):
+def pick_kernel(meta_ref, cells_ref, winds_ref, send_ref, edges_ref, east_ref, west_ref, main_ref, rest_ref):
     step = pl.program_id(0)
 
     @pl.when(step == 0)
     def _():
-        clear_rims(main_ref, PIECES * BANDS)
-        clear_rims(rest_ref, PIECES * BANDS)
+        clear_rims(main_ref, PICKS)
+        clear_rims(rest_ref, PICKS)
         west_ref[...] = cells_ref[0]
 
     weights = pick_weights(meta_ref)
@@ -177,19 +215,19 @@
         main = dot_nt(weights, cells_ref[y, :LANES, :])
         tail = jnp.concatenate([cells_ref[y, LANES:, :], winds_ref[y], blank], axis=0)
         rest = dot_nt(weights, tail)
-        at = pl.ds(step * CHUNK + y + 1, PIECES * BANDS, stride=ROWS)
+        at = pl.ds(step * CHUNK + y + 1, PICKS, stride=ROWS)
         main_ref[at, :] = main
         rest_ref[at, :] = rest
 
     @pl.when(step == XS // CHUNK - 1)
     def _():
-        pack_messages(main_ref, rest_ref, send_ref)
+        pack_messages(meta_ref, main_ref, rest_ref, send_ref, edges_ref)
         east_ref[:COLS, :] = cells_ref[CHUNK - 1]
         east_ref[COLS:, :] = winds_ref[CHUNK - 1, :LEV, :]
 
 
 STAGE = pltpu.VMEM((24 * ROWS, LANES), F32)
-PICKED = pltpu.VMEM((PIECES * BANDS * ROWS, LANES), F32)
+PICKED = pltpu.VMEM((PICKS * ROWS, LANES), F32)
 
 
 def pick_rows(meta, cells, winds):
@@ -198,6 +236,7 @@
         grid=(XS // CHUNK,),
         out_shape=(
             shape((BANDS, WIRE, LANES), BF16),
+            shape((2, HALO, LANES), BF16),
             shape((COLS + LEV, LANES), BF16),
             shape((COLS, LANES), BF16),
         ),
@@ -206,55 +245,78 @@
             pl.BlockSpec((CHUNK, COLS, LANES), lambda i: (i, 0, 0)),
             pl.BlockSpec((CHUNK, 2 * LEV, LANES), lambda i: (i, 0, 0)),
         ],
-        out_specs=(VM, VM, VM),
+        out_specs=(VM,) * 4,
         scratch_shapes=[PICKED, PICKED],
-        compiler_params=params(24),
+        compiler_params=params(58),
         name="pick",
     )(meta, cells, winds)
 
 
-def unpack_kernel(meta_ref, recv_ref, rows_ref, context_ref, to_east_ref, to_west_ref, halo_ref):
+def added(recv_ref, span):
+    total = recv_ref[0, span, :].astype(F32)
+    for s in range(1, BANDS):
+        total = total + recv_ref[s, span, :].astype(F32)
+    return total
+
+
+def unpack_kernel(recv_ref, rows_ref):
+    rows_ref[: 2 * ROWS, :] = added(recv_ref, slice(0, 2 * ROWS)).astype(BF16)
+    tail = added(recv_ref, slice(4 * ROWS, 5 * ROWS))
+    rows_ref[2 * ROWS :, :] = lanes_below(tail, 2 * LEV).astype(BF16)
+
+
+def unpack_rows(recv):
+    return pl.pallas_call(
+        unpack_kernel,
+        out_shape=shape((3 * ROWS, LANES), BF16),
+        in_specs=[VM],
+        out_specs=VM,
+        compiler_params=params(8),
+        name="unpack",
+    )(recv)
+
+
+def context_kernel(meta_ref, recv_ref, rows_ref, context_ref, to_east_ref, to_west_ref):
     me = meta_ref[0]
-
-    def added(tile):
-        span = slice(tile * ROWS, (tile + 1) * ROWS)
-        total = recv_ref[0, span, :].astype(F32)
-        for s in range(1, BANDS):
-            total = total + recv_ref[s, span, :].astype(F32)
-        return total
-
-    tiles = [added(p) for p in (0, 1, 2, 3, 4, 5, 7, 8, 9)]
-    for p, tile in enumerate(tiles):
-        context_ref[p * ROWS : (p + 1) * ROWS, :] = tile.astype(BF16)
-    rows_ref[:ROWS, :] = tiles[2].astype(BF16)
-    rows_ref[ROWS : 2 * ROWS, :] = tiles[3].astype(BF16)
-    rest = lanes_below(tiles[6], LEV) + pltpu.roll(lanes_below(tiles[7], LEV), LEV, axis=1)
-    rows_ref[2 * ROWS :, :] = rest.astype(BF16)
+    winds = added(recv_ref, slice(5 * ROWS, 6 * ROWS))
+    souths = unfolded(added(recv_ref, slice(6 * ROWS, WIRE)), 0, 2 * LEV, 2 * LEV)
+    tails = None
+    for e in range(2):
+        band = meta_ref[2 + 2 * me + e]
+        row = meta_ref[2 + BLOCKS + 2 * me + e]
+        north = jnp.maximum(pull(winds, (2 * e + 1) * LEV), 0.0)
+        south = jnp.minimum(pull(souths, e * LEV), 0.0)
+        main = recv_ref[band, (2 + e) * ROWS : (3 + e) * ROWS, :].astype(F32)
+        rest = pull(recv_ref[band, 4 * ROWS : 5 * ROWS, :].astype(F32), (2 + e) * LEV)
+        for source, there, coef in (
+            (jnp.minimum(band + 1, BANDS - 1), (row == LANES - 1) & (band < BANDS - 1), north),
+            (jnp.maximum(band - 1, 0), (row == 0) & (band > 0), -south),
+        ):
+            share = jnp.where(there, coef, 0.0)
+            main = main + wide(share) * recv_ref[source, (2 + e) * ROWS : (3 + e) * ROWS, :].astype(F32)
+            rest = rest + share * pull(recv_ref[source, 4 * ROWS : 5 * ROWS, :].astype(F32), (2 + e) * LEV)
+        context_ref[e] = main
+        tails = rest if e == 0 else tails + pltpu.roll(rest, LEV, axis=1)
+    context_ref[2] = tails
+    context_ref[3] = winds
+    context_ref[4] = souths
     clear(to_east_ref, to_west_ref)
-    for at, p in enumerate((2, 3, 6, 7)):
-        to_east_ref[at : at + 1, :] = tiles[p][XS : XS + 1]
-        to_west_ref[at : at + 1, :] = tiles[p][1:2]
-    for at, (near, there) in enumerate(((me - 1, me > 0), (me + 1, me < BANDS - 1))):
-        source = jnp.clip(near, 0, BANDS - 1)
-        main = recv_ref[source, 6 * ROWS : 7 * ROWS, :].astype(F32)
-        rest = recv_ref[source, 10 * ROWS :, :].astype(F32)
-        rest = pull(rest, 0) + pltpu.roll(pull(rest, 2 * LEV), LEV, axis=1)
-        halo_ref[2 * at] = jnp.where(there, main, 0.0)
-        halo_ref[2 * at + 1] = jnp.where(there, rest, 0.0)
-
-
-def unpack_rows(meta, recv):
+    rims = [rows_ref[p * ROWS : (p + 1) * ROWS, :].astype(F32) for p in range(3)] + [winds]
+    for at, tile in enumerate(rims):
+        to_east_ref[at : at + 1, :] = tile[XS : XS + 1]
+        to_west_ref[at : at + 1, :] = tile[1:2]
+
+
+def unpack_context(meta, recv, rows):
     edge = shape((8, LANES), F32)
     return pl.pallas_call(
-        unpack_kernel,
-        out_shape=(
-            shape((3 * ROWS, LANES), BF16), shape((9 * ROWS, LANES), BF16), edge, edge, shape((4, ROWS, LANES), F32)
-        ),
-        in_specs=[SM, VM],
-        out_specs=(VM,) * 5,
-        compiler_params=params(16),
-        name="unpack",
-    )(meta, recv)
+        context_kernel,
+        out_shape=(shape((5, ROWS, LANES), F32), edge, edge),
+        in_specs=[SM, VM, VM],
+        out_specs=(VM,) * 3,
+        compiler_params=params(8),
+        name="context",
+    )(meta, recv, rows)
 
 
 def spread_blocks(rows_ref):
@@ -296,35 +358,44 @@
         out_shape=shape((TARGETS, PACK, LANES), BF16),
         in_specs=[VM] * 4,
         out_specs=VM,
-        compiler_params=params(24),
+        compiler_params=params(12),
         name="product",
     )(rows, other, own_ops, other_ops)
 
 
-def total_kernel(meta_ref, recv_ref, *refs):
-    out_ref = refs[-1]
+def total_kernel(meta_ref, recv_ref, edges_ref, out_ref):
     total = recv_ref[0].astype(F32)
     for s in range(1, TARGETS):
         total = total + recv_ref[s].astype(F32)
     total = total.astype(BF16)
+    me = meta_ref[0]
     for d in range(BANDS):
         out_ref[d, :PACK, :] = total
-    if len(refs) > 1:
-        me = meta_ref[0]
-        for d in range(BANDS):
-            edge = jnp.where(d == me + 1, refs[0][1], jnp.zeros((HALO, LANES), BF16))
-            out_ref[d, PACK:, :] = jnp.where(d == me - 1, refs[0][0], edge)
-
-
-def totals(meta, recv, *halo):
+        edge = jnp.where(d == me + 1, edges_ref[1], jnp.zeros((HALO, LANES), BF16))
+        out_ref[d, PACK:, :] = jnp.where(d == me - 1, edges_ref[0], edge)
+
+
+def totals(meta, recv, edges):
     return pl.pallas_call(
         total_kernel,
-        out_shape=shape((BANDS, PACK + (HALO if halo else 0), LANES), BF16),
-        in_specs=[SM] + [VM] * (1 + len(halo)),
+        out_shape=shape((BANDS, PACK + HALO, LANES), BF16),
+        in_specs=[SM, VM, VM],
         out_specs=VM,
-        compiler_params=params(16),
+        compiler_params=params(8),
         name="total",
-    )(meta, recv, *halo)
+    )(meta, recv, edges)
+
+
+def halo_rows(meta_ref, recv_ref):
+    me = meta_ref[0]
+    halos = []
+    for near, there in ((me - 1, me > 0), (me + 1, me < BANDS - 1)):
+        source = jnp.clip(near, 0, BANDS - 1)
+        main = recv_ref[source, PACK : PACK + ROWS, :].astype(F32)
+        rest = recv_ref[source, PACK + ROWS :, :].astype(F32)
+        found = (main, unfolded(rest, 0, LEV, LEV), unfolded(rest, 2 * LEV, LEV, LEV))
+        halos.append([jnp.where(there, value, 0.0) for value in found])
+    return halos[0][:2], halos[1][:2], halos[0][2]
 
 
 def stage_blocks(recv_ref, main_ref, rest_ref):
@@ -349,72 +420,65 @@
     return main, rest
 
 
-def stage_corrections(meta_ref, recv_ref, halos, wind, main_ref, rest_ref):
+def stage_corrections(meta_ref, recv_ref, wind_recv_ref, main_ref, rest_ref):
     stage_blocks(recv_ref, main_ref, rest_ref)
     main_ref[18 * ROWS :, :] = jnp.zeros((6 * ROWS, LANES), F32)
     rest_ref[18 * ROWS :, :] = jnp.zeros((6 * ROWS, LANES), F32)
     me = meta_ref[0]
+    halos = halo_rows(meta_ref, recv_ref)
     for at, row in enumerate((me * LANES - 1, (me + 1) * LANES)):
         main, rest = block_sum(meta_ref, row, main_ref, rest_ref)
         k = (16 + at) * ROWS
-        main_ref[k : k + ROWS, :] = (halos[at][0] + main).astype(BF16).astype(F32)
-        rest_ref[k : k + ROWS, :] = (halos[at][1] + rest).astype(BF16).astype(F32)
-    rest_ref[18 * ROWS : 19 * ROWS, :] = keep(wind, LEV)
-
-
-def rows_kernel(meta_ref, context_ref, west_ref, east_ref, recv_ref, out_ref, main_ref, rest_ref):
+        main = (halos[at][0] + main).astype(BF16).astype(F32)
+        rest = (halos[at][1] + rest).astype(BF16).astype(F32)
+        main_ref[k : k + ROWS, :] = main
+        rest_ref[k : k + ROWS, :] = rest
+    wind = halo_rows(meta_ref, wind_recv_ref)[2]
+    rest_ref[18 * ROWS : 19 * ROWS, :] = pltpu.roll(wind, LEV, axis=1)
+
+
+def rows_kernel(meta_ref, before_ref, context_ref, west_ref, east_ref, recv_ref, out_ref, main_ref, rest_ref):
     stage_blocks(recv_ref, main_ref, rest_ref)
     me = meta_ref[0]
     sub = lax.broadcasted_iota(jnp.int32, (ROWS, LANES), 0)
     inner = (sub >= 1) & (sub <= XS)
 
-    def tile(p):
-        return context_ref[p * ROWS : (p + 1) * ROWS, :].astype(F32)
-
     def rimmed(value, at):
         value = jnp.where(sub == 0, west_ref[at : at + 1, :], value)
         return jnp.where(sub == XS + 1, east_ref[at : at + 1, :], value)
 
-    def rounded(value):
-        return value.astype(BF16).astype(F32)
-
-    def wide(value):
-        value = value + pltpu.roll(value, LEV, axis=1)
-        return value + pltpu.roll(value, 2 * LEV, axis=1)
+    def known(p):
+        return rimmed(before_ref[p * ROWS : (p + 1) * ROWS, :].astype(F32), p)
 
     last = None
-    behind = tile(8)
+    tail = known(2)
+    winds = rimmed(context_ref[3], 3)
     for e in range(2):
         row = global_row(meta_ref, 2 * me + e)
-        tail = rimmed(tile(6 + e), 2 + e)
-        mains = [tile(e), rimmed(tile(2 + e), e), tile(4 + e)]
-        rests = [pull(behind, e * LEV), pull(tail, 0), pull(tail, 3 * LEV)]
-        for near in range(3):
-            main, rest = block_sum(meta_ref, row + (near - 1), main_ref, rest_ref)
-            mains[near] = rounded(mains[near] + main)
-            rests[near] = rounded(rests[near] + rest)
-        across = pull(tail, LEV)
-        along = pull(tail, 2 * LEV)
-        before = pull(behind, (2 + e) * LEV)
+        across = pull(winds, 2 * e * LEV)
         east = jnp.maximum(across, 0.0)
         west = jnp.minimum(pltpu.roll(across, 1, axis=0), 0.0)
-        north = jnp.where(row == BANDS * LANES - 1, 0.0, jnp.maximum(along, 0.0))
-        south = jnp.minimum(before, 0.0)
+        north = jnp.where(row == BANDS * LANES - 1, 0.0, jnp.maximum(pull(winds, (2 * e + 1) * LEV), 0.0))
+        south = jnp.minimum(pull(context_ref[4], e * LEV), 0.0)
         coefs = (east, west, north, south)
-
-        def moved(coefs, values):
+        added = [block_sum(meta_ref, row + near, main_ref, rest_ref) for near in (-1, 0, 1)]
+
+        def moved(coefs, here, aside, behind, ahead):
             east, west, north, south = coefs
+            here = here.astype(BF16).astype(F32)
             centre = 1.0 - east + west - north + south
-            below, here, above = values
             made = (
                 centre * here
                 + (east * pltpu.roll(here, ROWS - 1, axis=0) - west * pltpu.roll(here, 1, axis=0))
-                + (north * above - south * below)
+                + (aside + (north * ahead - south * behind))
             )
             return jnp.where(inner, made, 0.0)
 
-        out_ref[e * ROWS : (e + 1) * ROWS, :] = moved([wide(c) for c in coefs], mains).astype(BF16)
-        rest = lanes_below(moved(coefs, rests), LEV)
+        main = moved([wide(c) for c in coefs], known(e) + added[1][0], context_ref[e], added[0][0], added[2][0])
+        out_ref[e * ROWS : (e + 1) * ROWS, :] = main.astype(BF16)
+        rest = pull(tail, e * LEV) + added[1][1]
+        rest = moved(coefs, rest, pull(context_ref[2], e * LEV), added[0][1], added[2][1])
+        rest = lanes_below(rest, LEV)
         last = rest if e == 0 else last + pltpu.roll(rest, LEV, axis=1)
     out_ref[2 * ROWS :, :] = last.astype(BF16)
 
@@ -423,7 +487,7 @@
     return pl.pallas_call(
         rows_kernel,
         out_shape=shape((3 * ROWS, LANES), BF16),
-        in_specs=[SM] + [VM] * 4,
+        in_specs=[SM] + [VM] * 5,
         out_specs=VM,
         scratch_shapes=[STAGE, STAGE],
         compiler_params=params(16),
@@ -506,11 +570,10 @@
 
 
 def first_kernel(
-    meta_ref, cells_ref, winds_ref, west_ref, east_ref, recv_ref, halo_ref,
+    meta_ref, cells_ref, winds_ref, west_ref, east_ref, recv_ref,
     out_ref, edges_ref, to_east_ref, to_west_ref, main_ref, rest_ref, smooth_ref, edge_ref, wind_ref,
 ):
-    halos = [(halo_ref[2 * at], lanes_below(halo_ref[2 * at + 1], LEV)) for at in range(2)]
-    stage_corrections(meta_ref, recv_ref, halos, halo_ref[1], main_ref, rest_ref)
+    stage_corrections(meta_ref, recv_ref, recv_ref, main_ref, rest_ref)
     smooth_all(
         place_weights(meta_ref), cells_ref, west_ref, east_ref, main_ref, rest_ref, smooth_ref, edge_ref, wind_ref
     )
@@ -550,16 +613,16 @@
             shape((COLS, LANES), BF16),
             shape((COLS, LANES), BF16),
         ),
-        in_specs=[SM] + [VM] * 6,
+        in_specs=[SM] + [VM] * 5,
         out_specs=(VM,) * 4,
         scratch_shapes=SCRATCH,
-        compiler_params=params(32),
+        compiler_params=params(16),
         name="first",
     )(*args)
 
 
 def last_kernel(
-    meta_ref, cells_ref, winds_ref, west_ref, east_ref, recv_ref, wind_halo_ref, wind_west_ref,
+    meta_ref, cells_ref, winds_ref, west_ref, east_ref, recv_ref, wind_recv_ref, wind_west_ref,
     out_ref, main_ref, rest_ref, smooth_ref, edge_ref, wind_ref,
 ):
     me = meta_ref[0]
@@ -567,14 +630,7 @@
 
     @pl.when(step == 0)
     def _():
-        halos = []
-        for near, there in ((me - 1, me > 0), (me + 1, me < BANDS - 1)):
-            source = jnp.clip(near, 0, BANDS - 1)
-            main = recv_ref[source, PACK : PACK + ROWS, :].astype(F32)
-            rest = recv_ref[source, PACK + ROWS :, :].astype(F32)
-            rest = jnp.concatenate([pull(rest, 0), pull(rest, LEV)], axis=0)
-            halos.append((jnp.where(there, main, 0.0), jnp.where(there, rest, 0.0)))
-        stage_corrections(meta_ref, recv_ref, halos, wind_halo_ref[1], main_ref, rest_ref)
+        stage_corrections(meta_ref, recv_ref, wind_recv_ref, main_ref, rest_ref)
         smooth_all(
             place_weights(meta_ref), cells_ref, west_ref, east_ref, main_ref, rest_ref, smooth_ref, edge_ref, wind_ref
         )
@@ -599,7 +655,7 @@
         in_specs=[SM] + [VM] * 7,
         out_specs=pl.BlockSpec((CHUNK, COLS, LANES), lambda i: (i, 0, 0)),
         scratch_shapes=SCRATCH,
-        compiler_params=params(32),
+        compiler_params=params(20),
         name="last",
     )(*args)
 
@@ -626,21 +682,23 @@
     meta = jnp.concatenate([me, core, block_band, block_row])
     own_ops, send_ops = prepare_operators(meta, jnp.pad(filter_ops, ((0, 0), (1, 2), (0, 0))))
     other_ops = lax.ppermute(send_ops, "lon", SWAP)
-    send, to_east, to_west = pick_rows(meta, cotangent, winds)
+    send, edges, to_east, to_west = pick_rows(meta, cotangent, winds)
     west = lax.ppermute(to_east, "lon", EASTWARD)
     east = lax.ppermute(to_west, "lon", WESTWARD)
-    rows, context, row_east, row_west, halo = unpack_rows(meta, by_lat(send))
+    recv, west, east = lax.optimization_barrier((by_lat(send), west, east))
+    rows = unpack_rows(recv)
     swapped = filtered(rows, own_ops, other_ops)
+    context, row_east, row_west = unpack_context(meta, recv, rows)
     row_from_west = lax.ppermute(row_east, "lon", EASTWARD)
     row_from_east = lax.ppermute(row_west, "lon", WESTWARD)
-    given = by_lat(totals(meta, swapped))
-    rows = next_rows(meta, context, row_from_west, row_from_east, given)
+    given = by_lat(totals(meta, swapped, edges))
+    rows = next_rows(meta, rows, context, row_from_west, row_from_east, given)
     swapped = filtered(rows, own_ops, other_ops)
-    state, edges, to_east, to_west = first_substep(meta, cotangent, winds, west, east, given, halo)
+    state, edges, to_east, to_west = first_substep(meta, cotangent, winds, west, east, given)
     west2 = lax.ppermute(to_east, "lon", EASTWARD)
     east2 = lax.ppermute(to_west, "lon", WESTWARD)
-    given = by_lat(totals(meta, swapped, edges))
-    return last_substep(meta, state, winds, west2, east2, given, halo, west)
+    given2 = by_lat(totals(meta, swapped, edges))
+    return last_substep(meta, state, winds, west2, east2, given2, given, west)
 
 
 def solution(mesh):

time: 137 us -> 124 us (0.905)
  waiting for transfers between devices: 37.3 us -> 14.2 us
  Pallas kernels: 31.7 us -> 37 us
  starting transfers between devices: 32.1 us -> 36.7 us
    all_to_all x3, waiting for transfers between devices: 22.5 us -> 6.39 us  [by_lat(): return lax.all_to_all(messages, 'lat', 0, 0, tiled=True)]
    ppermute x1, waiting for transfers between devices: 6.74 us -> 1.67 us  [shards(): east = lax.ppermute(to_west, 'lon', WESTWARD)]
    pallas_call x1, Pallas kernels: 4.39 us -> 9.39 us  [pick_rows(): pl.pallas_call(pick_kernel, grid=(XS // CHUNK,), out_shape=(shape((BANDS,...]
    ppermute x1, starting transfers between devices: 3.85 us -> 6.4 us  [shards(): east = lax.ppermute(to_west, 'lon', WESTWARD)]
    ppermute x1, waiting for transfers between devices: 2.33 us -> 0.01 us  [shards(): west = lax.ppermute(to_east, 'lon', EASTWARD)]
    unnamed x29 -> x37, local copies, waits for them, and re-layouts: 10 us -> 8.81 us
    pallas_call x3 -> x4, Pallas kernels: 3.37 us -> 3.68 us  [the longest x2 2.78 us: totals(): pl.pallas_call(total_kernel, out_shape=shape((BANDS, PACK + HALO, LANES),...]
  transfers between devices with their start and end apart: 13 -> 13, of which waited for: 9 -> 9; matrix products, arithmetic and copies ran while one was open for 0% -> 0% of each run, Pallas kernels for 9% -> 10%
where the time goes in v3:
time: 124 us; the launch traced here: 122 us
  Pallas kernels  37 us (30%)
  starting transfers between devices  36.7 us (30%)
  blocking collectives  24.1 us (19%)
  waiting for transfers between devices  14.2 us (11%)
  local copies, waits for them, and re-layouts  8.89 us (7%)
  other arithmetic  1.32 us (1%)
    all_to_all x1, blocking collectives, filtered(): lax.all_to_all(partial, 'lon', 0, 0, tiled=True, axis_index_groups=SAME_C...  24.1 us
    all_to_all x3, starting transfers between devices, by_lat(): return lax.all_to_all(messages, 'lat', 0, 0, tiled=True)  15.5 us
    pallas_call x1, Pallas kernels, first_substep(): pl.pallas_call(first_kernel, out_shape=(shape((XS, COLS, LANES), BF16), s...  10.6 us
    pallas_call x1, Pallas kernels, last_substep(): pl.pallas_call(last_kernel, grid=(XS // CHUNK,), out_shape=shape((XS, COL...  10.1 us
    pallas_call x1, Pallas kernels, pick_rows(): pl.pallas_call(pick_kernel, grid=(XS // CHUNK,), out_shape=(shape((BANDS,...  9.39 us
    unnamed x37, local copies, waits for them, and re-layouts  8.81 us
    all_to_all x1, starting transfers between devices, filtered(): lax.all_to_all(partial, 'lon', 0, 0, tiled=True, axis_index_groups=SAME_C...  6.4 us
    ppermute x1, starting transfers between devices, shards(): east = lax.ppermute(to_west, 'lon', WESTWARD)  6.4 us
  transfers between devices with their start and end apart: 13, of which 9 were waited for; matrix products, arithmetic and copies ran while one was open for 0% of the time, Pallas kernels for 10%

profile of v3, /device:TPU:2, one launch (start us, length us, event | category | flops | bytes accessed | tf_op | source)
XLA Modules:
  0.0 122.5 jit_solution(9578973714540843015)
XLA Ops:
  0.0 1.3 %pad_add_fusion.meta_ref = s32[34]{0:T(128)} fusion(s32[16]{0:T(128)} %param.9, s32[16]{0:T(128)} %param.8, s32[1]{0:T(128)} %bitcast.1, s32[1]{0:T(128)} %bitcast), kind=kLoop, calls=%fused_computation | loop fusion | flops 102 | bytes 272 | tf_op jit(solution)/shard_map/concatenate | solution.py:682
  1.3 9.4 %pick.1 = (bf16[8,312,128]{2,1,0:T(8,128)(2,1)}, bf16[2,72,128]{2,1,0:T(8,128)(2,1)}, bf16[192,128]{1,0:T(8,128)(2,1)}, bf16[160,128]{1,0:T(8,128)(2,1)}) custom-call(s32[34]{0:T(128)} %pad_add_fusion.meta_ref, bf16[45,160,128]{2,1,0:T(8,128)(2,1)} %cells_ref.3, bf16[45,64,128]{2,1,0:T(8,128)(2,1)} %winds_ref.5), custom_call_target="tpu_custom_call" | custom-call | tf_op jit(solution)/shard_map/pick/pallas_call | solution.py:234
  10.7 6.2 %all-to-all-start = ((bf16[8,312,128]{2,1,0:T(8,128)(2,1)}), bf16[8,312,128]{2,1,0:T(8,128)(2,1)S(1)}, u32[]{:S(2)}, u32[]{:S(2)}) async-start(bf16[8,312,128]{2,1,0:T(8,128)(2,1)} %get-tuple-element.21), calls=%async_computation | async-start | bytes 1277952 | tf_op jit(solution)/shard_map/all_to_all | solution.py:670
  17.0 0.1 pad.4.ops_ref
  17.1 1.2 operators.1
  18.3 0.1 collective-permute-start.3
  18.4 0.5 collective-permute-start
  18.9 6.4 %collective-permute-start.1 = (bf16[160,128]{1,0:T(8,128)(2,1)S(1)}, bf16[160,128]{1,0:T(8,128)(2,1)S(1)}, u32[]{:S(2)}, u32[]{:S(2)}) collective-permute-start(bf16[160,128]{1,0:T(8,128)(2,1)S(1)} %copy-done.17), channel_id=1, source_target_pairs={{0,248},{8,0},{16,8},{24,16},{32,24},{40,32},{48,40},{56,48},{64,5... | collective-permute-start | bytes 122888 | tf_op jit(solution)/shard_map/ppermute | solution.py:687
  25.3 1.7 %collective-permute-done.1.east_ref = bf16[160,128]{1,0:T(8,128)(2,1)S(1)} collective-permute-done((bf16[160,128]{1,0:T(8,128)(2,1)S(1)}, bf16[160,128]{1,0:T(8,128)(2,1)S(1)}, u32[]{:S(2)}, u32[]{:S(2)}) %collective-permute-start.1) | collective-permute-done | bytes 40992 | tf_op jit(solution)/shard_map/ppermute | solution.py:687
  27.0 0.6 copy-done.10
  27.6 1.3 %all-to-all-done.recv_ref = bf16[8,312,128]{2,1,0:T(8,128)(2,1)S(1)} async-done(((bf16[8,312,128]{2,1,0:T(8,128)(2,1)}), bf16[8,312,128]{2,1,0:T(8,128)(2,1)S(1)}, u32[]{:S(2)}, u32[]{:S(2)}) %all-to-all-start) | async-done | bytes 639008 | tf_op jit(solution)/shard_map/all_to_all | solution.py:670
  29.0 0.1 collective-permute-start.2
  29.1 0.0 collective-permute-done.3.other_ops_ref
  29.1 1.2 collective-permute-done.2.other_ref
  30.3 0.5 product.2
  30.8 24.1 %all_to_all.25.recv_ref = bf16[16,120,128]{2,1,0:T(8,128)(2,1)S(1)} all-to-all(bf16[16,120,128]{2,1,0:T(8,128)(2,1)S(1)} %product.2), channel_id=1, replica_groups={{0,16,32,48,64,80,96,112,128,144,160,176,192,208,224,240},{8,24,40,56,7..., dimensions={0} | all-to-all | bytes 983040 | tf_op jit(solution)/shard_map/all_to_all | solution.py:676
  54.9 1.4 %total.2 = bf16[8,192,128]{2,1,0:T(8,128)(2,1)} custom-call(s32[34]{0:T(128)S(1)} %copy-done.9, bf16[16,120,128]{2,1,0:T(8,128)(2,1)S(1)} %all_to_all.25.recv_ref, bf16[2,72,128]{2,1,0:T(8,128)(2,1)S(1)} %copy-done.12), custom_call_target="tpu_custom_call" | custom-call | tf_op jit(solution)/shard_map/total/pallas_call | solution.py:379
  56.3 3.8 %all-to-all-start.2 = ((bf16[8,192,128]{2,1,0:T(8,128)(2,1)}), bf16[8,192,128]{2,1,0:T(8,128)(2,1)S(1)}, u32[]{:S(2)}, u32[]{:S(2)}) async-start(bf16[8,192,128]{2,1,0:T(8,128)(2,1)} %total.2), calls=%async_computation.2 | async-start | bytes 786432 | tf_op jit(solution)/shard_map/all_to_all | solution.py:670
  60.1 1.1 copy-done.3
  61.1 0.9 context.1
  62.0 0.0 copy-start.7
  62.0 0.6 copy-done.7
  62.7 0.0 collective-permute-start.6
  62.7 3.9 %collective-permute-start.7 = (f32[8,128]{1,0:T(8,128)S(1)}, f32[8,128]{1,0:T(8,128)S(1)}, u32[]{:S(2)}, u32[]{:S(2)}) collective-permute-start(f32[8,128]{1,0:T(8,128)S(1)} %get-tuple-element.35), channel_id=1, source_target_pairs={{0,248},{8,0},{16,8},{24,16},{32,24},{40,32},{48,40},{56,48},{64,5... | collective-permute-start | bytes 12296 | tf_op jit(solution)/shard_map/ppermute | solution.py:693
  66.5 1.3 %collective-permute-done.6.west_ref = f32[8,128]{1,0:T(8,128)S(1)} collective-permute-done((f32[8,128]{1,0:T(8,128)S(1)}, f32[8,128]{1,0:T(8,128)S(1)}, u32[]{:S(2)}, u32[]{:S(2)}) %collective-permute-start.6) | collective-permute-done | bytes 4128 | tf_op jit(solution)/shard_map/ppermute | solution.py:692
  67.8 0.0 collective-permute-done.7.east_ref
  67.8 1.5 %all-to-all-done.2.recv_ref.wind_recv_ref = bf16[8,192,128]{2,1,0:T(8,128)(2,1)S(1)} async-done(((bf16[8,192,128]{2,1,0:T(8,128)(2,1)}), bf16[8,192,128]{2,1,0:T(8,128)(2,1)S(1)}, u32[]{:S(2)}, u32[]{:S(2)}) %all-to-all-start.2) | async-done | bytes 393248 | tf_op jit(solution)/shard_map/all_to_all | solution.py:670
  69.3 0.9 copy-done.8
  70.2 1.0 rows.1.rows_ref
  71.3 0.1 collective-permute-start.8
  71.4 1.2 collective-permute-done.8.other_ref
  72.6 0.5 product.3
  73.1 0.8 copy-done.4
  73.9 6.4 %all-to-all-start.3 = ((bf16[16,120,128]{2,1,0:T(8,128)(2,1)}), bf16[16,120,128]{2,1,0:T(8,128)(2,1)S(1)}, u32[]{:S(2)}, u32[]{:S(2)}) async-start(bf16[16,120,128]{2,1,0:T(8,128)(2,1)} %copy-done.4), calls=%async_computation.3 | async-start | bytes 983040 | tf_op jit(solution)/shard_map/all_to_all | solution.py:676
  80.3 0.8 copy-done.11
  81.1 10.6 %first.1 = (bf16[45,160,128]{2,1,0:T(8,128)(2,1)S(1)}, bf16[2,72,128]{2,1,0:T(8,128)(2,1)S(1)}, bf16[160,128]{1,0:T(8,128)(2,1)S(1)}, bf16[160,128]{1,0:T(8,128)(2,1)S(1)}) custom-call(s32[34]{0:T(128)S(1)} %copy-done.9, bf16[45,160,128]{2,1,0:T(8,128)(2,1)S(1)} %copy-done, bf16[45,64,128]{2,1,0:T(8,128)(2,1)S(1)} %copy-done.1, ...), custom_call_target="tpu_custom_call" | custom-call | tf_op jit(solution)/shard_map/first/pallas_call | solution.py:608
  91.7 1.2 %copy-done.5 = bf16[45,160,128]{2,1,0:T(8,128)(2,1)} copy-done((bf16[45,160,128]{2,1,0:T(8,128)(2,1)}, bf16[45,160,128]{2,1,0:T(8,128)(2,1)S(1)}, u32[]{:S(2)}) %copy-start.5) | copy-done | bytes 1843224
  92.9 0.6 copy-done.13
  93.5 0.6 copy-done.14
  94.1 0.5 all-to-all-done.3.recv_ref
  94.6 1.4 %total.3 = bf16[8,192,128]{2,1,0:T(8,128)(2,1)} custom-call(s32[34]{0:T(128)S(1)} %copy-done.9, bf16[16,120,128]{2,1,0:T(8,128)(2,1)S(1)} %all-to-all-done.3.recv_ref, bf16[2,72,128]{2,1,0:T(8,128)(2,1)S(1)} %get-tuple-element.36.edges_ref), custom_call_target="tpu_custom_call" | custom-call | tf_op jit(solution)/shard_map/total/pallas_call | solution.py:379
  96.0 5.5 %all-to-all-start.4 = ((bf16[8,192,128]{2,1,0:T(8,128)(2,1)}), bf16[8,192,128]{2,1,0:T(8,128)(2,1)S(1)}, u32[]{:S(2)}, u32[]{:S(2)}) async-start(bf16[8,192,128]{2,1,0:T(8,128)(2,1)} %total.3), calls=%async_computation.4 | async-start | bytes 786432 | tf_op jit(solution)/shard_map/all_to_all | solution.py:670
  101.4 3.8 %collective-permute-start.5 = (bf16[160,128]{1,0:T(8,128)(2,1)}, bf16[160,128]{1,0:T(8,128)(2,1)S(1)}, u32[]{:S(2)}, u32[]{:S(2)}) collective-permute-start(bf16[160,128]{1,0:T(8,128)(2,1)} %copy-done.13), channel_id=1, source_target_pairs={{0,248},{8,0},{16,8},{24,16},{32,24},{40,32},{48,40},{56,48},{64,5... | collective-permute-start | bytes 122888 | tf_op jit(solution)/shard_map/ppermute | solution.py:699
  105.3 2.0 %collective-permute-done.4.west_ref = bf16[160,128]{1,0:T(8,128)(2,1)S(1)} collective-permute-done((bf16[160,128]{1,0:T(8,128)(2,1)}, bf16[160,128]{1,0:T(8,128)(2,1)S(1)}, u32[]{:S(2)}, u32[]{:S(2)}) %collective-permute-start.4) | collective-permute-done | bytes 40992 | tf_op jit(solution)/shard_map/ppermute | solution.py:698
  107.3 0.0 collective-permute-done.5.east_ref
  107.3 3.6 %all-to-all-done.4.recv_ref = bf16[8,192,128]{2,1,0:T(8,128)(2,1)S(1)} async-done(((bf16[8,192,128]{2,1,0:T(8,128)(2,1)}), bf16[8,192,128]{2,1,0:T(8,128)(2,1)S(1)}, u32[]{:S(2)}, u32[]{:S(2)}) %all-to-all-start.4) | async-done | bytes 393248 | tf_op jit(solution)/shard_map/all_to_all | solution.py:670
  110.9 1.5 %copy-done.6 = bf16[45,160,128]{2,1,0:T(8,128)(2,1)S(1)} copy-done((bf16[45,160,128]{2,1,0:T(8,128)(2,1)S(1)}, bf16[45,160,128]{2,1,0:T(8,128)(2,1)}, u32[]{:S(2)}) %copy-start.6) | copy-done | bytes 1843224
  112.4 10.1 %last.1 = f32[45,160,128]{2,1,0:T(8,128)} custom-call(s32[34]{0:T(128)S(1)} %copy-done.9, bf16[45,160,128]{2,1,0:T(8,128)(2,1)S(1)} %copy-done.6, bf16[45,64,128]{2,1,0:T(8,128)(2,1)S(1)} %copy-done.1, bf16[160,128]{1,0:T(8,128)(2,1)S(1)} %collective-permute-done.4.west_ref, bf16[160,128]{1,0:T(8,128)(2,1)S(1)} %collective-permute-done.5.east_ref, ...), custom_call_target="tpu_custom_call" | custom-call | tf_op jit(solution)/shard_map/last/pallas_call | solution.py:651
  (29 shorter events, 0.1 us)
Async XLA Ops:
  1.3 15.6 %copy-start.15 = (bf16[2,45,1440]{2,0,1:T(2,128)(2,1)S(1)}, bf16[2,45,1440]{2,0,1:T(2,128)(2,1)}, u32[]{:S(2)}) copy-start(bf16[2,45,1440]{2,0,1:T(2,128)(2,1)} %param.7) | copy-start | bytes 777604
  10.7 6.4 %copy-start.9 = (s32[34]{0:T(128)S(1)}, s32[34]{0:T(128)}, u32[]{:S(2)}) copy-start(s32[34]{0:T(128)} %pad_add_fusion.meta_ref) | copy-start | bytes 412
  10.7 7.7 %copy-start.16 = (bf16[192,128]{1,0:T(8,128)(2,1)S(1)}, bf16[192,128]{1,0:T(8,128)(2,1)}, u32[]{:S(2)}) copy-start(bf16[192,128]{1,0:T(8,128)(2,1)} %get-tuple-element.22) | copy-start | bytes 147460
  10.7 8.2 %copy-start.17 = (bf16[160,128]{1,0:T(8,128)(2,1)S(1)}, bf16[160,128]{1,0:T(8,128)(2,1)}, u32[]{:S(2)}) copy-start(bf16[160,128]{1,0:T(8,128)(2,1)} %get-tuple-element.23) | copy-start | bytes 122884
  10.7 18.2 %all-to-all-start = ((bf16[8,312,128]{2,1,0:T(8,128)(2,1)}), bf16[8,312,128]{2,1,0:T(8,128)(2,1)S(1)}, u32[]{:S(2)}, u32[]{:S(2)}) async-start(bf16[8,312,128]{2,1,0:T(8,128)(2,1)} %get-tuple-element.21), calls=%async_computation | async-start | bytes 1277952 | tf_op jit(solution)/shard_map/all_to_all | solution.py:670
  17.0 37.9 %copy-start.12 = (bf16[2,72,128]{2,1,0:T(8,128)(2,1)S(1)}, bf16[2,72,128]{2,1,0:T(8,128)(2,1)}, u32[]{:S(2)}) copy-start(bf16[2,72,128]{2,1,0:T(8,128)(2,1)} %get-tuple-element.29.edges_ref) | copy-start | bytes 110596
  18.3 10.8 %collective-permute-start.3 = (bf16[768,96]{1,0:T(8,128)(2,1)S(1)}, bf16[768,96]{1,0:T(8,128)(2,1)S(1)}, u32[]{:S(2)}, u32[]{:S(2)}) collective-permute-start(bf16[768,96]{1,0:T(8,128)(2,1)S(1)} %get-tuple-element.28), channel_id=1, source_target_pairs={{0,8},{8,0},{16,24},{24,16},{32,40},{40,32},{48,56},{56,48},{64,72... | collective-permute-start | bytes 442376 | tf_op jit(solution)/shard_map/ppermute | solution.py:684
  18.4 9.2 %collective-permute-start = (bf16[192,128]{1,0:T(8,128)(2,1)S(1)}, bf16[192,128]{1,0:T(8,128)(2,1)S(1)}, u32[]{:S(2)}, u32[]{:S(2)}) collective-permute-start(bf16[192,128]{1,0:T(8,128)(2,1)S(1)} %copy-done.16), channel_id=1, source_target_pairs={{0,8},{8,16},{16,24},{24,32},{32,40},{40,48},{48,56},{56,64},{64,7... | collective-permute-start | bytes 147464 | tf_op jit(solution)/shard_map/ppermute | solution.py:686
  18.9 8.1 %collective-permute-start.1 = (bf16[160,128]{1,0:T(8,128)(2,1)S(1)}, bf16[160,128]{1,0:T(8,128)(2,1)S(1)}, u32[]{:S(2)}, u32[]{:S(2)}) collective-permute-start(bf16[160,128]{1,0:T(8,128)(2,1)S(1)} %copy-done.17), channel_id=1, source_target_pairs={{0,248},{8,0},{16,8},{24,16},{32,24},{40,32},{48,40},{56,48},{64,5... | collective-permute-start | bytes 122888 | tf_op jit(solution)/shard_map/ppermute | solution.py:687
  27.0 0.6 copy-start.10
  28.9 25.9 %copy-start.2 = (bf16[8,312,128]{2,1,0:T(8,128)(2,1)}, bf16[8,312,128]{2,1,0:T(8,128)(2,1)S(1)}, u32[]{:S(2)}) copy-start(bf16[8,312,128]{2,1,0:T(8,128)(2,1)S(1)} %all-to-all-done.recv_ref) | copy-start | bytes 1916932
  29.0 1.3 %collective-permute-start.2 = (bf16[144,128]{1,0:T(8,128)(2,1)S(1)}, bf16[144,128]{1,0:T(8,128)(2,1)S(1)}, u32[]{:S(2)}, u32[]{:S(2)}) collective-permute-start(bf16[144,128]{1,0:T(8,128)(2,1)S(1)} %unpack.1.rows_ref.before_ref), channel_id=1, source_target_pairs={{0,8},{8,0},{16,24},{24,16},{32,40},{40,32},{48,56},{56,48},{64,72... | collective-permute-start | bytes 110600 | tf_op jit(solution)/shard_map/ppermute | solution.py:674
  56.3 24.0 %copy-start = (bf16[45,160,128]{2,1,0:T(8,128)(2,1)S(1)}, bf16[45,160,128]{2,1,0:T(8,128)(2,1)}, u32[]{:S(2)}) copy-start(bf16[45,160,128]{2,1,0:T(8,128)(2,1)} %cells_ref.3) | copy-start | bytes 5529604
  56.3 24.0 %copy-start.1 = (bf16[45,64,128]{2,1,0:T(8,128)(2,1)S(1)}, bf16[45,64,128]{2,1,0:T(8,128)(2,1)}, u32[]{:S(2)}) copy-start(bf16[45,64,128]{2,1,0:T(8,128)(2,1)} %winds_ref.5) | copy-start | bytes 2211844
  56.3 13.1 %all-to-all-start.2 = ((bf16[8,192,128]{2,1,0:T(8,128)(2,1)}), bf16[8,192,128]{2,1,0:T(8,128)(2,1)S(1)}, u32[]{:S(2)}, u32[]{:S(2)}) async-start(bf16[8,192,128]{2,1,0:T(8,128)(2,1)} %total.2), calls=%async_computation.2 | async-start | bytes 786432 | tf_op jit(solution)/shard_map/all_to_all | solution.py:670
  60.1 1.1 copy-start.3
  62.0 0.7 copy-start.7
  62.7 5.1 %collective-permute-start.6 = (f32[8,128]{1,0:T(8,128)S(1)}, f32[8,128]{1,0:T(8,128)S(1)}, u32[]{:S(2)}, u32[]{:S(2)}) collective-permute-start(f32[8,128]{1,0:T(8,128)S(1)} %get-tuple-element.34), channel_id=1, source_target_pairs={{0,8},{8,16},{16,24},{24,32},{32,40},{40,48},{48,56},{56,64},{64,7... | collective-permute-start | bytes 12296 | tf_op jit(solution)/shard_map/ppermute | solution.py:692
  62.7 5.2 %collective-permute-start.7 = (f32[8,128]{1,0:T(8,128)S(1)}, f32[8,128]{1,0:T(8,128)S(1)}, u32[]{:S(2)}, u32[]{:S(2)}) collective-permute-start(f32[8,128]{1,0:T(8,128)S(1)} %get-tuple-element.35), channel_id=1, source_target_pairs={{0,248},{8,0},{16,8},{24,16},{32,24},{40,32},{48,40},{56,48},{64,5... | collective-permute-start | bytes 12296 | tf_op jit(solution)/shard_map/ppermute | solution.py:693
  69.3 0.9 copy-start.8
  71.3 1.3 %collective-permute-start.8 = (bf16[144,128]{1,0:T(8,128)(2,1)S(1)}, bf16[144,128]{1,0:T(8,128)(2,1)S(1)}, u32[]{:S(2)}, u32[]{:S(2)}) collective-permute-start(bf16[144,128]{1,0:T(8,128)(2,1)S(1)} %rows.1.rows_ref), channel_id=1, source_target_pairs={{0,8},{8,0},{16,24},{24,16},{32,40},{40,32},{48,56},{56,48},{64,72... | collective-permute-start | bytes 110600 | tf_op jit(solution)/shard_map/ppermute | solution.py:674
  73.1 0.8 copy-start.4
  73.9 20.7 %all-to-all-start.3 = ((bf16[16,120,128]{2,1,0:T(8,128)(2,1)}), bf16[16,120,128]{2,1,0:T(8,128)(2,1)S(1)}, u32[]{:S(2)}, u32[]{:S(2)}) async-start(bf16[16,120,128]{2,1,0:T(8,128)(2,1)} %copy-done.4), calls=%async_computation.3 | async-start | bytes 983040 | tf_op jit(solution)/shard_map/all_to_all | solution.py:676
  80.3 0.8 copy-start.11
  91.6 1.2 %copy-start.5 = (bf16[45,160,128]{2,1,0:T(8,128)(2,1)}, bf16[45,160,128]{2,1,0:T(8,128)(2,1)S(1)}, u32[]{:S(2)}) copy-start(bf16[45,160,128]{2,1,0:T(8,128)(2,1)S(1)} %get-tuple-element.30.cells_ref) | copy-start | bytes 5529604
  92.9 0.6 copy-start.13
  93.5 0.6 copy-start.14
  96.0 14.9 %all-to-all-start.4 = ((bf16[8,192,128]{2,1,0:T(8,128)(2,1)}), bf16[8,192,128]{2,1,0:T(8,128)(2,1)S(1)}, u32[]{:S(2)}, u32[]{:S(2)}) async-start(bf16[8,192,128]{2,1,0:T(8,128)(2,1)} %total.3), calls=%async_computation.4 | async-start | bytes 786432 | tf_op jit(solution)/shard_map/all_to_all | solution.py:670
  101.4 5.8 %collective-permute-start.4 = (bf16[160,128]{1,0:T(8,128)(2,1)}, bf16[160,128]{1,0:T(8,128)(2,1)S(1)}, u32[]{:S(2)}, u32[]{:S(2)}) collective-permute-start(bf16[160,128]{1,0:T(8,128)(2,1)} %copy-done.14), channel_id=1, source_target_pairs={{0,8},{8,16},{16,24},{24,32},{32,40},{40,48},{48,56},{56,64},{64,7... | collective-permute-start | bytes 122888 | tf_op jit(solution)/shard_map/ppermute | solution.py:698
  101.4 5.8 %collective-permute-start.5 = (bf16[160,128]{1,0:T(8,128)(2,1)}, bf16[160,128]{1,0:T(8,128)(2,1)S(1)}, u32[]{:S(2)}, u32[]{:S(2)}) collective-permute-start(bf16[160,128]{1,0:T(8,128)(2,1)} %copy-done.13), channel_id=1, source_target_pairs={{0,248},{8,0},{16,8},{24,16},{32,24},{40,32},{48,40},{56,48},{64,5... | collective-permute-start | bytes 122888 | tf_op jit(solution)/shard_map/ppermute | solution.py:699
  110.9 1.5 %copy-start.6 = (bf16[45,160,128]{2,1,0:T(8,128)(2,1)S(1)}, bf16[45,160,128]{2,1,0:T(8,128)(2,1)}, u32[]{:S(2)}) copy-start(bf16[45,160,128]{2,1,0:T(8,128)(2,1)} %copy-done.5) | copy-start | bytes 5529604

commit v4 on v3

--- a/solution.py
+++ b/solution.py
@@ -26,6 +26,9 @@
 BF16 = jnp.bfloat16
 VM = pl.BlockSpec(memory_space=pltpu.VMEM)
 SM = pl.BlockSpec(memory_space=pltpu.SMEM)
+HB = pl.BlockSpec(memory_space=pl.ANY)
+DMA = pltpu.SemaphoreType.DMA
+SPANS = [(start, min(8, XS - start)) for start in range(0, XS, 8)]
 
 
 def shape(dims, kind):
@@ -93,7 +96,7 @@
         out_shape=(out, out),
         in_specs=[SM, VM],
         out_specs=(VM, VM),
-        compiler_params=params(16),
+        compiler_params=params(6),
         name="operators",
     )(meta, ops)
 
@@ -114,16 +117,19 @@
 
 def pick_weights(meta_ref):
     me = meta_ref[0]
-    sub, lane = iotas((PICKS, LANES))
-    target = jnp.full(sub.shape, -1, jnp.int32)
+    lane = lax.broadcasted_iota(jnp.int32, (8, LANES), 1)
+    pick = lane & 63
+    target = jnp.full(lane.shape, -1, jnp.int32)
     for block in range(BLOCKS):
         at = global_row(meta_ref, block) - me * LANES
         for near in range(3):
-            k = near * BLOCKS + slot(block)
-            target = jnp.where(sub == k, at + (near - 1), target)
-    target = jnp.where(sub == 3 * BLOCKS, 0, target)
-    target = jnp.where(sub == 3 * BLOCKS + 1, LANES - 1, target)
-    return jnp.where(lane == target, 1.0, 0.0).astype(BF16)
+            target = jnp.where(pick == near * BLOCKS + slot(block), at + (near - 1), target)
+    target = jnp.where(pick == 3 * BLOCKS, 0, target)
+    target = jnp.where(pick == 3 * BLOCKS + 1, LANES - 1, target)
+    sub, lane = iotas((LANES, LANES))
+    hit = sub == jnp.broadcast_to(target[:1], (LANES, LANES))
+    halves = [jnp.where(hit & ((lane < 64) == side), 1.0, 0.0) for side in (True, False)]
+    return jnp.concatenate(halves, axis=0).astype(BF16)
 
 
 def keep(value, *starts):
@@ -155,38 +161,42 @@
     return jnp.concatenate([lanes_below(low, limit), lanes_below(high, limit)], axis=0)
 
 
-def pack_messages(meta_ref, main_ref, rest_ref, send_ref, edges_ref):
+def pack_messages(meta_ref, main_ref, rest_ref, send_ref, edges_ref, leaving):
     me = meta_ref[0]
 
     def picked(ref, k):
         return ref[k * ROWS : (k + 1) * ROWS, :]
 
-    for d in range(BANDS):
-        tails, winds, souths = [], [], []
-        for e in range(2):
-            k = e * BANDS + d
+    def add(d, start, count, value):
+        span = slice(start, start + count)
+        send_ref[d, span, :] = (send_ref[d, span, :].astype(F32) + value).astype(BF16)
+
+    for block in range(BLOCKS):
+        d, e = block // 2, block % 2
+        k = slot(block)
+        at = global_row(meta_ref, block) - me * LANES
+
+        @pl.when((at >= -1) & (at <= LANES))
+        def _():
+            mine = (at >= 0) & (at < LANES)
             here = picked(rest_ref, BLOCKS + k)
             behind = picked(rest_ref, k)
-            ahead = picked(rest_ref, 2 * BLOCKS + k)
-            mine = meta_ref[2 + 2 * d + e] == me
-            along = pull(here, 2 * LEV)
             before = pull(behind, 2 * LEV)
-            north = jnp.where(mine, jnp.maximum(along, 0.0), lanes_below(jnp.ones_like(along), LEV))
-            south = jnp.where(mine, jnp.minimum(before, 0.0), -lanes_below(jnp.ones_like(along), LEV))
+            one = lanes_below(jnp.ones_like(here), LEV)
+            north = jnp.where(mine, jnp.maximum(pull(here, 2 * LEV), 0.0), one)
+            south = jnp.where(mine, jnp.minimum(before, 0.0), -one)
             main = wide(north) * picked(main_ref, 2 * BLOCKS + k) - wide(south) * picked(main_ref, k)
-            rest = north * ahead - south * behind
+            rest = north * picked(rest_ref, 2 * BLOCKS + k) - south * behind
             send_ref[d, e * ROWS : (e + 1) * ROWS, :] = picked(main_ref, BLOCKS + k).astype(BF16)
             send_ref[d, (2 + e) * ROWS : (3 + e) * ROWS, :] = main.astype(BF16)
-            tails.append((keep(here, 0), rest))
-            winds.append(keep(here, LEV, 2 * LEV))
-            souths.append(before)
-        tail = tails[0][0] + pltpu.roll(tails[1][0], LEV, axis=1)
-        tail = tail + pltpu.roll(tails[0][1], 2 * LEV, axis=1) + pltpu.roll(tails[1][1], 3 * LEV, axis=1)
-        send_ref[d, 4 * ROWS : 5 * ROWS, :] = tail.astype(BF16)
-        wind = pltpu.roll(winds[0], 3 * LEV, axis=1) + pltpu.roll(winds[1], LEV, axis=1)
-        send_ref[d, 5 * ROWS : 6 * ROWS, :] = wind.astype(BF16)
-        south = souths[0] + pltpu.roll(souths[1], LEV, axis=1)
-        send_ref[d, 6 * ROWS :, :] = folded(south, 2 * LEV).astype(BF16)
+            tail = keep(here, 0) + pltpu.roll(rest, 2 * LEV, axis=1)
+            add(d, 4 * ROWS, ROWS, pltpu.roll(tail, LEV, axis=1) if e else tail)
+            add(d, 5 * ROWS, ROWS, pltpu.roll(keep(here, LEV, 2 * LEV), (1 if e else 3) * LEV, axis=1))
+            add(d, 6 * ROWS, ROWS // 2, folded(pltpu.roll(before, LEV, axis=1) if e else before, 2 * LEV))
+
+        if e:
+            leaving[d].start()
+
     for at in range(2):
         k = 3 * BLOCKS + at
         edges_ref[at, :ROWS, :] = picked(main_ref, k).astype(BF16)
@@ -200,30 +210,48 @@
         ref[...] = jnp.zeros(ref.shape, ref.dtype)
 
 
-def pick_kernel(meta_ref, cells_ref, winds_ref, send_ref, edges_ref, east_ref, west_ref, main_ref, rest_ref):
-    step = pl.program_id(0)
-
-    @pl.when(step == 0)
-    def _():
-        clear_rims(main_ref, PICKS)
-        clear_rims(rest_ref, PICKS)
-        west_ref[...] = cells_ref[0]
-
+def copies(source_ref, target_ref, sem_ref):
+    return [
+        pltpu.make_async_copy(source_ref.at[pl.ds(start, size)], target_ref.at[pl.ds(start, size)], sem_ref.at[n])
+        for n, (start, size) in enumerate(SPANS)
+    ]
+
+
+def pick_kernel(
+    meta_ref, cells_hbm, winds_hbm, send_hbm, edges_ref, east_ref, west_ref,
+    main_ref, rest_ref, cells_ref, winds_ref, send_ref, cells_sem, winds_sem, send_sem,
+):
+    arriving = list(zip(copies(cells_hbm, cells_ref, cells_sem), copies(winds_hbm, winds_ref, winds_sem)))
+    for pair in arriving:
+        for copy in pair:
+            copy.start()
+    clear_rims(main_ref, PICKS)
+    clear_rims(rest_ref, PICKS)
     weights = pick_weights(meta_ref)
-    blank = jnp.zeros((LEV, LANES), BF16)
-    for y in range(CHUNK):
-        main = dot_nt(weights, cells_ref[y, :LANES, :])
-        tail = jnp.concatenate([cells_ref[y, LANES:, :], winds_ref[y], blank], axis=0)
-        rest = dot_nt(weights, tail)
-        at = pl.ds(step * CHUNK + y + 1, PICKS, stride=ROWS)
-        main_ref[at, :] = main
-        rest_ref[at, :] = rest
-
-    @pl.when(step == XS // CHUNK - 1)
-    def _():
-        pack_messages(meta_ref, main_ref, rest_ref, send_ref, edges_ref)
-        east_ref[:COLS, :] = cells_ref[CHUNK - 1]
-        east_ref[COLS:, :] = winds_ref[CHUNK - 1, :LEV, :]
+    clear(send_ref)
+    blank = jnp.zeros((LEV, 2 * LANES), BF16)
+    for (start, size), pair in zip(SPANS, arriving):
+        for copy in pair:
+            copy.wait()
+        for y in range(start, start + size, 2):
+            both = (y, min(y + 1, XS - 1))
+            main = jnp.concatenate([cells_ref[z, :LANES, :] for z in both], axis=1)
+            rest = jnp.concatenate([cells_ref[z, LANES:, :] for z in both], axis=1)
+            wind = jnp.concatenate([winds_ref[z] for z in both], axis=1)
+            rest = jnp.concatenate([rest, wind, blank], axis=0)
+            main = jnp.dot(main, weights, preferred_element_type=F32).astype(BF16).T.astype(F32)
+            rest = jnp.dot(rest, weights, preferred_element_type=F32).astype(BF16).T.astype(F32)
+            for side in range(min(2, XS - y)):
+                at = pl.ds(y + side + 1, PICKS, stride=ROWS)
+                main_ref[at, :] = main[64 * side : 64 * side + PICKS]
+                rest_ref[at, :] = rest[64 * side : 64 * side + PICKS]
+    east_ref[:COLS, :] = cells_ref[XS - 1]
+    east_ref[COLS:, :] = winds_ref[XS - 1, :LEV, :]
+    west_ref[...] = cells_ref[0]
+    leaving = [pltpu.make_async_copy(send_ref.at[d], send_hbm.at[d], send_sem.at[d]) for d in range(BANDS)]
+    pack_messages(meta_ref, main_ref, rest_ref, send_ref, edges_ref, leaving)
+    for copy in leaving:
+        copy.wait()
 
 
 STAGE = pltpu.VMEM((24 * ROWS, LANES), F32)
@@ -233,20 +261,24 @@
 def pick_rows(meta, cells, winds):
     return pl.pallas_call(
         pick_kernel,
-        grid=(XS // CHUNK,),
         out_shape=(
             shape((BANDS, WIRE, LANES), BF16),
             shape((2, HALO, LANES), BF16),
             shape((COLS + LEV, LANES), BF16),
             shape((COLS, LANES), BF16),
         ),
-        in_specs=[
-            SM,
-            pl.BlockSpec((CHUNK, COLS, LANES), lambda i: (i, 0, 0)),
-            pl.BlockSpec((CHUNK, 2 * LEV, LANES), lambda i: (i, 0, 0)),
+        in_specs=[SM, HB, HB],
+        out_specs=(HB, VM, VM, VM),
+        scratch_shapes=[
+            PICKED,
+            PICKED,
+            pltpu.VMEM((XS, COLS, LANES), BF16),
+            pltpu.VMEM((XS, 2 * LEV, LANES), BF16),
+            pltpu.VMEM((BANDS, WIRE, LANES), BF16),
+            DMA((len(SPANS),)),
+            DMA((len(SPANS),)),
+            DMA((BANDS,)),
         ],
-        out_specs=(VM,) * 4,
-        scratch_shapes=[PICKED, PICKED],
         compiler_params=params(58),
         name="pick",
     )(meta, cells, winds)
@@ -358,7 +390,7 @@
         out_shape=shape((TARGETS, PACK, LANES), BF16),
         in_specs=[VM] * 4,
         out_specs=VM,
-        compiler_params=params(12),
+        compiler_params=params(6),
         name="product",
     )(rows, other, own_ops, other_ops)
 
@@ -381,7 +413,7 @@
         out_shape=shape((BANDS, PACK + HALO, LANES), BF16),
         in_specs=[SM, VM, VM],
         out_specs=VM,
-        compiler_params=params(8),
+        compiler_params=params(4),
         name="total",
     )(meta, recv, edges)
 
@@ -420,21 +452,37 @@
     return main, rest
 
 
-def stage_corrections(meta_ref, recv_ref, wind_recv_ref, main_ref, rest_ref):
-    stage_blocks(recv_ref, main_ref, rest_ref)
-    main_ref[18 * ROWS :, :] = jnp.zeros((6 * ROWS, LANES), F32)
-    rest_ref[18 * ROWS :, :] = jnp.zeros((6 * ROWS, LANES), F32)
+KEPT = 32
+GROUP = LANES // KEPT
+TALL = COLS + LEV
+
+
+def stage_corrections(meta_ref, recv_ref, wind_recv_ref, main_ref, rest_ref, tall_ref):
+    clear(main_ref, rest_ref)
     me = meta_ref[0]
     halos = halo_rows(meta_ref, recv_ref)
-    for at, row in enumerate((me * LANES - 1, (me + 1) * LANES)):
-        main, rest = block_sum(meta_ref, row, main_ref, rest_ref)
-        k = (16 + at) * ROWS
-        main = (halos[at][0] + main).astype(BF16).astype(F32)
-        rest = (halos[at][1] + rest).astype(BF16).astype(F32)
-        main_ref[k : k + ROWS, :] = main
-        rest_ref[k : k + ROWS, :] = rest
+    sums = [list(halos[0]), list(halos[1])]
+    for source in range(BANDS):
+        packed = recv_ref[source, 2 * ROWS : PACK, :].astype(F32)
+        for b in range(2):
+            k = b * BANDS + source
+            main = recv_ref[source, b * ROWS : (b + 1) * ROWS, :].astype(F32)
+            rest = unfolded(packed, b * LEV, 2 * LEV, LEV)
+            main_ref[pl.ds(k, ROWS, stride=KEPT), :] = main
+            rest_ref[pl.ds(k, ROWS, stride=KEPT), :] = rest
+            for at, row in enumerate((me * LANES - 1, (me + 1) * LANES)):
+                share = jnp.where(global_row(meta_ref, 2 * source + b) == row, 1.0, 0.0)
+                sums[at][0] = sums[at][0] + share * main
+                sums[at][1] = sums[at][1] + share * rest
+    for at in range(2):
+        main_ref[pl.ds(16 + at, ROWS, stride=KEPT), :] = sums[at][0].astype(BF16).astype(F32)
+        rest_ref[pl.ds(16 + at, ROWS, stride=KEPT), :] = sums[at][1].astype(BF16).astype(F32)
     wind = halo_rows(meta_ref, wind_recv_ref)[2]
-    rest_ref[18 * ROWS : 19 * ROWS, :] = pltpu.roll(wind, LEV, axis=1)
+    rest_ref[pl.ds(18, ROWS, stride=KEPT), :] = pltpu.roll(wind, LEV, axis=1)
+    for t in range(ROWS // GROUP):
+        span = slice(t * LANES, (t + 1) * LANES)
+        tall_ref[t * TALL : t * TALL + LANES, :] = main_ref[span, :].T.astype(BF16)
+        tall_ref[t * TALL + LANES : (t + 1) * TALL, :] = rest_ref[span, :].T[: 2 * LEV].astype(BF16)
 
 
 def rows_kernel(meta_ref, before_ref, context_ref, west_ref, east_ref, recv_ref, out_ref, main_ref, rest_ref):
@@ -490,46 +538,48 @@
         in_specs=[SM] + [VM] * 5,
         out_specs=VM,
         scratch_shapes=[STAGE, STAGE],
-        compiler_params=params(16),
+        compiler_params=params(4),
         name="rows",
     )(*args)
 
 
-def place_weights(meta_ref):
-    sub, lane = iotas((24, 2 * LANES))
+def place_weights(meta_ref, q):
+    sub, lane = iotas((LANES, 2 * LANES))
+    kept = sub - q * KEPT
     target = jnp.full(sub.shape, -1, jnp.int32)
     for block in range(BLOCKS):
         at = global_row(meta_ref, block) - meta_ref[0] * LANES
-        target = jnp.where(sub == slot(block), jnp.where((at >= 0) & (at < LANES), at, -1), target)
-    target = jnp.where((sub == 16) | (sub == 18), LANES, target)
-    target = jnp.where(sub == 17, 2 * LANES - 1, target)
+        target = jnp.where(kept == slot(block), jnp.where((at >= 0) & (at < LANES), at, -1), target)
+    target = jnp.where((kept == 16) | (kept == 18), LANES, target)
+    target = jnp.where(kept == 17, 2 * LANES - 1, target)
     return jnp.where(lane == target, 1.0, 0.0).astype(BF16)
 
 
-def smooth_all(weights, cells_ref, west_ref, east_ref, main_ref, rest_ref, smooth_ref, edge_ref, wind_ref):
-    def placed(r):
-        main = main_ref[pl.ds(r, 24, stride=ROWS), :].astype(BF16)
-        rest = rest_ref[pl.ds(r, 24, stride=ROWS), :].astype(BF16)
-        return dot_tn(main, weights), dot_tn(rest, weights)
-
-    def store(r, base):
-        main, rest = placed(r)
-        base = base.astype(F32)
-        smooth_ref[r, :LANES, :] = (base[:LANES] + main[:, :LANES]).astype(BF16).astype(F32)
-        smooth_ref[r, LANES:, :] = (base[LANES:] + rest[:LEV, :LANES]).astype(BF16).astype(F32)
-        return main, rest
-
-    store(0, west_ref[:COLS, :])
-    store(XS + 1, east_ref[...])
-
-    def body(x, carry):
-        main, rest = store(x + 1, cells_ref[x])
-        edge_ref[x, :LANES, :] = main[:, LANES:]
-        edge_ref[x, LANES:, :] = rest[:LEV, LANES:]
-        wind_ref[x] = rest[LEV : 2 * LEV, LANES:]
-        return carry
-
-    lax.fori_loop(0, XS, body, 0, unroll=3)
+def smooth_all(meta_ref, cells_ref, west_ref, east_ref, tall_ref, placed_ref, smooth_ref, edge_ref, wind_ref):
+    for q in range(GROUP):
+        placed_ref[...] = jnp.dot(tall_ref[...], place_weights(meta_ref, q), preferred_element_type=F32)
+
+        def store(t, r, base):
+            at = pl.multiple_of(t * TALL, TALL)
+            change = placed_ref[pl.ds(at, COLS), :LANES]
+            smooth_ref[r] = (base.astype(F32) + change).astype(BF16).astype(F32)
+
+        def body(t, carry):
+            r = GROUP * t + q
+            x = r - 1
+            store(t, r, cells_ref[x])
+            at = pl.multiple_of(t * TALL, TALL)
+            edge_ref[x] = placed_ref[pl.ds(at, COLS), LANES:]
+            wind_ref[x] = placed_ref[pl.ds(at + COLS, LEV), LANES:]
+            return carry
+
+        first = 1 if q == 0 else 0
+        last = (XS - q) // GROUP + 1
+        if q == 0:
+            store(0, 0, west_ref[:COLS, :])
+        if (XS + 1) % GROUP == q:
+            store((XS + 1) // GROUP, XS + 1, east_ref[...])
+        lax.fori_loop(first, last, body, 0, unroll=True)
 
 
 def stencil(x, top, winds_ref, west_ref, smooth_ref, edge_ref, wind_ref):
@@ -561,8 +611,10 @@
 
 
 SCRATCH = [
-    STAGE,
-    STAGE,
+    pltpu.VMEM((KEPT * ROWS, LANES), F32),
+    pltpu.VMEM((KEPT * ROWS, LANES), F32),
+    pltpu.VMEM((ROWS // GROUP * TALL, LANES), BF16),
+    pltpu.VMEM((ROWS // GROUP * TALL, 2 * LANES), F32),
     pltpu.VMEM((XS + 2, COLS, LANES), F32),
     pltpu.VMEM((XS, COLS, LANES), F32),
     pltpu.VMEM((XS, LEV, LANES), F32),
@@ -570,38 +622,53 @@
 
 
 def first_kernel(
-    meta_ref, cells_ref, winds_ref, west_ref, east_ref, recv_ref,
-    out_ref, edges_ref, to_east_ref, to_west_ref, main_ref, rest_ref, smooth_ref, edge_ref, wind_ref,
+    meta_ref, cells_hbm, winds_hbm, west_ref, east_ref, recv_ref,
+    out_hbm, edges_ref, to_east_hbm, to_west_hbm,
+    main_ref, rest_ref, tall_ref, placed_ref, smooth_ref, edge_ref, wind_ref, out_ref, out_sem, rim_sem,
+    cells_ref, cells_sem, winds_ref, winds_sem,
 ):
-    stage_corrections(meta_ref, recv_ref, recv_ref, main_ref, rest_ref)
-    smooth_all(
-        place_weights(meta_ref), cells_ref, west_ref, east_ref, main_ref, rest_ref, smooth_ref, edge_ref, wind_ref
-    )
-    clear_rims(main_ref, 2)
-    clear_rims(rest_ref, 2)
-    sub, lane = iotas((8, LANES))
-    ends = jnp.where((lane == 0) & (sub == 0) | (lane == LANES - 1) & (sub == 1), 1.0, 0.0).astype(BF16)
+    arriving = copies(cells_hbm, cells_ref, cells_sem) + copies(winds_hbm, winds_ref, winds_sem)
+    for copy in arriving:
+        copy.start()
+    stage_corrections(meta_ref, recv_ref, recv_ref, main_ref, rest_ref, tall_ref)
+    for copy in arriving:
+        copy.wait()
+    smooth_all(meta_ref, cells_ref, west_ref, east_ref, tall_ref, placed_ref, smooth_ref, edge_ref, wind_ref)
     top = meta_ref[0] == BANDS - 1
-    blank = jnp.zeros((3 * LEV, LANES), BF16)
 
     def body(x, carry):
-        made = [m.astype(BF16) for m in stencil(x, top, winds_ref, west_ref, smooth_ref, edge_ref, wind_ref)]
+        made = stencil(x, top, winds_ref, west_ref, smooth_ref, edge_ref, wind_ref)
         for v in range(VAR):
-            out_ref[x, v * LEV : (v + 1) * LEV, :] = made[v]
-        at = pl.ds(x + 1, 2, stride=ROWS)
-        main_ref[at, :] = dot_nt(ends, jnp.concatenate(made[:4], axis=0))[:2]
-        rest_ref[at, :] = dot_nt(ends, jnp.concatenate([made[4], blank], axis=0))[:2]
+            out_ref[x, v * LEV : (v + 1) * LEV, :] = made[v].astype(BF16)
         return carry
 
-    lax.fori_loop(0, XS, body, 0, unroll=3)
+    leaving = copies(out_ref, out_hbm, out_sem)
+    leaving.append(pltpu.make_async_copy(out_ref.at[0], to_west_hbm, rim_sem.at[0]))
+    leaving.append(pltpu.make_async_copy(out_ref.at[XS - 1], to_east_hbm, rim_sem.at[1]))
+    for (start, size), copy in zip(SPANS, leaving):
+        lax.fori_loop(start, start + size, body, 0, unroll=4)
+        copy.start()
+    for copy in leaving[-2:]:
+        copy.start()
+    sub, lane = iotas((LANES, LANES))
+    halves = [(sub == 0) & (lane == 2 * side) | (sub == LANES - 1) & (lane == 2 * side + 1) for side in range(2)]
+    ends = jnp.concatenate([jnp.where(hit, 1.0, 0.0) for hit in halves], axis=0).astype(BF16)
+    total = None
+    for x in range(0, XS, 2):
+        pair = jnp.concatenate([out_ref[min(x + side, XS - 1)] for side in range(2)], axis=1)
+        found = jnp.dot(pair, ends, preferred_element_type=F32)
+        if x == XS - 1:
+            found = jnp.where(lax.broadcasted_iota(jnp.int32, found.shape, 1) < 2, found, 0.0)
+        found = pltpu.roll(found, 2 * x + 2, axis=1)
+        total = found if total is None else total + found
+    main_ref[:LANES, :] = total[:LANES].T
+    rest = jnp.concatenate([total[LANES:], jnp.zeros((LANES - LEV, LANES), F32)], axis=0)
+    rest_ref[:LANES, :] = rest.T
     for at in range(2):
-        k = at * ROWS
-        edges_ref[at, :ROWS, :] = main_ref[k : k + ROWS, :].astype(BF16)
-        rest = rest_ref[k : k + ROWS, :]
-        packed = rest[: ROWS // 2] + pltpu.roll(rest[ROWS // 2 :], LEV, axis=1)
-        edges_ref[at, ROWS:, :] = packed.astype(BF16)
-    to_east_ref[...] = out_ref[XS - 1]
-    to_west_ref[...] = out_ref[0]
+        edges_ref[at, :ROWS, :] = main_ref[pl.ds(at, ROWS, stride=2), :].astype(BF16)
+        edges_ref[at, ROWS:, :] = folded(rest_ref[pl.ds(at, ROWS, stride=2), :], LEV).astype(BF16)
+    for copy in leaving:
+        copy.wait()
 
 
 def first_substep(*args):
@@ -613,27 +680,34 @@
             shape((COLS, LANES), BF16),
             shape((COLS, LANES), BF16),
         ),
-        in_specs=[SM] + [VM] * 5,
-        out_specs=(VM,) * 4,
-        scratch_shapes=SCRATCH,
-        compiler_params=params(16),
+        in_specs=[SM, HB, HB] + [VM] * 3,
+        out_specs=(HB, VM, HB, HB),
+        scratch_shapes=SCRATCH
+        + [
+            pltpu.VMEM((XS, COLS, LANES), BF16),
+            DMA((len(SPANS),)),
+            DMA((2,)),
+            pltpu.VMEM((XS, COLS, LANES), BF16),
+            DMA((len(SPANS),)),
+            pltpu.VMEM((XS, 2 * LEV, LANES), BF16),
+            DMA((len(SPANS),)),
+        ],
+        compiler_params=params(58),
         name="first",
     )(*args)
 
 
 def last_kernel(
     meta_ref, cells_ref, winds_ref, west_ref, east_ref, recv_ref, wind_recv_ref, wind_west_ref,
-    out_ref, main_ref, rest_ref, smooth_ref, edge_ref, wind_ref,
+    out_ref, main_ref, rest_ref, tall_ref, placed_ref, smooth_ref, edge_ref, wind_ref,
 ):
     me = meta_ref[0]
     step = pl.program_id(0)
 
     @pl.when(step == 0)
     def _():
-        stage_corrections(meta_ref, recv_ref, wind_recv_ref, main_ref, rest_ref)
-        smooth_all(
-            place_weights(meta_ref), cells_ref, west_ref, east_ref, main_ref, rest_ref, smooth_ref, edge_ref, wind_ref
-        )
+        stage_corrections(meta_ref, recv_ref, wind_recv_ref, main_ref, rest_ref, tall_ref)
+        smooth_all(meta_ref, cells_ref, west_ref, east_ref, tall_ref, placed_ref, smooth_ref, edge_ref, wind_ref)
 
     top = me == BANDS - 1
 
@@ -655,7 +729,7 @@
         in_specs=[SM] + [VM] * 7,
         out_specs=pl.BlockSpec((CHUNK, COLS, LANES), lambda i: (i, 0, 0)),
         scratch_shapes=SCRATCH,
-        compiler_params=params(20),
+        compiler_params=params(16),
         name="last",
     )(*args)
 
@@ -691,6 +765,7 @@
     context, row_east, row_west = unpack_context(meta, recv, rows)
     row_from_west = lax.ppermute(row_east, "lon", EASTWARD)
     row_from_east = lax.ppermute(row_west, "lon", WESTWARD)
+    swapped, row_from_west, row_from_east = lax.optimization_barrier((swapped, row_from_west, row_from_east))
     given = by_lat(totals(meta, swapped, edges))
     rows = next_rows(meta, rows, context, row_from_west, row_from_east, given)
     swapped = filtered(rows, own_ops, other_ops)

time: 124 us -> 116 us (0.935)
  waiting for transfers between devices: 14.2 us -> 25.7 us
  blocking collectives: 24.1 us -> 12.8 us
  local copies, waits for them, and re-layouts: 8.89 us -> 2.43 us
  Pallas kernels: 37 us -> 31.9 us
  starting transfers between devices: 36.7 us -> 41.3 us
    all_to_all x1, blocking collectives: 24.1 us -> 12.8 us  [by_lat(): return lax.all_to_all(messages, 'lat', 0, 0, tiled=True)]
    all_to_all x1 -> x2, starting transfers between devices: 6.4 us -> 16.6 us  [filtered(): lax.all_to_all(partial, 'lon', 0, 0, tiled=True, axis_index_groups=SAME_C...]
    all_to_all x1 -> x2, waiting for transfers between devices: 0.46 us -> 7.63 us  [filtered(): lax.all_to_all(partial, 'lon', 0, 0, tiled=True, axis_index_groups=SAME_C...]
    unnamed x37 -> x29, local copies, waits for them, and re-layouts: 8.81 us -> 2.35 us
    all_to_all x3 -> x2, starting transfers between devices: 15.5 us -> 9.66 us  [by_lat(): return lax.all_to_all(messages, 'lat', 0, 0, tiled=True)]
    ppermute x1, waiting for transfers between devices: 1.29 us -> 6.75 us  [shards(): row_from_west = lax.ppermute(row_east, 'lon', EASTWARD)]
    pallas_call x1, Pallas kernels: 10.1 us -> 7.51 us  [last_substep(): pl.pallas_call(last_kernel, grid=(XS // CHUNK,), out_shape=shape((XS, COL...]
    pallas_call x1, Pallas kernels: 9.39 us -> 7.17 us  [pick_rows(): pl.pallas_call(pick_kernel, out_shape=(shape((BANDS, WIRE, LANES), BF16),...]
  transfers between devices with their start and end apart: 13 -> 13, of which waited for: 9 -> 10; matrix products, arithmetic and copies ran while one was open for 0% -> 0% of each run, Pallas kernels for 10% -> 10%
where the time goes in v4:
time: 116 us
  starting transfers between devices  41.3 us (36%)
  Pallas kernels  31.9 us (28%)
  waiting for transfers between devices  25.7 us (22%)
  blocking collectives  12.8 us (11%)
  local copies, waits for them, and re-layouts  2.43 us (2%)
  other arithmetic  1.29 us (1%)
    all_to_all x2, starting transfers between devices, filtered(): lax.all_to_all(partial, 'lon', 0, 0, tiled=True, axis_index_groups=SAME_C...  16.6 us
    all_to_all x1, blocking collectives, by_lat(): return lax.all_to_all(messages, 'lat', 0, 0, tiled=True)  12.8 us
    all_to_all x2, starting transfers between devices, by_lat(): return lax.all_to_all(messages, 'lat', 0, 0, tiled=True)  9.66 us
    pallas_call x1, Pallas kernels, first_substep(): pl.pallas_call(first_kernel, out_shape=(shape((XS, COLS, LANES), BF16), s...  9.44 us
    all_to_all x2, waiting for transfers between devices, filtered(): lax.all_to_all(partial, 'lon', 0, 0, tiled=True, axis_index_groups=SAME_C...  7.63 us
    pallas_call x1, Pallas kernels, last_substep(): pl.pallas_call(last_kernel, grid=(XS // CHUNK,), out_shape=shape((XS, COL...  7.51 us
    pallas_call x1, Pallas kernels, pick_rows(): pl.pallas_call(pick_kernel, out_shape=(shape((BANDS, WIRE, LANES), BF16),...  7.17 us
    ppermute x1, waiting for transfers between devices, shards(): row_from_west = lax.ppermute(row_east, 'lon', EASTWARD)  6.75 us
  transfers between devices with their start and end apart: 13, of which 10 were waited for; matrix products, arithmetic and copies ran while one was open for 0% of the time, Pallas kernels for 10%

profile of v4, /device:TPU:2, one launch (start us, length us, event | category | flops | bytes accessed | tf_op | source)
XLA Modules:
  0.0 115.6 jit_solution(13683626811860300173)
XLA Ops:
  0.0 1.3 %pad_add_fusion.meta_ref = s32[34]{0:T(128)} fusion(s32[16]{0:T(128)} %param.9, s32[16]{0:T(128)} %param.8, s32[1]{0:T(128)} %bitcast.1, s32[1]{0:T(128)} %bitcast), kind=kLoop, calls=%fused_computation | loop fusion | flops 102 | bytes 272 | tf_op jit(solution)/shard_map/concatenate | solution.py:756
  1.3 7.2 %pick.1 = (bf16[8,312,128]{2,1,0:T(8,128)(2,1)}, bf16[2,72,128]{2,1,0:T(8,128)(2,1)}, bf16[192,128]{1,0:T(8,128)(2,1)}, bf16[160,128]{1,0:T(8,128)(2,1)}) custom-call(s32[34]{0:T(128)} %pad_add_fusion.meta_ref, bf16[45,160,128]{2,1,0:T(8,128)(2,1)} %cells_hbm.3, bf16[45,64,128]{2,1,0:T(8,128)(2,1)} %winds_ref.1), custom_call_target="tpu_custom_call" | custom-call | tf_op jit(solution)/shard_map/pick/pallas_call | solution.py:262
  8.5 6.2 %all-to-all-start = ((bf16[8,312,128]{2,1,0:T(8,128)(2,1)}), bf16[8,312,128]{2,1,0:T(8,128)(2,1)S(1)}, u32[]{:S(2)}, u32[]{:S(2)}) async-start(bf16[8,312,128]{2,1,0:T(8,128)(2,1)} %get-tuple-element.24), calls=%async_computation | async-start | bytes 1277952 | tf_op jit(solution)/shard_map/all_to_all | solution.py:744
  14.8 0.1 pad.4.ops_ref
  14.8 0.0 copy-done.6
  14.8 0.0 copy-start.8
  14.9 1.2 %operators.1 = (bf16[768,96]{1,0:T(8,128)(2,1)S(1)}, bf16[768,96]{1,0:T(8,128)(2,1)S(1)}) custom-call(s32[34]{0:T(128)S(1)} %copy-done.6, bf16[2,48,1440]{2,1,0:T(8,128)(2,1)S(1)} %pad.4.ops_ref), custom_call_target="tpu_custom_call" | custom-call | tf_op jit(solution)/shard_map/operators/pallas_call | solution.py:94
  16.1 0.1 collective-permute-start.3
  16.2 0.5 collective-permute-start
  16.7 6.4 %collective-permute-start.1 = (bf16[160,128]{1,0:T(8,128)(2,1)S(1)}, bf16[160,128]{1,0:T(8,128)(2,1)S(1)}, u32[]{:S(2)}, u32[]{:S(2)}) collective-permute-start(bf16[160,128]{1,0:T(8,128)(2,1)S(1)} %copy-done.13), channel_id=1, source_target_pairs={{0,248},{8,0},{16,8},{24,16},{32,24},{40,32},{48,40},{56,48},{64,5... | collective-permute-start | bytes 122888 | tf_op jit(solution)/shard_map/ppermute | solution.py:761
  23.1 1.7 %collective-permute-done.1.east_ref = bf16[160,128]{1,0:T(8,128)(2,1)S(1)} collective-permute-done((bf16[160,128]{1,0:T(8,128)(2,1)S(1)}, bf16[160,128]{1,0:T(8,128)(2,1)S(1)}, u32[]{:S(2)}, u32[]{:S(2)}) %collective-permute-start.1) | collective-permute-done | bytes 40992 | tf_op jit(solution)/shard_map/ppermute | solution.py:761
  24.8 0.0 collective-permute-done.west_ref.wind_west_ref
  24.8 1.9 %all-to-all-done.recv_ref = bf16[8,312,128]{2,1,0:T(8,128)(2,1)S(1)} async-done(((bf16[8,312,128]{2,1,0:T(8,128)(2,1)}), bf16[8,312,128]{2,1,0:T(8,128)(2,1)S(1)}, u32[]{:S(2)}, u32[]{:S(2)}) %all-to-all-start) | async-done | bytes 639008 | tf_op jit(solution)/shard_map/all_to_all | solution.py:744
  26.8 0.1 collective-permute-start.2
  26.9 0.0 collective-permute-done.3.other_ops_ref
  26.9 1.2 %collective-permute-done.2.other_ref = bf16[144,128]{1,0:T(8,128)(2,1)S(1)} collective-permute-done((bf16[144,128]{1,0:T(8,128)(2,1)S(1)}, bf16[144,128]{1,0:T(8,128)(2,1)S(1)}, u32[]{:S(2)}, u32[]{:S(2)}) %collective-permute-start.2) | collective-permute-done | bytes 36896 | tf_op jit(solution)/shard_map/ppermute | solution.py:748
  28.1 1.3 %product.2 = bf16[16,120,128]{2,1,0:T(8,128)(2,1)} custom-call(bf16[144,128]{1,0:T(8,128)(2,1)S(1)} %unpack.1.rows_ref.before_ref, bf16[144,128]{1,0:T(8,128)(2,1)S(1)} %collective-permute-done.2.other_ref, bf16[768,96]{1,0:T(8,128)(2,1)S(1)} %get-tuple-element.30.own_ops_ref, bf16[768,96]{1,0:T(8,128)(2,1)S(1)} %collective-permute-done.3.other_ops_ref), custom_call_target="tpu_custom_call" | custom-call | tf_op jit(solution)/shard_map/product/pallas_call | solution.py:388
  29.4 9.9 %all-to-all-start.1 = ((bf16[16,120,128]{2,1,0:T(8,128)(2,1)}), bf16[16,120,128]{2,1,0:T(8,128)(2,1)S(1)}, u32[]{:S(2)}, u32[]{:S(2)}) async-start(bf16[16,120,128]{2,1,0:T(8,128)(2,1)} %product.2), calls=%async_computation.1 | async-start | bytes 983040 | tf_op jit(solution)/shard_map/all_to_all | solution.py:750
  39.3 0.9 context.1
  40.2 0.1 collective-permute-start.4
  40.3 3.8 %collective-permute-start.5 = (f32[8,128]{1,0:T(8,128)S(1)}, f32[8,128]{1,0:T(8,128)S(1)}, u32[]{:S(2)}, u32[]{:S(2)}) collective-permute-start(f32[8,128]{1,0:T(8,128)S(1)} %get-tuple-element.33), channel_id=1, source_target_pairs={{0,248},{8,0},{16,8},{24,16},{32,24},{40,32},{48,40},{56,48},{64,5... | collective-permute-start | bytes 12296 | tf_op jit(solution)/shard_map/ppermute | solution.py:767
  44.1 6.7 %collective-permute-done.4.west_ref = f32[8,128]{1,0:T(8,128)S(1)} collective-permute-done((f32[8,128]{1,0:T(8,128)S(1)}, f32[8,128]{1,0:T(8,128)S(1)}, u32[]{:S(2)}, u32[]{:S(2)}) %collective-permute-start.4) | collective-permute-done | bytes 4128 | tf_op jit(solution)/shard_map/ppermute | solution.py:766
  50.8 0.0 collective-permute-done.5.east_ref
  50.8 2.8 %all-to-all-done.1.recv_ref = bf16[16,120,128]{2,1,0:T(8,128)(2,1)S(1)} async-done(((bf16[16,120,128]{2,1,0:T(8,128)(2,1)}), bf16[16,120,128]{2,1,0:T(8,128)(2,1)S(1)}, u32[]{:S(2)}, u32[]{:S(2)}) %all-to-all-start.1) | async-done | bytes 491552 | tf_op jit(solution)/shard_map/all_to_all | solution.py:750
  53.7 0.0 copy-done.8
  53.7 0.6 total.2
  54.3 0.0 copy-done.11
  54.3 0.0 copy-done.4
  54.3 12.8 %all_to_all.25.recv_ref.wind_recv_ref = bf16[8,192,128]{2,1,0:T(8,128)(2,1)S(1)} all-to-all(bf16[8,192,128]{2,1,0:T(8,128)(2,1)S(1)} %total.2), channel_id=1, replica_groups=mesh['lon'=32,'lat'=8] {'lat'}, dimensions={0} | all-to-all | bytes 786432 | tf_op jit(solution)/shard_map/all_to_all | solution.py:744
  67.2 1.0 rows.1.rows_ref
  68.2 0.1 collective-permute-start.8
  68.3 1.2 %collective-permute-done.8.other_ref = bf16[144,128]{1,0:T(8,128)(2,1)S(1)} collective-permute-done((bf16[144,128]{1,0:T(8,128)(2,1)S(1)}, bf16[144,128]{1,0:T(8,128)(2,1)S(1)}, u32[]{:S(2)}, u32[]{:S(2)}) %collective-permute-start.8) | collective-permute-done | bytes 36896 | tf_op jit(solution)/shard_map/ppermute | solution.py:748
  69.5 1.3 %product.3 = bf16[16,120,128]{2,1,0:T(8,128)(2,1)} custom-call(bf16[144,128]{1,0:T(8,128)(2,1)S(1)} %rows.1.rows_ref, bf16[144,128]{1,0:T(8,128)(2,1)S(1)} %collective-permute-done.8.other_ref, bf16[768,96]{1,0:T(8,128)(2,1)S(1)} %get-tuple-element.30.own_ops_ref, bf16[768,96]{1,0:T(8,128)(2,1)S(1)} %collective-permute-done.3.other_ops_ref), custom_call_target="tpu_custom_call" | custom-call | tf_op jit(solution)/shard_map/product/pallas_call | solution.py:388
  70.8 6.7 %all-to-all-start.3 = ((bf16[16,120,128]{2,1,0:T(8,128)(2,1)}), bf16[16,120,128]{2,1,0:T(8,128)(2,1)S(1)}, u32[]{:S(2)}, u32[]{:S(2)}) async-start(bf16[16,120,128]{2,1,0:T(8,128)(2,1)} %product.3), calls=%async_computation.3 | async-start | bytes 983040 | tf_op jit(solution)/shard_map/all_to_all | solution.py:750
  77.5 0.0 copy-start
  77.5 9.4 %first.1 = (bf16[45,160,128]{2,1,0:T(8,128)(2,1)}, bf16[2,72,128]{2,1,0:T(8,128)(2,1)}, bf16[160,128]{1,0:T(8,128)(2,1)}, bf16[160,128]{1,0:T(8,128)(2,1)}) custom-call(s32[34]{0:T(128)} %pad_add_fusion.meta_ref, bf16[45,160,128]{2,1,0:T(8,128)(2,1)} %cells_hbm.3, bf16[45,64,128]{2,1,0:T(8,128)(2,1)} %winds_ref.1, bf16[192,128]{1,0:T(8,128)(2,1)} %copy-done.4, ...), custom_call_target="tpu_custom_call" | custom-call | tf_op jit(solution)/shard_map/first/pallas_call | solution.py:675
  87.0 4.8 %all-to-all-done.3.recv_ref = bf16[16,120,128]{2,1,0:T(8,128)(2,1)S(1)} async-done(((bf16[16,120,128]{2,1,0:T(8,128)(2,1)}), bf16[16,120,128]{2,1,0:T(8,128)(2,1)S(1)}, u32[]{:S(2)}, u32[]{:S(2)}) %all-to-all-start.3) | async-done | bytes 491552 | tf_op jit(solution)/shard_map/all_to_all | solution.py:750
  91.8 0.8 copy-done.9
  92.6 1.4 %total.3 = bf16[8,192,128]{2,1,0:T(8,128)(2,1)} custom-call(s32[34]{0:T(128)S(1)} %copy-done.7, bf16[16,120,128]{2,1,0:T(8,128)(2,1)S(1)} %all-to-all-done.3.recv_ref, bf16[2,72,128]{2,1,0:T(8,128)(2,1)S(1)} %copy-done.9), custom_call_target="tpu_custom_call" | custom-call | tf_op jit(solution)/shard_map/total/pallas_call | solution.py:411
  93.9 3.5 %all-to-all-start.4 = ((bf16[8,192,128]{2,1,0:T(8,128)(2,1)}), bf16[8,192,128]{2,1,0:T(8,128)(2,1)S(1)}, u32[]{:S(2)}, u32[]{:S(2)}) async-start(bf16[8,192,128]{2,1,0:T(8,128)(2,1)} %total.3), calls=%async_computation.4 | async-start | bytes 786432 | tf_op jit(solution)/shard_map/all_to_all | solution.py:744
  97.4 0.1 collective-permute-start.6
  97.5 3.8 %collective-permute-start.7 = (bf16[160,128]{1,0:T(8,128)(2,1)}, bf16[160,128]{1,0:T(8,128)(2,1)S(1)}, u32[]{:S(2)}, u32[]{:S(2)}) collective-permute-start(bf16[160,128]{1,0:T(8,128)(2,1)} %get-tuple-element.38), channel_id=1, source_target_pairs={{0,248},{8,0},{16,8},{24,16},{32,24},{40,32},{48,40},{56,48},{64,5... | collective-permute-start | bytes 122888 | tf_op jit(solution)/shard_map/ppermute | solution.py:774
  101.3 1.9 %collective-permute-done.6.west_ref = bf16[160,128]{1,0:T(8,128)(2,1)S(1)} collective-permute-done((bf16[160,128]{1,0:T(8,128)(2,1)}, bf16[160,128]{1,0:T(8,128)(2,1)S(1)}, u32[]{:S(2)}, u32[]{:S(2)}) %collective-permute-start.6) | collective-permute-done | bytes 40992 | tf_op jit(solution)/shard_map/ppermute | solution.py:773
  103.2 0.1 collective-permute-done.7.east_ref
  103.3 3.3 %all-to-all-done.4.recv_ref = bf16[8,192,128]{2,1,0:T(8,128)(2,1)S(1)} async-done(((bf16[8,192,128]{2,1,0:T(8,128)(2,1)}), bf16[8,192,128]{2,1,0:T(8,128)(2,1)S(1)}, u32[]{:S(2)}, u32[]{:S(2)}) %all-to-all-start.4) | async-done | bytes 393248 | tf_op jit(solution)/shard_map/all_to_all | solution.py:744
  106.6 0.0 copy-start.3
  106.6 1.5 %copy-done.3 = bf16[45,160,128]{2,1,0:T(8,128)(2,1)S(1)} copy-done((bf16[45,160,128]{2,1,0:T(8,128)(2,1)S(1)}, bf16[45,160,128]{2,1,0:T(8,128)(2,1)}, u32[]{:S(2)}) %copy-start.3) | copy-done | bytes 1843224
  108.1 7.5 %last.1 = f32[45,160,128]{2,1,0:T(8,128)} custom-call(s32[34]{0:T(128)S(1)} %copy-done.7, bf16[45,160,128]{2,1,0:T(8,128)(2,1)S(1)} %copy-done.3, bf16[45,64,128]{2,1,0:T(8,128)(2,1)S(1)} %copy-done, bf16[160,128]{1,0:T(8,128)(2,1)S(1)} %collective-permute-done.6.west_ref, bf16[160,128]{1,0:T(8,128)(2,1)S(1)} %collective-permute-done.7.east_ref, ...), custom_call_target="tpu_custom_call" | custom-call | tf_op jit(solution)/shard_map/last/pallas_call | solution.py:725
  (21 shorter events, 0.1 us)
Async XLA Ops:
  1.3 13.4 %copy-start.10 = (bf16[2,45,1440]{2,0,1:T(2,128)(2,1)S(1)}, bf16[2,45,1440]{2,0,1:T(2,128)(2,1)}, u32[]{:S(2)}) copy-start(bf16[2,45,1440]{2,0,1:T(2,128)(2,1)} %param.7) | copy-start | bytes 777604
  8.5 6.4 %copy-start.6 = (s32[34]{0:T(128)S(1)}, s32[34]{0:T(128)}, u32[]{:S(2)}) copy-start(s32[34]{0:T(128)} %pad_add_fusion.meta_ref) | copy-start | bytes 412
  8.5 7.7 %copy-start.12 = (bf16[192,128]{1,0:T(8,128)(2,1)S(1)}, bf16[192,128]{1,0:T(8,128)(2,1)}, u32[]{:S(2)}) copy-start(bf16[192,128]{1,0:T(8,128)(2,1)} %get-tuple-element.25) | copy-start | bytes 147460
  8.5 8.2 %copy-start.13 = (bf16[160,128]{1,0:T(8,128)(2,1)S(1)}, bf16[160,128]{1,0:T(8,128)(2,1)}, u32[]{:S(2)}) copy-start(bf16[160,128]{1,0:T(8,128)(2,1)} %get-tuple-element.26) | copy-start | bytes 122884
  8.5 18.2 %all-to-all-start = ((bf16[8,312,128]{2,1,0:T(8,128)(2,1)}), bf16[8,312,128]{2,1,0:T(8,128)(2,1)S(1)}, u32[]{:S(2)}, u32[]{:S(2)}) async-start(bf16[8,312,128]{2,1,0:T(8,128)(2,1)} %get-tuple-element.24), calls=%async_computation | async-start | bytes 1277952 | tf_op jit(solution)/shard_map/all_to_all | solution.py:744
  14.8 38.8 %copy-start.8 = (bf16[2,72,128]{2,1,0:T(8,128)(2,1)S(1)}, bf16[2,72,128]{2,1,0:T(8,128)(2,1)}, u32[]{:S(2)}) copy-start(bf16[2,72,128]{2,1,0:T(8,128)(2,1)} %get-tuple-element.35.edges_ref) | copy-start | bytes 110596
  16.1 10.8 %collective-permute-start.3 = (bf16[768,96]{1,0:T(8,128)(2,1)S(1)}, bf16[768,96]{1,0:T(8,128)(2,1)S(1)}, u32[]{:S(2)}, u32[]{:S(2)}) collective-permute-start(bf16[768,96]{1,0:T(8,128)(2,1)S(1)} %get-tuple-element.31), channel_id=1, source_target_pairs={{0,8},{8,0},{16,24},{24,16},{32,40},{40,32},{48,56},{56,48},{64,72... | collective-permute-start | bytes 442376 | tf_op jit(solution)/shard_map/ppermute | solution.py:758
  16.2 8.6 %collective-permute-start = (bf16[192,128]{1,0:T(8,128)(2,1)S(1)}, bf16[192,128]{1,0:T(8,128)(2,1)S(1)}, u32[]{:S(2)}, u32[]{:S(2)}) collective-permute-start(bf16[192,128]{1,0:T(8,128)(2,1)S(1)} %copy-done.12), channel_id=1, source_target_pairs={{0,8},{8,16},{16,24},{24,32},{32,40},{40,48},{48,56},{56,64},{64,7... | collective-permute-start | bytes 147464 | tf_op jit(solution)/shard_map/ppermute | solution.py:760
  16.7 8.1 %collective-permute-start.1 = (bf16[160,128]{1,0:T(8,128)(2,1)S(1)}, bf16[160,128]{1,0:T(8,128)(2,1)S(1)}, u32[]{:S(2)}, u32[]{:S(2)}) collective-permute-start(bf16[160,128]{1,0:T(8,128)(2,1)S(1)} %copy-done.13), channel_id=1, source_target_pairs={{0,248},{8,0},{16,8},{24,16},{32,24},{40,32},{48,40},{56,48},{64,5... | collective-permute-start | bytes 122888 | tf_op jit(solution)/shard_map/ppermute | solution.py:761
  24.8 29.5 %copy-start.11 = (bf16[160,128]{1,0:T(8,128)(2,1)}, bf16[160,128]{1,0:T(8,128)(2,1)S(1)}, u32[]{:S(2)}) copy-start(bf16[160,128]{1,0:T(8,128)(2,1)S(1)} %collective-permute-done.1.east_ref) | copy-start | bytes 122884
  24.8 29.5 %copy-start.4 = (bf16[192,128]{1,0:T(8,128)(2,1)}, bf16[192,128]{1,0:T(8,128)(2,1)S(1)}, u32[]{:S(2)}) copy-start(bf16[192,128]{1,0:T(8,128)(2,1)S(1)} %collective-permute-done.west_ref.wind_west_ref) | copy-start | bytes 147460
  26.8 1.3 %collective-permute-start.2 = (bf16[144,128]{1,0:T(8,128)(2,1)S(1)}, bf16[144,128]{1,0:T(8,128)(2,1)S(1)}, u32[]{:S(2)}, u32[]{:S(2)}) collective-permute-start(bf16[144,128]{1,0:T(8,128)(2,1)S(1)} %unpack.1.rows_ref.before_ref), channel_id=1, source_target_pairs={{0,8},{8,0},{16,24},{24,16},{32,40},{40,32},{48,56},{56,48},{64,72... | collective-permute-start | bytes 110600 | tf_op jit(solution)/shard_map/ppermute | solution.py:748
  29.4 24.3 %all-to-all-start.1 = ((bf16[16,120,128]{2,1,0:T(8,128)(2,1)}), bf16[16,120,128]{2,1,0:T(8,128)(2,1)S(1)}, u32[]{:S(2)}, u32[]{:S(2)}) async-start(bf16[16,120,128]{2,1,0:T(8,128)(2,1)} %product.2), calls=%async_computation.1 | async-start | bytes 983040 | tf_op jit(solution)/shard_map/all_to_all | solution.py:750
  40.2 10.7 %collective-permute-start.4 = (f32[8,128]{1,0:T(8,128)S(1)}, f32[8,128]{1,0:T(8,128)S(1)}, u32[]{:S(2)}, u32[]{:S(2)}) collective-permute-start(f32[8,128]{1,0:T(8,128)S(1)} %get-tuple-element.32), channel_id=1, source_target_pairs={{0,8},{8,16},{16,24},{24,32},{32,40},{40,48},{48,56},{56,64},{64,7... | collective-permute-start | bytes 12296 | tf_op jit(solution)/shard_map/ppermute | solution.py:766
  40.3 10.6 %collective-permute-start.5 = (f32[8,128]{1,0:T(8,128)S(1)}, f32[8,128]{1,0:T(8,128)S(1)}, u32[]{:S(2)}, u32[]{:S(2)}) collective-permute-start(f32[8,128]{1,0:T(8,128)S(1)} %get-tuple-element.33), channel_id=1, source_target_pairs={{0,248},{8,0},{16,8},{24,16},{32,24},{40,32},{48,40},{56,48},{64,5... | collective-permute-start | bytes 12296 | tf_op jit(solution)/shard_map/ppermute | solution.py:767
  67.2 10.3 %copy-start.1 = (bf16[8,192,128]{2,1,0:T(8,128)(2,1)}, bf16[8,192,128]{2,1,0:T(8,128)(2,1)S(1)}, u32[]{:S(2)}) copy-start(bf16[8,192,128]{2,1,0:T(8,128)(2,1)S(1)} %all_to_all.25.recv_ref.wind_recv_ref) | copy-start | bytes 1179652
  68.2 1.3 %collective-permute-start.8 = (bf16[144,128]{1,0:T(8,128)(2,1)S(1)}, bf16[144,128]{1,0:T(8,128)(2,1)S(1)}, u32[]{:S(2)}, u32[]{:S(2)}) collective-permute-start(bf16[144,128]{1,0:T(8,128)(2,1)S(1)} %rows.1.rows_ref), channel_id=1, source_target_pairs={{0,8},{8,0},{16,24},{24,16},{32,40},{40,32},{48,56},{56,48},{64,72... | collective-permute-start | bytes 110600 | tf_op jit(solution)/shard_map/ppermute | solution.py:748
  70.8 21.0 %copy-start.7 = (s32[34]{0:T(128)S(1)}, s32[34]{0:T(128)}, u32[]{:S(2)}) copy-start(s32[34]{0:T(128)} %pad_add_fusion.meta_ref) | copy-start | bytes 412
  70.8 21.0 %all-to-all-start.3 = ((bf16[16,120,128]{2,1,0:T(8,128)(2,1)}), bf16[16,120,128]{2,1,0:T(8,128)(2,1)S(1)}, u32[]{:S(2)}, u32[]{:S(2)}) async-start(bf16[16,120,128]{2,1,0:T(8,128)(2,1)} %product.3), calls=%async_computation.3 | async-start | bytes 983040 | tf_op jit(solution)/shard_map/all_to_all | solution.py:750
  77.5 29.1 %copy-start = (bf16[45,64,128]{2,1,0:T(8,128)(2,1)S(1)}, bf16[45,64,128]{2,1,0:T(8,128)(2,1)}, u32[]{:S(2)}) copy-start(bf16[45,64,128]{2,1,0:T(8,128)(2,1)} %winds_ref.1) | copy-start | bytes 2211844
  77.5 29.1 %copy-start.5 = (bf16[192,128]{1,0:T(8,128)(2,1)S(1)}, bf16[192,128]{1,0:T(8,128)(2,1)}, u32[]{:S(2)}) copy-start(bf16[192,128]{1,0:T(8,128)(2,1)} %copy-done.4) | copy-start | bytes 147460
  87.0 19.6 %copy-start.2 = (bf16[8,192,128]{2,1,0:T(8,128)(2,1)S(1)}, bf16[8,192,128]{2,1,0:T(8,128)(2,1)}, u32[]{:S(2)}) copy-start(bf16[8,192,128]{2,1,0:T(8,128)(2,1)} %copy-done.1) | copy-start | bytes 1179652
  91.8 0.8 copy-start.9
  93.9 12.6 %all-to-all-start.4 = ((bf16[8,192,128]{2,1,0:T(8,128)(2,1)}), bf16[8,192,128]{2,1,0:T(8,128)(2,1)S(1)}, u32[]{:S(2)}, u32[]{:S(2)}) async-start(bf16[8,192,128]{2,1,0:T(8,128)(2,1)} %total.3), calls=%async_computation.4 | async-start | bytes 786432 | tf_op jit(solution)/shard_map/all_to_all | solution.py:744
  97.4 5.8 %collective-permute-start.6 = (bf16[160,128]{1,0:T(8,128)(2,1)}, bf16[160,128]{1,0:T(8,128)(2,1)S(1)}, u32[]{:S(2)}, u32[]{:S(2)}) collective-permute-start(bf16[160,128]{1,0:T(8,128)(2,1)} %get-tuple-element.37), channel_id=1, source_target_pairs={{0,8},{8,16},{16,24},{24,32},{32,40},{40,48},{48,56},{56,64},{64,7... | collective-permute-start | bytes 122888 | tf_op jit(solution)/shard_map/ppermute | solution.py:773
  97.5 5.8 %collective-permute-start.7 = (bf16[160,128]{1,0:T(8,128)(2,1)}, bf16[160,128]{1,0:T(8,128)(2,1)S(1)}, u32[]{:S(2)}, u32[]{:S(2)}) collective-permute-start(bf16[160,128]{1,0:T(8,128)(2,1)} %get-tuple-element.38), channel_id=1, source_target_pairs={{0,248},{8,0},{16,8},{24,16},{32,24},{40,32},{48,40},{56,48},{64,5... | collective-permute-start | bytes 122888 | tf_op jit(solution)/shard_map/ppermute | solution.py:774
  106.6 1.5 %copy-start.3 = (bf16[45,160,128]{2,1,0:T(8,128)(2,1)S(1)}, bf16[45,160,128]{2,1,0:T(8,128)(2,1)}, u32[]{:S(2)}) copy-start(bf16[45,160,128]{2,1,0:T(8,128)(2,1)} %get-tuple-element.36.cells_ref) | copy-start | bytes 5529604

commit v5 on v4

--- a/solution.py
+++ b/solution.py
@@ -14,7 +14,8 @@
 BANDS = 8
 NLON = 1440
 LON_DEV = 32
-TARGETS = 16
+TARGETS = 8
+TEAM = 4
 BLOCKS = 16
 PICKS = 56
 WIRE = 6 * ROWS + 24
@@ -59,12 +60,12 @@
     return lax.dot_general(a, b, (((0,), (0,)), ((), ())), preferred_element_type=F32)
 
 
-def operator_kernel(meta_ref, ops_ref, own_ref, send_ref):
-    core = meta_ref[1]
+def operator_kernel(meta_ref, ops_ref, *out_refs):
+    place = meta_ref[1]
     for t in range(TARGETS):
         tiles = []
-        for parity in range(2):
-            start = XS * (2 * t + parity) - 1
+        for member in range(TEAM):
+            start = XS * ((member // 2) * 2 * TARGETS + 2 * t + member % 2) - 1
             total = None
             first = max(start, 0) // LANES * LANES
             spans = [(first, min(first + 2 * LANES, NLON))]
@@ -84,18 +85,20 @@
                 total = part if total is None else total + part
             tiles.append(total)
         rows = slice(ROWS * t, ROWS * (t + 1))
-        mine = core == 0
-        own_ref[rows, :] = jnp.where(mine, tiles[0], tiles[1]).astype(BF16)
-        send_ref[rows, :] = jnp.where(mine, tiles[1], tiles[0]).astype(BF16)
+        for other in range(TEAM):
+            value = tiles[other]
+            for member in range(1, TEAM):
+                value = jnp.where(place == member, tiles[member ^ other], value)
+            out_refs[other][rows, :] = value.astype(BF16)
 
 
 def prepare_operators(meta, ops):
     out = shape((TARGETS * ROWS, 2 * ROWS), BF16)
     return pl.pallas_call(
         operator_kernel,
-        out_shape=(out, out),
+        out_shape=(out,) * TEAM,
         in_specs=[SM, VM],
-        out_specs=(VM, VM),
+        out_specs=(VM,) * TEAM,
         compiler_params=params(6),
         name="operators",
     )(meta, ops)
@@ -217,10 +220,21 @@
     ]
 
 
+class Scalars:
+    def __init__(self, me, band_ref, row_ref):
+        self.me, self.band_ref, self.row_ref = me, band_ref, row_ref
+
+    def __getitem__(self, at):
+        if at == 0:
+            return self.me
+        return self.band_ref[at - 2] if at < 2 + BLOCKS else self.row_ref[at - 2 - BLOCKS]
+
+
 def pick_kernel(
-    meta_ref, cells_hbm, winds_hbm, send_hbm, edges_ref, east_ref, west_ref,
+    band_ref, row_ref, cells_hbm, winds_hbm, send_hbm, edges_ref, east_ref, west_ref,
     main_ref, rest_ref, cells_ref, winds_ref, send_ref, cells_sem, winds_sem, send_sem,
 ):
+    meta_ref = Scalars(lax.axis_index("lat").astype(jnp.int32), band_ref, row_ref)
     arriving = list(zip(copies(cells_hbm, cells_ref, cells_sem), copies(winds_hbm, winds_ref, winds_sem)))
     for pair in arriving:
         for copy in pair:
@@ -258,7 +272,7 @@
 PICKED = pltpu.VMEM((PICKS * ROWS, LANES), F32)
 
 
-def pick_rows(meta, cells, winds):
+def pick_rows(band, row, cells, winds):
     return pl.pallas_call(
         pick_kernel,
         out_shape=(
@@ -267,7 +281,7 @@
             shape((COLS + LEV, LANES), BF16),
             shape((COLS, LANES), BF16),
         ),
-        in_specs=[SM, HB, HB],
+        in_specs=[SM, SM, HB, HB],
         out_specs=(HB, VM, VM, VM),
         scratch_shapes=[
             PICKED,
@@ -281,7 +295,7 @@
         ],
         compiler_params=params(58),
         name="pick",
-    )(meta, cells, winds)
+    )(band, row, cells, winds)
 
 
 def added(recv_ref, span):
@@ -367,35 +381,37 @@
     )
 
 
-def product_kernel(rows_ref, other_ref, own_ops_ref, other_ops_ref, out_ref):
-    mine = spread_blocks(rows_ref)
-    theirs = spread_blocks(other_ref)
-    for q in range(4):
+def product_kernel(*refs):
+    out_ref = refs[-1]
+    rows = [spread_blocks(ref) for ref in refs[:TEAM]]
+    for q in range(2):
         span = slice(4 * ROWS * q, 4 * ROWS * (q + 1))
-        made = jnp.dot(own_ops_ref[span, :], mine, preferred_element_type=F32)
-        made = made + jnp.dot(other_ops_ref[span, :], theirs, preferred_element_type=F32)
+        made = None
+        for ops_ref, values in zip(refs[TEAM : 2 * TEAM], rows):
+            part = jnp.dot(ops_ref[span, :], values, preferred_element_type=F32)
+            made = part if made is None else made + part
         for s in range(4):
             part = made[ROWS * s : ROWS * (s + 1)]
-            rest = part[:, 2 * LANES :]
             t = 4 * q + s
             out_ref[t, :ROWS, :] = part[:, :LANES].astype(BF16)
             out_ref[t, ROWS : 2 * ROWS, :] = part[:, LANES : 2 * LANES].astype(BF16)
-            packed = rest[: ROWS // 2] + pltpu.roll(rest[ROWS // 2 :], 2 * LEV, axis=1)
-            out_ref[t, 2 * ROWS :, :] = packed.astype(BF16)
-
-
-def products(rows, other, own_ops, other_ops):
+            out_ref[t, 2 * ROWS :, :] = folded(part[:, 2 * LANES :], 2 * LEV).astype(BF16)
+
+
+def products(rows, ops):
     return pl.pallas_call(
         product_kernel,
         out_shape=shape((TARGETS, PACK, LANES), BF16),
-        in_specs=[VM] * 4,
+        in_specs=[VM] * (2 * TEAM),
         out_specs=VM,
         compiler_params=params(6),
         name="product",
-    )(rows, other, own_ops, other_ops)
-
-
-def total_kernel(meta_ref, recv_ref, edges_ref, out_ref):
+    )(*rows, *ops)
+
+
+def total_kernel(meta_ref, recv_ref, edges_hbm, out_ref, edges_ref, sem_ref):
+    arriving = pltpu.make_async_copy(edges_hbm, edges_ref, sem_ref.at[0])
+    arriving.start()
     total = recv_ref[0].astype(F32)
     for s in range(1, TARGETS):
         total = total + recv_ref[s].astype(F32)
@@ -403,6 +419,8 @@
     me = meta_ref[0]
     for d in range(BANDS):
         out_ref[d, :PACK, :] = total
+    arriving.wait()
+    for d in range(BANDS):
         edge = jnp.where(d == me + 1, edges_ref[1], jnp.zeros((HALO, LANES), BF16))
         out_ref[d, PACK:, :] = jnp.where(d == me - 1, edges_ref[0], edge)
 
@@ -411,8 +429,9 @@
     return pl.pallas_call(
         total_kernel,
         out_shape=shape((BANDS, PACK + HALO, LANES), BF16),
-        in_specs=[SM, VM, VM],
+        in_specs=[SM, VM, HB],
         out_specs=VM,
+        scratch_shapes=[pltpu.VMEM((2, HALO, LANES), BF16), DMA((1,))],
         compiler_params=params(4),
         name="total",
     )(meta, recv, edges)
@@ -555,41 +574,40 @@
     return jnp.where(lane == target, 1.0, 0.0).astype(BF16)
 
 
-def smooth_all(meta_ref, cells_ref, west_ref, east_ref, tall_ref, placed_ref, smooth_ref, edge_ref, wind_ref):
+def advance(meta_ref, cells_ref, winds_ref, west_ref, east_ref, wind_west_ref, tall_ref, placed_ref, smooth_ref, emit):
     for q in range(GROUP):
-        placed_ref[...] = jnp.dot(tall_ref[...], place_weights(meta_ref, q), preferred_element_type=F32)
-
-        def store(t, r, base):
-            at = pl.multiple_of(t * TALL, TALL)
-            change = placed_ref[pl.ds(at, COLS), :LANES]
-            smooth_ref[r] = (base.astype(F32) + change).astype(BF16).astype(F32)
-
-        def body(t, carry):
-            r = GROUP * t + q
-            x = r - 1
-            store(t, r, cells_ref[x])
-            at = pl.multiple_of(t * TALL, TALL)
-            edge_ref[x] = placed_ref[pl.ds(at, COLS), LANES:]
-            wind_ref[x] = placed_ref[pl.ds(at + COLS, LEV), LANES:]
-            return carry
-
-        first = 1 if q == 0 else 0
-        last = (XS - q) // GROUP + 1
-        if q == 0:
-            store(0, 0, west_ref[:COLS, :])
-        if (XS + 1) % GROUP == q:
-            store((XS + 1) // GROUP, XS + 1, east_ref[...])
-        lax.fori_loop(first, last, body, 0, unroll=True)
-
-
-def stencil(x, top, winds_ref, west_ref, smooth_ref, edge_ref, wind_ref):
+        placed_ref[q] = jnp.dot(tall_ref[...], place_weights(meta_ref, q), preferred_element_type=F32)
+    top = meta_ref[0] == BANDS - 1
+
+    def smooth(r, base):
+        at = pl.multiple_of((r // GROUP) * TALL, TALL)
+        change = placed_ref[r % GROUP, pl.ds(at, COLS), :LANES]
+        smooth_ref[r] = (base.astype(F32) + change).astype(BF16).astype(F32)
+
+    smooth(0, west_ref[:COLS, :])
+    smooth(1, cells_ref[0])
+    smooth(XS + 1, east_ref[...])
+
+    def body(x, carry):
+        r = jnp.minimum(x + 2, XS)
+        smooth(r, cells_ref[r - 1])
+        made = stencil(x, top, winds_ref, wind_west_ref, smooth_ref, placed_ref)
+        emit(x, made)
+        return carry
+
+    return body
+
+
+def stencil(x, top, winds_ref, west_ref, smooth_ref, placed_ref):
+    at = pl.multiple_of(((x + 1) // GROUP) * TALL, TALL)
+    q = (x + 1) % GROUP
     lane = lax.broadcasted_iota(jnp.int32, (LEV, LANES), 1)
     courant = winds_ref[x].astype(F32)
     before = winds_ref[jnp.maximum(x - 1, 0), :LEV, :].astype(F32)
     before = jnp.where(x == 0, west_ref[COLS:, :].astype(F32), before)
     across = courant[:LEV]
     along = jnp.where(top & (lane == LANES - 1), 0.0, courant[LEV:])
-    south_along = jnp.where(lane == 0, wind_ref[x], pltpu.roll(along, 1, axis=1))
+    south_along = jnp.where(lane == 0, placed_ref[q, pl.ds(at + COLS, LEV), LANES:], pltpu.roll(along, 1, axis=1))
     east = jnp.maximum(across, 0.0)
     west = jnp.minimum(before, 0.0)
     north = jnp.maximum(along, 0.0)
@@ -599,7 +617,7 @@
     for v in range(VAR):
         span = slice(v * LEV, (v + 1) * LEV)
         here = smooth_ref[x + 1, span, :]
-        edge = edge_ref[x, span, :]
+        edge = placed_ref[q, pl.ds(at + v * LEV, LEV), LANES:]
         above = jnp.where(lane == LANES - 1, edge, pltpu.roll(here, LANES - 1, axis=1))
         below = jnp.where(lane == 0, edge, pltpu.roll(here, 1, axis=1))
         made.append(
@@ -614,17 +632,15 @@
     pltpu.VMEM((KEPT * ROWS, LANES), F32),
     pltpu.VMEM((KEPT * ROWS, LANES), F32),
     pltpu.VMEM((ROWS // GROUP * TALL, LANES), BF16),
-    pltpu.VMEM((ROWS // GROUP * TALL, 2 * LANES), F32),
+    pltpu.VMEM((GROUP, ROWS // GROUP * TALL, 2 * LANES), F32),
     pltpu.VMEM((XS + 2, COLS, LANES), F32),
-    pltpu.VMEM((XS, COLS, LANES), F32),
-    pltpu.VMEM((XS, LEV, LANES), F32),
 ]
 
 
 def first_kernel(
     meta_ref, cells_hbm, winds_hbm, west_ref, east_ref, recv_ref,
     out_hbm, edges_ref, to_east_hbm, to_west_hbm,
-    main_ref, rest_ref, tall_ref, placed_ref, smooth_ref, edge_ref, wind_ref, out_ref, out_sem, rim_sem,
+    main_ref, rest_ref, tall_ref, placed_ref, smooth_ref, out_ref, out_sem, rim_sem,
     cells_ref, cells_sem, winds_ref, winds_sem,
 ):
     arriving = copies(cells_hbm, cells_ref, cells_sem) + copies(winds_hbm, winds_ref, winds_sem)
@@ -633,15 +649,14 @@
     stage_corrections(meta_ref, recv_ref, recv_ref, main_ref, rest_ref, tall_ref)
     for copy in arriving:
         copy.wait()
-    smooth_all(meta_ref, cells_ref, west_ref, east_ref, tall_ref, placed_ref, smooth_ref, edge_ref, wind_ref)
-    top = meta_ref[0] == BANDS - 1
-
-    def body(x, carry):
-        made = stencil(x, top, winds_ref, west_ref, smooth_ref, edge_ref, wind_ref)
+
+    def emit(x, made):
         for v in range(VAR):
             out_ref[x, v * LEV : (v + 1) * LEV, :] = made[v].astype(BF16)
-        return carry
-
+
+    body = advance(
+        meta_ref, cells_ref, winds_ref, west_ref, east_ref, west_ref, tall_ref, placed_ref, smooth_ref, emit
+    )
     leaving = copies(out_ref, out_hbm, out_sem)
     leaving.append(pltpu.make_async_copy(out_ref.at[0], to_west_hbm, rim_sem.at[0]))
     leaving.append(pltpu.make_async_copy(out_ref.at[XS - 1], to_east_hbm, rim_sem.at[1]))
@@ -699,81 +714,99 @@
 
 def last_kernel(
     meta_ref, cells_ref, winds_ref, west_ref, east_ref, recv_ref, wind_recv_ref, wind_west_ref,
-    out_ref, main_ref, rest_ref, tall_ref, placed_ref, smooth_ref, edge_ref, wind_ref,
+    out_hbm, main_ref, rest_ref, tall_ref, placed_ref, smooth_ref, out_ref, out_sem,
 ):
-    me = meta_ref[0]
-    step = pl.program_id(0)
-
-    @pl.when(step == 0)
-    def _():
-        stage_corrections(meta_ref, recv_ref, wind_recv_ref, main_ref, rest_ref, tall_ref)
-        smooth_all(meta_ref, cells_ref, west_ref, east_ref, tall_ref, placed_ref, smooth_ref, edge_ref, wind_ref)
-
-    top = me == BANDS - 1
-
-    def body(y, carry):
-        x = step * CHUNK + y
-        made = stencil(x, top, winds_ref, wind_west_ref, smooth_ref, edge_ref, wind_ref)
+    stage_corrections(meta_ref, recv_ref, wind_recv_ref, main_ref, rest_ref, tall_ref)
+
+    def emit(x, made):
         for v in range(VAR):
-            out_ref[y, v * LEV : (v + 1) * LEV, :] = made[v]
-        return carry
-
-    lax.fori_loop(0, CHUNK, body, 0, unroll=3)
+            out_ref[x, v * LEV : (v + 1) * LEV, :] = made[v]
+
+    body = advance(
+        meta_ref, cells_ref, winds_ref, west_ref, east_ref, wind_west_ref, tall_ref, placed_ref, smooth_ref, emit
+    )
+    leaving = copies(out_ref, out_hbm, out_sem)
+    for (start, size), copy in zip(SPANS, leaving):
+        lax.fori_loop(start, start + size, body, 0, unroll=4)
+        copy.start()
+    for copy in leaving:
+        copy.wait()
 
 
 def last_substep(*args):
     return pl.pallas_call(
         last_kernel,
-        grid=(XS // CHUNK,),
         out_shape=shape((XS, COLS, LANES), F32),
         in_specs=[SM] + [VM] * 7,
-        out_specs=pl.BlockSpec((CHUNK, COLS, LANES), lambda i: (i, 0, 0)),
-        scratch_shapes=SCRATCH,
-        compiler_params=params(16),
+        out_specs=HB,
+        scratch_shapes=SCRATCH + [pltpu.VMEM((XS, COLS, LANES), F32), DMA((len(SPANS),))],
+        compiler_params=params(24),
         name="last",
     )(*args)
 
 
-SWAP = [(i, i ^ 1) for i in range(LON_DEV)]
+def stay_kernel(cells_hbm, message_hbm, cells_ref, sem_ref):
+    arriving = copies(cells_hbm, cells_ref, sem_ref)
+    for copy in arriving:
+        copy.start()
+    for copy in arriving:
+        copy.wait()
+
+
+def bring_back(cells, message):
+    return pl.pallas_call(
+        stay_kernel,
+        out_shape=shape((XS, COLS, LANES), BF16),
+        in_specs=[HB, HB],
+        out_specs=VM,
+        scratch_shapes=[DMA((len(SPANS),))],
+        compiler_params=params(4),
+        name="stay",
+    )(cells, message)
+
+
+TEAMMATES = [[(i, i ^ (16 * (other // 2) + other % 2)) for i in range(LON_DEV)] for other in range(1, TEAM)]
 EASTWARD = [(i, (i + 1) % LON_DEV) for i in range(LON_DEV)]
 WESTWARD = [(i, (i - 1) % LON_DEV) for i in range(LON_DEV)]
-SAME_CORE = [[2 * t + core for t in range(TARGETS)] for core in range(2)]
+ALONG_Z = [[16 * (place // 2) + 2 * t + place % 2 for t in range(TARGETS)] for place in range(TEAM)]
 
 
 def by_lat(messages):
     return lax.all_to_all(messages, "lat", 0, 0, tiled=True)
 
 
-def filtered(rows, own_ops, other_ops):
-    other = lax.ppermute(rows, "lon", SWAP)
-    partial = products(rows, other, own_ops, other_ops)
-    return lax.all_to_all(partial, "lon", 0, 0, tiled=True, axis_index_groups=SAME_CORE)
+def filtered(rows, ops):
+    team = [rows] + [lax.ppermute(rows, "lon", mates) for mates in TEAMMATES]
+    partial = products(team, ops)
+    return lax.all_to_all(partial, "lon", 0, 0, tiled=True, axis_index_groups=ALONG_Z)
 
 
 def shards(cotangent, winds, filter_ops, block_band, block_row):
     me = lax.axis_index("lat").astype(jnp.int32).reshape(1)
-    core = (lax.axis_index("lon") & 1).astype(jnp.int32).reshape(1)
-    meta = jnp.concatenate([me, core, block_band, block_row])
-    own_ops, send_ops = prepare_operators(meta, jnp.pad(filter_ops, ((0, 0), (1, 2), (0, 0))))
-    other_ops = lax.ppermute(send_ops, "lon", SWAP)
-    send, edges, to_east, to_west = pick_rows(meta, cotangent, winds)
+    at = lax.axis_index("lon").astype(jnp.int32)
+    place = ((at >> 4) * 2 + (at & 1)).reshape(1)
+    meta = jnp.concatenate([me, place, block_band, block_row])
+    made = prepare_operators(meta, jnp.pad(filter_ops, ((0, 0), (1, 2), (0, 0))))
+    ops = [made[0]] + [lax.ppermute(part, "lon", mates) for part, mates in zip(made[1:], TEAMMATES)]
+    send, edges, to_east, to_west = pick_rows(block_band, block_row, cotangent, winds)
     west = lax.ppermute(to_east, "lon", EASTWARD)
     east = lax.ppermute(to_west, "lon", WESTWARD)
     recv, west, east = lax.optimization_barrier((by_lat(send), west, east))
     rows = unpack_rows(recv)
-    swapped = filtered(rows, own_ops, other_ops)
+    swapped = filtered(rows, ops)
     context, row_east, row_west = unpack_context(meta, recv, rows)
     row_from_west = lax.ppermute(row_east, "lon", EASTWARD)
     row_from_east = lax.ppermute(row_west, "lon", WESTWARD)
     swapped, row_from_west, row_from_east = lax.optimization_barrier((swapped, row_from_west, row_from_east))
     given = by_lat(totals(meta, swapped, edges))
     rows = next_rows(meta, rows, context, row_from_west, row_from_east, given)
-    swapped = filtered(rows, own_ops, other_ops)
+    swapped = filtered(rows, ops)
     state, edges, to_east, to_west = first_substep(meta, cotangent, winds, west, east, given)
     west2 = lax.ppermute(to_east, "lon", EASTWARD)
     east2 = lax.ppermute(to_west, "lon", WESTWARD)
-    given2 = by_lat(totals(meta, swapped, edges))
-    return last_substep(meta, state, winds, west2, east2, given2, given, west)
+    message = totals(meta, swapped, edges)
+    given2 = by_lat(message)
+    return last_substep(meta, bring_back(state, message), winds, west2, east2, given2, given, west)
 
 
 def solution(mesh):

time: 116 us -> 112 us (0.966)
  waiting for transfers between devices: 25.7 us -> 22.1 us
  other arithmetic: 1.29 us -> 0.08 us
    ppermute x1, waiting for transfers between devices: 6.75 us -> 1.44 us  [shards(): row_from_west = lax.ppermute(row_east, 'lon', EASTWARD)]
    all_to_all x2, starting transfers between devices: 16.6 us -> 12 us  [filtered(): lax.all_to_all(partial, 'lon', 0, 0, tiled=True, axis_index_groups=ALONG_Z)]
    ppermute x3 -> x9, starting transfers between devices: 0.28 us -> 4.8 us  [the longest x6 4.11 us: filtered(): team = [rows] + [lax.ppermute(rows, 'lon', mates) for mates in TEAMMATES]]
    ppermute x3 -> x9, waiting for transfers between devices: 2.39 us -> 4.57 us  [the longest x6 4.56 us: filtered(): team = [rows] + [lax.ppermute(rows, 'lon', mates) for mates in TEAMMATES]]
    ppermute x1, waiting for transfers between devices: 1.89 us -> 0.01 us  [shards(): west2 = lax.ppermute(to_east, 'lon', EASTWARD)]
    all_to_all x2, waiting for transfers between devices: 5.2 us -> 6.54 us  [by_lat(): return lax.all_to_all(messages, 'lat', 0, 0, tiled=True)]
    concatenate x1, other arithmetic: 1.29 us -> 0.08 us  [shards(): meta = jnp.concatenate([me, place, block_band, block_row])]
    pallas_call x2 -> x3, Pallas kernels: 8.72 us -> 9.02 us  [the longest x1 6.97 us: last_substep(): pl.pallas_call(last_kernel, out_shape=shape((XS, COLS, LANES), F32), in_s...]
  transfers between devices with their start and end apart: 13 -> 19, of which waited for: 10 -> 11; matrix products, arithmetic and copies ran while one was open for 0% -> 0% of each run, Pallas kernels for 10% -> 11%
where the time goes in v5:
time: 112 us
  starting transfers between devices  41 us (37%)
  Pallas kernels  32.4 us (29%)
  waiting for transfers between devices  22.1 us (20%)
  blocking collectives  13.3 us (12%)
  local copies, waits for them, and re-layouts  2.44 us (2%)
    all_to_all x1, blocking collectives, by_lat(): return lax.all_to_all(messages, 'lat', 0, 0, tiled=True)  13.3 us
    all_to_all x2, starting transfers between devices, filtered(): lax.all_to_all(partial, 'lon', 0, 0, tiled=True, axis_index_groups=ALONG_Z)  12 us
    pallas_call x1, Pallas kernels, first_substep(): pl.pallas_call(first_kernel, out_shape=(shape((XS, COLS, LANES), BF16), s...  9.73 us
    all_to_all x2, starting transfers between devices, by_lat(): return lax.all_to_all(messages, 'lat', 0, 0, tiled=True)  9.45 us
    all_to_all x2, waiting for transfers between devices, filtered(): lax.all_to_all(partial, 'lon', 0, 0, tiled=True, axis_index_groups=ALONG_Z)  8.39 us
    pallas_call x1, Pallas kernels, pick_rows(): pl.pallas_call(pick_kernel, out_shape=(shape((BANDS, WIRE, LANES), BF16),...  7.15 us
    pallas_call x1, Pallas kernels, last_substep(): pl.pallas_call(last_kernel, out_shape=shape((XS, COLS, LANES), F32), in_s...  6.97 us
    all_to_all x2, waiting for transfers between devices, by_lat(): return lax.all_to_all(messages, 'lat', 0, 0, tiled=True)  6.54 us
  transfers between devices with their start and end apart: 19, of which 11 were waited for; matrix products, arithmetic and copies ran while one was open for 0% of the time, Pallas kernels for 11%

profile of v5, /device:TPU:2, one launch (start us, length us, event | category | flops | bytes accessed | tf_op | source)
XLA Modules:
  0.0 111.8 jit_solution(9683146200276506904)
XLA Ops:
  0.0 7.2 %pick.1 = (bf16[8,312,128]{2,1,0:T(8,128)(2,1)}, bf16[2,72,128]{2,1,0:T(8,128)(2,1)}, bf16[192,128]{1,0:T(8,128)(2,1)}, bf16[160,128]{1,0:T(8,128)(2,1)}) custom-call(s32[16]{0:T(128)} %band_ref.1, s32[16]{0:T(128)} %row_ref.1, bf16[45,160,128]{2,1,0:T(8,128)(2,1)} %cells_hbm.3, bf16[45,64,128]{2,1,0:T(8,128)(2,1)} %winds_ref.1), custom_call_target="tpu_custom_call" | custom-call | tf_op jit(solution)/shard_map/pick/pallas_call | solution.py:276
  7.2 0.0 copy-start.12
  7.2 0.0 copy-start.13
  7.2 6.0 %all-to-all-start = ((bf16[8,312,128]{2,1,0:T(8,128)(2,1)}), bf16[8,312,128]{2,1,0:T(8,128)(2,1)S(1)}, u32[]{:S(2)}, u32[]{:S(2)}) async-start(bf16[8,312,128]{2,1,0:T(8,128)(2,1)} %get-tuple-element.26), calls=%async_computation | async-start | bytes 1277952 | tf_op jit(solution)/shard_map/all_to_all | solution.py:775
  13.3 0.1 pad.4.ops_ref
  13.4 0.1 pad_add_fusion.meta_ref
  13.4 1.2 %operators.1 = (bf16[384,96]{1,0:T(8,128)(2,1)S(1)}, bf16[384,96]{1,0:T(8,128)(2,1)S(1)}, bf16[384,96]{1,0:T(8,128)(2,1)S(1)}, bf16[384,96]{1,0:T(8,128)(2,1)S(1)}) custom-call(s32[34]{0:T(128)S(1)} %pad_add_fusion.meta_ref, bf16[2,48,1440]{2,1,0:T(8,128)(2,1)S(1)} %pad.4.ops_ref), custom_call_target="tpu_custom_call" | custom-call | tf_op jit(solution)/shard_map/operators/pallas_call | solution.py:97
  14.7 0.1 collective-permute-start.5
  14.8 0.5 collective-permute-start
  15.3 6.4 %collective-permute-start.1 = (bf16[160,128]{1,0:T(8,128)(2,1)S(1)}, bf16[160,128]{1,0:T(8,128)(2,1)S(1)}, u32[]{:S(2)}, u32[]{:S(2)}) collective-permute-start(bf16[160,128]{1,0:T(8,128)(2,1)S(1)} %copy-done.15), channel_id=1, source_target_pairs={{0,248},{8,0},{16,8},{24,16},{32,24},{40,32},{48,40},{56,48},{64,5... | collective-permute-start | bytes 122888 | tf_op jit(solution)/shard_map/ppermute | solution.py:793
  21.7 0.6 collective-permute-start.6
  22.3 0.0 collective-permute-start.7
  22.3 1.1 collective-permute-done.1.east_ref
  23.4 0.1 collective-permute-done.west_ref.wind_west_ref
  23.5 2.3 %all-to-all-done.recv_ref = bf16[8,312,128]{2,1,0:T(8,128)(2,1)S(1)} async-done(((bf16[8,312,128]{2,1,0:T(8,128)(2,1)}), bf16[8,312,128]{2,1,0:T(8,128)(2,1)S(1)}, u32[]{:S(2)}, u32[]{:S(2)}) %all-to-all-start) | async-done | bytes 639008 | tf_op jit(solution)/shard_map/all_to_all | solution.py:775
  25.8 0.1 collective-permute-start.4
  25.9 1.5 %collective-permute-start.3 = (bf16[144,128]{1,0:T(8,128)(2,1)S(1)}, bf16[144,128]{1,0:T(8,128)(2,1)S(1)}, u32[]{:S(2)}, u32[]{:S(2)}) collective-permute-start(bf16[144,128]{1,0:T(8,128)(2,1)S(1)} %unpack.1.refs_0_.rows_ref.before_ref), channel_id=1, source_target_pairs={{0,128},{8,136},{16,144},{24,152},{32,160},{40,168},{48,176},{56,1... | collective-permute-start | bytes 110600 | tf_op jit(solution)/shard_map/ppermute | solution.py:779
  27.4 0.3 collective-permute-start.2
  27.8 1.9 %collective-permute-done.4.refs_3_ = bf16[144,128]{1,0:T(8,128)(2,1)S(1)} collective-permute-done((bf16[144,128]{1,0:T(8,128)(2,1)S(1)}, bf16[144,128]{1,0:T(8,128)(2,1)S(1)}, u32[]{:S(2)}, u32[]{:S(2)}) %collective-permute-start.4) | collective-permute-done | bytes 36896 | tf_op jit(solution)/shard_map/ppermute | solution.py:779
  29.7 0.4 collective-permute-done.3.refs_2_
  30.1 1.2 %product.2 = bf16[8,120,128]{2,1,0:T(8,128)(2,1)} custom-call(bf16[144,128]{1,0:T(8,128)(2,1)S(1)} %unpack.1.refs_0_.rows_ref.before_ref, bf16[144,128]{1,0:T(8,128)(2,1)S(1)} %collective-permute-done.2.refs_1_, bf16[144,128]{1,0:T(8,128)(2,1)S(1)} %collective-permute-done.3.refs_2_, bf16[144,128]{1,0:T(8,128)(2,1)S(1)} %collective-permute-done.4.refs_3_, ...), custom_call_target="tpu_custom_call" | custom-call | tf_op jit(solution)/shard_map/product/pallas_call | solution.py:402
  31.3 8.5 %all-to-all-start.1 = ((bf16[8,120,128]{2,1,0:T(8,128)(2,1)}), bf16[8,120,128]{2,1,0:T(8,128)(2,1)S(1)}, u32[]{:S(2)}, u32[]{:S(2)}) async-start(bf16[8,120,128]{2,1,0:T(8,128)(2,1)} %product.2), calls=%async_computation.1 | async-start | bytes 491520 | tf_op jit(solution)/shard_map/all_to_all | solution.py:781
  39.7 0.9 context.1
  40.6 0.1 collective-permute-start.8
  40.7 3.8 %collective-permute-start.9 = (f32[8,128]{1,0:T(8,128)S(1)}, f32[8,128]{1,0:T(8,128)S(1)}, u32[]{:S(2)}, u32[]{:S(2)}) collective-permute-start(f32[8,128]{1,0:T(8,128)S(1)} %get-tuple-element.37), channel_id=1, source_target_pairs={{0,248},{8,0},{16,8},{24,16},{32,24},{40,32},{48,40},{56,48},{64,5... | collective-permute-start | bytes 12296 | tf_op jit(solution)/shard_map/ppermute | solution.py:799
  44.5 1.4 %collective-permute-done.8.west_ref = f32[8,128]{1,0:T(8,128)S(1)} collective-permute-done((f32[8,128]{1,0:T(8,128)S(1)}, f32[8,128]{1,0:T(8,128)S(1)}, u32[]{:S(2)}, u32[]{:S(2)}) %collective-permute-start.8) | collective-permute-done | bytes 4128 | tf_op jit(solution)/shard_map/ppermute | solution.py:798
  46.0 5.7 %all-to-all-done.1.recv_ref = bf16[8,120,128]{2,1,0:T(8,128)(2,1)S(1)} async-done(((bf16[8,120,128]{2,1,0:T(8,128)(2,1)}), bf16[8,120,128]{2,1,0:T(8,128)(2,1)S(1)}, u32[]{:S(2)}, u32[]{:S(2)}) %all-to-all-start.1) | async-done | bytes 245792 | tf_op jit(solution)/shard_map/all_to_all | solution.py:781
  51.7 0.7 total.2
  52.4 13.3 %all_to_all.25.recv_ref.wind_recv_ref = bf16[8,192,128]{2,1,0:T(8,128)(2,1)S(1)} all-to-all(bf16[8,192,128]{2,1,0:T(8,128)(2,1)S(1)} %total.2), channel_id=1, replica_groups=mesh['lon'=32,'lat'=8] {'lat'}, dimensions={0} | all-to-all | bytes 786432 | tf_op jit(solution)/shard_map/all_to_all | solution.py:775
  65.7 1.0 rows.1.refs_0_
  66.7 0.3 collective-permute-start.12
  67.0 1.9 %collective-permute-start.11 = (bf16[144,128]{1,0:T(8,128)(2,1)S(1)}, bf16[144,128]{1,0:T(8,128)(2,1)S(1)}, u32[]{:S(2)}, u32[]{:S(2)}) collective-permute-start(bf16[144,128]{1,0:T(8,128)(2,1)S(1)} %rows.1.refs_0_), channel_id=1, source_target_pairs={{0,128},{8,136},{16,144},{24,152},{32,160},{40,168},{48,176},{56,1... | collective-permute-start | bytes 110600 | tf_op jit(solution)/shard_map/ppermute | solution.py:779
  68.9 0.0 collective-permute-start.10
  68.9 1.5 %collective-permute-done.12.refs_3_ = bf16[144,128]{1,0:T(8,128)(2,1)S(1)} collective-permute-done((bf16[144,128]{1,0:T(8,128)(2,1)S(1)}, bf16[144,128]{1,0:T(8,128)(2,1)S(1)}, u32[]{:S(2)}, u32[]{:S(2)}) %collective-permute-start.12) | collective-permute-done | bytes 36896 | tf_op jit(solution)/shard_map/ppermute | solution.py:779
  70.4 0.7 collective-permute-done.11.refs_2_
  71.2 1.2 %product.3 = bf16[8,120,128]{2,1,0:T(8,128)(2,1)} custom-call(bf16[144,128]{1,0:T(8,128)(2,1)S(1)} %rows.1.refs_0_, bf16[144,128]{1,0:T(8,128)(2,1)S(1)} %collective-permute-done.10.refs_1_, bf16[144,128]{1,0:T(8,128)(2,1)S(1)} %collective-permute-done.11.refs_2_, bf16[144,128]{1,0:T(8,128)(2,1)S(1)} %collective-permute-done.12.refs_3_, ...), custom_call_target="tpu_custom_call" | custom-call | tf_op jit(solution)/shard_map/product/pallas_call | solution.py:402
  72.4 3.5 %all-to-all-start.3 = ((bf16[8,120,128]{2,1,0:T(8,128)(2,1)}), bf16[8,120,128]{2,1,0:T(8,128)(2,1)S(1)}, u32[]{:S(2)}, u32[]{:S(2)}) async-start(bf16[8,120,128]{2,1,0:T(8,128)(2,1)} %product.3), calls=%async_computation.3 | async-start | bytes 491520 | tf_op jit(solution)/shard_map/all_to_all | solution.py:781
  75.9 9.7 %first.1 = (bf16[45,160,128]{2,1,0:T(8,128)(2,1)}, bf16[2,72,128]{2,1,0:T(8,128)(2,1)}, bf16[160,128]{1,0:T(8,128)(2,1)}, bf16[160,128]{1,0:T(8,128)(2,1)}) custom-call(s32[34]{0:T(128)} %copy-done.8, bf16[45,160,128]{2,1,0:T(8,128)(2,1)} %cells_hbm.3, bf16[45,64,128]{2,1,0:T(8,128)(2,1)} %winds_ref.1, bf16[192,128]{1,0:T(8,128)(2,1)} %copy-done.4, ...), custom_call_target="tpu_custom_call" | custom-call | tf_op jit(solution)/shard_map/first/pallas_call | solution.py:690
  85.7 2.7 %all-to-all-done.3.recv_ref = bf16[8,120,128]{2,1,0:T(8,128)(2,1)S(1)} async-done(((bf16[8,120,128]{2,1,0:T(8,128)(2,1)}), bf16[8,120,128]{2,1,0:T(8,128)(2,1)S(1)}, u32[]{:S(2)}, u32[]{:S(2)}) %all-to-all-start.3) | async-done | bytes 245792 | tf_op jit(solution)/shard_map/all_to_all | solution.py:781
  88.4 0.8 copy-done.7
  89.1 1.4 %total.3.message_hbm = bf16[8,192,128]{2,1,0:T(8,128)(2,1)} custom-call(s32[34]{0:T(128)S(1)} %copy-done.9, bf16[8,120,128]{2,1,0:T(8,128)(2,1)S(1)} %all-to-all-done.3.recv_ref, bf16[2,72,128]{2,1,0:T(8,128)(2,1)S(1)} %copy-done.7), custom_call_target="tpu_custom_call" | custom-call | tf_op jit(solution)/shard_map/total/pallas_call | solution.py:429
  90.6 3.5 %all-to-all-start.4 = ((bf16[8,192,128]{2,1,0:T(8,128)(2,1)}), bf16[8,192,128]{2,1,0:T(8,128)(2,1)S(1)}, u32[]{:S(2)}, u32[]{:S(2)}) async-start(bf16[8,192,128]{2,1,0:T(8,128)(2,1)} %total.3.message_hbm), calls=%async_computation.4 | async-start | bytes 786432 | tf_op jit(solution)/shard_map/all_to_all | solution.py:775
  94.0 0.1 collective-permute-start.13
  94.2 3.8 %collective-permute-start.14 = (bf16[160,128]{1,0:T(8,128)(2,1)}, bf16[160,128]{1,0:T(8,128)(2,1)S(1)}, u32[]{:S(2)}, u32[]{:S(2)}) collective-permute-start(bf16[160,128]{1,0:T(8,128)(2,1)} %get-tuple-element.46), channel_id=1, source_target_pairs={{0,248},{8,0},{16,8},{24,16},{32,24},{40,32},{48,40},{56,48},{64,5... | collective-permute-start | bytes 122888 | tf_op jit(solution)/shard_map/ppermute | solution.py:806
  98.0 1.5 %copy-done.3 = bf16[45,160,128]{2,1,0:T(8,128)(2,1)S(1)} copy-done((bf16[45,160,128]{2,1,0:T(8,128)(2,1)S(1)}, bf16[45,160,128]{2,1,0:T(8,128)(2,1)}, u32[]{:S(2)}) %copy-start.3) | copy-done | bytes 1843224
  99.5 0.8 stay.1.cells_ref
  100.3 4.2 %all-to-all-done.4.recv_ref = bf16[8,192,128]{2,1,0:T(8,128)(2,1)S(1)} async-done(((bf16[8,192,128]{2,1,0:T(8,128)(2,1)}), bf16[8,192,128]{2,1,0:T(8,128)(2,1)S(1)}, u32[]{:S(2)}, u32[]{:S(2)}) %all-to-all-start.4) | async-done | bytes 393248 | tf_op jit(solution)/shard_map/all_to_all | solution.py:775
  104.6 7.0 %last.1 = f32[45,160,128]{2,1,0:T(8,128)} custom-call(s32[34]{0:T(128)S(1)} %copy-done.9, bf16[45,160,128]{2,1,0:T(8,128)(2,1)S(1)} %stay.1.cells_ref, bf16[45,64,128]{2,1,0:T(8,128)(2,1)S(1)} %copy-done, bf16[160,128]{1,0:T(8,128)(2,1)S(1)} %collective-permute-done.13.west_ref, bf16[160,128]{1,0:T(8,128)(2,1)S(1)} %collective-permute-done.14.east_ref, ...), custom_call_target="tpu_custom_call" | custom-call | tf_op jit(solution)/shard_map/last/pallas_call | solution.py:737
  (38 shorter events, 0.2 us)
Async XLA Ops:
  0.0 13.2 %copy-start.10 = (bf16[2,45,1440]{2,0,1:T(2,128)(2,1)S(1)}, bf16[2,45,1440]{2,0,1:T(2,128)(2,1)}, u32[]{:S(2)}) copy-start(bf16[2,45,1440]{2,0,1:T(2,128)(2,1)} %param.7) | copy-start | bytes 777604
  7.2 6.2 %copy-start.12 = (s32[16]{0:T(128)S(1)}, s32[16]{0:T(128)}, u32[]{:S(2)}) copy-start(s32[16]{0:T(128)} %row_ref.1) | copy-start | bytes 196
  7.2 6.2 %copy-start.13 = (s32[16]{0:T(128)S(1)}, s32[16]{0:T(128)}, u32[]{:S(2)}) copy-start(s32[16]{0:T(128)} %band_ref.1) | copy-start | bytes 196
  7.2 7.6 %copy-start.14 = (bf16[192,128]{1,0:T(8,128)(2,1)S(1)}, bf16[192,128]{1,0:T(8,128)(2,1)}, u32[]{:S(2)}) copy-start(bf16[192,128]{1,0:T(8,128)(2,1)} %get-tuple-element.27) | copy-start | bytes 147460
  7.2 8.1 %copy-start.15 = (bf16[160,128]{1,0:T(8,128)(2,1)S(1)}, bf16[160,128]{1,0:T(8,128)(2,1)}, u32[]{:S(2)}) copy-start(bf16[160,128]{1,0:T(8,128)(2,1)} %get-tuple-element.28) | copy-start | bytes 122884
  7.2 18.6 %all-to-all-start = ((bf16[8,312,128]{2,1,0:T(8,128)(2,1)}), bf16[8,312,128]{2,1,0:T(8,128)(2,1)S(1)}, u32[]{:S(2)}, u32[]{:S(2)}) async-start(bf16[8,312,128]{2,1,0:T(8,128)(2,1)} %get-tuple-element.26), calls=%async_computation | async-start | bytes 1277952 | tf_op jit(solution)/shard_map/all_to_all | solution.py:775
  13.2 38.5 %copy-start.6 = (bf16[2,72,128]{2,1,0:T(8,128)(2,1)S(1)}, bf16[2,72,128]{2,1,0:T(8,128)(2,1)}, u32[]{:S(2)}) copy-start(bf16[2,72,128]{2,1,0:T(8,128)(2,1)} %get-tuple-element.39.edges_hbm) | copy-start | bytes 110596
  13.4 52.2 %copy-start.8 = (s32[34]{0:T(128)}, s32[34]{0:T(128)S(1)}, u32[]{:S(2)}) copy-start(s32[34]{0:T(128)S(1)} %pad_add_fusion.meta_ref) | copy-start | bytes 412
  14.7 12.8 %collective-permute-start.5 = (bf16[384,96]{1,0:T(8,128)(2,1)S(1)}, bf16[384,96]{1,0:T(8,128)(2,1)S(1)}, u32[]{:S(2)}, u32[]{:S(2)}) collective-permute-start(bf16[384,96]{1,0:T(8,128)(2,1)S(1)} %get-tuple-element.33), channel_id=1, source_target_pairs={{0,8},{8,0},{16,24},{24,16},{32,40},{40,32},{48,56},{56,48},{64,72... | collective-permute-start | bytes 221192 | tf_op jit(solution)/shard_map/ppermute | solution.py:790
  14.8 8.7 %collective-permute-start = (bf16[192,128]{1,0:T(8,128)(2,1)S(1)}, bf16[192,128]{1,0:T(8,128)(2,1)S(1)}, u32[]{:S(2)}, u32[]{:S(2)}) collective-permute-start(bf16[192,128]{1,0:T(8,128)(2,1)S(1)} %copy-done.14), channel_id=1, source_target_pairs={{0,8},{8,16},{16,24},{24,32},{32,40},{40,48},{48,56},{56,64},{64,7... | collective-permute-start | bytes 147464 | tf_op jit(solution)/shard_map/ppermute | solution.py:792
  15.3 8.1 %collective-permute-start.1 = (bf16[160,128]{1,0:T(8,128)(2,1)S(1)}, bf16[160,128]{1,0:T(8,128)(2,1)S(1)}, u32[]{:S(2)}, u32[]{:S(2)}) collective-permute-start(bf16[160,128]{1,0:T(8,128)(2,1)S(1)} %copy-done.15), channel_id=1, source_target_pairs={{0,248},{8,0},{16,8},{24,16},{32,24},{40,32},{48,40},{56,48},{64,5... | collective-permute-start | bytes 122888 | tf_op jit(solution)/shard_map/ppermute | solution.py:793
  21.7 6.1 %collective-permute-start.6 = (bf16[384,96]{1,0:T(8,128)(2,1)S(1)}, bf16[384,96]{1,0:T(8,128)(2,1)S(1)}, u32[]{:S(2)}, u32[]{:S(2)}) collective-permute-start(bf16[384,96]{1,0:T(8,128)(2,1)S(1)} %get-tuple-element.34), channel_id=1, source_target_pairs={{0,128},{8,136},{16,144},{24,152},{32,160},{40,168},{48,176},{56,1... | collective-permute-start | bytes 221192 | tf_op jit(solution)/shard_map/ppermute | solution.py:790
  22.3 5.5 %collective-permute-start.7 = (bf16[384,96]{1,0:T(8,128)(2,1)S(1)}, bf16[384,96]{1,0:T(8,128)(2,1)S(1)}, u32[]{:S(2)}, u32[]{:S(2)}) collective-permute-start(bf16[384,96]{1,0:T(8,128)(2,1)S(1)} %get-tuple-element.35), channel_id=1, source_target_pairs={{0,136},{8,128},{16,152},{24,144},{32,168},{40,160},{48,184},{56,1... | collective-permute-start | bytes 221192 | tf_op jit(solution)/shard_map/ppermute | solution.py:790
  23.4 42.3 %copy-start.11 = (bf16[160,128]{1,0:T(8,128)(2,1)}, bf16[160,128]{1,0:T(8,128)(2,1)S(1)}, u32[]{:S(2)}) copy-start(bf16[160,128]{1,0:T(8,128)(2,1)S(1)} %collective-permute-done.1.east_ref) | copy-start | bytes 122884
  23.5 42.2 %copy-start.4 = (bf16[192,128]{1,0:T(8,128)(2,1)}, bf16[192,128]{1,0:T(8,128)(2,1)S(1)}, u32[]{:S(2)}) copy-start(bf16[192,128]{1,0:T(8,128)(2,1)S(1)} %collective-permute-done.west_ref.wind_west_ref) | copy-start | bytes 147460
  25.8 3.9 %collective-permute-start.4 = (bf16[144,128]{1,0:T(8,128)(2,1)S(1)}, bf16[144,128]{1,0:T(8,128)(2,1)S(1)}, u32[]{:S(2)}, u32[]{:S(2)}) collective-permute-start(bf16[144,128]{1,0:T(8,128)(2,1)S(1)} %unpack.1.refs_0_.rows_ref.before_ref), channel_id=1, source_target_pairs={{0,136},{8,128},{16,152},{24,144},{32,168},{40,160},{48,184},{56,1... | collective-permute-start | bytes 110600 | tf_op jit(solution)/shard_map/ppermute | solution.py:779
  25.9 4.2 %collective-permute-start.3 = (bf16[144,128]{1,0:T(8,128)(2,1)S(1)}, bf16[144,128]{1,0:T(8,128)(2,1)S(1)}, u32[]{:S(2)}, u32[]{:S(2)}) collective-permute-start(bf16[144,128]{1,0:T(8,128)(2,1)S(1)} %unpack.1.refs_0_.rows_ref.before_ref), channel_id=1, source_target_pairs={{0,128},{8,136},{16,144},{24,152},{32,160},{40,168},{48,176},{56,1... | collective-permute-start | bytes 110600 | tf_op jit(solution)/shard_map/ppermute | solution.py:779
  27.4 2.6 %collective-permute-start.2 = (bf16[144,128]{1,0:T(8,128)(2,1)S(1)}, bf16[144,128]{1,0:T(8,128)(2,1)S(1)}, u32[]{:S(2)}, u32[]{:S(2)}) collective-permute-start(bf16[144,128]{1,0:T(8,128)(2,1)S(1)} %unpack.1.refs_0_.rows_ref.before_ref), channel_id=1, source_target_pairs={{0,8},{8,0},{16,24},{24,16},{32,40},{40,32},{48,56},{56,48},{64,72... | collective-permute-start | bytes 110600 | tf_op jit(solution)/shard_map/ppermute | solution.py:779
  31.3 20.4 %all-to-all-start.1 = ((bf16[8,120,128]{2,1,0:T(8,128)(2,1)}), bf16[8,120,128]{2,1,0:T(8,128)(2,1)S(1)}, u32[]{:S(2)}, u32[]{:S(2)}) async-start(bf16[8,120,128]{2,1,0:T(8,128)(2,1)} %product.2), calls=%async_computation.1 | async-start | bytes 491520 | tf_op jit(solution)/shard_map/all_to_all | solution.py:781
  40.6 5.4 %collective-permute-start.8 = (f32[8,128]{1,0:T(8,128)S(1)}, f32[8,128]{1,0:T(8,128)S(1)}, u32[]{:S(2)}, u32[]{:S(2)}) collective-permute-start(f32[8,128]{1,0:T(8,128)S(1)} %get-tuple-element.36), channel_id=1, source_target_pairs={{0,8},{8,16},{16,24},{24,32},{32,40},{40,48},{48,56},{56,64},{64,7... | collective-permute-start | bytes 12296 | tf_op jit(solution)/shard_map/ppermute | solution.py:798
  40.7 5.3 %collective-permute-start.9 = (f32[8,128]{1,0:T(8,128)S(1)}, f32[8,128]{1,0:T(8,128)S(1)}, u32[]{:S(2)}, u32[]{:S(2)}) collective-permute-start(f32[8,128]{1,0:T(8,128)S(1)} %get-tuple-element.37), channel_id=1, source_target_pairs={{0,248},{8,0},{16,8},{24,16},{32,24},{40,32},{48,40},{56,48},{64,5... | collective-permute-start | bytes 12296 | tf_op jit(solution)/shard_map/ppermute | solution.py:799
  65.7 10.3 %copy-start.1 = (bf16[8,192,128]{2,1,0:T(8,128)(2,1)}, bf16[8,192,128]{2,1,0:T(8,128)(2,1)S(1)}, u32[]{:S(2)}) copy-start(bf16[8,192,128]{2,1,0:T(8,128)(2,1)S(1)} %all_to_all.25.recv_ref.wind_recv_ref) | copy-start | bytes 1179652
  66.7 3.7 %collective-permute-start.12 = (bf16[144,128]{1,0:T(8,128)(2,1)S(1)}, bf16[144,128]{1,0:T(8,128)(2,1)S(1)}, u32[]{:S(2)}, u32[]{:S(2)}) collective-permute-start(bf16[144,128]{1,0:T(8,128)(2,1)S(1)} %rows.1.refs_0_), channel_id=1, source_target_pairs={{0,136},{8,128},{16,152},{24,144},{32,168},{40,160},{48,184},{56,1... | collective-permute-start | bytes 110600 | tf_op jit(solution)/shard_map/ppermute | solution.py:779
  67.0 4.2 %collective-permute-start.11 = (bf16[144,128]{1,0:T(8,128)(2,1)S(1)}, bf16[144,128]{1,0:T(8,128)(2,1)S(1)}, u32[]{:S(2)}, u32[]{:S(2)}) collective-permute-start(bf16[144,128]{1,0:T(8,128)(2,1)S(1)} %rows.1.refs_0_), channel_id=1, source_target_pairs={{0,128},{8,136},{16,144},{24,152},{32,160},{40,168},{48,176},{56,1... | collective-permute-start | bytes 110600 | tf_op jit(solution)/shard_map/ppermute | solution.py:779
  68.9 2.3 %collective-permute-start.10 = (bf16[144,128]{1,0:T(8,128)(2,1)S(1)}, bf16[144,128]{1,0:T(8,128)(2,1)S(1)}, u32[]{:S(2)}, u32[]{:S(2)}) collective-permute-start(bf16[144,128]{1,0:T(8,128)(2,1)S(1)} %rows.1.refs_0_), channel_id=1, source_target_pairs={{0,8},{8,0},{16,24},{24,16},{32,40},{40,32},{48,56},{56,48},{64,72... | collective-permute-start | bytes 110600 | tf_op jit(solution)/shard_map/ppermute | solution.py:779
  72.4 16.0 %copy-start.9 = (s32[34]{0:T(128)S(1)}, s32[34]{0:T(128)}, u32[]{:S(2)}) copy-start(s32[34]{0:T(128)} %copy-done.8) | copy-start | bytes 412
  72.4 16.0 %all-to-all-start.3 = ((bf16[8,120,128]{2,1,0:T(8,128)(2,1)}), bf16[8,120,128]{2,1,0:T(8,128)(2,1)S(1)}, u32[]{:S(2)}, u32[]{:S(2)}) async-start(bf16[8,120,128]{2,1,0:T(8,128)(2,1)} %product.3), calls=%async_computation.3 | async-start | bytes 491520 | tf_op jit(solution)/shard_map/all_to_all | solution.py:781
  88.4 0.8 copy-start.7
  90.6 14.0 %all-to-all-start.4 = ((bf16[8,192,128]{2,1,0:T(8,128)(2,1)}), bf16[8,192,128]{2,1,0:T(8,128)(2,1)S(1)}, u32[]{:S(2)}, u32[]{:S(2)}) async-start(bf16[8,192,128]{2,1,0:T(8,128)(2,1)} %total.3.message_hbm), calls=%async_computation.4 | async-start | bytes 786432 | tf_op jit(solution)/shard_map/all_to_all | solution.py:775
  94.0 6.3 %collective-permute-start.13 = (bf16[160,128]{1,0:T(8,128)(2,1)}, bf16[160,128]{1,0:T(8,128)(2,1)S(1)}, u32[]{:S(2)}, u32[]{:S(2)}) collective-permute-start(bf16[160,128]{1,0:T(8,128)(2,1)} %get-tuple-element.45), channel_id=1, source_target_pairs={{0,8},{8,16},{16,24},{24,32},{32,40},{40,48},{48,56},{56,64},{64,7... | collective-permute-start | bytes 122888 | tf_op jit(solution)/shard_map/ppermute | solution.py:805
  94.2 6.1 %collective-permute-start.14 = (bf16[160,128]{1,0:T(8,128)(2,1)}, bf16[160,128]{1,0:T(8,128)(2,1)S(1)}, u32[]{:S(2)}, u32[]{:S(2)}) collective-permute-start(bf16[160,128]{1,0:T(8,128)(2,1)} %get-tuple-element.46), channel_id=1, source_target_pairs={{0,248},{8,0},{16,8},{24,16},{32,24},{40,32},{48,40},{56,48},{64,5... | collective-permute-start | bytes 122888 | tf_op jit(solution)/shard_map/ppermute | solution.py:806
  98.0 1.5 %copy-start.3 = (bf16[45,160,128]{2,1,0:T(8,128)(2,1)S(1)}, bf16[45,160,128]{2,1,0:T(8,128)(2,1)}, u32[]{:S(2)}) copy-start(bf16[45,160,128]{2,1,0:T(8,128)(2,1)} %get-tuple-element.40.cells_hbm) | copy-start | bytes 5529604
  99.5 5.1 %copy-start = (bf16[45,64,128]{2,1,0:T(8,128)(2,1)S(1)}, bf16[45,64,128]{2,1,0:T(8,128)(2,1)}, u32[]{:S(2)}) copy-start(bf16[45,64,128]{2,1,0:T(8,128)(2,1)} %winds_ref.1) | copy-start | bytes 2211844
  99.5 5.1 %copy-start.2 = (bf16[8,192,128]{2,1,0:T(8,128)(2,1)S(1)}, bf16[8,192,128]{2,1,0:T(8,128)(2,1)}, u32[]{:S(2)}) copy-start(bf16[8,192,128]{2,1,0:T(8,128)(2,1)} %copy-done.1) | copy-start | bytes 1179652
  99.5 5.1 %copy-start.5 = (bf16[192,128]{1,0:T(8,128)(2,1)S(1)}, bf16[192,128]{1,0:T(8,128)(2,1)}, u32[]{:S(2)}) copy-start(bf16[192,128]{1,0:T(8,128)(2,1)} %copy-done.4) | copy-start | bytes 147460

commit v6 on v5

--- a/solution.py
+++ b/solution.py
@@ -574,32 +574,42 @@
     return jnp.where(lane == target, 1.0, 0.0).astype(BF16)
 
 
-def advance(meta_ref, cells_ref, winds_ref, west_ref, east_ref, wind_west_ref, tall_ref, placed_ref, smooth_ref, emit):
+def advance(
+    meta_ref, cells_ref, winds_ref, west_ref, east_ref, wind_west_ref, tall_ref, placed_ref, smooth_ref, emit, leaving,
+    rounded,
+):
     for q in range(GROUP):
         placed_ref[q] = jnp.dot(tall_ref[...], place_weights(meta_ref, q), preferred_element_type=F32)
     top = meta_ref[0] == BANDS - 1
 
     def smooth(r, base):
-        at = pl.multiple_of((r // GROUP) * TALL, TALL)
-        change = placed_ref[r % GROUP, pl.ds(at, COLS), :LANES]
-        smooth_ref[r] = (base.astype(F32) + change).astype(BF16).astype(F32)
+        at = (r // GROUP) * TALL
+        value = base.astype(F32) + placed_ref[r % GROUP, pl.ds(at, COLS), :LANES]
+        if rounded:
+            value = value.astype(BF16).astype(F32)
+        smooth_ref[r] = value
+        return value
+
+    def step(x, ahead):
+        ahead = smooth(x + 2, ahead)
+        emit(x, stencil(x, top, winds_ref, wind_west_ref, smooth_ref, ahead, placed_ref))
+
+    def body(x, carry):
+        step(x, cells_ref[x + 1])
+        return carry
 
     smooth(0, west_ref[:COLS, :])
     smooth(1, cells_ref[0])
-    smooth(XS + 1, east_ref[...])
-
-    def body(x, carry):
-        r = jnp.minimum(x + 2, XS)
-        smooth(r, cells_ref[r - 1])
-        made = stencil(x, top, winds_ref, wind_west_ref, smooth_ref, placed_ref)
-        emit(x, made)
-        return carry
-
-    return body
-
-
-def stencil(x, top, winds_ref, west_ref, smooth_ref, placed_ref):
-    at = pl.multiple_of(((x + 1) // GROUP) * TALL, TALL)
+    for (start, size), copy in zip(SPANS, leaving):
+        for x in range(start, min(start + size, XS - 1)):
+            body(x, 0)
+        if start + size == XS:
+            step(XS - 1, east_ref[...])
+        copy.start()
+
+
+def stencil(x, top, winds_ref, west_ref, smooth_ref, ahead, placed_ref):
+    at = ((x + 1) // GROUP) * TALL
     q = (x + 1) % GROUP
     lane = lax.broadcasted_iota(jnp.int32, (LEV, LANES), 1)
     courant = winds_ref[x].astype(F32)
@@ -622,7 +632,7 @@
         below = jnp.where(lane == 0, edge, pltpu.roll(here, 1, axis=1))
         made.append(
             centre * here
-            + (east * smooth_ref[x + 2, span, :] - west * smooth_ref[x, span, :])
+            + (east * ahead[span] - west * smooth_ref[x, span, :])
             + (north * above - south * below)
         )
     return made
@@ -654,16 +664,16 @@
         for v in range(VAR):
             out_ref[x, v * LEV : (v + 1) * LEV, :] = made[v].astype(BF16)
 
-    body = advance(
-        meta_ref, cells_ref, winds_ref, west_ref, east_ref, west_ref, tall_ref, placed_ref, smooth_ref, emit
+    leaving = copies(out_ref, out_hbm, out_sem)
+    advance(
+        meta_ref, cells_ref, winds_ref, west_ref, east_ref, west_ref, tall_ref, placed_ref, smooth_ref, emit, leaving,
+        True,
     )
-    leaving = copies(out_ref, out_hbm, out_sem)
-    leaving.append(pltpu.make_async_copy(out_ref.at[0], to_west_hbm, rim_sem.at[0]))
-    leaving.append(pltpu.make_async_copy(out_ref.at[XS - 1], to_east_hbm, rim_sem.at[1]))
-    for (start, size), copy in zip(SPANS, leaving):
-        lax.fori_loop(start, start + size, body, 0, unroll=4)
-        copy.start()
-    for copy in leaving[-2:]:
+    rims = [
+        pltpu.make_async_copy(out_ref.at[0], to_west_hbm, rim_sem.at[0]),
+        pltpu.make_async_copy(out_ref.at[XS - 1], to_east_hbm, rim_sem.at[1]),
+    ]
+    for copy in rims:
         copy.start()
     sub, lane = iotas((LANES, LANES))
     halves = [(sub == 0) & (lane == 2 * side) | (sub == LANES - 1) & (lane == 2 * side + 1) for side in range(2)]
@@ -682,7 +692,7 @@
     for at in range(2):
         edges_ref[at, :ROWS, :] = main_ref[pl.ds(at, ROWS, stride=2), :].astype(BF16)
         edges_ref[at, ROWS:, :] = folded(rest_ref[pl.ds(at, ROWS, stride=2), :], LEV).astype(BF16)
-    for copy in leaving:
+    for copy in leaving + rims:
         copy.wait()
 
 
@@ -722,13 +732,11 @@
         for v in range(VAR):
             out_ref[x, v * LEV : (v + 1) * LEV, :] = made[v]
 
-    body = advance(
-        meta_ref, cells_ref, winds_ref, west_ref, east_ref, wind_west_ref, tall_ref, placed_ref, smooth_ref, emit
+    leaving = copies(out_ref, out_hbm, out_sem)
+    advance(
+        meta_ref, cells_ref, winds_ref, west_ref, east_ref, wind_west_ref, tall_ref, placed_ref, smooth_ref, emit,
+        leaving, False,
     )
-    leaving = copies(out_ref, out_hbm, out_sem)
-    for (start, size), copy in zip(SPANS, leaving):
-        lax.fori_loop(start, start + size, body, 0, unroll=4)
-        copy.start()
     for copy in leaving:
         copy.wait()
 
@@ -740,7 +748,7 @@
         in_specs=[SM] + [VM] * 7,
         out_specs=HB,
         scratch_shapes=SCRATCH + [pltpu.VMEM((XS, COLS, LANES), F32), DMA((len(SPANS),))],
-        compiler_params=params(24),
+        compiler_params=params(30),
         name="last",
     )(*args)
 

time: 112 us -> 111 us (level)
  Pallas kernels: 32.4 us -> 28.8 us
  waiting for transfers between devices: 22.1 us -> 24.2 us
    pallas_call x1, Pallas kernels: 9.73 us -> 7.66 us  [first_substep(): pl.pallas_call(first_kernel, out_shape=(shape((XS, COLS, LANES), BF16), s...]
    all_to_all x2, waiting for transfers between devices: 8.39 us -> 10.5 us  [filtered(): lax.all_to_all(partial, 'lon', 0, 0, tiled=True, axis_index_groups=ALONG_Z)]
    pallas_call x1, Pallas kernels: 6.97 us -> 5.39 us  [last_substep(): pl.pallas_call(last_kernel, out_shape=shape((XS, COLS, LANES), F32), in_s...]
  transfers between devices with their start and end apart: 19 -> 19, of which waited for: 11 -> 11; matrix products, arithmetic and copies ran while one was open for 0% -> 0% of each run, Pallas kernels for 11% -> 10%
where the time goes in v6:
time: 111 us; the launch traced here: 110 us
  starting transfers between devices  41.2 us (37%)
  Pallas kernels  28.8 us (26%)
  waiting for transfers between devices  24.2 us (22%)
  blocking collectives  13.3 us (12%)
  local copies, waits for them, and re-layouts  2.44 us (2%)
    all_to_all x1, blocking collectives, by_lat(): return lax.all_to_all(messages, 'lat', 0, 0, tiled=True)  13.3 us
    all_to_all x2, starting transfers between devices, filtered(): lax.all_to_all(partial, 'lon', 0, 0, tiled=True, axis_index_groups=ALONG_Z)  12 us
    all_to_all x2, waiting for transfers between devices, filtered(): lax.all_to_all(partial, 'lon', 0, 0, tiled=True, axis_index_groups=ALONG_Z)  10.5 us
    all_to_all x2, starting transfers between devices, by_lat(): return lax.all_to_all(messages, 'lat', 0, 0, tiled=True)  9.67 us
    pallas_call x1, Pallas kernels, first_substep(): pl.pallas_call(first_kernel, out_shape=(shape((XS, COLS, LANES), BF16), s...  7.66 us
    pallas_call x1, Pallas kernels, pick_rows(): pl.pallas_call(pick_kernel, out_shape=(shape((BANDS, WIRE, LANES), BF16),...  7.17 us
    all_to_all x2, waiting for transfers between devices, by_lat(): return lax.all_to_all(messages, 'lat', 0, 0, tiled=True)  6.53 us
    ppermute x1, starting transfers between devices, shards(): east = lax.ppermute(to_west, 'lon', WESTWARD)  6.41 us
  transfers between devices with their start and end apart: 19, of which 11 were waited for; matrix products, arithmetic and copies ran while one was open for 0% of the time, Pallas kernels for 10%

profile of v6, /device:TPU:2, one launch (start us, length us, event | category | flops | bytes accessed | tf_op | source)
XLA Modules:
  0.0 110.4 jit_solution(10132798036744378864)
XLA Ops:
  0.0 7.2 %pick.1 = (bf16[8,312,128]{2,1,0:T(8,128)(2,1)}, bf16[2,72,128]{2,1,0:T(8,128)(2,1)}, bf16[192,128]{1,0:T(8,128)(2,1)}, bf16[160,128]{1,0:T(8,128)(2,1)}) custom-call(s32[16]{0:T(128)} %band_ref.1, s32[16]{0:T(128)} %row_ref.1, bf16[45,160,128]{2,1,0:T(8,128)(2,1)} %cells_hbm.3, bf16[45,64,128]{2,1,0:T(8,128)(2,1)} %winds_ref.1), custom_call_target="tpu_custom_call" | custom-call | tf_op jit(solution)/shard_map/pick/pallas_call | solution.py:276
  7.2 0.0 copy-start.12
  7.2 0.0 copy-start.13
  7.2 6.2 %all-to-all-start = ((bf16[8,312,128]{2,1,0:T(8,128)(2,1)}), bf16[8,312,128]{2,1,0:T(8,128)(2,1)S(1)}, u32[]{:S(2)}, u32[]{:S(2)}) async-start(bf16[8,312,128]{2,1,0:T(8,128)(2,1)} %get-tuple-element.26), calls=%async_computation | async-start | bytes 1277952 | tf_op jit(solution)/shard_map/all_to_all | solution.py:783
  13.5 0.1 pad.4.ops_ref
  13.6 0.1 pad_add_fusion.meta_ref
  13.7 1.2 %operators.1 = (bf16[384,96]{1,0:T(8,128)(2,1)S(1)}, bf16[384,96]{1,0:T(8,128)(2,1)S(1)}, bf16[384,96]{1,0:T(8,128)(2,1)S(1)}, bf16[384,96]{1,0:T(8,128)(2,1)S(1)}) custom-call(s32[34]{0:T(128)S(1)} %pad_add_fusion.meta_ref, bf16[2,48,1440]{2,1,0:T(8,128)(2,1)S(1)} %pad.4.ops_ref), custom_call_target="tpu_custom_call" | custom-call | tf_op jit(solution)/shard_map/operators/pallas_call | solution.py:97
  14.9 0.1 collective-permute-start.5
  15.0 0.5 collective-permute-start
  15.5 6.4 %collective-permute-start.1 = (bf16[160,128]{1,0:T(8,128)(2,1)S(1)}, bf16[160,128]{1,0:T(8,128)(2,1)S(1)}, u32[]{:S(2)}, u32[]{:S(2)}) collective-permute-start(bf16[160,128]{1,0:T(8,128)(2,1)S(1)} %copy-done.15), channel_id=1, source_target_pairs={{0,248},{8,0},{16,8},{24,16},{32,24},{40,32},{48,40},{56,48},{64,5... | collective-permute-start | bytes 122888 | tf_op jit(solution)/shard_map/ppermute | solution.py:801
  21.9 0.6 collective-permute-start.6
  22.5 0.0 collective-permute-start.7
  22.5 1.1 collective-permute-done.1.east_ref
  23.6 0.1 collective-permute-done.west_ref.wind_west_ref
  23.7 2.3 %all-to-all-done.recv_ref = bf16[8,312,128]{2,1,0:T(8,128)(2,1)S(1)} async-done(((bf16[8,312,128]{2,1,0:T(8,128)(2,1)}), bf16[8,312,128]{2,1,0:T(8,128)(2,1)S(1)}, u32[]{:S(2)}, u32[]{:S(2)}) %all-to-all-start) | async-done | bytes 639008 | tf_op jit(solution)/shard_map/all_to_all | solution.py:783
  26.0 0.1 collective-permute-start.4
  26.1 1.5 %collective-permute-start.3 = (bf16[144,128]{1,0:T(8,128)(2,1)S(1)}, bf16[144,128]{1,0:T(8,128)(2,1)S(1)}, u32[]{:S(2)}, u32[]{:S(2)}) collective-permute-start(bf16[144,128]{1,0:T(8,128)(2,1)S(1)} %unpack.1.refs_0_.rows_ref.before_ref), channel_id=1, source_target_pairs={{0,128},{8,136},{16,144},{24,152},{32,160},{40,168},{48,176},{56,1... | collective-permute-start | bytes 110600 | tf_op jit(solution)/shard_map/ppermute | solution.py:787
  27.7 0.3 collective-permute-start.2
  28.0 1.9 %collective-permute-done.4.refs_3_ = bf16[144,128]{1,0:T(8,128)(2,1)S(1)} collective-permute-done((bf16[144,128]{1,0:T(8,128)(2,1)S(1)}, bf16[144,128]{1,0:T(8,128)(2,1)S(1)}, u32[]{:S(2)}, u32[]{:S(2)}) %collective-permute-start.4) | collective-permute-done | bytes 36896 | tf_op jit(solution)/shard_map/ppermute | solution.py:787
  29.9 0.4 collective-permute-done.3.refs_2_
  30.3 1.2 %product.2 = bf16[8,120,128]{2,1,0:T(8,128)(2,1)} custom-call(bf16[144,128]{1,0:T(8,128)(2,1)S(1)} %unpack.1.refs_0_.rows_ref.before_ref, bf16[144,128]{1,0:T(8,128)(2,1)S(1)} %collective-permute-done.2.refs_1_, bf16[144,128]{1,0:T(8,128)(2,1)S(1)} %collective-permute-done.3.refs_2_, bf16[144,128]{1,0:T(8,128)(2,1)S(1)} %collective-permute-done.4.refs_3_, ...), custom_call_target="tpu_custom_call" | custom-call | tf_op jit(solution)/shard_map/product/pallas_call | solution.py:402
  31.5 8.5 %all-to-all-start.1 = ((bf16[8,120,128]{2,1,0:T(8,128)(2,1)}), bf16[8,120,128]{2,1,0:T(8,128)(2,1)S(1)}, u32[]{:S(2)}, u32[]{:S(2)}) async-start(bf16[8,120,128]{2,1,0:T(8,128)(2,1)} %product.2), calls=%async_computation.1 | async-start | bytes 491520 | tf_op jit(solution)/shard_map/all_to_all | solution.py:789
  40.0 0.9 context.1
  40.8 0.1 collective-permute-start.8
  40.9 3.8 %collective-permute-start.9 = (f32[8,128]{1,0:T(8,128)S(1)}, f32[8,128]{1,0:T(8,128)S(1)}, u32[]{:S(2)}, u32[]{:S(2)}) collective-permute-start(f32[8,128]{1,0:T(8,128)S(1)} %get-tuple-element.37), channel_id=1, source_target_pairs={{0,248},{8,0},{16,8},{24,16},{32,24},{40,32},{48,40},{56,48},{64,5... | collective-permute-start | bytes 12296 | tf_op jit(solution)/shard_map/ppermute | solution.py:807
  44.8 1.4 %collective-permute-done.8.west_ref = f32[8,128]{1,0:T(8,128)S(1)} collective-permute-done((f32[8,128]{1,0:T(8,128)S(1)}, f32[8,128]{1,0:T(8,128)S(1)}, u32[]{:S(2)}, u32[]{:S(2)}) %collective-permute-start.8) | collective-permute-done | bytes 4128 | tf_op jit(solution)/shard_map/ppermute | solution.py:806
  46.2 5.7 %all-to-all-done.1.recv_ref = bf16[8,120,128]{2,1,0:T(8,128)(2,1)S(1)} async-done(((bf16[8,120,128]{2,1,0:T(8,128)(2,1)}), bf16[8,120,128]{2,1,0:T(8,128)(2,1)S(1)}, u32[]{:S(2)}, u32[]{:S(2)}) %all-to-all-start.1) | async-done | bytes 245792 | tf_op jit(solution)/shard_map/all_to_all | solution.py:789
  51.9 0.7 total.2
  52.6 13.3 %all_to_all.25.recv_ref.wind_recv_ref = bf16[8,192,128]{2,1,0:T(8,128)(2,1)S(1)} all-to-all(bf16[8,192,128]{2,1,0:T(8,128)(2,1)S(1)} %total.2), channel_id=1, replica_groups=mesh['lon'=32,'lat'=8] {'lat'}, dimensions={0} | all-to-all | bytes 786432 | tf_op jit(solution)/shard_map/all_to_all | solution.py:783
  65.9 1.0 rows.1.refs_0_
  67.0 0.3 collective-permute-start.12
  67.2 1.9 %collective-permute-start.11 = (bf16[144,128]{1,0:T(8,128)(2,1)S(1)}, bf16[144,128]{1,0:T(8,128)(2,1)S(1)}, u32[]{:S(2)}, u32[]{:S(2)}) collective-permute-start(bf16[144,128]{1,0:T(8,128)(2,1)S(1)} %rows.1.refs_0_), channel_id=1, source_target_pairs={{0,128},{8,136},{16,144},{24,152},{32,160},{40,168},{48,176},{56,1... | collective-permute-start | bytes 110600 | tf_op jit(solution)/shard_map/ppermute | solution.py:787
  69.1 0.0 collective-permute-start.10
  69.1 1.5 %collective-permute-done.12.refs_3_ = bf16[144,128]{1,0:T(8,128)(2,1)S(1)} collective-permute-done((bf16[144,128]{1,0:T(8,128)(2,1)S(1)}, bf16[144,128]{1,0:T(8,128)(2,1)S(1)}, u32[]{:S(2)}, u32[]{:S(2)}) %collective-permute-start.12) | collective-permute-done | bytes 36896 | tf_op jit(solution)/shard_map/ppermute | solution.py:787
  70.7 0.7 collective-permute-done.11.refs_2_
  71.4 1.2 %product.3 = bf16[8,120,128]{2,1,0:T(8,128)(2,1)} custom-call(bf16[144,128]{1,0:T(8,128)(2,1)S(1)} %rows.1.refs_0_, bf16[144,128]{1,0:T(8,128)(2,1)S(1)} %collective-permute-done.10.refs_1_, bf16[144,128]{1,0:T(8,128)(2,1)S(1)} %collective-permute-done.11.refs_2_, bf16[144,128]{1,0:T(8,128)(2,1)S(1)} %collective-permute-done.12.refs_3_, ...), custom_call_target="tpu_custom_call" | custom-call | tf_op jit(solution)/shard_map/product/pallas_call | solution.py:402
  72.6 3.5 %all-to-all-start.3 = ((bf16[8,120,128]{2,1,0:T(8,128)(2,1)}), bf16[8,120,128]{2,1,0:T(8,128)(2,1)S(1)}, u32[]{:S(2)}, u32[]{:S(2)}) async-start(bf16[8,120,128]{2,1,0:T(8,128)(2,1)} %product.3), calls=%async_computation.3 | async-start | bytes 491520 | tf_op jit(solution)/shard_map/all_to_all | solution.py:789
  76.2 7.7 %first.1 = (bf16[45,160,128]{2,1,0:T(8,128)(2,1)}, bf16[2,72,128]{2,1,0:T(8,128)(2,1)}, bf16[160,128]{1,0:T(8,128)(2,1)}, bf16[160,128]{1,0:T(8,128)(2,1)}) custom-call(s32[34]{0:T(128)} %copy-done.8, bf16[45,160,128]{2,1,0:T(8,128)(2,1)} %cells_hbm.3, bf16[45,64,128]{2,1,0:T(8,128)(2,1)} %winds_ref.1, bf16[192,128]{1,0:T(8,128)(2,1)} %copy-done.4, ...), custom_call_target="tpu_custom_call" | custom-call | tf_op jit(solution)/shard_map/first/pallas_call | solution.py:700
  83.9 4.7 %all-to-all-done.3.recv_ref = bf16[8,120,128]{2,1,0:T(8,128)(2,1)S(1)} async-done(((bf16[8,120,128]{2,1,0:T(8,128)(2,1)}), bf16[8,120,128]{2,1,0:T(8,128)(2,1)S(1)}, u32[]{:S(2)}, u32[]{:S(2)}) %all-to-all-start.3) | async-done | bytes 245792 | tf_op jit(solution)/shard_map/all_to_all | solution.py:789
  88.6 0.8 copy-done.7
  89.4 1.4 %total.3.message_hbm = bf16[8,192,128]{2,1,0:T(8,128)(2,1)} custom-call(s32[34]{0:T(128)S(1)} %copy-done.9, bf16[8,120,128]{2,1,0:T(8,128)(2,1)S(1)} %all-to-all-done.3.recv_ref, bf16[2,72,128]{2,1,0:T(8,128)(2,1)S(1)} %copy-done.7), custom_call_target="tpu_custom_call" | custom-call | tf_op jit(solution)/shard_map/total/pallas_call | solution.py:429
  90.8 3.5 %all-to-all-start.4 = ((bf16[8,192,128]{2,1,0:T(8,128)(2,1)}), bf16[8,192,128]{2,1,0:T(8,128)(2,1)S(1)}, u32[]{:S(2)}, u32[]{:S(2)}) async-start(bf16[8,192,128]{2,1,0:T(8,128)(2,1)} %total.3.message_hbm), calls=%async_computation.4 | async-start | bytes 786432 | tf_op jit(solution)/shard_map/all_to_all | solution.py:783
  94.3 0.1 collective-permute-start.13
  94.4 3.8 %collective-permute-start.14 = (bf16[160,128]{1,0:T(8,128)(2,1)}, bf16[160,128]{1,0:T(8,128)(2,1)S(1)}, u32[]{:S(2)}, u32[]{:S(2)}) collective-permute-start(bf16[160,128]{1,0:T(8,128)(2,1)} %get-tuple-element.46), channel_id=1, source_target_pairs={{0,248},{8,0},{16,8},{24,16},{32,24},{40,32},{48,40},{56,48},{64,5... | collective-permute-start | bytes 122888 | tf_op jit(solution)/shard_map/ppermute | solution.py:814
  98.2 1.5 %copy-done.3 = bf16[45,160,128]{2,1,0:T(8,128)(2,1)S(1)} copy-done((bf16[45,160,128]{2,1,0:T(8,128)(2,1)S(1)}, bf16[45,160,128]{2,1,0:T(8,128)(2,1)}, u32[]{:S(2)}) %copy-start.3) | copy-done | bytes 1843224
  99.7 0.8 stay.1.cells_ref
  100.6 4.2 %all-to-all-done.4.recv_ref = bf16[8,192,128]{2,1,0:T(8,128)(2,1)S(1)} async-done(((bf16[8,192,128]{2,1,0:T(8,128)(2,1)}), bf16[8,192,128]{2,1,0:T(8,128)(2,1)S(1)}, u32[]{:S(2)}, u32[]{:S(2)}) %all-to-all-start.4) | async-done | bytes 393248 | tf_op jit(solution)/shard_map/all_to_all | solution.py:783
  104.8 5.4 %last.1 = f32[45,160,128]{2,1,0:T(8,128)} custom-call(s32[34]{0:T(128)S(1)} %copy-done.9, bf16[45,160,128]{2,1,0:T(8,128)(2,1)S(1)} %stay.1.cells_ref, bf16[45,64,128]{2,1,0:T(8,128)(2,1)S(1)} %copy-done, bf16[160,128]{1,0:T(8,128)(2,1)S(1)} %collective-permute-done.13.west_ref, bf16[160,128]{1,0:T(8,128)(2,1)S(1)} %collective-permute-done.14.east_ref, ...), custom_call_target="tpu_custom_call" | custom-call | tf_op jit(solution)/shard_map/last/pallas_call | solution.py:745
  (38 shorter events, 0.2 us)
Async XLA Ops:
  0.0 13.4 %copy-start.10 = (bf16[2,45,1440]{2,0,1:T(2,128)(2,1)S(1)}, bf16[2,45,1440]{2,0,1:T(2,128)(2,1)}, u32[]{:S(2)}) copy-start(bf16[2,45,1440]{2,0,1:T(2,128)(2,1)} %param.7) | copy-start | bytes 777604
  7.2 6.4 %copy-start.12 = (s32[16]{0:T(128)S(1)}, s32[16]{0:T(128)}, u32[]{:S(2)}) copy-start(s32[16]{0:T(128)} %row_ref.1) | copy-start | bytes 196
  7.2 6.4 %copy-start.13 = (s32[16]{0:T(128)S(1)}, s32[16]{0:T(128)}, u32[]{:S(2)}) copy-start(s32[16]{0:T(128)} %band_ref.1) | copy-start | bytes 196
  7.2 7.8 %copy-start.14 = (bf16[192,128]{1,0:T(8,128)(2,1)S(1)}, bf16[192,128]{1,0:T(8,128)(2,1)}, u32[]{:S(2)}) copy-start(bf16[192,128]{1,0:T(8,128)(2,1)} %get-tuple-element.27) | copy-start | bytes 147460
  7.2 8.3 %copy-start.15 = (bf16[160,128]{1,0:T(8,128)(2,1)S(1)}, bf16[160,128]{1,0:T(8,128)(2,1)}, u32[]{:S(2)}) copy-start(bf16[160,128]{1,0:T(8,128)(2,1)} %get-tuple-element.28) | copy-start | bytes 122884
  7.2 18.8 %all-to-all-start = ((bf16[8,312,128]{2,1,0:T(8,128)(2,1)}), bf16[8,312,128]{2,1,0:T(8,128)(2,1)S(1)}, u32[]{:S(2)}, u32[]{:S(2)}) async-start(bf16[8,312,128]{2,1,0:T(8,128)(2,1)} %get-tuple-element.26), calls=%async_computation | async-start | bytes 1277952 | tf_op jit(solution)/shard_map/all_to_all | solution.py:783
  13.5 38.5 %copy-start.6 = (bf16[2,72,128]{2,1,0:T(8,128)(2,1)S(1)}, bf16[2,72,128]{2,1,0:T(8,128)(2,1)}, u32[]{:S(2)}) copy-start(bf16[2,72,128]{2,1,0:T(8,128)(2,1)} %get-tuple-element.39.edges_hbm) | copy-start | bytes 110596
  13.7 52.2 %copy-start.8 = (s32[34]{0:T(128)}, s32[34]{0:T(128)S(1)}, u32[]{:S(2)}) copy-start(s32[34]{0:T(128)S(1)} %pad_add_fusion.meta_ref) | copy-start | bytes 412
  14.9 12.8 %collective-permute-start.5 = (bf16[384,96]{1,0:T(8,128)(2,1)S(1)}, bf16[384,96]{1,0:T(8,128)(2,1)S(1)}, u32[]{:S(2)}, u32[]{:S(2)}) collective-permute-start(bf16[384,96]{1,0:T(8,128)(2,1)S(1)} %get-tuple-element.33), channel_id=1, source_target_pairs={{0,8},{8,0},{16,24},{24,16},{32,40},{40,32},{48,56},{56,48},{64,72... | collective-permute-start | bytes 221192 | tf_op jit(solution)/shard_map/ppermute | solution.py:798
  15.0 8.7 %collective-permute-start = (bf16[192,128]{1,0:T(8,128)(2,1)S(1)}, bf16[192,128]{1,0:T(8,128)(2,1)S(1)}, u32[]{:S(2)}, u32[]{:S(2)}) collective-permute-start(bf16[192,128]{1,0:T(8,128)(2,1)S(1)} %copy-done.14), channel_id=1, source_target_pairs={{0,8},{8,16},{16,24},{24,32},{32,40},{40,48},{48,56},{56,64},{64,7... | collective-permute-start | bytes 147464 | tf_op jit(solution)/shard_map/ppermute | solution.py:800
  15.5 8.1 %collective-permute-start.1 = (bf16[160,128]{1,0:T(8,128)(2,1)S(1)}, bf16[160,128]{1,0:T(8,128)(2,1)S(1)}, u32[]{:S(2)}, u32[]{:S(2)}) collective-permute-start(bf16[160,128]{1,0:T(8,128)(2,1)S(1)} %copy-done.15), channel_id=1, source_target_pairs={{0,248},{8,0},{16,8},{24,16},{32,24},{40,32},{48,40},{56,48},{64,5... | collective-permute-start | bytes 122888 | tf_op jit(solution)/shard_map/ppermute | solution.py:801
  21.9 6.1 %collective-permute-start.6 = (bf16[384,96]{1,0:T(8,128)(2,1)S(1)}, bf16[384,96]{1,0:T(8,128)(2,1)S(1)}, u32[]{:S(2)}, u32[]{:S(2)}) collective-permute-start(bf16[384,96]{1,0:T(8,128)(2,1)S(1)} %get-tuple-element.34), channel_id=1, source_target_pairs={{0,128},{8,136},{16,144},{24,152},{32,160},{40,168},{48,176},{56,1... | collective-permute-start | bytes 221192 | tf_op jit(solution)/shard_map/ppermute | solution.py:798
  22.5 5.5 %collective-permute-start.7 = (bf16[384,96]{1,0:T(8,128)(2,1)S(1)}, bf16[384,96]{1,0:T(8,128)(2,1)S(1)}, u32[]{:S(2)}, u32[]{:S(2)}) collective-permute-start(bf16[384,96]{1,0:T(8,128)(2,1)S(1)} %get-tuple-element.35), channel_id=1, source_target_pairs={{0,136},{8,128},{16,152},{24,144},{32,168},{40,160},{48,184},{56,1... | collective-permute-start | bytes 221192 | tf_op jit(solution)/shard_map/ppermute | solution.py:798
  23.6 42.3 %copy-start.11 = (bf16[160,128]{1,0:T(8,128)(2,1)}, bf16[160,128]{1,0:T(8,128)(2,1)S(1)}, u32[]{:S(2)}) copy-start(bf16[160,128]{1,0:T(8,128)(2,1)S(1)} %collective-permute-done.1.east_ref) | copy-start | bytes 122884
  23.7 42.2 %copy-start.4 = (bf16[192,128]{1,0:T(8,128)(2,1)}, bf16[192,128]{1,0:T(8,128)(2,1)S(1)}, u32[]{:S(2)}) copy-start(bf16[192,128]{1,0:T(8,128)(2,1)S(1)} %collective-permute-done.west_ref.wind_west_ref) | copy-start | bytes 147460
  26.0 3.9 %collective-permute-start.4 = (bf16[144,128]{1,0:T(8,128)(2,1)S(1)}, bf16[144,128]{1,0:T(8,128)(2,1)S(1)}, u32[]{:S(2)}, u32[]{:S(2)}) collective-permute-start(bf16[144,128]{1,0:T(8,128)(2,1)S(1)} %unpack.1.refs_0_.rows_ref.before_ref), channel_id=1, source_target_pairs={{0,136},{8,128},{16,152},{24,144},{32,168},{40,160},{48,184},{56,1... | collective-permute-start | bytes 110600 | tf_op jit(solution)/shard_map/ppermute | solution.py:787
  26.1 4.2 %collective-permute-start.3 = (bf16[144,128]{1,0:T(8,128)(2,1)S(1)}, bf16[144,128]{1,0:T(8,128)(2,1)S(1)}, u32[]{:S(2)}, u32[]{:S(2)}) collective-permute-start(bf16[144,128]{1,0:T(8,128)(2,1)S(1)} %unpack.1.refs_0_.rows_ref.before_ref), channel_id=1, source_target_pairs={{0,128},{8,136},{16,144},{24,152},{32,160},{40,168},{48,176},{56,1... | collective-permute-start | bytes 110600 | tf_op jit(solution)/shard_map/ppermute | solution.py:787
  27.7 2.6 %collective-permute-start.2 = (bf16[144,128]{1,0:T(8,128)(2,1)S(1)}, bf16[144,128]{1,0:T(8,128)(2,1)S(1)}, u32[]{:S(2)}, u32[]{:S(2)}) collective-permute-start(bf16[144,128]{1,0:T(8,128)(2,1)S(1)} %unpack.1.refs_0_.rows_ref.before_ref), channel_id=1, source_target_pairs={{0,8},{8,0},{16,24},{24,16},{32,40},{40,32},{48,56},{56,48},{64,72... | collective-permute-start | bytes 110600 | tf_op jit(solution)/shard_map/ppermute | solution.py:787
  31.5 20.4 %all-to-all-start.1 = ((bf16[8,120,128]{2,1,0:T(8,128)(2,1)}), bf16[8,120,128]{2,1,0:T(8,128)(2,1)S(1)}, u32[]{:S(2)}, u32[]{:S(2)}) async-start(bf16[8,120,128]{2,1,0:T(8,128)(2,1)} %product.2), calls=%async_computation.1 | async-start | bytes 491520 | tf_op jit(solution)/shard_map/all_to_all | solution.py:789
  40.8 5.4 %collective-permute-start.8 = (f32[8,128]{1,0:T(8,128)S(1)}, f32[8,128]{1,0:T(8,128)S(1)}, u32[]{:S(2)}, u32[]{:S(2)}) collective-permute-start(f32[8,128]{1,0:T(8,128)S(1)} %get-tuple-element.36), channel_id=1, source_target_pairs={{0,8},{8,16},{16,24},{24,32},{32,40},{40,48},{48,56},{56,64},{64,7... | collective-permute-start | bytes 12296 | tf_op jit(solution)/shard_map/ppermute | solution.py:806
  40.9 5.3 %collective-permute-start.9 = (f32[8,128]{1,0:T(8,128)S(1)}, f32[8,128]{1,0:T(8,128)S(1)}, u32[]{:S(2)}, u32[]{:S(2)}) collective-permute-start(f32[8,128]{1,0:T(8,128)S(1)} %get-tuple-element.37), channel_id=1, source_target_pairs={{0,248},{8,0},{16,8},{24,16},{32,24},{40,32},{48,40},{56,48},{64,5... | collective-permute-start | bytes 12296 | tf_op jit(solution)/shard_map/ppermute | solution.py:807
  65.9 10.3 %copy-start.1 = (bf16[8,192,128]{2,1,0:T(8,128)(2,1)}, bf16[8,192,128]{2,1,0:T(8,128)(2,1)S(1)}, u32[]{:S(2)}) copy-start(bf16[8,192,128]{2,1,0:T(8,128)(2,1)S(1)} %all_to_all.25.recv_ref.wind_recv_ref) | copy-start | bytes 1179652
  67.0 3.7 %collective-permute-start.12 = (bf16[144,128]{1,0:T(8,128)(2,1)S(1)}, bf16[144,128]{1,0:T(8,128)(2,1)S(1)}, u32[]{:S(2)}, u32[]{:S(2)}) collective-permute-start(bf16[144,128]{1,0:T(8,128)(2,1)S(1)} %rows.1.refs_0_), channel_id=1, source_target_pairs={{0,136},{8,128},{16,152},{24,144},{32,168},{40,160},{48,184},{56,1... | collective-permute-start | bytes 110600 | tf_op jit(solution)/shard_map/ppermute | solution.py:787
  67.2 4.2 %collective-permute-start.11 = (bf16[144,128]{1,0:T(8,128)(2,1)S(1)}, bf16[144,128]{1,0:T(8,128)(2,1)S(1)}, u32[]{:S(2)}, u32[]{:S(2)}) collective-permute-start(bf16[144,128]{1,0:T(8,128)(2,1)S(1)} %rows.1.refs_0_), channel_id=1, source_target_pairs={{0,128},{8,136},{16,144},{24,152},{32,160},{40,168},{48,176},{56,1... | collective-permute-start | bytes 110600 | tf_op jit(solution)/shard_map/ppermute | solution.py:787
  69.1 2.3 %collective-permute-start.10 = (bf16[144,128]{1,0:T(8,128)(2,1)S(1)}, bf16[144,128]{1,0:T(8,128)(2,1)S(1)}, u32[]{:S(2)}, u32[]{:S(2)}) collective-permute-start(bf16[144,128]{1,0:T(8,128)(2,1)S(1)} %rows.1.refs_0_), channel_id=1, source_target_pairs={{0,8},{8,0},{16,24},{24,16},{32,40},{40,32},{48,56},{56,48},{64,72... | collective-permute-start | bytes 110600 | tf_op jit(solution)/shard_map/ppermute | solution.py:787
  72.6 16.0 %copy-start.9 = (s32[34]{0:T(128)S(1)}, s32[34]{0:T(128)}, u32[]{:S(2)}) copy-start(s32[34]{0:T(128)} %copy-done.8) | copy-start | bytes 412
  72.6 16.0 %all-to-all-start.3 = ((bf16[8,120,128]{2,1,0:T(8,128)(2,1)}), bf16[8,120,128]{2,1,0:T(8,128)(2,1)S(1)}, u32[]{:S(2)}, u32[]{:S(2)}) async-start(bf16[8,120,128]{2,1,0:T(8,128)(2,1)} %product.3), calls=%async_computation.3 | async-start | bytes 491520 | tf_op jit(solution)/shard_map/all_to_all | solution.py:789
  88.6 0.8 copy-start.7
  90.8 14.0 %all-to-all-start.4 = ((bf16[8,192,128]{2,1,0:T(8,128)(2,1)}), bf16[8,192,128]{2,1,0:T(8,128)(2,1)S(1)}, u32[]{:S(2)}, u32[]{:S(2)}) async-start(bf16[8,192,128]{2,1,0:T(8,128)(2,1)} %total.3.message_hbm), calls=%async_computation.4 | async-start | bytes 786432 | tf_op jit(solution)/shard_map/all_to_all | solution.py:783
  94.3 6.3 %collective-permute-start.13 = (bf16[160,128]{1,0:T(8,128)(2,1)}, bf16[160,128]{1,0:T(8,128)(2,1)S(1)}, u32[]{:S(2)}, u32[]{:S(2)}) collective-permute-start(bf16[160,128]{1,0:T(8,128)(2,1)} %get-tuple-element.45), channel_id=1, source_target_pairs={{0,8},{8,16},{16,24},{24,32},{32,40},{40,48},{48,56},{56,64},{64,7... | collective-permute-start | bytes 122888 | tf_op jit(solution)/shard_map/ppermute | solution.py:813
  94.4 6.1 %collective-permute-start.14 = (bf16[160,128]{1,0:T(8,128)(2,1)}, bf16[160,128]{1,0:T(8,128)(2,1)S(1)}, u32[]{:S(2)}, u32[]{:S(2)}) collective-permute-start(bf16[160,128]{1,0:T(8,128)(2,1)} %get-tuple-element.46), channel_id=1, source_target_pairs={{0,248},{8,0},{16,8},{24,16},{32,24},{40,32},{48,40},{56,48},{64,5... | collective-permute-start | bytes 122888 | tf_op jit(solution)/shard_map/ppermute | solution.py:814
  98.2 1.5 %copy-start.3 = (bf16[45,160,128]{2,1,0:T(8,128)(2,1)S(1)}, bf16[45,160,128]{2,1,0:T(8,128)(2,1)}, u32[]{:S(2)}) copy-start(bf16[45,160,128]{2,1,0:T(8,128)(2,1)} %get-tuple-element.40.cells_hbm) | copy-start | bytes 5529604
  99.7 5.1 %copy-start = (bf16[45,64,128]{2,1,0:T(8,128)(2,1)S(1)}, bf16[45,64,128]{2,1,0:T(8,128)(2,1)}, u32[]{:S(2)}) copy-start(bf16[45,64,128]{2,1,0:T(8,128)(2,1)} %winds_ref.1) | copy-start | bytes 2211844
  99.7 5.1 %copy-start.2 = (bf16[8,192,128]{2,1,0:T(8,128)(2,1)S(1)}, bf16[8,192,128]{2,1,0:T(8,128)(2,1)}, u32[]{:S(2)}) copy-start(bf16[8,192,128]{2,1,0:T(8,128)(2,1)} %copy-done.1) | copy-start | bytes 1179652
  99.7 5.1 %copy-start.5 = (bf16[192,128]{1,0:T(8,128)(2,1)S(1)}, bf16[192,128]{1,0:T(8,128)(2,1)}, u32[]{:S(2)}) copy-start(bf16[192,128]{1,0:T(8,128)(2,1)} %copy-done.4) | copy-start | bytes 147460

commit v7 on v6

--- a/solution.py
+++ b/solution.py
@@ -202,10 +202,10 @@
 
     for at in range(2):
         k = 3 * BLOCKS + at
-        edges_ref[at, :ROWS, :] = picked(main_ref, k).astype(BF16)
+        edges_ref[at][:ROWS, :] = picked(main_ref, k).astype(BF16)
         rest = picked(rest_ref, k)
         rest = folded(keep(rest, 0), LEV) + folded(keep(rest, 2 * LEV), LEV)
-        edges_ref[at, ROWS:, :] = rest.astype(BF16)
+        edges_ref[at][ROWS:, :] = rest.astype(BF16)
 
 
 def clear(*refs):
@@ -231,7 +231,7 @@
 
 
 def pick_kernel(
-    band_ref, row_ref, cells_hbm, winds_hbm, send_hbm, edges_ref, east_ref, west_ref,
+    band_ref, row_ref, cells_hbm, winds_hbm, send_hbm, south_ref, north_ref, east_ref, west_ref,
     main_ref, rest_ref, cells_ref, winds_ref, send_ref, cells_sem, winds_sem, send_sem,
 ):
     meta_ref = Scalars(lax.axis_index("lat").astype(jnp.int32), band_ref, row_ref)
@@ -263,7 +263,7 @@
     east_ref[COLS:, :] = winds_ref[XS - 1, :LEV, :]
     west_ref[...] = cells_ref[0]
     leaving = [pltpu.make_async_copy(send_ref.at[d], send_hbm.at[d], send_sem.at[d]) for d in range(BANDS)]
-    pack_messages(meta_ref, main_ref, rest_ref, send_ref, edges_ref, leaving)
+    pack_messages(meta_ref, main_ref, rest_ref, send_ref, (south_ref, north_ref), leaving)
     for copy in leaving:
         copy.wait()
 
@@ -277,12 +277,13 @@
         pick_kernel,
         out_shape=(
             shape((BANDS, WIRE, LANES), BF16),
-            shape((2, HALO, LANES), BF16),
+            shape((HALO, LANES), BF16),
+            shape((HALO, LANES), BF16),
             shape((COLS + LEV, LANES), BF16),
             shape((COLS, LANES), BF16),
         ),
         in_specs=[SM, SM, HB, HB],
-        out_specs=(HB, VM, VM, VM),
+        out_specs=(HB, VM, VM, VM, VM),
         scratch_shapes=[
             PICKED,
             PICKED,
@@ -409,7 +410,27 @@
     )(*rows, *ops)
 
 
-def total_kernel(meta_ref, recv_ref, edges_hbm, out_ref, edges_ref, sem_ref):
+def total_kernel(recv_ref, out_ref):
+    total = recv_ref[0].astype(F32)
+    for s in range(1, TARGETS):
+        total = total + recv_ref[s].astype(F32)
+    total = total.astype(BF16)
+    for d in range(BANDS):
+        out_ref[d] = total
+
+
+def totals(recv):
+    return pl.pallas_call(
+        total_kernel,
+        out_shape=shape((BANDS, PACK, LANES), BF16),
+        in_specs=[VM],
+        out_specs=VM,
+        compiler_params=params(4),
+        name="total",
+    )(recv)
+
+
+def total_with_edges_kernel(meta_ref, recv_ref, edges_hbm, out_ref, edges_ref, sem_ref):
     arriving = pltpu.make_async_copy(edges_hbm, edges_ref, sem_ref.at[0])
     arriving.start()
     total = recv_ref[0].astype(F32)
@@ -425,15 +446,15 @@
         out_ref[d, PACK:, :] = jnp.where(d == me - 1, edges_ref[0], edge)
 
 
-def totals(meta, recv, edges):
-    return pl.pallas_call(
-        total_kernel,
+def totals_with_edges(meta, recv, edges):
+    return pl.pallas_call(
+        total_with_edges_kernel,
         out_shape=shape((BANDS, PACK + HALO, LANES), BF16),
         in_specs=[SM, VM, HB],
         out_specs=VM,
         scratch_shapes=[pltpu.VMEM((2, HALO, LANES), BF16), DMA((1,))],
         compiler_params=params(4),
-        name="total",
+        name="edged",
     )(meta, recv, edges)
 
 
@@ -443,10 +464,14 @@
     for near, there in ((me - 1, me > 0), (me + 1, me < BANDS - 1)):
         source = jnp.clip(near, 0, BANDS - 1)
         main = recv_ref[source, PACK : PACK + ROWS, :].astype(F32)
-        rest = recv_ref[source, PACK + ROWS :, :].astype(F32)
-        found = (main, unfolded(rest, 0, LEV, LEV), unfolded(rest, 2 * LEV, LEV, LEV))
-        halos.append([jnp.where(there, value, 0.0) for value in found])
-    return halos[0][:2], halos[1][:2], halos[0][2]
+        rest = unfolded(recv_ref[source, PACK + ROWS :, :].astype(F32), 0, LEV, LEV)
+        halos.append([jnp.where(there, value, 0.0) for value in (main, rest)])
+    return halos
+
+
+def halo_row(edge_ref):
+    rest = edge_ref[ROWS:, :].astype(F32)
+    return edge_ref[:ROWS, :].astype(F32), unfolded(rest, 0, LEV, LEV), unfolded(rest, 2 * LEV, LEV, LEV)
 
 
 def stage_blocks(recv_ref, main_ref, rest_ref):
@@ -476,11 +501,10 @@
 TALL = COLS + LEV
 
 
-def stage_corrections(meta_ref, recv_ref, wind_recv_ref, main_ref, rest_ref, tall_ref):
+def stage_corrections(meta_ref, recv_ref, halos, wind_ref, main_ref, rest_ref, tall_ref):
     clear(main_ref, rest_ref)
     me = meta_ref[0]
-    halos = halo_rows(meta_ref, recv_ref)
-    sums = [list(halos[0]), list(halos[1])]
+    sums = [list(halo) for halo in halos]
     for source in range(BANDS):
         packed = recv_ref[source, 2 * ROWS : PACK, :].astype(F32)
         for b in range(2):
@@ -496,7 +520,7 @@
     for at in range(2):
         main_ref[pl.ds(16 + at, ROWS, stride=KEPT), :] = sums[at][0].astype(BF16).astype(F32)
         rest_ref[pl.ds(16 + at, ROWS, stride=KEPT), :] = sums[at][1].astype(BF16).astype(F32)
-    wind = halo_rows(meta_ref, wind_recv_ref)[2]
+    wind = halo_row(wind_ref)[2]
     rest_ref[pl.ds(18, ROWS, stride=KEPT), :] = pltpu.roll(wind, LEV, axis=1)
     for t in range(ROWS // GROUP):
         span = slice(t * LANES, (t + 1) * LANES)
@@ -648,7 +672,7 @@
 
 
 def first_kernel(
-    meta_ref, cells_hbm, winds_hbm, west_ref, east_ref, recv_ref,
+    meta_ref, cells_hbm, winds_hbm, west_ref, east_ref, recv_ref, south_ref, north_ref,
     out_hbm, edges_ref, to_east_hbm, to_west_hbm,
     main_ref, rest_ref, tall_ref, placed_ref, smooth_ref, out_ref, out_sem, rim_sem,
     cells_ref, cells_sem, winds_ref, winds_sem,
@@ -656,7 +680,8 @@
     arriving = copies(cells_hbm, cells_ref, cells_sem) + copies(winds_hbm, winds_ref, winds_sem)
     for copy in arriving:
         copy.start()
-    stage_corrections(meta_ref, recv_ref, recv_ref, main_ref, rest_ref, tall_ref)
+    halos = [halo_row(ref)[:2] for ref in (south_ref, north_ref)]
+    stage_corrections(meta_ref, recv_ref, halos, south_ref, main_ref, rest_ref, tall_ref)
     for copy in arriving:
         copy.wait()
 
@@ -705,7 +730,7 @@
             shape((COLS, LANES), BF16),
             shape((COLS, LANES), BF16),
         ),
-        in_specs=[SM, HB, HB] + [VM] * 3,
+        in_specs=[SM, HB, HB] + [VM] * 5,
         out_specs=(HB, VM, HB, HB),
         scratch_shapes=SCRATCH
         + [
@@ -723,10 +748,10 @@
 
 
 def last_kernel(
-    meta_ref, cells_ref, winds_ref, west_ref, east_ref, recv_ref, wind_recv_ref, wind_west_ref,
+    meta_ref, cells_ref, winds_ref, west_ref, east_ref, recv_ref, wind_ref, wind_west_ref,
     out_hbm, main_ref, rest_ref, tall_ref, placed_ref, smooth_ref, out_ref, out_sem,
 ):
-    stage_corrections(meta_ref, recv_ref, wind_recv_ref, main_ref, rest_ref, tall_ref)
+    stage_corrections(meta_ref, recv_ref, halo_rows(meta_ref, recv_ref), wind_ref, main_ref, rest_ref, tall_ref)
 
     def emit(x, made):
         for v in range(VAR):
@@ -774,6 +799,8 @@
 
 
 TEAMMATES = [[(i, i ^ (16 * (other // 2) + other % 2)) for i in range(LON_DEV)] for other in range(1, TEAM)]
+SOUTHWARD = [(i + 1, i) for i in range(BANDS - 1)]
+NORTHWARD = [(i, i + 1) for i in range(BANDS - 1)]
 EASTWARD = [(i, (i + 1) % LON_DEV) for i in range(LON_DEV)]
 WESTWARD = [(i, (i - 1) % LON_DEV) for i in range(LON_DEV)]
 ALONG_Z = [[16 * (place // 2) + 2 * t + place % 2 for t in range(TARGETS)] for place in range(TEAM)]
@@ -796,25 +823,29 @@
     meta = jnp.concatenate([me, place, block_band, block_row])
     made = prepare_operators(meta, jnp.pad(filter_ops, ((0, 0), (1, 2), (0, 0))))
     ops = [made[0]] + [lax.ppermute(part, "lon", mates) for part, mates in zip(made[1:], TEAMMATES)]
-    send, edges, to_east, to_west = pick_rows(block_band, block_row, cotangent, winds)
+    send, to_south, to_north, to_east, to_west = pick_rows(block_band, block_row, cotangent, winds)
     west = lax.ppermute(to_east, "lon", EASTWARD)
     east = lax.ppermute(to_west, "lon", WESTWARD)
-    recv, west, east = lax.optimization_barrier((by_lat(send), west, east))
+    recv, west, east, to_south, to_north = lax.optimization_barrier((by_lat(send), west, east, to_south, to_north))
     rows = unpack_rows(recv)
     swapped = filtered(rows, ops)
     context, row_east, row_west = unpack_context(meta, recv, rows)
     row_from_west = lax.ppermute(row_east, "lon", EASTWARD)
     row_from_east = lax.ppermute(row_west, "lon", WESTWARD)
-    swapped, row_from_west, row_from_east = lax.optimization_barrier((swapped, row_from_west, row_from_east))
-    given = by_lat(totals(meta, swapped, edges))
+    south = lax.ppermute(to_north, "lat", NORTHWARD)
+    north = lax.ppermute(to_south, "lat", SOUTHWARD)
+    swapped, row_from_west, row_from_east, south, north = lax.optimization_barrier(
+        (swapped, row_from_west, row_from_east, south, north)
+    )
+    given = by_lat(totals(swapped))
     rows = next_rows(meta, rows, context, row_from_west, row_from_east, given)
     swapped = filtered(rows, ops)
-    state, edges, to_east, to_west = first_substep(meta, cotangent, winds, west, east, given)
+    state, edges, to_east, to_west = first_substep(meta, cotangent, winds, west, east, given, south, north)
+    message = totals_with_edges(meta, swapped, edges)
+    given2 = by_lat(message)
     west2 = lax.ppermute(to_east, "lon", EASTWARD)
     east2 = lax.ppermute(to_west, "lon", WESTWARD)
-    message = totals(meta, swapped, edges)
-    given2 = by_lat(message)
-    return last_substep(meta, bring_back(state, message), winds, west2, east2, given2, given, west)
+    return last_substep(meta, bring_back(state, message), winds, west2, east2, given2, south, west)
 
 
 def solution(mesh):

time: 111 us -> 112 us (level)
  starting transfers between devices: 41.2 us -> 48.1 us
  waiting for transfers between devices: 24.2 us -> 18.1 us
  blocking collectives: 13.3 us -> 14.6 us
    all_to_all x2, waiting for transfers between devices: 10.5 us -> 5.84 us  [filtered(): lax.all_to_all(partial, 'lon', 0, 0, tiled=True, axis_index_groups=ALONG_Z)]
    ppermute x0 -> x2, starting transfers between devices: none -> 4.26 us  [the longest x1 2.97 us: shards(): south = lax.ppermute(to_north, 'lat', NORTHWARD)]
    all_to_all x2, starting transfers between devices: 12 us -> 14.9 us  [filtered(): lax.all_to_all(partial, 'lon', 0, 0, tiled=True, axis_index_groups=ALONG_Z)]
    all_to_all x2, waiting for transfers between devices: 6.53 us -> 5.16 us  [by_lat(): return lax.all_to_all(messages, 'lat', 0, 0, tiled=True)]
    all_to_all x1, blocking collectives: 13.3 us -> 14.6 us  [by_lat(): return lax.all_to_all(messages, 'lat', 0, 0, tiled=True)]
    unnamed x33 -> x39, local copies, waits for them, and re-layouts: 2.36 us -> 2.37 us
  transfers between devices with their start and end apart: 19 -> 21, of which waited for: 11 -> 11; matrix products, arithmetic and copies ran while one was open for 0% -> 0% of each run, Pallas kernels for 10% -> 9%
where the time goes in v7:
time: 112 us
  starting transfers between devices  48.1 us (43%)
  Pallas kernels  27.9 us (25%)
  waiting for transfers between devices  18.1 us (16%)
  blocking collectives  14.6 us (13%)
  local copies, waits for them, and re-layouts  2.45 us (2%)
    all_to_all x2, starting transfers between devices, filtered(): lax.all_to_all(partial, 'lon', 0, 0, tiled=True, axis_index_groups=ALONG_Z)  14.9 us
    all_to_all x1, blocking collectives, by_lat(): return lax.all_to_all(messages, 'lat', 0, 0, tiled=True)  14.6 us
    all_to_all x2, starting transfers between devices, by_lat(): return lax.all_to_all(messages, 'lat', 0, 0, tiled=True)  9.42 us
    pallas_call x1, Pallas kernels, first_substep(): pl.pallas_call(first_kernel, out_shape=(shape((XS, COLS, LANES), BF16), s...  7.45 us
    pallas_call x1, Pallas kernels, pick_rows(): pl.pallas_call(pick_kernel, out_shape=(shape((BANDS, WIRE, LANES), BF16),...  7.21 us
    ppermute x1, starting transfers between devices, shards(): east = lax.ppermute(to_west, 'lon', WESTWARD)  6.41 us
    all_to_all x2, waiting for transfers between devices, filtered(): lax.all_to_all(partial, 'lon', 0, 0, tiled=True, axis_index_groups=ALONG_Z)  5.84 us
    pallas_call x1, Pallas kernels, last_substep(): pl.pallas_call(last_kernel, out_shape=shape((XS, COLS, LANES), F32), in_s...  5.31 us
  transfers between devices with their start and end apart: 21, of which 11 were waited for; matrix products, arithmetic and copies ran while one was open for 0% of the time, Pallas kernels for 9%

profile of v7, /device:TPU:2, one launch (start us, length us, event | category | flops | bytes accessed | tf_op | source)
XLA Modules:
  0.0 111.6 jit_solution(1833270609714541180)
XLA Ops:
  0.0 7.2 %pick.1 = (bf16[8,312,128]{2,1,0:T(8,128)(2,1)}, bf16[72,128]{1,0:T(8,128)(2,1)}, bf16[72,128]{1,0:T(8,128)(2,1)}, bf16[192,128]{1,0:T(8,128)(2,1)}, bf16[160,128]{1,0:T(8,128)(2,1)}) custom-call(s32[16]{0:T(128)} %band_ref.1, s32[16]{0:T(128)} %row_ref.1, bf16[45,160,128]{2,1,0:T(8,128)(2,1)} %cells_hbm.3, bf16[45,64,128]{2,1,0:T(8,128)(2,1)} %winds_ref.1), custom_call_target="tpu_custom_call" | custom-call | tf_op jit(solution)/shard_map/pick/pallas_call | solution.py:276
  7.2 0.0 copy-start.14
  7.3 6.0 %all-to-all-start = ((bf16[8,312,128]{2,1,0:T(8,128)(2,1)}), bf16[8,312,128]{2,1,0:T(8,128)(2,1)S(1)}, u32[]{:S(2)}, u32[]{:S(2)}) async-start(bf16[8,312,128]{2,1,0:T(8,128)(2,1)} %get-tuple-element.31), calls=%async_computation | async-start | bytes 1277952 | tf_op jit(solution)/shard_map/all_to_all | solution.py:810
  13.3 0.1 pad.4.ops_ref
  13.4 0.1 pad_add_fusion.meta_ref
  13.5 1.2 %operators.1 = (bf16[384,96]{1,0:T(8,128)(2,1)S(1)}, bf16[384,96]{1,0:T(8,128)(2,1)S(1)}, bf16[384,96]{1,0:T(8,128)(2,1)S(1)}, bf16[384,96]{1,0:T(8,128)(2,1)S(1)}) custom-call(s32[34]{0:T(128)S(1)} %pad_add_fusion.meta_ref, bf16[2,48,1440]{2,1,0:T(8,128)(2,1)S(1)} %pad.4.ops_ref), custom_call_target="tpu_custom_call" | custom-call | tf_op jit(solution)/shard_map/operators/pallas_call | solution.py:97
  14.7 0.1 collective-permute-start.5
  14.8 0.5 collective-permute-start
  15.3 6.4 %collective-permute-start.1 = (bf16[160,128]{1,0:T(8,128)(2,1)S(1)}, bf16[160,128]{1,0:T(8,128)(2,1)S(1)}, u32[]{:S(2)}, u32[]{:S(2)}) collective-permute-start(bf16[160,128]{1,0:T(8,128)(2,1)S(1)} %copy-done.16), channel_id=1, source_target_pairs={{0,248},{8,0},{16,8},{24,16},{32,24},{40,32},{48,40},{56,48},{64,5... | collective-permute-start | bytes 122888 | tf_op jit(solution)/shard_map/ppermute | solution.py:828
  21.7 0.6 collective-permute-start.6
  22.3 1.1 collective-permute-done.1.east_ref
  23.4 0.1 collective-permute-done.west_ref.wind_west_ref
  23.5 2.3 %all-to-all-done.recv_ref = bf16[8,312,128]{2,1,0:T(8,128)(2,1)S(1)} async-done(((bf16[8,312,128]{2,1,0:T(8,128)(2,1)}), bf16[8,312,128]{2,1,0:T(8,128)(2,1)S(1)}, u32[]{:S(2)}, u32[]{:S(2)}) %all-to-all-start) | async-done | bytes 639008 | tf_op jit(solution)/shard_map/all_to_all | solution.py:810
  25.8 0.1 collective-permute-start.4
  25.9 1.5 %collective-permute-start.3 = (bf16[144,128]{1,0:T(8,128)(2,1)S(1)}, bf16[144,128]{1,0:T(8,128)(2,1)S(1)}, u32[]{:S(2)}, u32[]{:S(2)}) collective-permute-start(bf16[144,128]{1,0:T(8,128)(2,1)S(1)} %unpack.1.refs_0_.rows_ref.before_ref), channel_id=1, source_target_pairs={{0,128},{8,136},{16,144},{24,152},{32,160},{40,168},{48,176},{56,1... | collective-permute-start | bytes 110600 | tf_op jit(solution)/shard_map/ppermute | solution.py:814
  27.5 0.3 collective-permute-start.2
  27.8 1.9 %collective-permute-done.4.refs_3_ = bf16[144,128]{1,0:T(8,128)(2,1)S(1)} collective-permute-done((bf16[144,128]{1,0:T(8,128)(2,1)S(1)}, bf16[144,128]{1,0:T(8,128)(2,1)S(1)}, u32[]{:S(2)}, u32[]{:S(2)}) %collective-permute-start.4) | collective-permute-done | bytes 36896 | tf_op jit(solution)/shard_map/ppermute | solution.py:814
  29.7 0.4 collective-permute-done.3.refs_2_
  30.1 1.2 %product.2 = bf16[8,120,128]{2,1,0:T(8,128)(2,1)} custom-call(bf16[144,128]{1,0:T(8,128)(2,1)S(1)} %unpack.1.refs_0_.rows_ref.before_ref, bf16[144,128]{1,0:T(8,128)(2,1)S(1)} %collective-permute-done.2.refs_1_, bf16[144,128]{1,0:T(8,128)(2,1)S(1)} %collective-permute-done.3.refs_2_, bf16[144,128]{1,0:T(8,128)(2,1)S(1)} %collective-permute-done.4.refs_3_, ...), custom_call_target="tpu_custom_call" | custom-call | tf_op jit(solution)/shard_map/product/pallas_call | solution.py:403
  31.3 8.5 %all-to-all-start.1 = ((bf16[8,120,128]{2,1,0:T(8,128)(2,1)}), bf16[8,120,128]{2,1,0:T(8,128)(2,1)S(1)}, u32[]{:S(2)}, u32[]{:S(2)}) async-start(bf16[8,120,128]{2,1,0:T(8,128)(2,1)} %product.2), calls=%async_computation.1 | async-start | bytes 491520 | tf_op jit(solution)/shard_map/all_to_all | solution.py:816
  39.8 3.0 %collective-permute-start.10 = (bf16[72,128]{1,0:T(8,128)(2,1)S(1)}, bf16[72,128]{1,0:T(8,128)(2,1)S(1)}, u32[]{:S(2)}, u32[]{:S(2)}) collective-permute-start(bf16[72,128]{1,0:T(8,128)(2,1)S(1)} %copy-done.18), channel_id=1, source_target_pairs={{0,1},{1,2},{2,3},{3,4},{4,5},{5,6},{6,7},{8,9},{9,10},{10,11},{11... | collective-permute-start | bytes 55304 | tf_op jit(solution)/shard_map/ppermute | solution.py:835
  42.8 1.3 %collective-permute-start.11 = (bf16[72,128]{1,0:T(8,128)(2,1)S(1)}, bf16[72,128]{1,0:T(8,128)(2,1)S(1)}, u32[]{:S(2)}, u32[]{:S(2)}) collective-permute-start(bf16[72,128]{1,0:T(8,128)(2,1)S(1)} %copy-done.17), channel_id=1, source_target_pairs={{1,0},{2,1},{3,2},{4,3},{5,4},{6,5},{7,6},{9,8},{10,9},{11,10},{12... | collective-permute-start | bytes 55304 | tf_op jit(solution)/shard_map/ppermute | solution.py:836
  44.1 0.9 context.1
  44.9 0.1 collective-permute-start.8
  45.0 3.8 %collective-permute-start.9 = (f32[8,128]{1,0:T(8,128)S(1)}, f32[8,128]{1,0:T(8,128)S(1)}, u32[]{:S(2)}, u32[]{:S(2)}) collective-permute-start(f32[8,128]{1,0:T(8,128)S(1)} %get-tuple-element.44), channel_id=1, source_target_pairs={{0,248},{8,0},{16,8},{24,16},{32,24},{40,32},{48,40},{56,48},{64,5... | collective-permute-start | bytes 12296 | tf_op jit(solution)/shard_map/ppermute | solution.py:834
  48.9 1.3 %collective-permute-done.8.west_ref = f32[8,128]{1,0:T(8,128)S(1)} collective-permute-done((f32[8,128]{1,0:T(8,128)S(1)}, f32[8,128]{1,0:T(8,128)S(1)}, u32[]{:S(2)}, u32[]{:S(2)}) %collective-permute-start.8) | collective-permute-done | bytes 4128 | tf_op jit(solution)/shard_map/ppermute | solution.py:833
  50.2 0.0 collective-permute-done.9.east_ref
  50.2 1.5 %all-to-all-done.1.recv_ref = bf16[8,120,128]{2,1,0:T(8,128)(2,1)S(1)} async-done(((bf16[8,120,128]{2,1,0:T(8,128)(2,1)}), bf16[8,120,128]{2,1,0:T(8,128)(2,1)S(1)}, u32[]{:S(2)}, u32[]{:S(2)}) %all-to-all-start.1) | async-done | bytes 245792 | tf_op jit(solution)/shard_map/all_to_all | solution.py:816
  51.7 14.6 %all_to_all.25.recv_ref = bf16[8,120,128]{2,1,0:T(8,128)(2,1)S(1)} all-to-all(bf16[8,120,128]{2,1,0:T(8,128)(2,1)S(1)} %total.1), channel_id=1, replica_groups=mesh['lon'=32,'lat'=8] {'lat'}, dimensions={0} | all-to-all | bytes 491520 | tf_op jit(solution)/shard_map/all_to_all | solution.py:810
  66.3 1.0 rows.1.refs_0_
  67.4 0.3 collective-permute-start.14
  67.7 1.6 %collective-permute-start.13 = (bf16[144,128]{1,0:T(8,128)(2,1)S(1)}, bf16[144,128]{1,0:T(8,128)(2,1)S(1)}, u32[]{:S(2)}, u32[]{:S(2)}) collective-permute-start(bf16[144,128]{1,0:T(8,128)(2,1)S(1)} %rows.1.refs_0_), channel_id=1, source_target_pairs={{0,128},{8,136},{16,144},{24,152},{32,160},{40,168},{48,176},{56,1... | collective-permute-start | bytes 110600 | tf_op jit(solution)/shard_map/ppermute | solution.py:814
  69.3 0.2 collective-permute-start.12
  69.5 1.8 %collective-permute-done.14.refs_3_ = bf16[144,128]{1,0:T(8,128)(2,1)S(1)} collective-permute-done((bf16[144,128]{1,0:T(8,128)(2,1)S(1)}, bf16[144,128]{1,0:T(8,128)(2,1)S(1)}, u32[]{:S(2)}, u32[]{:S(2)}) %collective-permute-start.14) | collective-permute-done | bytes 36896 | tf_op jit(solution)/shard_map/ppermute | solution.py:814
  71.3 0.5 collective-permute-done.13.refs_2_
  71.8 1.2 %product.3 = bf16[8,120,128]{2,1,0:T(8,128)(2,1)} custom-call(bf16[144,128]{1,0:T(8,128)(2,1)S(1)} %rows.1.refs_0_, bf16[144,128]{1,0:T(8,128)(2,1)S(1)} %collective-permute-done.12.refs_1_, bf16[144,128]{1,0:T(8,128)(2,1)S(1)} %collective-permute-done.13.refs_2_, bf16[144,128]{1,0:T(8,128)(2,1)S(1)} %collective-permute-done.14.refs_3_, ...), custom_call_target="tpu_custom_call" | custom-call | tf_op jit(solution)/shard_map/product/pallas_call | solution.py:403
  73.1 6.4 %all-to-all-start.3 = ((bf16[8,120,128]{2,1,0:T(8,128)(2,1)}), bf16[8,120,128]{2,1,0:T(8,128)(2,1)S(1)}, u32[]{:S(2)}, u32[]{:S(2)}) async-start(bf16[8,120,128]{2,1,0:T(8,128)(2,1)} %product.3), calls=%async_computation.3 | async-start | bytes 491520 | tf_op jit(solution)/shard_map/all_to_all | solution.py:816
  79.5 7.4 %first.1 = (bf16[45,160,128]{2,1,0:T(8,128)(2,1)}, bf16[2,72,128]{2,1,0:T(8,128)(2,1)}, bf16[160,128]{1,0:T(8,128)(2,1)}, bf16[160,128]{1,0:T(8,128)(2,1)}) custom-call(s32[34]{0:T(128)} %copy-done.8, bf16[45,160,128]{2,1,0:T(8,128)(2,1)} %cells_hbm.3, bf16[45,64,128]{2,1,0:T(8,128)(2,1)} %winds_ref.1, bf16[192,128]{1,0:T(8,128)(2,1)} %copy-done.3, ...), custom_call_target="tpu_custom_call" | custom-call | tf_op jit(solution)/shard_map/first/pallas_call | solution.py:725
  87.0 4.4 %all-to-all-done.3.recv_ref = bf16[8,120,128]{2,1,0:T(8,128)(2,1)S(1)} async-done(((bf16[8,120,128]{2,1,0:T(8,128)(2,1)}), bf16[8,120,128]{2,1,0:T(8,128)(2,1)S(1)}, u32[]{:S(2)}, u32[]{:S(2)}) %all-to-all-start.3) | async-done | bytes 245792 | tf_op jit(solution)/shard_map/all_to_all | solution.py:816
  91.3 0.8 copy-done.7
  92.1 1.4 %edged.1.message_hbm = bf16[8,192,128]{2,1,0:T(8,128)(2,1)} custom-call(s32[34]{0:T(128)S(1)} %copy-done.9, bf16[8,120,128]{2,1,0:T(8,128)(2,1)S(1)} %all-to-all-done.3.recv_ref, bf16[2,72,128]{2,1,0:T(8,128)(2,1)S(1)} %copy-done.7), custom_call_target="tpu_custom_call" | custom-call | tf_op jit(solution)/shard_map/edged/pallas_call | solution.py:450
  93.5 3.5 %all-to-all-start.4 = ((bf16[8,192,128]{2,1,0:T(8,128)(2,1)}), bf16[8,192,128]{2,1,0:T(8,128)(2,1)S(1)}, u32[]{:S(2)}, u32[]{:S(2)}) async-start(bf16[8,192,128]{2,1,0:T(8,128)(2,1)} %edged.1.message_hbm), calls=%async_computation.4 | async-start | bytes 786432 | tf_op jit(solution)/shard_map/all_to_all | solution.py:810
  97.0 0.1 collective-permute-start.15
  97.1 3.8 %collective-permute-start.16 = (bf16[160,128]{1,0:T(8,128)(2,1)}, bf16[160,128]{1,0:T(8,128)(2,1)S(1)}, u32[]{:S(2)}, u32[]{:S(2)}) collective-permute-start(bf16[160,128]{1,0:T(8,128)(2,1)} %get-tuple-element.56), channel_id=1, source_target_pairs={{0,248},{8,0},{16,8},{24,16},{32,24},{40,32},{48,40},{56,48},{64,5... | collective-permute-start | bytes 122888 | tf_op jit(solution)/shard_map/ppermute | solution.py:847
  100.9 1.5 %copy-done.2 = bf16[45,160,128]{2,1,0:T(8,128)(2,1)S(1)} copy-done((bf16[45,160,128]{2,1,0:T(8,128)(2,1)S(1)}, bf16[45,160,128]{2,1,0:T(8,128)(2,1)}, u32[]{:S(2)}) %copy-start.2) | copy-done | bytes 1843224
  102.4 0.8 stay.1.cells_ref
  103.3 2.9 %all-to-all-done.4.recv_ref = bf16[8,192,128]{2,1,0:T(8,128)(2,1)S(1)} async-done(((bf16[8,192,128]{2,1,0:T(8,128)(2,1)}), bf16[8,192,128]{2,1,0:T(8,128)(2,1)S(1)}, u32[]{:S(2)}, u32[]{:S(2)}) %all-to-all-start.4) | async-done | bytes 393248 | tf_op jit(solution)/shard_map/all_to_all | solution.py:810
  106.2 5.3 %last.1 = f32[45,160,128]{2,1,0:T(8,128)} custom-call(s32[34]{0:T(128)S(1)} %copy-done.9, bf16[45,160,128]{2,1,0:T(8,128)(2,1)S(1)} %stay.1.cells_ref, bf16[45,64,128]{2,1,0:T(8,128)(2,1)S(1)} %copy-done, bf16[160,128]{1,0:T(8,128)(2,1)S(1)} %collective-permute-done.15.west_ref, bf16[160,128]{1,0:T(8,128)(2,1)S(1)} %collective-permute-done.16.east_ref, ...), custom_call_target="tpu_custom_call" | custom-call | tf_op jit(solution)/shard_map/last/pallas_call | solution.py:770
  (48 shorter events, 0.2 us)
Async XLA Ops:
  0.0 13.2 %copy-start.10 = (bf16[2,45,1440]{2,0,1:T(2,128)(2,1)S(1)}, bf16[2,45,1440]{2,0,1:T(2,128)(2,1)}, u32[]{:S(2)}) copy-start(bf16[2,45,1440]{2,0,1:T(2,128)(2,1)} %param.7) | copy-start | bytes 777604
  7.2 6.2 %copy-start.13 = (s32[16]{0:T(128)S(1)}, s32[16]{0:T(128)}, u32[]{:S(2)}) copy-start(s32[16]{0:T(128)} %row_ref.1) | copy-start | bytes 196
  7.2 6.2 %copy-start.14 = (s32[16]{0:T(128)S(1)}, s32[16]{0:T(128)}, u32[]{:S(2)}) copy-start(s32[16]{0:T(128)} %band_ref.1) | copy-start | bytes 196
  7.2 7.6 %copy-start.15 = (bf16[192,128]{1,0:T(8,128)(2,1)S(1)}, bf16[192,128]{1,0:T(8,128)(2,1)}, u32[]{:S(2)}) copy-start(bf16[192,128]{1,0:T(8,128)(2,1)} %get-tuple-element.32) | copy-start | bytes 147460
  7.3 8.1 %copy-start.16 = (bf16[160,128]{1,0:T(8,128)(2,1)S(1)}, bf16[160,128]{1,0:T(8,128)(2,1)}, u32[]{:S(2)}) copy-start(bf16[160,128]{1,0:T(8,128)(2,1)} %get-tuple-element.33) | copy-start | bytes 122884
  7.3 18.5 %all-to-all-start = ((bf16[8,312,128]{2,1,0:T(8,128)(2,1)}), bf16[8,312,128]{2,1,0:T(8,128)(2,1)S(1)}, u32[]{:S(2)}, u32[]{:S(2)}) async-start(bf16[8,312,128]{2,1,0:T(8,128)(2,1)} %get-tuple-element.31), calls=%async_computation | async-start | bytes 1277952 | tf_op jit(solution)/shard_map/all_to_all | solution.py:810
  13.2 26.6 %copy-start.18 = (bf16[72,128]{1,0:T(8,128)(2,1)S(1)}, bf16[72,128]{1,0:T(8,128)(2,1)}, u32[]{:S(2)}) copy-start(bf16[72,128]{1,0:T(8,128)(2,1)} %get-tuple-element.45) | copy-start | bytes 55300
  13.2 29.5 %copy-start.17 = (bf16[72,128]{1,0:T(8,128)(2,1)S(1)}, bf16[72,128]{1,0:T(8,128)(2,1)}, u32[]{:S(2)}) copy-start(bf16[72,128]{1,0:T(8,128)(2,1)} %get-tuple-element.46) | copy-start | bytes 55300
  13.5 52.8 %copy-start.8 = (s32[34]{0:T(128)}, s32[34]{0:T(128)S(1)}, u32[]{:S(2)}) copy-start(s32[34]{0:T(128)S(1)} %pad_add_fusion.meta_ref) | copy-start | bytes 412
  14.7 12.7 %collective-permute-start.5 = (bf16[384,96]{1,0:T(8,128)(2,1)S(1)}, bf16[384,96]{1,0:T(8,128)(2,1)S(1)}, u32[]{:S(2)}, u32[]{:S(2)}) collective-permute-start(bf16[384,96]{1,0:T(8,128)(2,1)S(1)} %get-tuple-element.40), channel_id=1, source_target_pairs={{0,8},{8,0},{16,24},{24,16},{32,40},{40,32},{48,56},{56,48},{64,72... | collective-permute-start | bytes 221192 | tf_op jit(solution)/shard_map/ppermute | solution.py:825
  14.8 8.7 %collective-permute-start = (bf16[192,128]{1,0:T(8,128)(2,1)S(1)}, bf16[192,128]{1,0:T(8,128)(2,1)S(1)}, u32[]{:S(2)}, u32[]{:S(2)}) collective-permute-start(bf16[192,128]{1,0:T(8,128)(2,1)S(1)} %copy-done.15), channel_id=1, source_target_pairs={{0,8},{8,16},{16,24},{24,32},{32,40},{40,48},{48,56},{56,64},{64,7... | collective-permute-start | bytes 147464 | tf_op jit(solution)/shard_map/ppermute | solution.py:827
  15.3 8.1 %collective-permute-start.1 = (bf16[160,128]{1,0:T(8,128)(2,1)S(1)}, bf16[160,128]{1,0:T(8,128)(2,1)S(1)}, u32[]{:S(2)}, u32[]{:S(2)}) collective-permute-start(bf16[160,128]{1,0:T(8,128)(2,1)S(1)} %copy-done.16), channel_id=1, source_target_pairs={{0,248},{8,0},{16,8},{24,16},{32,24},{40,32},{48,40},{56,48},{64,5... | collective-permute-start | bytes 122888 | tf_op jit(solution)/shard_map/ppermute | solution.py:828
  21.7 6.1 %collective-permute-start.6 = (bf16[384,96]{1,0:T(8,128)(2,1)S(1)}, bf16[384,96]{1,0:T(8,128)(2,1)S(1)}, u32[]{:S(2)}, u32[]{:S(2)}) collective-permute-start(bf16[384,96]{1,0:T(8,128)(2,1)S(1)} %get-tuple-element.41), channel_id=1, source_target_pairs={{0,128},{8,136},{16,144},{24,152},{32,160},{40,168},{48,176},{56,1... | collective-permute-start | bytes 221192 | tf_op jit(solution)/shard_map/ppermute | solution.py:825
  22.3 5.5 %collective-permute-start.7 = (bf16[384,96]{1,0:T(8,128)(2,1)S(1)}, bf16[384,96]{1,0:T(8,128)(2,1)S(1)}, u32[]{:S(2)}, u32[]{:S(2)}) collective-permute-start(bf16[384,96]{1,0:T(8,128)(2,1)S(1)} %get-tuple-element.42), channel_id=1, source_target_pairs={{0,136},{8,128},{16,152},{24,144},{32,168},{40,160},{48,184},{56,1... | collective-permute-start | bytes 221192 | tf_op jit(solution)/shard_map/ppermute | solution.py:825
  23.4 44.0 %copy-start.11 = (bf16[160,128]{1,0:T(8,128)(2,1)}, bf16[160,128]{1,0:T(8,128)(2,1)S(1)}, u32[]{:S(2)}) copy-start(bf16[160,128]{1,0:T(8,128)(2,1)S(1)} %collective-permute-done.1.east_ref) | copy-start | bytes 122884
  23.5 43.9 %copy-start.3 = (bf16[192,128]{1,0:T(8,128)(2,1)}, bf16[192,128]{1,0:T(8,128)(2,1)S(1)}, u32[]{:S(2)}) copy-start(bf16[192,128]{1,0:T(8,128)(2,1)S(1)} %collective-permute-done.west_ref.wind_west_ref) | copy-start | bytes 147460
  25.8 3.9 %collective-permute-start.4 = (bf16[144,128]{1,0:T(8,128)(2,1)S(1)}, bf16[144,128]{1,0:T(8,128)(2,1)S(1)}, u32[]{:S(2)}, u32[]{:S(2)}) collective-permute-start(bf16[144,128]{1,0:T(8,128)(2,1)S(1)} %unpack.1.refs_0_.rows_ref.before_ref), channel_id=1, source_target_pairs={{0,136},{8,128},{16,152},{24,144},{32,168},{40,160},{48,184},{56,1... | collective-permute-start | bytes 110600 | tf_op jit(solution)/shard_map/ppermute | solution.py:814
  25.9 4.1 %collective-permute-start.3 = (bf16[144,128]{1,0:T(8,128)(2,1)S(1)}, bf16[144,128]{1,0:T(8,128)(2,1)S(1)}, u32[]{:S(2)}, u32[]{:S(2)}) collective-permute-start(bf16[144,128]{1,0:T(8,128)(2,1)S(1)} %unpack.1.refs_0_.rows_ref.before_ref), channel_id=1, source_target_pairs={{0,128},{8,136},{16,144},{24,152},{32,160},{40,168},{48,176},{56,1... | collective-permute-start | bytes 110600 | tf_op jit(solution)/shard_map/ppermute | solution.py:814
  27.5 2.6 %collective-permute-start.2 = (bf16[144,128]{1,0:T(8,128)(2,1)S(1)}, bf16[144,128]{1,0:T(8,128)(2,1)S(1)}, u32[]{:S(2)}, u32[]{:S(2)}) collective-permute-start(bf16[144,128]{1,0:T(8,128)(2,1)S(1)} %unpack.1.refs_0_.rows_ref.before_ref), channel_id=1, source_target_pairs={{0,8},{8,0},{16,24},{24,16},{32,40},{40,32},{48,56},{56,48},{64,72... | collective-permute-start | bytes 110600 | tf_op jit(solution)/shard_map/ppermute | solution.py:814
  31.3 20.4 %all-to-all-start.1 = ((bf16[8,120,128]{2,1,0:T(8,128)(2,1)}), bf16[8,120,128]{2,1,0:T(8,128)(2,1)S(1)}, u32[]{:S(2)}, u32[]{:S(2)}) async-start(bf16[8,120,128]{2,1,0:T(8,128)(2,1)} %product.2), calls=%async_computation.1 | async-start | bytes 491520 | tf_op jit(solution)/shard_map/all_to_all | solution.py:816
  39.8 10.4 %collective-permute-start.10 = (bf16[72,128]{1,0:T(8,128)(2,1)S(1)}, bf16[72,128]{1,0:T(8,128)(2,1)S(1)}, u32[]{:S(2)}, u32[]{:S(2)}) collective-permute-start(bf16[72,128]{1,0:T(8,128)(2,1)S(1)} %copy-done.18), channel_id=1, source_target_pairs={{0,1},{1,2},{2,3},{3,4},{4,5},{5,6},{6,7},{8,9},{9,10},{10,11},{11... | collective-permute-start | bytes 55304 | tf_op jit(solution)/shard_map/ppermute | solution.py:835
  42.8 7.4 %collective-permute-start.11 = (bf16[72,128]{1,0:T(8,128)(2,1)S(1)}, bf16[72,128]{1,0:T(8,128)(2,1)S(1)}, u32[]{:S(2)}, u32[]{:S(2)}) collective-permute-start(bf16[72,128]{1,0:T(8,128)(2,1)S(1)} %copy-done.17), channel_id=1, source_target_pairs={{1,0},{2,1},{3,2},{4,3},{5,4},{6,5},{7,6},{9,8},{10,9},{11,10},{12... | collective-permute-start | bytes 55304 | tf_op jit(solution)/shard_map/ppermute | solution.py:836
  44.9 5.2 %collective-permute-start.8 = (f32[8,128]{1,0:T(8,128)S(1)}, f32[8,128]{1,0:T(8,128)S(1)}, u32[]{:S(2)}, u32[]{:S(2)}) collective-permute-start(f32[8,128]{1,0:T(8,128)S(1)} %get-tuple-element.43), channel_id=1, source_target_pairs={{0,8},{8,16},{16,24},{24,32},{32,40},{40,48},{48,56},{56,64},{64,7... | collective-permute-start | bytes 12296 | tf_op jit(solution)/shard_map/ppermute | solution.py:833
  45.0 5.2 %collective-permute-start.9 = (f32[8,128]{1,0:T(8,128)S(1)}, f32[8,128]{1,0:T(8,128)S(1)}, u32[]{:S(2)}, u32[]{:S(2)}) collective-permute-start(f32[8,128]{1,0:T(8,128)S(1)} %get-tuple-element.44), channel_id=1, source_target_pairs={{0,248},{8,0},{16,8},{24,16},{32,24},{40,32},{48,40},{56,48},{64,5... | collective-permute-start | bytes 12296 | tf_op jit(solution)/shard_map/ppermute | solution.py:834
  50.2 29.3 %copy-start.5 = (bf16[72,128]{1,0:T(8,128)(2,1)}, bf16[72,128]{1,0:T(8,128)(2,1)S(1)}, u32[]{:S(2)}) copy-start(bf16[72,128]{1,0:T(8,128)(2,1)S(1)} %collective-permute-done.10.south_ref.wind_ref) | copy-start | bytes 55300
  50.2 29.3 %copy-start.12 = (bf16[72,128]{1,0:T(8,128)(2,1)}, bf16[72,128]{1,0:T(8,128)(2,1)S(1)}, u32[]{:S(2)}) copy-start(bf16[72,128]{1,0:T(8,128)(2,1)S(1)} %collective-permute-done.11.north_ref) | copy-start | bytes 55300
  66.3 13.2 %copy-start.1 = (bf16[8,120,128]{2,1,0:T(8,128)(2,1)}, bf16[8,120,128]{2,1,0:T(8,128)(2,1)S(1)}, u32[]{:S(2)}) copy-start(bf16[8,120,128]{2,1,0:T(8,128)(2,1)S(1)} %all_to_all.25.recv_ref) | copy-start | bytes 737284
  67.4 4.0 %collective-permute-start.14 = (bf16[144,128]{1,0:T(8,128)(2,1)S(1)}, bf16[144,128]{1,0:T(8,128)(2,1)S(1)}, u32[]{:S(2)}, u32[]{:S(2)}) collective-permute-start(bf16[144,128]{1,0:T(8,128)(2,1)S(1)} %rows.1.refs_0_), channel_id=1, source_target_pairs={{0,136},{8,128},{16,152},{24,144},{32,168},{40,160},{48,184},{56,1... | collective-permute-start | bytes 110600 | tf_op jit(solution)/shard_map/ppermute | solution.py:814
  67.7 4.2 %collective-permute-start.13 = (bf16[144,128]{1,0:T(8,128)(2,1)S(1)}, bf16[144,128]{1,0:T(8,128)(2,1)S(1)}, u32[]{:S(2)}, u32[]{:S(2)}) collective-permute-start(bf16[144,128]{1,0:T(8,128)(2,1)S(1)} %rows.1.refs_0_), channel_id=1, source_target_pairs={{0,128},{8,136},{16,144},{24,152},{32,160},{40,168},{48,176},{56,1... | collective-permute-start | bytes 110600 | tf_op jit(solution)/shard_map/ppermute | solution.py:814
  69.3 2.6 %collective-permute-start.12 = (bf16[144,128]{1,0:T(8,128)(2,1)S(1)}, bf16[144,128]{1,0:T(8,128)(2,1)S(1)}, u32[]{:S(2)}, u32[]{:S(2)}) collective-permute-start(bf16[144,128]{1,0:T(8,128)(2,1)S(1)} %rows.1.refs_0_), channel_id=1, source_target_pairs={{0,8},{8,0},{16,24},{24,16},{32,40},{40,32},{48,56},{56,48},{64,72... | collective-permute-start | bytes 110600 | tf_op jit(solution)/shard_map/ppermute | solution.py:814
  73.1 18.2 %copy-start.9 = (s32[34]{0:T(128)S(1)}, s32[34]{0:T(128)}, u32[]{:S(2)}) copy-start(s32[34]{0:T(128)} %copy-done.8) | copy-start | bytes 412
  73.1 18.2 %all-to-all-start.3 = ((bf16[8,120,128]{2,1,0:T(8,128)(2,1)}), bf16[8,120,128]{2,1,0:T(8,128)(2,1)S(1)}, u32[]{:S(2)}, u32[]{:S(2)}) async-start(bf16[8,120,128]{2,1,0:T(8,128)(2,1)} %product.3), calls=%async_computation.3 | async-start | bytes 491520 | tf_op jit(solution)/shard_map/all_to_all | solution.py:816
  91.3 0.8 copy-start.7
  93.5 12.7 %all-to-all-start.4 = ((bf16[8,192,128]{2,1,0:T(8,128)(2,1)}), bf16[8,192,128]{2,1,0:T(8,128)(2,1)S(1)}, u32[]{:S(2)}, u32[]{:S(2)}) async-start(bf16[8,192,128]{2,1,0:T(8,128)(2,1)} %edged.1.message_hbm), calls=%async_computation.4 | async-start | bytes 786432 | tf_op jit(solution)/shard_map/all_to_all | solution.py:810
  97.0 6.3 %collective-permute-start.15 = (bf16[160,128]{1,0:T(8,128)(2,1)}, bf16[160,128]{1,0:T(8,128)(2,1)S(1)}, u32[]{:S(2)}, u32[]{:S(2)}) collective-permute-start(bf16[160,128]{1,0:T(8,128)(2,1)} %get-tuple-element.55), channel_id=1, source_target_pairs={{0,8},{8,16},{16,24},{24,32},{32,40},{40,48},{48,56},{56,64},{64,7... | collective-permute-start | bytes 122888 | tf_op jit(solution)/shard_map/ppermute | solution.py:846
  97.1 6.2 %collective-permute-start.16 = (bf16[160,128]{1,0:T(8,128)(2,1)}, bf16[160,128]{1,0:T(8,128)(2,1)S(1)}, u32[]{:S(2)}, u32[]{:S(2)}) collective-permute-start(bf16[160,128]{1,0:T(8,128)(2,1)} %get-tuple-element.56), channel_id=1, source_target_pairs={{0,248},{8,0},{16,8},{24,16},{32,24},{40,32},{48,40},{56,48},{64,5... | collective-permute-start | bytes 122888 | tf_op jit(solution)/shard_map/ppermute | solution.py:847
  100.9 1.5 %copy-start.2 = (bf16[45,160,128]{2,1,0:T(8,128)(2,1)S(1)}, bf16[45,160,128]{2,1,0:T(8,128)(2,1)}, u32[]{:S(2)}) copy-start(bf16[45,160,128]{2,1,0:T(8,128)(2,1)} %get-tuple-element.50.cells_hbm) | copy-start | bytes 5529604
  102.4 3.8 %copy-start = (bf16[45,64,128]{2,1,0:T(8,128)(2,1)S(1)}, bf16[45,64,128]{2,1,0:T(8,128)(2,1)}, u32[]{:S(2)}) copy-start(bf16[45,64,128]{2,1,0:T(8,128)(2,1)} %winds_ref.1) | copy-start | bytes 2211844
  102.4 3.8 %copy-start.4 = (bf16[192,128]{1,0:T(8,128)(2,1)S(1)}, bf16[192,128]{1,0:T(8,128)(2,1)}, u32[]{:S(2)}) copy-start(bf16[192,128]{1,0:T(8,128)(2,1)} %copy-done.3) | copy-start | bytes 147460
  102.4 3.8 %copy-start.6 = (bf16[72,128]{1,0:T(8,128)(2,1)S(1)}, bf16[72,128]{1,0:T(8,128)(2,1)}, u32[]{:S(2)}) copy-start(bf16[72,128]{1,0:T(8,128)(2,1)} %copy-done.5) | copy-start | bytes 55300

commit v8 on v6

--- a/solution.py
+++ b/solution.py
@@ -29,7 +29,7 @@
 SM = pl.BlockSpec(memory_space=pltpu.SMEM)
 HB = pl.BlockSpec(memory_space=pl.ANY)
 DMA = pltpu.SemaphoreType.DMA
-SPANS = [(start, min(8, XS - start)) for start in range(0, XS, 8)]
+SPANS = [(0, 6), (6, 8), (14, 10), (24, 10), (34, 8), (42, 3)]
 
 
 def shape(dims, kind):
@@ -437,6 +437,33 @@
     )(meta, recv, edges)
 
 
+def fill_kernel(recv_ref, message_hbm, out_hbm, total_ref, sem_ref):
+    total = recv_ref[0].astype(F32)
+    for s in range(1, TARGETS):
+        total = total + recv_ref[s].astype(F32)
+    total_ref[...] = total.astype(BF16)
+    leaving = [
+        pltpu.make_async_copy(total_ref, out_hbm.at[d, pl.ds(0, PACK)], sem_ref.at[d]) for d in range(BANDS)
+    ]
+    for copy in leaving:
+        copy.start()
+    for copy in leaving:
+        copy.wait()
+
+
+def fill_message(recv, message):
+    return pl.pallas_call(
+        fill_kernel,
+        out_shape=pltpu.HBM((BANDS, PACK + HALO, LANES), BF16),
+        in_specs=[VM, HB],
+        out_specs=HB,
+        scratch_shapes=[pltpu.VMEM((PACK, LANES), BF16), DMA((BANDS,))],
+        input_output_aliases={1: 0},
+        compiler_params=params(4),
+        name="fill",
+    )(recv, pltpu.with_memory_space_constraint(message, pltpu.HBM))
+
+
 def halo_rows(meta_ref, recv_ref):
     me = meta_ref[0]
     halos = []
@@ -500,8 +527,8 @@
     rest_ref[pl.ds(18, ROWS, stride=KEPT), :] = pltpu.roll(wind, LEV, axis=1)
     for t in range(ROWS // GROUP):
         span = slice(t * LANES, (t + 1) * LANES)
-        tall_ref[t * TALL : t * TALL + LANES, :] = main_ref[span, :].T.astype(BF16)
-        tall_ref[t * TALL + LANES : (t + 1) * TALL, :] = rest_ref[span, :].T[: 2 * LEV].astype(BF16)
+        tall_ref[t * TALL : t * TALL + LANES, :] = main_ref[span, :].astype(BF16).T
+        tall_ref[t * TALL + LANES : (t + 1) * TALL, :] = rest_ref[span, :].astype(BF16).T[: 2 * LEV]
 
 
 def rows_kernel(meta_ref, before_ref, context_ref, west_ref, east_ref, recv_ref, out_ref, main_ref, rest_ref):
@@ -649,9 +676,9 @@
 
 def first_kernel(
     meta_ref, cells_hbm, winds_hbm, west_ref, east_ref, recv_ref,
-    out_hbm, edges_ref, to_east_hbm, to_west_hbm,
+    out_hbm, message_hbm, to_east_hbm, to_west_hbm,
     main_ref, rest_ref, tall_ref, placed_ref, smooth_ref, out_ref, out_sem, rim_sem,
-    cells_ref, cells_sem, winds_ref, winds_sem,
+    cells_ref, cells_sem, winds_ref, winds_sem, edges_ref, edges_sem,
 ):
     arriving = copies(cells_hbm, cells_ref, cells_sem) + copies(winds_hbm, winds_ref, winds_sem)
     for copy in arriving:
@@ -689,9 +716,16 @@
     main_ref[:LANES, :] = total[:LANES].T
     rest = jnp.concatenate([total[LANES:], jnp.zeros((LANES - LEV, LANES), F32)], axis=0)
     rest_ref[:LANES, :] = rest.T
-    for at in range(2):
-        edges_ref[at, :ROWS, :] = main_ref[pl.ds(at, ROWS, stride=2), :].astype(BF16)
-        edges_ref[at, ROWS:, :] = folded(rest_ref[pl.ds(at, ROWS, stride=2), :], LEV).astype(BF16)
+    me = meta_ref[0]
+    for at, there in ((0, me - 1), (1, me + 1)):
+        main = main_ref[pl.ds(at, ROWS, stride=2), :].astype(BF16)
+        rest = folded(rest_ref[pl.ds(at, ROWS, stride=2), :], LEV).astype(BF16)
+        edge = jnp.concatenate([main.astype(F32), rest.astype(F32)], axis=0).astype(BF16)
+        for d in range(BANDS):
+            before = jnp.zeros_like(edge) if at == 0 else edges_ref[d]
+            edges_ref[d] = jnp.where(d == there, edge, before)
+    rims.append(pltpu.make_async_copy(edges_ref, message_hbm.at[:, pl.ds(PACK, HALO)], edges_sem.at[0]))
+    rims[-1].start()
     for copy in leaving + rims:
         copy.wait()
 
@@ -701,12 +735,12 @@
         first_kernel,
         out_shape=(
             shape((XS, COLS, LANES), BF16),
-            shape((2, HALO, LANES), BF16),
+            shape((BANDS, PACK + HALO, LANES), BF16),
             shape((COLS, LANES), BF16),
             shape((COLS, LANES), BF16),
         ),
         in_specs=[SM, HB, HB] + [VM] * 3,
-        out_specs=(HB, VM, HB, HB),
+        out_specs=(HB, HB, HB, HB),
         scratch_shapes=SCRATCH
         + [
             pltpu.VMEM((XS, COLS, LANES), BF16),
@@ -716,6 +750,8 @@
             DMA((len(SPANS),)),
             pltpu.VMEM((XS, 2 * LEV, LANES), BF16),
             DMA((len(SPANS),)),
+            pltpu.VMEM((BANDS, HALO, LANES), BF16),
+            DMA((1,)),
         ],
         compiler_params=params(58),
         name="first",
@@ -770,7 +806,7 @@
         scratch_shapes=[DMA((len(SPANS),))],
         compiler_params=params(4),
         name="stay",
-    )(cells, message)
+    )(pltpu.with_memory_space_constraint(cells, pltpu.HBM), pltpu.with_memory_space_constraint(message, pltpu.HBM))
 
 
 TEAMMATES = [[(i, i ^ (16 * (other // 2) + other % 2)) for i in range(LON_DEV)] for other in range(1, TEAM)]
@@ -809,10 +845,10 @@
     given = by_lat(totals(meta, swapped, edges))
     rows = next_rows(meta, rows, context, row_from_west, row_from_east, given)
     swapped = filtered(rows, ops)
-    state, edges, to_east, to_west = first_substep(meta, cotangent, winds, west, east, given)
+    state, message, to_east, to_west = first_substep(meta, cotangent, winds, west, east, given)
     west2 = lax.ppermute(to_east, "lon", EASTWARD)
     east2 = lax.ppermute(to_west, "lon", WESTWARD)
-    message = totals(meta, swapped, edges)
+    message = fill_message(swapped, message)
     given2 = by_lat(message)
     return last_substep(meta, bring_back(state, message), winds, west2, east2, given2, given, west)
 

time: 111 us -> 109 us (0.982)
  local copies, waits for them, and re-layouts: 2.44 us -> 0.17 us
    unnamed x33 -> x29, local copies, waits for them, and re-layouts: 2.36 us -> 0.09 us
    pallas_call x2 -> x1, Pallas kernels: 2.09 us -> 0.67 us  [totals(): pl.pallas_call(total_kernel, out_shape=shape((BANDS, PACK + HALO, LANES),...]
  transfers between devices with their start and end apart: 19 -> 19, of which waited for: 11 -> 13; matrix products, arithmetic and copies ran while one was open for 0% -> 0% of each run, Pallas kernels for 10% -> 11%
where the time goes in v8:
time: 109 us
  starting transfers between devices  40.9 us (38%)
  Pallas kernels  29 us (27%)
  waiting for transfers between devices  24.8 us (23%)
  blocking collectives  13.3 us (12%)
    all_to_all x1, blocking collectives, by_lat(): return lax.all_to_all(messages, 'lat', 0, 0, tiled=True)  13.3 us
    all_to_all x2, starting transfers between devices, filtered(): lax.all_to_all(partial, 'lon', 0, 0, tiled=True, axis_index_groups=ALONG_Z)  11.9 us
    all_to_all x2, waiting for transfers between devices, filtered(): lax.all_to_all(partial, 'lon', 0, 0, tiled=True, axis_index_groups=ALONG_Z)  10.3 us
    all_to_all x2, starting transfers between devices, by_lat(): return lax.all_to_all(messages, 'lat', 0, 0, tiled=True)  9.45 us
    pallas_call x1, Pallas kernels, first_substep(): pl.pallas_call(first_kernel, out_shape=(shape((XS, COLS, LANES), BF16), s...  7.79 us
    pallas_call x1, Pallas kernels, pick_rows(): pl.pallas_call(pick_kernel, out_shape=(shape((BANDS, WIRE, LANES), BF16),...  7.18 us
    all_to_all x2, waiting for transfers between devices, by_lat(): return lax.all_to_all(messages, 'lat', 0, 0, tiled=True)  6.91 us
    ppermute x1, starting transfers between devices, shards(): east = lax.ppermute(to_west, 'lon', WESTWARD)  6.42 us
  transfers between devices with their start and end apart: 19, of which 13 were waited for; matrix products, arithmetic and copies ran while one was open for 0% of the time, Pallas kernels for 11%

profile of v8, /device:TPU:2, one launch (start us, length us, event | category | flops | bytes accessed | tf_op | source)
XLA Modules:
  0.0 108.6 jit_solution(1187422236010670995)
XLA Ops:
  0.0 7.2 %pick.1 = (bf16[8,312,128]{2,1,0:T(8,128)(2,1)}, bf16[2,72,128]{2,1,0:T(8,128)(2,1)}, bf16[192,128]{1,0:T(8,128)(2,1)}, bf16[160,128]{1,0:T(8,128)(2,1)}) custom-call(s32[16]{0:T(128)} %band_ref.1, s32[16]{0:T(128)} %row_ref.1, bf16[45,160,128]{2,1,0:T(8,128)(2,1)} %cells_hbm.3, bf16[45,64,128]{2,1,0:T(8,128)(2,1)} %winds_ref.1), custom_call_target="tpu_custom_call" | custom-call | tf_op jit(solution)/shard_map/pick/pallas_call | solution.py:276
  7.2 0.0 copy-start.10
  7.2 0.0 copy-start.11
  7.2 6.0 %all-to-all-start = ((bf16[8,312,128]{2,1,0:T(8,128)(2,1)}), bf16[8,312,128]{2,1,0:T(8,128)(2,1)S(1)}, u32[]{:S(2)}, u32[]{:S(2)}) async-start(bf16[8,312,128]{2,1,0:T(8,128)(2,1)} %get-tuple-element.26), calls=%async_computation | async-start | bytes 1277952 | tf_op jit(solution)/shard_map/all_to_all | solution.py:819
  13.3 0.1 pad.4.ops_ref
  13.4 0.1 pad_add_fusion.meta_ref
  13.5 1.2 %operators.1 = (bf16[384,96]{1,0:T(8,128)(2,1)S(1)}, bf16[384,96]{1,0:T(8,128)(2,1)S(1)}, bf16[384,96]{1,0:T(8,128)(2,1)S(1)}, bf16[384,96]{1,0:T(8,128)(2,1)S(1)}) custom-call(s32[34]{0:T(128)S(1)} %pad_add_fusion.meta_ref, bf16[2,48,1440]{2,1,0:T(8,128)(2,1)S(1)} %pad.4.ops_ref), custom_call_target="tpu_custom_call" | custom-call | tf_op jit(solution)/shard_map/operators/pallas_call | solution.py:97
  14.7 0.1 collective-permute-start.5
  14.8 0.5 collective-permute-start
  15.3 6.4 %collective-permute-start.1 = (bf16[160,128]{1,0:T(8,128)(2,1)S(1)}, bf16[160,128]{1,0:T(8,128)(2,1)S(1)}, u32[]{:S(2)}, u32[]{:S(2)}) collective-permute-start(bf16[160,128]{1,0:T(8,128)(2,1)S(1)} %copy-done.13), channel_id=1, source_target_pairs={{0,248},{8,0},{16,8},{24,16},{32,24},{40,32},{48,40},{56,48},{64,5... | collective-permute-start | bytes 122888 | tf_op jit(solution)/shard_map/ppermute | solution.py:837
  21.7 0.6 collective-permute-start.6
  22.3 1.1 collective-permute-done.1.east_ref
  23.4 0.1 collective-permute-done.west_ref.wind_west_ref
  23.5 2.3 %all-to-all-done.recv_ref = bf16[8,312,128]{2,1,0:T(8,128)(2,1)S(1)} async-done(((bf16[8,312,128]{2,1,0:T(8,128)(2,1)}), bf16[8,312,128]{2,1,0:T(8,128)(2,1)S(1)}, u32[]{:S(2)}, u32[]{:S(2)}) %all-to-all-start) | async-done | bytes 639008 | tf_op jit(solution)/shard_map/all_to_all | solution.py:819
  25.8 0.1 collective-permute-start.4
  25.9 1.5 %collective-permute-start.3 = (bf16[144,128]{1,0:T(8,128)(2,1)S(1)}, bf16[144,128]{1,0:T(8,128)(2,1)S(1)}, u32[]{:S(2)}, u32[]{:S(2)}) collective-permute-start(bf16[144,128]{1,0:T(8,128)(2,1)S(1)} %unpack.1.refs_0_.rows_ref.before_ref), channel_id=1, source_target_pairs={{0,128},{8,136},{16,144},{24,152},{32,160},{40,168},{48,176},{56,1... | collective-permute-start | bytes 110600 | tf_op jit(solution)/shard_map/ppermute | solution.py:823
  27.5 0.0 collective-permute-done.5.refs_5_
  27.5 0.3 collective-permute-start.2
  27.8 1.9 %collective-permute-done.4.refs_3_ = bf16[144,128]{1,0:T(8,128)(2,1)S(1)} collective-permute-done((bf16[144,128]{1,0:T(8,128)(2,1)S(1)}, bf16[144,128]{1,0:T(8,128)(2,1)S(1)}, u32[]{:S(2)}, u32[]{:S(2)}) %collective-permute-start.4) | collective-permute-done | bytes 36896 | tf_op jit(solution)/shard_map/ppermute | solution.py:823
  29.7 0.4 collective-permute-done.3.refs_2_
  30.1 1.2 %product.2 = bf16[8,120,128]{2,1,0:T(8,128)(2,1)} custom-call(bf16[144,128]{1,0:T(8,128)(2,1)S(1)} %unpack.1.refs_0_.rows_ref.before_ref, bf16[144,128]{1,0:T(8,128)(2,1)S(1)} %collective-permute-done.2.refs_1_, bf16[144,128]{1,0:T(8,128)(2,1)S(1)} %collective-permute-done.3.refs_2_, bf16[144,128]{1,0:T(8,128)(2,1)S(1)} %collective-permute-done.4.refs_3_, ...), custom_call_target="tpu_custom_call" | custom-call | tf_op jit(solution)/shard_map/product/pallas_call | solution.py:402
  31.3 8.5 %all-to-all-start.1 = ((bf16[8,120,128]{2,1,0:T(8,128)(2,1)}), bf16[8,120,128]{2,1,0:T(8,128)(2,1)S(1)}, u32[]{:S(2)}, u32[]{:S(2)}) async-start(bf16[8,120,128]{2,1,0:T(8,128)(2,1)} %product.2), calls=%async_computation.1 | async-start | bytes 491520 | tf_op jit(solution)/shard_map/all_to_all | solution.py:825
  39.8 0.9 context.1
  40.6 0.1 collective-permute-start.8
  40.7 3.8 %collective-permute-start.9 = (f32[8,128]{1,0:T(8,128)S(1)}, f32[8,128]{1,0:T(8,128)S(1)}, u32[]{:S(2)}, u32[]{:S(2)}) collective-permute-start(f32[8,128]{1,0:T(8,128)S(1)} %get-tuple-element.37), channel_id=1, source_target_pairs={{0,248},{8,0},{16,8},{24,16},{32,24},{40,32},{48,40},{56,48},{64,5... | collective-permute-start | bytes 12296 | tf_op jit(solution)/shard_map/ppermute | solution.py:843
  44.6 1.4 %collective-permute-done.8.west_ref = f32[8,128]{1,0:T(8,128)S(1)} collective-permute-done((f32[8,128]{1,0:T(8,128)S(1)}, f32[8,128]{1,0:T(8,128)S(1)}, u32[]{:S(2)}, u32[]{:S(2)}) %collective-permute-start.8) | collective-permute-done | bytes 4128 | tf_op jit(solution)/shard_map/ppermute | solution.py:842
  46.0 5.7 %all-to-all-done.1.recv_ref = bf16[8,120,128]{2,1,0:T(8,128)(2,1)S(1)} async-done(((bf16[8,120,128]{2,1,0:T(8,128)(2,1)}), bf16[8,120,128]{2,1,0:T(8,128)(2,1)S(1)}, u32[]{:S(2)}, u32[]{:S(2)}) %all-to-all-start.1) | async-done | bytes 245792 | tf_op jit(solution)/shard_map/all_to_all | solution.py:825
  51.7 0.7 total.1
  52.4 13.3 %all_to_all.25.recv_ref.wind_recv_ref = bf16[8,192,128]{2,1,0:T(8,128)(2,1)S(1)} all-to-all(bf16[8,192,128]{2,1,0:T(8,128)(2,1)S(1)} %total.1), channel_id=1, replica_groups=mesh['lon'=32,'lat'=8] {'lat'}, dimensions={0} | all-to-all | bytes 786432 | tf_op jit(solution)/shard_map/all_to_all | solution.py:819
  65.7 1.0 rows.1.refs_0_
  66.8 0.3 collective-permute-start.12
  67.0 1.9 %collective-permute-start.11 = (bf16[144,128]{1,0:T(8,128)(2,1)S(1)}, bf16[144,128]{1,0:T(8,128)(2,1)S(1)}, u32[]{:S(2)}, u32[]{:S(2)}) collective-permute-start(bf16[144,128]{1,0:T(8,128)(2,1)S(1)} %rows.1.refs_0_), channel_id=1, source_target_pairs={{0,128},{8,136},{16,144},{24,152},{32,160},{40,168},{48,176},{56,1... | collective-permute-start | bytes 110600 | tf_op jit(solution)/shard_map/ppermute | solution.py:823
  68.9 0.0 collective-permute-start.10
  68.9 1.5 %collective-permute-done.12.refs_3_ = bf16[144,128]{1,0:T(8,128)(2,1)S(1)} collective-permute-done((bf16[144,128]{1,0:T(8,128)(2,1)S(1)}, bf16[144,128]{1,0:T(8,128)(2,1)S(1)}, u32[]{:S(2)}, u32[]{:S(2)}) %collective-permute-start.12) | collective-permute-done | bytes 36896 | tf_op jit(solution)/shard_map/ppermute | solution.py:823
  70.5 0.7 collective-permute-done.11.refs_2_
  71.2 1.2 %product.3 = bf16[8,120,128]{2,1,0:T(8,128)(2,1)} custom-call(bf16[144,128]{1,0:T(8,128)(2,1)S(1)} %rows.1.refs_0_, bf16[144,128]{1,0:T(8,128)(2,1)S(1)} %collective-permute-done.10.refs_1_, bf16[144,128]{1,0:T(8,128)(2,1)S(1)} %collective-permute-done.11.refs_2_, bf16[144,128]{1,0:T(8,128)(2,1)S(1)} %collective-permute-done.12.refs_3_, ...), custom_call_target="tpu_custom_call" | custom-call | tf_op jit(solution)/shard_map/product/pallas_call | solution.py:402
  72.4 3.4 %all-to-all-start.3 = ((bf16[8,120,128]{2,1,0:T(8,128)(2,1)}), bf16[8,120,128]{2,1,0:T(8,128)(2,1)S(1)}, u32[]{:S(2)}, u32[]{:S(2)}) async-start(bf16[8,120,128]{2,1,0:T(8,128)(2,1)} %product.3), calls=%async_computation.3 | async-start | bytes 491520 | tf_op jit(solution)/shard_map/all_to_all | solution.py:825
  75.8 7.8 %first.1 = (bf16[45,160,128]{2,1,0:T(8,128)(2,1)}, bf16[8,192,128]{2,1,0:T(8,128)(2,1)}, bf16[160,128]{1,0:T(8,128)(2,1)}, bf16[160,128]{1,0:T(8,128)(2,1)}) custom-call(s32[34]{0:T(128)} %copy-done.6, bf16[45,160,128]{2,1,0:T(8,128)(2,1)} %cells_hbm.3, bf16[45,64,128]{2,1,0:T(8,128)(2,1)} %winds_ref.1, bf16[192,128]{1,0:T(8,128)(2,1)} %copy-done.3, ...), custom_call_target="tpu_custom_call" | custom-call | tf_op jit(solution)/shard_map/first/pallas_call | solution.py:734
  83.6 4.6 %all-to-all-done.3.recv_ref = bf16[8,120,128]{2,1,0:T(8,128)(2,1)S(1)} async-done(((bf16[8,120,128]{2,1,0:T(8,128)(2,1)}), bf16[8,120,128]{2,1,0:T(8,128)(2,1)S(1)}, u32[]{:S(2)}, u32[]{:S(2)}) %all-to-all-start.3) | async-done | bytes 245792 | tf_op jit(solution)/shard_map/all_to_all | solution.py:825
  88.2 0.8 fill.1.message_hbm
  89.1 3.5 %all-to-all-start.4 = ((bf16[8,192,128]{2,1,0:T(8,128)(2,1)}), bf16[8,192,128]{2,1,0:T(8,128)(2,1)S(1)}, u32[]{:S(2)}, u32[]{:S(2)}) async-start(bf16[8,192,128]{2,1,0:T(8,128)(2,1)} %fill.1.message_hbm), calls=%async_computation.4 | async-start | bytes 786432 | tf_op jit(solution)/shard_map/all_to_all | solution.py:819
  92.6 0.1 collective-permute-start.13
  92.7 3.8 %collective-permute-start.14 = (bf16[160,128]{1,0:T(8,128)(2,1)}, bf16[160,128]{1,0:T(8,128)(2,1)S(1)}, u32[]{:S(2)}, u32[]{:S(2)}) collective-permute-start(bf16[160,128]{1,0:T(8,128)(2,1)} %get-tuple-element.46), channel_id=1, source_target_pairs={{0,248},{8,0},{16,8},{24,16},{32,24},{40,32},{48,40},{56,48},{64,5... | collective-permute-start | bytes 122888 | tf_op jit(solution)/shard_map/ppermute | solution.py:850
  96.5 1.6 %stay.1.cells_ref = bf16[45,160,128]{2,1,0:T(8,128)(2,1)S(1)} custom-call(bf16[45,160,128]{2,1,0:T(8,128)(2,1)} %get-tuple-element.40.cells_hbm, bf16[8,192,128]{2,1,0:T(8,128)(2,1)} %fill.1.message_hbm), custom_call_target="tpu_custom_call" | custom-call | tf_op jit(solution)/shard_map/stay/pallas_call | solution.py:801
  98.1 0.3 collective-permute-done.13.west_ref
  98.4 0.1 collective-permute-done.14.east_ref
  98.5 4.6 %all-to-all-done.4.recv_ref = bf16[8,192,128]{2,1,0:T(8,128)(2,1)S(1)} async-done(((bf16[8,192,128]{2,1,0:T(8,128)(2,1)}), bf16[8,192,128]{2,1,0:T(8,128)(2,1)S(1)}, u32[]{:S(2)}, u32[]{:S(2)}) %all-to-all-start.4) | async-done | bytes 393248 | tf_op jit(solution)/shard_map/all_to_all | solution.py:819
  103.1 5.3 %last.1 = f32[45,160,128]{2,1,0:T(8,128)} custom-call(s32[34]{0:T(128)S(1)} %copy-done.7, bf16[45,160,128]{2,1,0:T(8,128)(2,1)S(1)} %stay.1.cells_ref, bf16[45,64,128]{2,1,0:T(8,128)(2,1)S(1)} %copy-done, bf16[160,128]{1,0:T(8,128)(2,1)S(1)} %collective-permute-done.13.west_ref, bf16[160,128]{1,0:T(8,128)(2,1)S(1)} %collective-permute-done.14.east_ref, ...), custom_call_target="tpu_custom_call" | custom-call | tf_op jit(solution)/shard_map/last/pallas_call | solution.py:781
  (34 shorter events, 0.1 us)
Async XLA Ops:
  0.0 13.2 %copy-start.8 = (bf16[2,45,1440]{2,0,1:T(2,128)(2,1)S(1)}, bf16[2,45,1440]{2,0,1:T(2,128)(2,1)}, u32[]{:S(2)}) copy-start(bf16[2,45,1440]{2,0,1:T(2,128)(2,1)} %param.7) | copy-start | bytes 777604
  7.2 6.2 %copy-start.10 = (s32[16]{0:T(128)S(1)}, s32[16]{0:T(128)}, u32[]{:S(2)}) copy-start(s32[16]{0:T(128)} %row_ref.1) | copy-start | bytes 196
  7.2 6.2 %copy-start.11 = (s32[16]{0:T(128)S(1)}, s32[16]{0:T(128)}, u32[]{:S(2)}) copy-start(s32[16]{0:T(128)} %band_ref.1) | copy-start | bytes 196
  7.2 7.6 %copy-start.12 = (bf16[192,128]{1,0:T(8,128)(2,1)S(1)}, bf16[192,128]{1,0:T(8,128)(2,1)}, u32[]{:S(2)}) copy-start(bf16[192,128]{1,0:T(8,128)(2,1)} %get-tuple-element.27) | copy-start | bytes 147460
  7.2 8.1 %copy-start.13 = (bf16[160,128]{1,0:T(8,128)(2,1)S(1)}, bf16[160,128]{1,0:T(8,128)(2,1)}, u32[]{:S(2)}) copy-start(bf16[160,128]{1,0:T(8,128)(2,1)} %get-tuple-element.28) | copy-start | bytes 122884
  7.2 18.6 %all-to-all-start = ((bf16[8,312,128]{2,1,0:T(8,128)(2,1)}), bf16[8,312,128]{2,1,0:T(8,128)(2,1)S(1)}, u32[]{:S(2)}, u32[]{:S(2)}) async-start(bf16[8,312,128]{2,1,0:T(8,128)(2,1)} %get-tuple-element.26), calls=%async_computation | async-start | bytes 1277952 | tf_op jit(solution)/shard_map/all_to_all | solution.py:819
  13.3 38.5 %copy-start.5 = (bf16[2,72,128]{2,1,0:T(8,128)(2,1)S(1)}, bf16[2,72,128]{2,1,0:T(8,128)(2,1)}, u32[]{:S(2)}) copy-start(bf16[2,72,128]{2,1,0:T(8,128)(2,1)} %get-tuple-element.39.edges_hbm) | copy-start | bytes 110596
  13.5 52.2 %copy-start.6 = (s32[34]{0:T(128)}, s32[34]{0:T(128)S(1)}, u32[]{:S(2)}) copy-start(s32[34]{0:T(128)S(1)} %pad_add_fusion.meta_ref) | copy-start | bytes 412
  14.7 12.8 %collective-permute-start.5 = (bf16[384,96]{1,0:T(8,128)(2,1)S(1)}, bf16[384,96]{1,0:T(8,128)(2,1)S(1)}, u32[]{:S(2)}, u32[]{:S(2)}) collective-permute-start(bf16[384,96]{1,0:T(8,128)(2,1)S(1)} %get-tuple-element.33), channel_id=1, source_target_pairs={{0,8},{8,0},{16,24},{24,16},{32,40},{40,32},{48,56},{56,48},{64,72... | collective-permute-start | bytes 221192 | tf_op jit(solution)/shard_map/ppermute | solution.py:834
  14.8 8.7 %collective-permute-start = (bf16[192,128]{1,0:T(8,128)(2,1)S(1)}, bf16[192,128]{1,0:T(8,128)(2,1)S(1)}, u32[]{:S(2)}, u32[]{:S(2)}) collective-permute-start(bf16[192,128]{1,0:T(8,128)(2,1)S(1)} %copy-done.12), channel_id=1, source_target_pairs={{0,8},{8,16},{16,24},{24,32},{32,40},{40,48},{48,56},{56,64},{64,7... | collective-permute-start | bytes 147464 | tf_op jit(solution)/shard_map/ppermute | solution.py:836
  15.3 8.1 %collective-permute-start.1 = (bf16[160,128]{1,0:T(8,128)(2,1)S(1)}, bf16[160,128]{1,0:T(8,128)(2,1)S(1)}, u32[]{:S(2)}, u32[]{:S(2)}) collective-permute-start(bf16[160,128]{1,0:T(8,128)(2,1)S(1)} %copy-done.13), channel_id=1, source_target_pairs={{0,248},{8,0},{16,8},{24,16},{32,24},{40,32},{48,40},{56,48},{64,5... | collective-permute-start | bytes 122888 | tf_op jit(solution)/shard_map/ppermute | solution.py:837
  21.7 6.1 %collective-permute-start.6 = (bf16[384,96]{1,0:T(8,128)(2,1)S(1)}, bf16[384,96]{1,0:T(8,128)(2,1)S(1)}, u32[]{:S(2)}, u32[]{:S(2)}) collective-permute-start(bf16[384,96]{1,0:T(8,128)(2,1)S(1)} %get-tuple-element.34), channel_id=1, source_target_pairs={{0,128},{8,136},{16,144},{24,152},{32,160},{40,168},{48,176},{56,1... | collective-permute-start | bytes 221192 | tf_op jit(solution)/shard_map/ppermute | solution.py:834
  22.3 5.5 %collective-permute-start.7 = (bf16[384,96]{1,0:T(8,128)(2,1)S(1)}, bf16[384,96]{1,0:T(8,128)(2,1)S(1)}, u32[]{:S(2)}, u32[]{:S(2)}) collective-permute-start(bf16[384,96]{1,0:T(8,128)(2,1)S(1)} %get-tuple-element.35), channel_id=1, source_target_pairs={{0,136},{8,128},{16,152},{24,144},{32,168},{40,160},{48,184},{56,1... | collective-permute-start | bytes 221192 | tf_op jit(solution)/shard_map/ppermute | solution.py:834
  23.4 42.3 %copy-start.9 = (bf16[160,128]{1,0:T(8,128)(2,1)}, bf16[160,128]{1,0:T(8,128)(2,1)S(1)}, u32[]{:S(2)}) copy-start(bf16[160,128]{1,0:T(8,128)(2,1)S(1)} %collective-permute-done.1.east_ref) | copy-start | bytes 122884
  23.5 42.2 %copy-start.3 = (bf16[192,128]{1,0:T(8,128)(2,1)}, bf16[192,128]{1,0:T(8,128)(2,1)S(1)}, u32[]{:S(2)}) copy-start(bf16[192,128]{1,0:T(8,128)(2,1)S(1)} %collective-permute-done.west_ref.wind_west_ref) | copy-start | bytes 147460
  25.8 3.9 %collective-permute-start.4 = (bf16[144,128]{1,0:T(8,128)(2,1)S(1)}, bf16[144,128]{1,0:T(8,128)(2,1)S(1)}, u32[]{:S(2)}, u32[]{:S(2)}) collective-permute-start(bf16[144,128]{1,0:T(8,128)(2,1)S(1)} %unpack.1.refs_0_.rows_ref.before_ref), channel_id=1, source_target_pairs={{0,136},{8,128},{16,152},{24,144},{32,168},{40,160},{48,184},{56,1... | collective-permute-start | bytes 110600 | tf_op jit(solution)/shard_map/ppermute | solution.py:823
  25.9 4.1 %collective-permute-start.3 = (bf16[144,128]{1,0:T(8,128)(2,1)S(1)}, bf16[144,128]{1,0:T(8,128)(2,1)S(1)}, u32[]{:S(2)}, u32[]{:S(2)}) collective-permute-start(bf16[144,128]{1,0:T(8,128)(2,1)S(1)} %unpack.1.refs_0_.rows_ref.before_ref), channel_id=1, source_target_pairs={{0,128},{8,136},{16,144},{24,152},{32,160},{40,168},{48,176},{56,1... | collective-permute-start | bytes 110600 | tf_op jit(solution)/shard_map/ppermute | solution.py:823
  27.5 2.6 %collective-permute-start.2 = (bf16[144,128]{1,0:T(8,128)(2,1)S(1)}, bf16[144,128]{1,0:T(8,128)(2,1)S(1)}, u32[]{:S(2)}, u32[]{:S(2)}) collective-permute-start(bf16[144,128]{1,0:T(8,128)(2,1)S(1)} %unpack.1.refs_0_.rows_ref.before_ref), channel_id=1, source_target_pairs={{0,8},{8,0},{16,24},{24,16},{32,40},{40,32},{48,56},{56,48},{64,72... | collective-permute-start | bytes 110600 | tf_op jit(solution)/shard_map/ppermute | solution.py:823
  31.3 20.4 %all-to-all-start.1 = ((bf16[8,120,128]{2,1,0:T(8,128)(2,1)}), bf16[8,120,128]{2,1,0:T(8,128)(2,1)S(1)}, u32[]{:S(2)}, u32[]{:S(2)}) async-start(bf16[8,120,128]{2,1,0:T(8,128)(2,1)} %product.2), calls=%async_computation.1 | async-start | bytes 491520 | tf_op jit(solution)/shard_map/all_to_all | solution.py:825
  40.6 5.4 %collective-permute-start.8 = (f32[8,128]{1,0:T(8,128)S(1)}, f32[8,128]{1,0:T(8,128)S(1)}, u32[]{:S(2)}, u32[]{:S(2)}) collective-permute-start(f32[8,128]{1,0:T(8,128)S(1)} %get-tuple-element.36), channel_id=1, source_target_pairs={{0,8},{8,16},{16,24},{24,32},{32,40},{40,48},{48,56},{56,64},{64,7... | collective-permute-start | bytes 12296 | tf_op jit(solution)/shard_map/ppermute | solution.py:842
  40.7 5.3 %collective-permute-start.9 = (f32[8,128]{1,0:T(8,128)S(1)}, f32[8,128]{1,0:T(8,128)S(1)}, u32[]{:S(2)}, u32[]{:S(2)}) collective-permute-start(f32[8,128]{1,0:T(8,128)S(1)} %get-tuple-element.37), channel_id=1, source_target_pairs={{0,248},{8,0},{16,8},{24,16},{32,24},{40,32},{48,40},{56,48},{64,5... | collective-permute-start | bytes 12296 | tf_op jit(solution)/shard_map/ppermute | solution.py:843
  65.7 10.1 %copy-start.1 = (bf16[8,192,128]{2,1,0:T(8,128)(2,1)}, bf16[8,192,128]{2,1,0:T(8,128)(2,1)S(1)}, u32[]{:S(2)}) copy-start(bf16[8,192,128]{2,1,0:T(8,128)(2,1)S(1)} %all_to_all.25.recv_ref.wind_recv_ref) | copy-start | bytes 1179652
  66.8 3.7 %collective-permute-start.12 = (bf16[144,128]{1,0:T(8,128)(2,1)S(1)}, bf16[144,128]{1,0:T(8,128)(2,1)S(1)}, u32[]{:S(2)}, u32[]{:S(2)}) collective-permute-start(bf16[144,128]{1,0:T(8,128)(2,1)S(1)} %rows.1.refs_0_), channel_id=1, source_target_pairs={{0,136},{8,128},{16,152},{24,144},{32,168},{40,160},{48,184},{56,1... | collective-permute-start | bytes 110600 | tf_op jit(solution)/shard_map/ppermute | solution.py:823
  67.0 4.2 %collective-permute-start.11 = (bf16[144,128]{1,0:T(8,128)(2,1)S(1)}, bf16[144,128]{1,0:T(8,128)(2,1)S(1)}, u32[]{:S(2)}, u32[]{:S(2)}) collective-permute-start(bf16[144,128]{1,0:T(8,128)(2,1)S(1)} %rows.1.refs_0_), channel_id=1, source_target_pairs={{0,128},{8,136},{16,144},{24,152},{32,160},{40,168},{48,176},{56,1... | collective-permute-start | bytes 110600 | tf_op jit(solution)/shard_map/ppermute | solution.py:823
  68.9 2.3 %collective-permute-start.10 = (bf16[144,128]{1,0:T(8,128)(2,1)S(1)}, bf16[144,128]{1,0:T(8,128)(2,1)S(1)}, u32[]{:S(2)}, u32[]{:S(2)}) collective-permute-start(bf16[144,128]{1,0:T(8,128)(2,1)S(1)} %rows.1.refs_0_), channel_id=1, source_target_pairs={{0,8},{8,0},{16,24},{24,16},{32,40},{40,32},{48,56},{56,48},{64,72... | collective-permute-start | bytes 110600 | tf_op jit(solution)/shard_map/ppermute | solution.py:823
  72.4 15.8 %all-to-all-start.3 = ((bf16[8,120,128]{2,1,0:T(8,128)(2,1)}), bf16[8,120,128]{2,1,0:T(8,128)(2,1)S(1)}, u32[]{:S(2)}, u32[]{:S(2)}) async-start(bf16[8,120,128]{2,1,0:T(8,128)(2,1)} %product.3), calls=%async_computation.3 | async-start | bytes 491520 | tf_op jit(solution)/shard_map/all_to_all | solution.py:825
  89.1 14.0 %all-to-all-start.4 = ((bf16[8,192,128]{2,1,0:T(8,128)(2,1)}), bf16[8,192,128]{2,1,0:T(8,128)(2,1)S(1)}, u32[]{:S(2)}, u32[]{:S(2)}) async-start(bf16[8,192,128]{2,1,0:T(8,128)(2,1)} %fill.1.message_hbm), calls=%async_computation.4 | async-start | bytes 786432 | tf_op jit(solution)/shard_map/all_to_all | solution.py:819
  92.6 5.8 %collective-permute-start.13 = (bf16[160,128]{1,0:T(8,128)(2,1)}, bf16[160,128]{1,0:T(8,128)(2,1)S(1)}, u32[]{:S(2)}, u32[]{:S(2)}) collective-permute-start(bf16[160,128]{1,0:T(8,128)(2,1)} %get-tuple-element.45), channel_id=1, source_target_pairs={{0,8},{8,16},{16,24},{24,32},{32,40},{40,48},{48,56},{56,64},{64,7... | collective-permute-start | bytes 122888 | tf_op jit(solution)/shard_map/ppermute | solution.py:849
  92.7 5.8 %collective-permute-start.14 = (bf16[160,128]{1,0:T(8,128)(2,1)}, bf16[160,128]{1,0:T(8,128)(2,1)S(1)}, u32[]{:S(2)}, u32[]{:S(2)}) collective-permute-start(bf16[160,128]{1,0:T(8,128)(2,1)} %get-tuple-element.46), channel_id=1, source_target_pairs={{0,248},{8,0},{16,8},{24,16},{32,24},{40,32},{48,40},{56,48},{64,5... | collective-permute-start | bytes 122888 | tf_op jit(solution)/shard_map/ppermute | solution.py:850
  96.5 6.6 %copy-start = (bf16[45,64,128]{2,1,0:T(8,128)(2,1)S(1)}, bf16[45,64,128]{2,1,0:T(8,128)(2,1)}, u32[]{:S(2)}) copy-start(bf16[45,64,128]{2,1,0:T(8,128)(2,1)} %winds_ref.1) | copy-start | bytes 2211844
  96.5 6.6 %copy-start.2 = (bf16[8,192,128]{2,1,0:T(8,128)(2,1)S(1)}, bf16[8,192,128]{2,1,0:T(8,128)(2,1)}, u32[]{:S(2)}) copy-start(bf16[8,192,128]{2,1,0:T(8,128)(2,1)} %copy-done.1) | copy-start | bytes 1179652
  96.5 6.6 %copy-start.4 = (bf16[192,128]{1,0:T(8,128)(2,1)S(1)}, bf16[192,128]{1,0:T(8,128)(2,1)}, u32[]{:S(2)}) copy-start(bf16[192,128]{1,0:T(8,128)(2,1)} %copy-done.3) | copy-start | bytes 147460
  96.5 6.6 %copy-start.7 = (s32[34]{0:T(128)S(1)}, s32[34]{0:T(128)}, u32[]{:S(2)}) copy-start(s32[34]{0:T(128)} %copy-done.6) | copy-start | bytes 412

commit v9 on v8

--- a/solution.py
+++ b/solution.py
@@ -382,7 +382,8 @@
 
 
 def product_kernel(*refs):
-    out_ref = refs[-1]
+    out_hbm, out_ref, sem_ref = refs[2 * TEAM :]
+    leaving = []
     rows = [spread_blocks(ref) for ref in refs[:TEAM]]
     for q in range(2):
         span = slice(4 * ROWS * q, 4 * ROWS * (q + 1))
@@ -396,14 +397,20 @@
             out_ref[t, :ROWS, :] = part[:, :LANES].astype(BF16)
             out_ref[t, ROWS : 2 * ROWS, :] = part[:, LANES : 2 * LANES].astype(BF16)
             out_ref[t, 2 * ROWS :, :] = folded(part[:, 2 * LANES :], 2 * LEV).astype(BF16)
+        half = pl.ds(4 * q, 4)
+        leaving.append(pltpu.make_async_copy(out_ref.at[half], out_hbm.at[half], sem_ref.at[q]))
+        leaving[-1].start()
+    for copy in leaving:
+        copy.wait()
 
 
 def products(rows, ops):
     return pl.pallas_call(
         product_kernel,
-        out_shape=shape((TARGETS, PACK, LANES), BF16),
+        out_shape=pltpu.HBM((TARGETS, PACK, LANES), BF16),
         in_specs=[VM] * (2 * TEAM),
-        out_specs=VM,
+        out_specs=HB,
+        scratch_shapes=[pltpu.VMEM((TARGETS, PACK, LANES), BF16), DMA((2,))],
         compiler_params=params(6),
         name="product",
     )(*rows, *ops)

time: 109 us -> 109 us (level)
  no operation moved by 1% of the time
where the time goes in v9:
time: 109 us
  starting transfers between devices  40.9 us (38%)
  Pallas kernels  28.9 us (27%)
  waiting for transfers between devices  24.8 us (23%)
  blocking collectives  13.3 us (12%)
    all_to_all x1, blocking collectives, by_lat(): return lax.all_to_all(messages, 'lat', 0, 0, tiled=True)  13.3 us
    all_to_all x2, starting transfers between devices, filtered(): lax.all_to_all(partial, 'lon', 0, 0, tiled=True, axis_index_groups=ALONG_Z)  11.9 us
    all_to_all x2, waiting for transfers between devices, filtered(): lax.all_to_all(partial, 'lon', 0, 0, tiled=True, axis_index_groups=ALONG_Z)  10.3 us
    all_to_all x2, starting transfers between devices, by_lat(): return lax.all_to_all(messages, 'lat', 0, 0, tiled=True)  9.49 us
    pallas_call x1, Pallas kernels, first_substep(): pl.pallas_call(first_kernel, out_shape=(shape((XS, COLS, LANES), BF16), s...  7.8 us
    pallas_call x1, Pallas kernels, pick_rows(): pl.pallas_call(pick_kernel, out_shape=(shape((BANDS, WIRE, LANES), BF16),...  7.16 us
    all_to_all x2, waiting for transfers between devices, by_lat(): return lax.all_to_all(messages, 'lat', 0, 0, tiled=True)  6.91 us
    ppermute x1, starting transfers between devices, shards(): east = lax.ppermute(to_west, 'lon', WESTWARD)  6.42 us
  transfers between devices with their start and end apart: 19, of which 13 were waited for; matrix products, arithmetic and copies ran while one was open for 0% of the time, Pallas kernels for 11%

profile of v9, /device:TPU:2, one launch (start us, length us, event | category | flops | bytes accessed | tf_op | source)
XLA Modules:
  0.0 108.6 jit_solution(883153055864532856)
XLA Ops:
  0.0 7.2 %pick.1 = (bf16[8,312,128]{2,1,0:T(8,128)(2,1)}, bf16[2,72,128]{2,1,0:T(8,128)(2,1)}, bf16[192,128]{1,0:T(8,128)(2,1)}, bf16[160,128]{1,0:T(8,128)(2,1)}) custom-call(s32[16]{0:T(128)} %band_ref.1, s32[16]{0:T(128)} %row_ref.1, bf16[45,160,128]{2,1,0:T(8,128)(2,1)} %cells_hbm.3, bf16[45,64,128]{2,1,0:T(8,128)(2,1)} %winds_ref.1), custom_call_target="tpu_custom_call" | custom-call | tf_op jit(solution)/shard_map/pick/pallas_call | solution.py:276
  7.2 0.0 copy-start.10
  7.2 0.0 copy-start.11
  7.2 6.0 %all-to-all-start = ((bf16[8,312,128]{2,1,0:T(8,128)(2,1)}), bf16[8,312,128]{2,1,0:T(8,128)(2,1)S(1)}, u32[]{:S(2)}, u32[]{:S(2)}) async-start(bf16[8,312,128]{2,1,0:T(8,128)(2,1)} %get-tuple-element.26), calls=%async_computation | async-start | bytes 1277952 | tf_op jit(solution)/shard_map/all_to_all | solution.py:826
  13.3 0.1 pad.4.ops_ref
  13.4 0.1 pad_add_fusion.meta_ref
  13.5 1.2 %operators.1 = (bf16[384,96]{1,0:T(8,128)(2,1)S(1)}, bf16[384,96]{1,0:T(8,128)(2,1)S(1)}, bf16[384,96]{1,0:T(8,128)(2,1)S(1)}, bf16[384,96]{1,0:T(8,128)(2,1)S(1)}) custom-call(s32[34]{0:T(128)S(1)} %pad_add_fusion.meta_ref, bf16[2,48,1440]{2,1,0:T(8,128)(2,1)S(1)} %pad.4.ops_ref), custom_call_target="tpu_custom_call" | custom-call | tf_op jit(solution)/shard_map/operators/pallas_call | solution.py:97
  14.7 0.1 collective-permute-start.5
  14.8 0.5 collective-permute-start
  15.3 6.4 %collective-permute-start.1 = (bf16[160,128]{1,0:T(8,128)(2,1)S(1)}, bf16[160,128]{1,0:T(8,128)(2,1)S(1)}, u32[]{:S(2)}, u32[]{:S(2)}) collective-permute-start(bf16[160,128]{1,0:T(8,128)(2,1)S(1)} %copy-done.13), channel_id=1, source_target_pairs={{0,248},{8,0},{16,8},{24,16},{32,24},{40,32},{48,40},{56,48},{64,5... | collective-permute-start | bytes 122888 | tf_op jit(solution)/shard_map/ppermute | solution.py:844
  21.7 0.6 collective-permute-start.6
  22.3 0.0 collective-permute-start.7
  22.3 1.1 collective-permute-done.1.east_ref
  23.4 0.1 collective-permute-done.west_ref.wind_west_ref
  23.5 2.3 %all-to-all-done.recv_ref = bf16[8,312,128]{2,1,0:T(8,128)(2,1)S(1)} async-done(((bf16[8,312,128]{2,1,0:T(8,128)(2,1)}), bf16[8,312,128]{2,1,0:T(8,128)(2,1)S(1)}, u32[]{:S(2)}, u32[]{:S(2)}) %all-to-all-start) | async-done | bytes 639008 | tf_op jit(solution)/shard_map/all_to_all | solution.py:826
  25.9 0.1 collective-permute-start.4
  26.0 1.5 %collective-permute-start.3 = (bf16[144,128]{1,0:T(8,128)(2,1)S(1)}, bf16[144,128]{1,0:T(8,128)(2,1)S(1)}, u32[]{:S(2)}, u32[]{:S(2)}) collective-permute-start(bf16[144,128]{1,0:T(8,128)(2,1)S(1)} %unpack.1.refs_0_.rows_ref.before_ref), channel_id=1, source_target_pairs={{0,128},{8,136},{16,144},{24,152},{32,160},{40,168},{48,176},{56,1... | collective-permute-start | bytes 110600 | tf_op jit(solution)/shard_map/ppermute | solution.py:830
  27.5 0.3 collective-permute-start.2
  27.8 1.9 %collective-permute-done.4.refs_3_ = bf16[144,128]{1,0:T(8,128)(2,1)S(1)} collective-permute-done((bf16[144,128]{1,0:T(8,128)(2,1)S(1)}, bf16[144,128]{1,0:T(8,128)(2,1)S(1)}, u32[]{:S(2)}, u32[]{:S(2)}) %collective-permute-start.4) | collective-permute-done | bytes 36896 | tf_op jit(solution)/shard_map/ppermute | solution.py:830
  29.7 0.4 collective-permute-done.3.refs_2_
  30.1 1.2 %product.2 = bf16[8,120,128]{2,1,0:T(8,128)(2,1)} custom-call(bf16[144,128]{1,0:T(8,128)(2,1)S(1)} %unpack.1.refs_0_.rows_ref.before_ref, bf16[144,128]{1,0:T(8,128)(2,1)S(1)} %collective-permute-done.2.refs_1_, bf16[144,128]{1,0:T(8,128)(2,1)S(1)} %collective-permute-done.3.refs_2_, bf16[144,128]{1,0:T(8,128)(2,1)S(1)} %collective-permute-done.4.refs_3_, ...), custom_call_target="tpu_custom_call" | custom-call | tf_op jit(solution)/shard_map/product/pallas_call | solution.py:408
  31.3 8.5 %all-to-all-start.1 = ((bf16[8,120,128]{2,1,0:T(8,128)(2,1)}), bf16[8,120,128]{2,1,0:T(8,128)(2,1)S(1)}, u32[]{:S(2)}, u32[]{:S(2)}) async-start(bf16[8,120,128]{2,1,0:T(8,128)(2,1)} %product.2), calls=%async_computation.1 | async-start | bytes 491520 | tf_op jit(solution)/shard_map/all_to_all | solution.py:832
  39.8 0.9 context.1
  40.6 0.1 collective-permute-start.8
  40.7 3.8 %collective-permute-start.9 = (f32[8,128]{1,0:T(8,128)S(1)}, f32[8,128]{1,0:T(8,128)S(1)}, u32[]{:S(2)}, u32[]{:S(2)}) collective-permute-start(f32[8,128]{1,0:T(8,128)S(1)} %get-tuple-element.37), channel_id=1, source_target_pairs={{0,248},{8,0},{16,8},{24,16},{32,24},{40,32},{48,40},{56,48},{64,5... | collective-permute-start | bytes 12296 | tf_op jit(solution)/shard_map/ppermute | solution.py:850
  44.6 1.4 %collective-permute-done.8.west_ref = f32[8,128]{1,0:T(8,128)S(1)} collective-permute-done((f32[8,128]{1,0:T(8,128)S(1)}, f32[8,128]{1,0:T(8,128)S(1)}, u32[]{:S(2)}, u32[]{:S(2)}) %collective-permute-start.8) | collective-permute-done | bytes 4128 | tf_op jit(solution)/shard_map/ppermute | solution.py:849
  46.0 5.7 %all-to-all-done.1.recv_ref = bf16[8,120,128]{2,1,0:T(8,128)(2,1)S(1)} async-done(((bf16[8,120,128]{2,1,0:T(8,128)(2,1)}), bf16[8,120,128]{2,1,0:T(8,128)(2,1)S(1)}, u32[]{:S(2)}, u32[]{:S(2)}) %all-to-all-start.1) | async-done | bytes 245792 | tf_op jit(solution)/shard_map/all_to_all | solution.py:832
  51.7 0.7 total.1
  52.4 13.3 %all_to_all.25.recv_ref.wind_recv_ref = bf16[8,192,128]{2,1,0:T(8,128)(2,1)S(1)} all-to-all(bf16[8,192,128]{2,1,0:T(8,128)(2,1)S(1)} %total.1), channel_id=1, replica_groups=mesh['lon'=32,'lat'=8] {'lat'}, dimensions={0} | all-to-all | bytes 786432 | tf_op jit(solution)/shard_map/all_to_all | solution.py:826
  65.7 1.0 rows.1.refs_0_
  66.8 0.3 collective-permute-start.12
  67.0 1.9 %collective-permute-start.11 = (bf16[144,128]{1,0:T(8,128)(2,1)S(1)}, bf16[144,128]{1,0:T(8,128)(2,1)S(1)}, u32[]{:S(2)}, u32[]{:S(2)}) collective-permute-start(bf16[144,128]{1,0:T(8,128)(2,1)S(1)} %rows.1.refs_0_), channel_id=1, source_target_pairs={{0,128},{8,136},{16,144},{24,152},{32,160},{40,168},{48,176},{56,1... | collective-permute-start | bytes 110600 | tf_op jit(solution)/shard_map/ppermute | solution.py:830
  68.9 0.0 collective-permute-start.10
  68.9 1.5 %collective-permute-done.12.refs_3_ = bf16[144,128]{1,0:T(8,128)(2,1)S(1)} collective-permute-done((bf16[144,128]{1,0:T(8,128)(2,1)S(1)}, bf16[144,128]{1,0:T(8,128)(2,1)S(1)}, u32[]{:S(2)}, u32[]{:S(2)}) %collective-permute-start.12) | collective-permute-done | bytes 36896 | tf_op jit(solution)/shard_map/ppermute | solution.py:830
  70.5 0.7 collective-permute-done.11.refs_2_
  71.2 1.2 %product.3 = bf16[8,120,128]{2,1,0:T(8,128)(2,1)} custom-call(bf16[144,128]{1,0:T(8,128)(2,1)S(1)} %rows.1.refs_0_, bf16[144,128]{1,0:T(8,128)(2,1)S(1)} %collective-permute-done.10.refs_1_, bf16[144,128]{1,0:T(8,128)(2,1)S(1)} %collective-permute-done.11.refs_2_, bf16[144,128]{1,0:T(8,128)(2,1)S(1)} %collective-permute-done.12.refs_3_, ...), custom_call_target="tpu_custom_call" | custom-call | tf_op jit(solution)/shard_map/product/pallas_call | solution.py:408
  72.4 3.4 %all-to-all-start.3 = ((bf16[8,120,128]{2,1,0:T(8,128)(2,1)}), bf16[8,120,128]{2,1,0:T(8,128)(2,1)S(1)}, u32[]{:S(2)}, u32[]{:S(2)}) async-start(bf16[8,120,128]{2,1,0:T(8,128)(2,1)} %product.3), calls=%async_computation.3 | async-start | bytes 491520 | tf_op jit(solution)/shard_map/all_to_all | solution.py:832
  75.8 7.8 %first.1 = (bf16[45,160,128]{2,1,0:T(8,128)(2,1)}, bf16[8,192,128]{2,1,0:T(8,128)(2,1)}, bf16[160,128]{1,0:T(8,128)(2,1)}, bf16[160,128]{1,0:T(8,128)(2,1)}) custom-call(s32[34]{0:T(128)} %copy-done.6, bf16[45,160,128]{2,1,0:T(8,128)(2,1)} %cells_hbm.3, bf16[45,64,128]{2,1,0:T(8,128)(2,1)} %winds_ref.1, bf16[192,128]{1,0:T(8,128)(2,1)} %copy-done.3, ...), custom_call_target="tpu_custom_call" | custom-call | tf_op jit(solution)/shard_map/first/pallas_call | solution.py:741
  83.6 4.6 %all-to-all-done.3.recv_ref = bf16[8,120,128]{2,1,0:T(8,128)(2,1)S(1)} async-done(((bf16[8,120,128]{2,1,0:T(8,128)(2,1)}), bf16[8,120,128]{2,1,0:T(8,128)(2,1)S(1)}, u32[]{:S(2)}, u32[]{:S(2)}) %all-to-all-start.3) | async-done | bytes 245792 | tf_op jit(solution)/shard_map/all_to_all | solution.py:832
  88.2 0.8 fill.1.message_hbm
  89.1 3.5 %all-to-all-start.4 = ((bf16[8,192,128]{2,1,0:T(8,128)(2,1)}), bf16[8,192,128]{2,1,0:T(8,128)(2,1)S(1)}, u32[]{:S(2)}, u32[]{:S(2)}) async-start(bf16[8,192,128]{2,1,0:T(8,128)(2,1)} %fill.1.message_hbm), calls=%async_computation.4 | async-start | bytes 786432 | tf_op jit(solution)/shard_map/all_to_all | solution.py:826
  92.6 0.1 collective-permute-start.13
  92.7 3.8 %collective-permute-start.14 = (bf16[160,128]{1,0:T(8,128)(2,1)}, bf16[160,128]{1,0:T(8,128)(2,1)S(1)}, u32[]{:S(2)}, u32[]{:S(2)}) collective-permute-start(bf16[160,128]{1,0:T(8,128)(2,1)} %get-tuple-element.46), channel_id=1, source_target_pairs={{0,248},{8,0},{16,8},{24,16},{32,24},{40,32},{48,40},{56,48},{64,5... | collective-permute-start | bytes 122888 | tf_op jit(solution)/shard_map/ppermute | solution.py:857
  96.5 1.6 %stay.1.cells_ref = bf16[45,160,128]{2,1,0:T(8,128)(2,1)S(1)} custom-call(bf16[45,160,128]{2,1,0:T(8,128)(2,1)} %get-tuple-element.40.cells_hbm, bf16[8,192,128]{2,1,0:T(8,128)(2,1)} %fill.1.message_hbm), custom_call_target="tpu_custom_call" | custom-call | tf_op jit(solution)/shard_map/stay/pallas_call | solution.py:808
  98.1 0.3 collective-permute-done.13.west_ref
  98.4 0.1 collective-permute-done.14.east_ref
  98.5 4.6 %all-to-all-done.4.recv_ref = bf16[8,192,128]{2,1,0:T(8,128)(2,1)S(1)} async-done(((bf16[8,192,128]{2,1,0:T(8,128)(2,1)}), bf16[8,192,128]{2,1,0:T(8,128)(2,1)S(1)}, u32[]{:S(2)}, u32[]{:S(2)}) %all-to-all-start.4) | async-done | bytes 393248 | tf_op jit(solution)/shard_map/all_to_all | solution.py:826
  103.1 5.3 %last.1 = f32[45,160,128]{2,1,0:T(8,128)} custom-call(s32[34]{0:T(128)S(1)} %copy-done.7, bf16[45,160,128]{2,1,0:T(8,128)(2,1)S(1)} %stay.1.cells_ref, bf16[45,64,128]{2,1,0:T(8,128)(2,1)S(1)} %copy-done, bf16[160,128]{1,0:T(8,128)(2,1)S(1)} %collective-permute-done.13.west_ref, bf16[160,128]{1,0:T(8,128)(2,1)S(1)} %collective-permute-done.14.east_ref, ...), custom_call_target="tpu_custom_call" | custom-call | tf_op jit(solution)/shard_map/last/pallas_call | solution.py:788
  (34 shorter events, 0.1 us)
Async XLA Ops:
  0.0 13.2 %copy-start.8 = (bf16[2,45,1440]{2,0,1:T(2,128)(2,1)S(1)}, bf16[2,45,1440]{2,0,1:T(2,128)(2,1)}, u32[]{:S(2)}) copy-start(bf16[2,45,1440]{2,0,1:T(2,128)(2,1)} %param.7) | copy-start | bytes 777604
  7.2 6.2 %copy-start.10 = (s32[16]{0:T(128)S(1)}, s32[16]{0:T(128)}, u32[]{:S(2)}) copy-start(s32[16]{0:T(128)} %row_ref.1) | copy-start | bytes 196
  7.2 6.2 %copy-start.11 = (s32[16]{0:T(128)S(1)}, s32[16]{0:T(128)}, u32[]{:S(2)}) copy-start(s32[16]{0:T(128)} %band_ref.1) | copy-start | bytes 196
  7.2 7.6 %copy-start.12 = (bf16[192,128]{1,0:T(8,128)(2,1)S(1)}, bf16[192,128]{1,0:T(8,128)(2,1)}, u32[]{:S(2)}) copy-start(bf16[192,128]{1,0:T(8,128)(2,1)} %get-tuple-element.27) | copy-start | bytes 147460
  7.2 8.1 %copy-start.13 = (bf16[160,128]{1,0:T(8,128)(2,1)S(1)}, bf16[160,128]{1,0:T(8,128)(2,1)}, u32[]{:S(2)}) copy-start(bf16[160,128]{1,0:T(8,128)(2,1)} %get-tuple-element.28) | copy-start | bytes 122884
  7.2 18.6 %all-to-all-start = ((bf16[8,312,128]{2,1,0:T(8,128)(2,1)}), bf16[8,312,128]{2,1,0:T(8,128)(2,1)S(1)}, u32[]{:S(2)}, u32[]{:S(2)}) async-start(bf16[8,312,128]{2,1,0:T(8,128)(2,1)} %get-tuple-element.26), calls=%async_computation | async-start | bytes 1277952 | tf_op jit(solution)/shard_map/all_to_all | solution.py:826
  13.3 38.5 %copy-start.5 = (bf16[2,72,128]{2,1,0:T(8,128)(2,1)S(1)}, bf16[2,72,128]{2,1,0:T(8,128)(2,1)}, u32[]{:S(2)}) copy-start(bf16[2,72,128]{2,1,0:T(8,128)(2,1)} %get-tuple-element.39.edges_hbm) | copy-start | bytes 110596
  13.5 52.2 %copy-start.6 = (s32[34]{0:T(128)}, s32[34]{0:T(128)S(1)}, u32[]{:S(2)}) copy-start(s32[34]{0:T(128)S(1)} %pad_add_fusion.meta_ref) | copy-start | bytes 412
  14.7 12.8 %collective-permute-start.5 = (bf16[384,96]{1,0:T(8,128)(2,1)S(1)}, bf16[384,96]{1,0:T(8,128)(2,1)S(1)}, u32[]{:S(2)}, u32[]{:S(2)}) collective-permute-start(bf16[384,96]{1,0:T(8,128)(2,1)S(1)} %get-tuple-element.33), channel_id=1, source_target_pairs={{0,8},{8,0},{16,24},{24,16},{32,40},{40,32},{48,56},{56,48},{64,72... | collective-permute-start | bytes 221192 | tf_op jit(solution)/shard_map/ppermute | solution.py:841
  14.8 8.7 %collective-permute-start = (bf16[192,128]{1,0:T(8,128)(2,1)S(1)}, bf16[192,128]{1,0:T(8,128)(2,1)S(1)}, u32[]{:S(2)}, u32[]{:S(2)}) collective-permute-start(bf16[192,128]{1,0:T(8,128)(2,1)S(1)} %copy-done.12), channel_id=1, source_target_pairs={{0,8},{8,16},{16,24},{24,32},{32,40},{40,48},{48,56},{56,64},{64,7... | collective-permute-start | bytes 147464 | tf_op jit(solution)/shard_map/ppermute | solution.py:843
  15.3 8.1 %collective-permute-start.1 = (bf16[160,128]{1,0:T(8,128)(2,1)S(1)}, bf16[160,128]{1,0:T(8,128)(2,1)S(1)}, u32[]{:S(2)}, u32[]{:S(2)}) collective-permute-start(bf16[160,128]{1,0:T(8,128)(2,1)S(1)} %copy-done.13), channel_id=1, source_target_pairs={{0,248},{8,0},{16,8},{24,16},{32,24},{40,32},{48,40},{56,48},{64,5... | collective-permute-start | bytes 122888 | tf_op jit(solution)/shard_map/ppermute | solution.py:844
  21.7 6.1 %collective-permute-start.6 = (bf16[384,96]{1,0:T(8,128)(2,1)S(1)}, bf16[384,96]{1,0:T(8,128)(2,1)S(1)}, u32[]{:S(2)}, u32[]{:S(2)}) collective-permute-start(bf16[384,96]{1,0:T(8,128)(2,1)S(1)} %get-tuple-element.34), channel_id=1, source_target_pairs={{0,128},{8,136},{16,144},{24,152},{32,160},{40,168},{48,176},{56,1... | collective-permute-start | bytes 221192 | tf_op jit(solution)/shard_map/ppermute | solution.py:841
  22.3 5.5 %collective-permute-start.7 = (bf16[384,96]{1,0:T(8,128)(2,1)S(1)}, bf16[384,96]{1,0:T(8,128)(2,1)S(1)}, u32[]{:S(2)}, u32[]{:S(2)}) collective-permute-start(bf16[384,96]{1,0:T(8,128)(2,1)S(1)} %get-tuple-element.35), channel_id=1, source_target_pairs={{0,136},{8,128},{16,152},{24,144},{32,168},{40,160},{48,184},{56,1... | collective-permute-start | bytes 221192 | tf_op jit(solution)/shard_map/ppermute | solution.py:841
  23.4 42.3 %copy-start.9 = (bf16[160,128]{1,0:T(8,128)(2,1)}, bf16[160,128]{1,0:T(8,128)(2,1)S(1)}, u32[]{:S(2)}) copy-start(bf16[160,128]{1,0:T(8,128)(2,1)S(1)} %collective-permute-done.1.east_ref) | copy-start | bytes 122884
  23.5 42.2 %copy-start.3 = (bf16[192,128]{1,0:T(8,128)(2,1)}, bf16[192,128]{1,0:T(8,128)(2,1)S(1)}, u32[]{:S(2)}) copy-start(bf16[192,128]{1,0:T(8,128)(2,1)S(1)} %collective-permute-done.west_ref.wind_west_ref) | copy-start | bytes 147460
  25.9 3.9 %collective-permute-start.4 = (bf16[144,128]{1,0:T(8,128)(2,1)S(1)}, bf16[144,128]{1,0:T(8,128)(2,1)S(1)}, u32[]{:S(2)}, u32[]{:S(2)}) collective-permute-start(bf16[144,128]{1,0:T(8,128)(2,1)S(1)} %unpack.1.refs_0_.rows_ref.before_ref), channel_id=1, source_target_pairs={{0,136},{8,128},{16,152},{24,144},{32,168},{40,160},{48,184},{56,1... | collective-permute-start | bytes 110600 | tf_op jit(solution)/shard_map/ppermute | solution.py:830
  26.0 4.1 %collective-permute-start.3 = (bf16[144,128]{1,0:T(8,128)(2,1)S(1)}, bf16[144,128]{1,0:T(8,128)(2,1)S(1)}, u32[]{:S(2)}, u32[]{:S(2)}) collective-permute-start(bf16[144,128]{1,0:T(8,128)(2,1)S(1)} %unpack.1.refs_0_.rows_ref.before_ref), channel_id=1, source_target_pairs={{0,128},{8,136},{16,144},{24,152},{32,160},{40,168},{48,176},{56,1... | collective-permute-start | bytes 110600 | tf_op jit(solution)/shard_map/ppermute | solution.py:830
  27.5 2.6 %collective-permute-start.2 = (bf16[144,128]{1,0:T(8,128)(2,1)S(1)}, bf16[144,128]{1,0:T(8,128)(2,1)S(1)}, u32[]{:S(2)}, u32[]{:S(2)}) collective-permute-start(bf16[144,128]{1,0:T(8,128)(2,1)S(1)} %unpack.1.refs_0_.rows_ref.before_ref), channel_id=1, source_target_pairs={{0,8},{8,0},{16,24},{24,16},{32,40},{40,32},{48,56},{56,48},{64,72... | collective-permute-start | bytes 110600 | tf_op jit(solution)/shard_map/ppermute | solution.py:830
  31.3 20.4 %all-to-all-start.1 = ((bf16[8,120,128]{2,1,0:T(8,128)(2,1)}), bf16[8,120,128]{2,1,0:T(8,128)(2,1)S(1)}, u32[]{:S(2)}, u32[]{:S(2)}) async-start(bf16[8,120,128]{2,1,0:T(8,128)(2,1)} %product.2), calls=%async_computation.1 | async-start | bytes 491520 | tf_op jit(solution)/shard_map/all_to_all | solution.py:832
  40.6 5.4 %collective-permute-start.8 = (f32[8,128]{1,0:T(8,128)S(1)}, f32[8,128]{1,0:T(8,128)S(1)}, u32[]{:S(2)}, u32[]{:S(2)}) collective-permute-start(f32[8,128]{1,0:T(8,128)S(1)} %get-tuple-element.36), channel_id=1, source_target_pairs={{0,8},{8,16},{16,24},{24,32},{32,40},{40,48},{48,56},{56,64},{64,7... | collective-permute-start | bytes 12296 | tf_op jit(solution)/shard_map/ppermute | solution.py:849
  40.7 5.3 %collective-permute-start.9 = (f32[8,128]{1,0:T(8,128)S(1)}, f32[8,128]{1,0:T(8,128)S(1)}, u32[]{:S(2)}, u32[]{:S(2)}) collective-permute-start(f32[8,128]{1,0:T(8,128)S(1)} %get-tuple-element.37), channel_id=1, source_target_pairs={{0,248},{8,0},{16,8},{24,16},{32,24},{40,32},{48,40},{56,48},{64,5... | collective-permute-start | bytes 12296 | tf_op jit(solution)/shard_map/ppermute | solution.py:850
  65.7 10.1 %copy-start.1 = (bf16[8,192,128]{2,1,0:T(8,128)(2,1)}, bf16[8,192,128]{2,1,0:T(8,128)(2,1)S(1)}, u32[]{:S(2)}) copy-start(bf16[8,192,128]{2,1,0:T(8,128)(2,1)S(1)} %all_to_all.25.recv_ref.wind_recv_ref) | copy-start | bytes 1179652
  66.8 3.7 %collective-permute-start.12 = (bf16[144,128]{1,0:T(8,128)(2,1)S(1)}, bf16[144,128]{1,0:T(8,128)(2,1)S(1)}, u32[]{:S(2)}, u32[]{:S(2)}) collective-permute-start(bf16[144,128]{1,0:T(8,128)(2,1)S(1)} %rows.1.refs_0_), channel_id=1, source_target_pairs={{0,136},{8,128},{16,152},{24,144},{32,168},{40,160},{48,184},{56,1... | collective-permute-start | bytes 110600 | tf_op jit(solution)/shard_map/ppermute | solution.py:830
  67.0 4.2 %collective-permute-start.11 = (bf16[144,128]{1,0:T(8,128)(2,1)S(1)}, bf16[144,128]{1,0:T(8,128)(2,1)S(1)}, u32[]{:S(2)}, u32[]{:S(2)}) collective-permute-start(bf16[144,128]{1,0:T(8,128)(2,1)S(1)} %rows.1.refs_0_), channel_id=1, source_target_pairs={{0,128},{8,136},{16,144},{24,152},{32,160},{40,168},{48,176},{56,1... | collective-permute-start | bytes 110600 | tf_op jit(solution)/shard_map/ppermute | solution.py:830
  68.9 2.3 %collective-permute-start.10 = (bf16[144,128]{1,0:T(8,128)(2,1)S(1)}, bf16[144,128]{1,0:T(8,128)(2,1)S(1)}, u32[]{:S(2)}, u32[]{:S(2)}) collective-permute-start(bf16[144,128]{1,0:T(8,128)(2,1)S(1)} %rows.1.refs_0_), channel_id=1, source_target_pairs={{0,8},{8,0},{16,24},{24,16},{32,40},{40,32},{48,56},{56,48},{64,72... | collective-permute-start | bytes 110600 | tf_op jit(solution)/shard_map/ppermute | solution.py:830
  72.4 15.8 %all-to-all-start.3 = ((bf16[8,120,128]{2,1,0:T(8,128)(2,1)}), bf16[8,120,128]{2,1,0:T(8,128)(2,1)S(1)}, u32[]{:S(2)}, u32[]{:S(2)}) async-start(bf16[8,120,128]{2,1,0:T(8,128)(2,1)} %product.3), calls=%async_computation.3 | async-start | bytes 491520 | tf_op jit(solution)/shard_map/all_to_all | solution.py:832
  89.1 14.0 %all-to-all-start.4 = ((bf16[8,192,128]{2,1,0:T(8,128)(2,1)}), bf16[8,192,128]{2,1,0:T(8,128)(2,1)S(1)}, u32[]{:S(2)}, u32[]{:S(2)}) async-start(bf16[8,192,128]{2,1,0:T(8,128)(2,1)} %fill.1.message_hbm), calls=%async_computation.4 | async-start | bytes 786432 | tf_op jit(solution)/shard_map/all_to_all | solution.py:826
  92.6 5.8 %collective-permute-start.13 = (bf16[160,128]{1,0:T(8,128)(2,1)}, bf16[160,128]{1,0:T(8,128)(2,1)S(1)}, u32[]{:S(2)}, u32[]{:S(2)}) collective-permute-start(bf16[160,128]{1,0:T(8,128)(2,1)} %get-tuple-element.45), channel_id=1, source_target_pairs={{0,8},{8,16},{16,24},{24,32},{32,40},{40,48},{48,56},{56,64},{64,7... | collective-permute-start | bytes 122888 | tf_op jit(solution)/shard_map/ppermute | solution.py:856
  92.7 5.8 %collective-permute-start.14 = (bf16[160,128]{1,0:T(8,128)(2,1)}, bf16[160,128]{1,0:T(8,128)(2,1)S(1)}, u32[]{:S(2)}, u32[]{:S(2)}) collective-permute-start(bf16[160,128]{1,0:T(8,128)(2,1)} %get-tuple-element.46), channel_id=1, source_target_pairs={{0,248},{8,0},{16,8},{24,16},{32,24},{40,32},{48,40},{56,48},{64,5... | collective-permute-start | bytes 122888 | tf_op jit(solution)/shard_map/ppermute | solution.py:857
  96.5 6.6 %copy-start = (bf16[45,64,128]{2,1,0:T(8,128)(2,1)S(1)}, bf16[45,64,128]{2,1,0:T(8,128)(2,1)}, u32[]{:S(2)}) copy-start(bf16[45,64,128]{2,1,0:T(8,128)(2,1)} %winds_ref.1) | copy-start | bytes 2211844
  96.5 6.6 %copy-start.2 = (bf16[8,192,128]{2,1,0:T(8,128)(2,1)S(1)}, bf16[8,192,128]{2,1,0:T(8,128)(2,1)}, u32[]{:S(2)}) copy-start(bf16[8,192,128]{2,1,0:T(8,128)(2,1)} %copy-done.1) | copy-start | bytes 1179652
  96.5 6.6 %copy-start.4 = (bf16[192,128]{1,0:T(8,128)(2,1)S(1)}, bf16[192,128]{1,0:T(8,128)(2,1)}, u32[]{:S(2)}) copy-start(bf16[192,128]{1,0:T(8,128)(2,1)} %copy-done.3) | copy-start | bytes 147460
  96.5 6.6 %copy-start.7 = (s32[34]{0:T(128)S(1)}, s32[34]{0:T(128)}, u32[]{:S(2)}) copy-start(s32[34]{0:T(128)} %copy-done.6) | copy-start | bytes 412
